TPU v7x, 32 devices: a whole 2x2x4 slice. The times are simulated.
32 devices in a mesh: groups: 2 (over y), slide: 4 (over z), rep: 2 (over x), chan: 2 (over core).
Axes of the slice: x: 2, y: 2, z: 4, core: 2. Of those that a mesh axis runs over, the one named last changes fastest.
Arguments:
- tile_pixels: bfloat16 [4, 64, 6144], P(('groups', 'rep'), ('slide', 'chan')), parts along dimension 0, may hold values from -6 to 6
- tile_cell: int32 [4, 64], P(('groups', 'rep'), ('slide', 'chan')), parts along dimension 0, may hold values from -1 to 2047, as said below
- agg_cot: float32 [4, 64, 192, 128], P(('groups', 'rep'), 'slide', 'chan'), parts along dimension 0, may hold values from -6 to 6
- dw_weight: float32 [49, 96], replicated, may hold values from -0.6 to 0.6
- norm_gain: float32 [96], replicated, may hold values from 0.25 to 1.75
- up_weight: bfloat16 [96, 384], replicated, may hold values from -0.625 to 0.625
- proj_weight: bfloat16 [384, 96], replicated, may hold values from -0.3125 to 0.3125
- layer_scale: float32 [96], replicated, may hold values from 0.3 to 1
- ds_gain: float32 [96], replicated, may hold values from 0.25 to 1.75
- ds_weight: bfloat16 [384, 192], replicated, may hold values from -0.3125 to 0.3125
- agg_weight: bfloat16 [9, 192, 192], P(None, None, 'chan'), may hold values from -0.15625 to 0.15625
Outputs:
- agg_map: bfloat16 [4, 64, 192, 128], P(('groups', 'rep'), 'slide', 'chan'), parts along dimension 0
- agg_grad: float32 [18, 192, 192], P('groups', None, 'chan'), parts along dimension 0
- dw_grad: float32 [98, 96], P('groups'), parts along dimension 0
- up_grad: float32 [192, 384], P('groups'), parts along dimension 0
- proj_grad: float32 [768, 96], P('groups'), parts along dimension 0
- ds_grad: float32 [768, 192], P('groups'), parts along dimension 0
There are 2 independent parts, one for each index of `groups`. A program takes and returns all parts, laid end to end along the dimension named above; an argument that names none is the same for every part. Nothing has to cross between parts.
Inputs may be any that keep to these rules, and one draw needn't show every extreme that they name: `tile_cell`: A value r * 64 + q names a tile of grid row r and column q of a 32 x 64 slide grid; -1 marks an empty slot. No cell appears twice in one slide. Of the slots of one device (8 consecutive slots), at most 2 lie in one band of 8 tile rows, and in every slide one band holds exactly 2 tiles from every device.
All inputs are finite; a program needn't handle non-finite values.
Results may differ from a plain program's by a relative error of at most 0.018.
Values may be sent and summed in bfloat16 or wider, within the bound.
No kernel may reach another device: no remote copies, remote signals or barrier semaphores. Data moves between devices by JAX's collectives and lax.ppermute only.
A program may use at most 128 MiB of HBM per device.

v0:
```python
import math

import jax
import jax.numpy as jnp
from jax import lax
from jax.sharding import PartitionSpec as P

TILE_SIDE = 8
CAP = 2
GR = 8
GW = 64
BAND_CELLS = 512
FEAT = 3072


def shifted(value, axis, steps):
    count = lax.axis_size(axis)
    first, last = (max(0, -steps), min(count, count - steps))
    return lax.ppermute(value, axis, [(source, source + steps) for source in range(first, last)])


def layer_norm(values, gain):
    center = values - jnp.mean(values, axis=-1, keepdims=True)
    spread = jnp.mean(center * center, axis=-1, keepdims=True)
    return center * lax.rsqrt(spread + 1e-06) * gain


def stem(params, tile_rows):
    dw_weight, norm_gain, up_weight, proj_weight, layer_scale, ds_gain, ds_weight = params
    tile_count = tile_rows.shape[0]
    tile_side = TILE_SIDE
    channels = dw_weight.shape[1]
    inputs = tile_rows.reshape(tile_count, tile_side, tile_side, channels).astype(jnp.float32)
    padded = jnp.pad(inputs, ((0, 0), (3, 3), (3, 3), (0, 0)))
    spatial = jnp.zeros_like(inputs)
    for row_tap in range(7):
        for col_tap in range(7):
            spatial = (
                spatial
                + dw_weight[row_tap * 7 + col_tap]
                * padded[:, row_tap : row_tap + tile_side, col_tap : col_tap + tile_side, :]
            )
    normed = (
        layer_norm(spatial, norm_gain)
        .reshape(tile_count * tile_side * tile_side, channels)
        .astype(jnp.bfloat16)
    )
    hidden = jax.nn.gelu(
        jnp.dot(normed, up_weight, preferred_element_type=jnp.float32), approximate=False
    ).astype(jnp.bfloat16)
    branch = jnp.dot(hidden, proj_weight, preferred_element_type=jnp.float32)
    mixed_rows = inputs.reshape(tile_count * tile_side * tile_side, channels) + layer_scale * branch
    lowered = layer_norm(mixed_rows, ds_gain).astype(jnp.bfloat16)
    half_side = tile_side // 2
    patches = lowered.reshape(tile_count, half_side, 2, half_side, 2, channels).transpose(
        0, 1, 3, 2, 4, 5
    )
    patches = patches.reshape(tile_count * half_side * half_side, 4 * channels)
    result = jnp.dot(patches, ds_weight, preferred_element_type=jnp.float32)
    return result.reshape(tile_count, half_side * half_side * ds_weight.shape[1])


def aggregate(padded, weight_half):
    out_rows = (padded.shape[0] - 1) // 2
    out_cols = (padded.shape[1] - 1) // 2
    accumulated = jnp.zeros((out_rows * out_cols, weight_half.shape[2]), jnp.float32)
    for row_tap in range(3):
        for col_tap in range(3):
            window = padded[
                row_tap : row_tap + 2 * out_rows - 1 : 2,
                col_tap : col_tap + 2 * out_cols - 1 : 2,
                :,
            ]
            accumulated = accumulated + jnp.dot(
                window.reshape(out_rows * out_cols, padded.shape[2]),
                weight_half[row_tap * 3 + col_tap],
                preferred_element_type=jnp.float32,
            )
    return accumulated.reshape(out_rows, out_cols, weight_half.shape[2])


def on_device(
    tile_pixels,
    tile_cell,
    agg_cot,
    dw_weight,
    norm_gain,
    up_weight,
    proj_weight,
    layer_scale,
    ds_gain,
    ds_weight,
    agg_weight,
):
    params = (dw_weight, norm_gain, up_weight, proj_weight, layer_scale, ds_gain, ds_weight)
    tile_rows = tile_pixels[0]
    cell_ids = tile_cell[0]
    band_count = lax.axis_size("slide")
    chan_count = lax.axis_size("chan")
    feat_side = TILE_SIDE // 2
    checked_stem = jax.checkpoint(stem)
    tile_out, pull_stem = jax.vjp(lambda chosen: checked_stem(chosen, tile_rows), params)
    features = tile_out.astype(jnp.bfloat16)
    present = cell_ids >= 0
    dest_band = jnp.where(present, cell_ids // BAND_CELLS, band_count)
    within = jnp.where(present, cell_ids % BAND_CELLS, BAND_CELLS)
    slot_order = jnp.arange(cell_ids.shape[0], dtype=jnp.int32)
    earlier = (dest_band[:, None] == dest_band[None, :]) & (
        slot_order[None, :] < slot_order[:, None]
    )
    place_rank = jnp.sum(earlier.astype(jnp.int32), axis=1)
    position = jnp.where(present, dest_band * CAP + place_rank, band_count * CAP)
    send_rows = (
        jnp.zeros((band_count * CAP, FEAT), jnp.bfloat16).at[position].set(features, mode="drop")
    )
    send_cells = (
        jnp.full((band_count * CAP,), BAND_CELLS, jnp.int32).at[position].set(within, mode="drop")
    )
    own_rows, own_cells = (
        lax.all_to_all(send_rows, "slide", split_axis=0, concat_axis=0, tiled=True),
        lax.all_to_all(send_cells, "slide", split_axis=0, concat_axis=0, tiled=True),
    )
    recv_rows, recv_cells = (
        lax.all_gather(own_rows, "chan", axis=0, tiled=True),
        lax.all_gather(own_cells, "chan", axis=0, tiled=True),
    )
    cells_map = (
        jnp.zeros((BAND_CELLS, FEAT), jnp.bfloat16).at[recv_cells].set(recv_rows, mode="drop")
    )
    band_grid = cells_map.reshape(GR, GW, feat_side, feat_side, -1).transpose(0, 2, 1, 3, 4)
    band_grid = band_grid.reshape(GR * feat_side, GW * feat_side, -1)
    top_row = shifted(band_grid[-1], "slide", 1)
    padded = jnp.pad(jnp.concatenate([top_row[None], band_grid], axis=0), ((0, 0), (1, 0), (0, 0)))
    total_rows = agg_cot.shape[1] * band_count * lax.axis_size("rep") * agg_cot.shape[3]
    loss_scale = 1.0 / math.sqrt(total_rows)
    cotangent = agg_cot[0].transpose(0, 2, 1) * loss_scale
    result, pull_agg = jax.vjp(aggregate, padded, agg_weight)
    agg_map = result.astype(jnp.bfloat16).transpose(0, 2, 1)[None]
    d_padded, d_weight = pull_agg(cotangent)
    from_below = shifted(d_padded[0, 1:], "slide", -1)
    map_grad = (
        d_padded[1:, 1:]
        .astype(jnp.float32)
        .at[-1]
        .add(from_below.astype(jnp.float32))
        .astype(jnp.bfloat16)
    )
    grad_cells = (
        map_grad.reshape(GR, feat_side, GW, feat_side, -1)
        .transpose(0, 2, 1, 3, 4)
        .reshape(BAND_CELLS, FEAT)
    )
    slot_grads = jnp.where(
        (recv_cells < BAND_CELLS)[:, None],
        grad_cells[jnp.minimum(recv_cells, BAND_CELLS - 1)],
        jnp.zeros((), jnp.bfloat16),
    )
    by_source = slot_grads.reshape(chan_count, band_count, CAP, FEAT).transpose(1, 0, 2, 3)
    by_source = by_source.reshape(band_count * chan_count * CAP, FEAT)
    arrived = lax.all_to_all(by_source, "slide", split_axis=0, concat_axis=0, tiled=True)
    arrived = arrived.reshape(band_count, chan_count, CAP, FEAT).astype(jnp.float32)
    summed = lax.psum_scatter(
        arrived.astype(jnp.bfloat16), "chan", scatter_dimension=1, tiled=True
    ).astype(jnp.float32)
    gathered_grads = summed.reshape(band_count * CAP, FEAT)
    feature_grad = jnp.where(
        present[:, None], gathered_grads[jnp.minimum(position, band_count * CAP - 1)], 0.0
    )
    stem_grads = pull_stem(feature_grad)[0]
    dw_term = stem_grads[0]
    up_term = stem_grads[2].astype(jnp.float32)
    proj_term = stem_grads[3].astype(jnp.float32)
    ds_term = stem_grads[6].astype(jnp.float32)
    agg_term = d_weight.astype(jnp.float32)
    half_width = agg_term.shape[2]
    embedded = lax.dynamic_update_slice(
        jnp.zeros((9, agg_term.shape[1], half_width * chan_count), jnp.float32),
        agg_term,
        (0, 0, lax.axis_index("chan") * half_width),
    )
    summed_all = lax.psum(
        (dw_term, up_term, proj_term, ds_term, embedded), ("slide", "rep", "chan")
    )
    dw_grad = summed_all[0]
    up_grad = summed_all[1]
    proj_grad = summed_all[2]
    ds_grad = summed_all[3]
    agg_grad = lax.dynamic_slice_in_dim(
        summed_all[4], lax.axis_index("chan") * half_width, half_width, 2
    )
    return (agg_map, agg_grad, dw_grad, up_grad, proj_grad, ds_grad)


def solution(mesh):
    in_specs = (
        P(("groups", "rep"), ("slide", "chan"), None),
        P(("groups", "rep"), ("slide", "chan")),
        P(("groups", "rep"), "slide", "chan", None),
        P(),
        P(),
        P(),
        P(),
        P(),
        P(),
        P(),
        P(None, None, "chan"),
    )
    out_specs = (
        P(("groups", "rep"), "slide", "chan", None),
        P("groups", None, "chan"),
        P("groups", None),
        P("groups", None),
        P("groups", None),
        P("groups", None),
    )
    return jax.shard_map(
        on_device, mesh=mesh, in_specs=in_specs, out_specs=out_specs, check_vma=False
    )
```

profile of v0, /device:TPU:0, one launch (start us, length us, event | category | flops | bytes accessed | tf_op | source)
XLA Modules:
  0.0 863.3 jit_solution(13993026256152667323)
XLA Ops:
  18.9 31.4 %pad.226 = bf16[33,257,192]{1,2,0:T(8,128)(2,1)} pad(bf16[16,128,192]{1,2,0:T(8,128)(2,1)} %bitcast.629, bf16[]{:T(256)} %constant.57.clone.1), padding=2_0_1x2_0_1x0_0_0 | pad | bytes 4043138 | tf_op jit(solution)/shard_map/transpose(jvp())/pad | solution.py:69
  50.3 30.9 %pad.227 = bf16[33,257,192]{1,2,0:T(8,128)(2,1)} pad(bf16[16,128,192]{1,2,0:T(8,128)(2,1)} %bitcast.630, bf16[]{:T(256)} %constant.57.clone.1), padding=2_0_1x1_1_1x0_0_0 | pad | bytes 4043138 | tf_op jit(solution)/shard_map/transpose(jvp())/pad | solution.py:69
  81.2 2.2 copy.253
  83.5 31.0 %pad.228 = bf16[33,257,192]{1,2,0:T(8,128)(2,1)} pad(bf16[16,128,192]{1,2,0:T(8,128)(2,1)} %bitcast.631, bf16[]{:T(256)} %constant.57.clone.1), padding=2_0_1x0_2_1x0_0_0 | pad | bytes 4043138 | tf_op jit(solution)/shard_map/transpose(jvp())/pad | solution.py:69
  114.4 2.2 copy.252
  116.7 30.9 %pad.229 = bf16[33,257,192]{1,2,0:T(8,128)(2,1)} pad(bf16[16,128,192]{1,2,0:T(8,128)(2,1)} %bitcast.632, bf16[]{:T(256)} %constant.57.clone.1), padding=1_1_1x2_0_1x0_0_0 | pad | bytes 4043138 | tf_op jit(solution)/shard_map/transpose(jvp())/pad | solution.py:69
  147.5 2.2 copy.251
  149.8 30.9 %pad.230 = bf16[33,257,192]{1,2,0:T(8,128)(2,1)} pad(bf16[16,128,192]{1,2,0:T(8,128)(2,1)} %bitcast.633, bf16[]{:T(256)} %constant.57.clone.1), padding=1_1_1x1_1_1x0_0_0 | pad | bytes 4043138 | tf_op jit(solution)/shard_map/transpose(jvp())/pad | solution.py:69
  181.8 30.9 %pad.231 = bf16[33,257,192]{1,2,0:T(8,128)(2,1)} pad(bf16[16,128,192]{1,2,0:T(8,128)(2,1)} %bitcast.634, bf16[]{:T(256)} %constant.57.clone.1), padding=1_1_1x0_2_1x0_0_0 | pad | bytes 4043138 | tf_op jit(solution)/shard_map/transpose(jvp())/pad | solution.py:69
  212.9 30.2 %pad.232 = bf16[33,257,192]{1,2,0:T(8,128)(2,1)} pad(bf16[16,128,192]{1,2,0:T(8,128)(2,1)S(1)} %bitcast.635, bf16[]{:T(256)} %constant.57.clone.1), padding=0_2_1x2_0_1x0_0_0 | pad | bytes 4043138 | tf_op jit(solution)/shard_map/transpose(jvp())/pad | solution.py:69
  243.3 30.0 %pad.233 = bf16[33,257,192]{1,2,0:T(8,128)(2,1)} pad(bf16[16,128,192]{1,2,0:T(8,128)(2,1)S(1)} %bitcast.636, bf16[]{:T(256)} %constant.57.clone.1), padding=0_2_1x1_1_1x0_0_0 | pad | bytes 4043138 | tf_op jit(solution)/shard_map/transpose(jvp())/pad | solution.py:69
  273.4 30.0 %pad.234 = bf16[33,257,192]{1,2,0:T(8,128)(2,1)} pad(bf16[16,128,192]{1,2,0:T(8,128)(2,1)S(1)} %bitcast.637, bf16[]{:T(256)} %constant.57.clone.1), padding=0_2_1x0_2_1x0_0_0 | pad | bytes 4043138 | tf_op jit(solution)/shard_map/transpose(jvp())/pad | solution.py:69
  303.5 14.5 %add_add_fusion = bf16[33,257,192]{1,2,0:T(8,128)(2,1)S(1)} fusion(bf16[33,257,192]{1,2,0:T(8,128)(2,1)} %pad.234, bf16[33,257,192]{1,2,0:T(8,128)(2,1)} %pad.233, bf16[33,257,192]{1,2,0:T(8,128)(2,1)} %pad.232, bf16[33,257,192]{1,2,0:T(8,128)(2,1)} %pad.231, bf16[33,257,192]{1,2,0:T(8,128)(2,1)} %pad.230, bf16[33,257,192]{1,2,0:T(8,128)(2,1)} %pad.229, ...), kind=kLoop, calls=%fused_computation.105 | loop fusion | flops 13026816 | bytes 32567040 | tf_op jit(solution)/shard_map/transpose(jvp())/add_any | solution.py:69
  318.0 2.3 copy-done.2
  323.2 8.2 all-to-all-start
  331.4 6.3 slice_convert_fusion
  346.7 5.1 all-to-all-start.1
  355.3 2.2 all-to-all-done.1
  359.5 2.3 scatter_custom_fusion.2
  361.9 6.3 reshape.714
  368.2 6.5 copy.108
  374.6 7.6 reshape.715
  382.2 5.5 copy.109
  388.3 3.4 collective-permute-start
  393.4 4.9 convert_element_type.212
  398.3 6.1 copy.132
  404.4 7.1 reshape.736
  411.4 5.8 copy.133
  417.2 8.5 reshape.737
  425.7 3.0 gather_fusion
  431.1 3.3 all-to-all-start.2
  434.5 6.2 fusion.2
  440.6 28.3 %slice.767 = bf16[16,128,192]{1,2,0:T(8,128)(2,1)S(1)} slice(bf16[33,257,192]{1,2,0:T(8,128)(2,1)} %fusion.2), slice={[0:31:2], [0:255:2], [0:192:1]} | slice | bytes 1572864 | tf_op jit(solution)/shard_map/jvp()/slice | solution.py:69
  468.9 28.7 %slice.769 = bf16[16,128,192]{1,2,0:T(8,128)(2,1)} slice(bf16[33,257,192]{1,2,0:T(8,128)(2,1)} %fusion.2), slice={[0:31:2], [1:256:2], [0:192:1]} | slice | bytes 1572864 | tf_op jit(solution)/shard_map/jvp()/slice | solution.py:69
  497.7 28.7 %slice.771 = bf16[16,128,192]{1,2,0:T(8,128)(2,1)} slice(bf16[33,257,192]{1,2,0:T(8,128)(2,1)} %fusion.2), slice={[0:31:2], [2:257:2], [0:192:1]} | slice | bytes 1572864 | tf_op jit(solution)/shard_map/jvp()/slice | solution.py:69
  526.4 28.8 %slice.773 = bf16[16,128,192]{1,2,0:T(8,128)(2,1)} slice(bf16[33,257,192]{1,2,0:T(8,128)(2,1)} %fusion.2), slice={[1:32:2], [0:255:2], [0:192:1]} | slice | bytes 1572864 | tf_op jit(solution)/shard_map/jvp()/slice | solution.py:69
  555.2 28.7 %slice.775 = bf16[16,128,192]{1,2,0:T(8,128)(2,1)} slice(bf16[33,257,192]{1,2,0:T(8,128)(2,1)} %fusion.2), slice={[1:32:2], [1:256:2], [0:192:1]} | slice | bytes 1572864 | tf_op jit(solution)/shard_map/jvp()/slice | solution.py:69
  583.9 28.7 %slice.777 = bf16[16,128,192]{1,2,0:T(8,128)(2,1)} slice(bf16[33,257,192]{1,2,0:T(8,128)(2,1)} %fusion.2), slice={[1:32:2], [2:257:2], [0:192:1]} | slice | bytes 1572864 | tf_op jit(solution)/shard_map/jvp()/slice | solution.py:69
  612.6 29.0 %slice.779 = bf16[16,128,192]{1,2,0:T(8,128)(2,1)} slice(bf16[33,257,192]{1,2,0:T(8,128)(2,1)} %fusion.2), slice={[2:33:2], [0:255:2], [0:192:1]} | slice | bytes 1572864 | tf_op jit(solution)/shard_map/jvp()/slice | solution.py:69
  641.6 28.2 %slice.781 = bf16[16,128,192]{1,2,0:T(8,128)(2,1)S(1)} slice(bf16[33,257,192]{1,2,0:T(8,128)(2,1)} %fusion.2), slice={[2:33:2], [1:256:2], [0:192:1]} | slice | bytes 1572864 | tf_op jit(solution)/shard_map/jvp()/slice | solution.py:69
  669.8 28.3 %slice.783 = bf16[16,128,192]{1,2,0:T(8,128)(2,1)S(1)} slice(bf16[33,257,192]{1,2,0:T(8,128)(2,1)} %fusion.2), slice={[2:33:2], [2:257:2], [0:192:1]} | slice | bytes 1572864 | tf_op jit(solution)/shard_map/jvp()/slice | solution.py:69
  699.8 2.1 fusion.34
  712.9 3.2 dynamic_update_slice.3
  716.1 15.7 %all-reduce.76.cloned.1.call-done = bf16[4,2,2,3072]{3,0,2,1:T(4,128)(2,1)} async-done(((bf16[4,2,2,3072]{3,0,2,1:T(4,128)(2,1)}), bf16[4,2,2,3072]{3,0,2,1:T(4,128)(2,1)}) %all-reduce.76.cloned.1.call-update) | async-done | bytes 98320
  736.5 3.8 multiply_convert_fusion
  749.9 62.6 %psum.36 = f32[49,96]{1,0:T(8,128)} all-reduce(f32[49,96]{1,0:T(8,128)S(1)} %pad_add_fusion), channel_id=1, replica_groups=mesh['groups'=2,'slide'=4,'rep'=2,'chan'=2] {'slide','rep','chan'}, use_global_device_ids=true, to_apply=%region_67.68 | all-reduce | flops 4704 | bytes 37632 | tf_op jit(solution)/shard_map/psum | solution.py:181
  812.5 36.1 %all-reduce.78.cloned.1.call-done = (f32[9,192,192]{2,1,0:T(8,128)}, f32[96,384]{1,0:T(8,128)}, f32[384,96]{0,1:T(8,128)}, f32[384,192]{0,1:T(8,128)}) async-done(((f32[9,192,192]{2,1,0:T(8,128)}, f32[96,384]{1,0:T(8,128)}, f32[384,96]{0,1:T(8,128)}, f32[384,192]{0,1:T(8,128)}), (f32[9,192,192]{2,1,0:T(8,128)}, f32[96,384]{1,0:T(8,128)}, f32[384,96]{0,1:T(8,128)}, ...) | async-done | bytes 1916944 | tf_op jit(solution)/shard_map/psum | solution.py:181
  848.6 2.7 constant_dynamic-slice_fusion
  (210 shorter events, 65.9 us)
Async XLA Ops:
  7.2 336.4 %copy-start = (bf16[384,192]{0,1:T(8,128)(2,1)S(1)}, bf16[384,192]{0,1:T(8,128)(2,1)}, u32[]{:S(2)}) copy-start(bf16[384,192]{0,1:T(8,128)(2,1)} %param.22) | copy-start | bytes 442372
  7.2 5.6 copy-start.10
  303.5 18.2 %copy-start.31 = (s32[1,8]{1,0:T(1,128)S(1)}, s32[1,8]{1,0:T(1,128)}, u32[]{:S(2)}) copy-start(s32[1,8]{1,0:T(1,128)} %param.14) | copy-start | bytes 100
  318.0 2.3 copy-start.2
  320.2 18.1 %copy-start.20 = (f32[49,96]{1,0:T(8,128)S(1)}, f32[49,96]{1,0:T(8,128)}, u32[]{:S(2)}) copy-start(f32[49,96]{1,0:T(8,128)} %param.16) | copy-start | bytes 56452
  320.2 18.1 %copy-start.12 = (bf16[1,8,6144]{2,1,0:T(8,128)(2,1)S(1)}, bf16[1,8,6144]{2,1,0:T(8,128)(2,1)}, u32[]{:S(2)}) copy-start(bf16[1,8,6144]{2,1,0:T(8,128)(2,1)} %param.13) | copy-start | bytes 294916
  320.3 71.3 %collective-permute-start.1 = (bf16[256,192]{0,1:T(8,128)(2,1)S(1)}, bf16[256,192]{0,1:T(8,128)(2,1)}, u32[]{:S(2)}, u32[]{:S(2)}) collective-permute-start(bf16[256,192]{0,1:T(8,128)(2,1)S(1)} %slice_bitcast_fusion), channel_id=1, source_target_pairs={{4,0},{8,4},{12,8},{5,1},{9,5},{13,9},{6,2},{10,6},{14,10},{7,3},{... | collective-permute-start | bytes 294920 | tf_op jit(solution)/shard_map/ppermute | solution.py:19
  323.2 23.5 %all-to-all-start = ((s32[4,2,1]{1,2,0:T(1,128)}), s32[4,2,1]{1,2,0:T(1,128)S(1)}, u32[]{:S(2)}, u32[]{:S(2)}) async-start(s32[4,2,1]{1,2,0:T(1,128)} %bitcast.5), calls=%async_computation | async-start | bytes 4096 | tf_op jit(solution)/shard_map/all_to_all | solution.py:121
  331.4 9.3 %copy-start.26 = (f32[96]{0:T(128)S(1)}, f32[96]{0:T(128)}, u32[]{:S(2)}) copy-start(f32[96]{0:T(128)} %param.17) | copy-start | bytes 1156
  331.4 9.5 %copy-start.22 = (bf16[384,96]{0,1:T(8,128)(2,1)S(1)}, bf16[384,96]{0,1:T(8,128)(2,1)}, u32[]{:S(2)}) copy-start(bf16[384,96]{0,1:T(8,128)(2,1)} %param.19) | copy-start | bytes 221188
  331.4 9.5 %copy-start.24 = (bf16[96,384]{1,0:T(8,128)(2,1)S(1)}, bf16[96,384]{1,0:T(8,128)(2,1)}, u32[]{:S(2)}) copy-start(bf16[96,384]{1,0:T(8,128)(2,1)} %param.18) | copy-start | bytes 221188
  331.4 9.5 %copy-start.28 = (f32[96]{0:T(128)S(1)}, f32[96]{0:T(128)}, u32[]{:S(2)}) copy-start(f32[96]{0:T(128)} %param.20) | copy-start | bytes 1156
  341.0 2.2 copy-start.27
  341.0 4.4 copy-start.29
  346.7 10.8 %all-to-all-start.1 = ((bf16[4,2,3072]{2,1,0:T(2,128)(2,1)}), bf16[4,2,3072]{2,1,0:T(2,128)(2,1)S(1)}, u32[]{:S(2)}, u32[]{:S(2)}) async-start(bf16[4,2,3072]{2,1,0:T(2,128)(2,1)} %all_to_all.25), calls=%async_computation.1 | async-start | bytes 98304 | tf_op jit(solution)/shard_map/all_to_all | solution.py:120
  388.3 46.2 %collective-permute-start = (bf16[256,192]{0,1:T(8,128)(2,1)}, bf16[256,192]{0,1:T(8,128)(2,1)}, u32[]{:S(2)}, u32[]{:S(2)}) collective-permute-start(bf16[256,192]{0,1:T(8,128)(2,1)} %slice_bitcast_fusion.1), channel_id=1, source_target_pairs={{0,4},{4,8},{8,12},{1,5},{5,9},{9,13},{2,6},{6,10},{10,14},{3,7},{... | collective-permute-start | bytes 294920 | tf_op jit(solution)/shard_map/ppermute | solution.py:19
  431.1 280.6 %all-to-all-start.2 = ((bf16[4,4,3072]{2,1,0:T(4,128)(2,1)}), bf16[4,4,3072]{2,1,0:T(4,128)(2,1)S(1)}, u32[]{:S(2)}, u32[]{:S(2)}) async-start(bf16[4,4,3072]{2,1,0:T(4,128)(2,1)} %copy.135), calls=%async_computation.2 | async-start | bytes 196608 | tf_op jit(solution)/shard_map/all_to_all | solution.py:160
  434.4 297.3 %all-reduce.76.cloned.1.call-start = ((), (), s32[]{:S(2)}) async-start(), calls=%async_computation.3 | async-start | bytes 196608
  526.4 171.7 %copy-start.1 = (f32[1,16,96,128]{3,2,1,0:T(8,128)S(1)}, f32[1,16,96,128]{3,2,1,0:T(8,128)}, u32[]{:S(2)}) copy-start(f32[1,16,96,128]{3,2,1,0:T(8,128)} %param.15) | copy-start | bytes 2359300
  698.1 3.9 copy-start.7
  698.1 4.8 copy-start.6
  698.1 5.8 copy-start.5
  698.1 6.8 copy-start.4
  698.5 7.4 copy-start.3
  702.0 5.9 copy-start.8
  702.0 5.9 copy-start.11
  709.4 3.0 copy-start.13
  709.4 3.0 copy-start.14
  709.5 3.0 copy-start.15
  709.5 3.0 copy-start.16
  709.5 3.0 copy-start.17
  709.5 3.0 copy-start.18
  709.5 3.0 copy-start.19
  710.1 23.7 %copy-start.30 = (pred[8]{0:T(512)(128)(4,1)S(1)}, pred[8]{0:T(512)(128)(4,1)}, u32[]{:S(2)}) copy-start(pred[8]{0:T(512)(128)(4,1)} %bitcast_compare_fusion) | copy-start | bytes 28
  710.2 23.8 %copy-start.21 = (f32[49,96]{1,0:T(8,128)S(1)}, f32[49,96]{1,0:T(8,128)}, u32[]{:S(2)}) copy-start(f32[49,96]{1,0:T(8,128)} %param.16) | copy-start | bytes 56452
  712.4 136.2 %all-reduce.78.cloned.1.call-start = ((), (), s32[]{:S(2)}) async-start(), calls=%async_computation.4 | async-start | bytes 4718592 | tf_op jit(solution)/shard_map/psum | solution.py:181
  716.1 24.2 %copy-start.9 = (f32[9,192,192]{2,1,0:T(8,128)}, f32[9,192,192]{2,1,0:T(8,128)S(1)}, u32[]{:S(2)}) copy-start(f32[9,192,192]{2,1,0:T(8,128)S(1)} %dynamic_update_slice.3) | copy-start | bytes 3981316
  736.5 3.8 copy-start.23
  740.3 4.3 copy-start.25
Sparse Core Ops, SparseCore 0:
  712.5 19.1 all-reduce.75
  748.0 100.5 all-reduce.77
where the time goes:
time: 869 us; the launch traced here: 863 us
  local copies, waits for them, and re-layouts  628 us (72%)
  blocking collectives  66.4 us (8%)
  waiting for transfers between devices  54.1 us (6%)
  other arithmetic  44.9 us (5%)
  matrix products  32.1 us (4%)
  starting transfers between devices  21.4 us (2%)
  between operations  16 us (2%)
    pad x9, local copies, waits for them, and re-layouts, aggregate(): padded[row_tap:row_tap + 2 * out_rows - 1:2, col_tap:col_tap + 2 * out_co...  276 us
    slice x9, local copies, waits for them, and re-layouts, aggregate(): padded[row_tap:row_tap + 2 * out_rows - 1:2, col_tap:col_tap + 2 * out_co...  257 us
    psum x1, blocking collectives, on_device(): lax.psum((dw_term, up_term, proj_term, ds_term, embedded), ('slide', 'rep...  62.6 us
    psum x1, waiting for transfers between devices, on_device(): lax.psum((dw_term, up_term, proj_term, ds_term, embedded), ('slide', 'rep...  36.1 us
    dot_general x27, matrix products, aggregate(): jnp.dot(window.reshape(out_rows * out_cols, padded.shape[2]), weight_half...  20.7 us
  transfers between devices with their start and end apart: 7, of which 3 were waited for; matrix products, arithmetic and copies ran while one was open for 42% of the time, Pallas kernels for 0%

commit v1 on v0

v1 whole, which is shorter than its diff:
```python
import math

import jax
import jax.numpy as jnp
from jax import lax
from jax.experimental import pallas as pl
from jax.experimental.pallas import tpu as pltpu
from jax.sharding import PartitionSpec as P

SIDE = 8
CAP = 2
GW = 64
BAND_CELLS = 512
PIX = SIDE * SIDE
META = 128
HALF_ROWS = 656
GATHER_LIMIT = 16 << 20
F32 = jnp.float32
BF16 = jnp.bfloat16
VMEM = pl.BlockSpec(memory_space=pltpu.VMEM)
SMEM = pl.BlockSpec(memory_space=pltpu.SMEM)


def params_of(steps=1):
    return pltpu.CompilerParams(
        dimension_semantics=("arbitrary",) * steps, vmem_limit_bytes=48 << 20
    )


def nn(left, right):
    return lax.dot_general(left, right, (((1,), (0,)), ((), ())), preferred_element_type=F32)


def nt(left, right):
    return lax.dot_general(left, right, (((1,), (1,)), ((), ())), preferred_element_type=F32)


def tn(left, right):
    return lax.dot_general(left, right, (((0,), (0,)), ((), ())), preferred_element_type=F32)


def shifted(value, axis, steps):
    count = lax.axis_size(axis)
    first, last = (max(0, -steps), min(count, count - steps))
    return lax.ppermute(value, axis, [(source, source + steps) for source in range(first, last)])


def swapped(value, axis, step):
    count = lax.axis_size(axis)
    return lax.ppermute(value, axis, [(place, place ^ step) for place in range(count)])


def reach(tap):
    return (1, 2) if tap == 0 else (0, 1)


def pack_kernel(cells_ref, pixels_ref, out_ref):
    slots = pixels_ref.shape[0]
    rows = out_ref.shape[0]
    pixch = pixels_ref.shape[1]
    cells = [cells_ref[0, t] for t in range(slots)]
    live = [cell >= 0 for cell in cells]
    bands = [cell // BAND_CELLS for cell in cells]
    places = []
    for t in range(slots):
        rank = jnp.int32(0)
        for s in range(t):
            rank = rank + ((bands[s] == bands[t]) & live[s]).astype(jnp.int32)
        places.append(jnp.where(live[t], bands[t] * CAP + rank, -1))
    dest = lax.broadcasted_iota(jnp.int32, (rows, slots), 0)
    slot = lax.broadcasted_iota(jnp.int32, (rows, slots), 1)
    place = jnp.full((rows, slots), -1, jnp.int32)
    for t in range(slots):
        place = jnp.where(slot == t, places[t], place)
    route = (place == dest).astype(F32).astype(BF16)
    out_ref[:, :pixch] = nn(route, pixels_ref[...]).astype(BF16)
    lane = lax.broadcasted_iota(jnp.int32, (rows, META), 1)
    base = (lax.broadcasted_iota(jnp.int32, (rows, META), 0) // CAP) * CAP
    notes = jnp.zeros((rows, META), F32)
    for t in range(slots):
        within = cells[t] % BAND_CELLS
        own_row = (within // GW).astype(F32)
        own_col = (within % GW).astype(F32)
        for rank in range(CAP):
            hit = base + rank == places[t]
            for at, value in enumerate((own_row, own_col, jnp.float32(1.0))):
                notes = jnp.where(hit & (lane == 3 * rank + at), value, notes)
    out_ref[:, pixch:] = notes.astype(BF16)


def patch_kernel(chan_ref, meta_ref, cot_ref, below_ref, key_ref, all_ref, own_ref, send_ref):
    sources = meta_ref.shape[0]
    chunks = sources // 8
    out_rows = cot_ref.shape[0]
    meta = meta_ref[...].astype(F32)
    lane = lax.broadcasted_iota(jnp.int32, (8, 128), 1).astype(F32)
    blocks = []
    for rank in range(CAP):
        for chunk in range(chunks):
            part = meta[chunk * 8 : chunk * 8 + 8]
            row = jnp.broadcast_to(part[:, 3 * rank : 3 * rank + 1], (8, 128))
            col = jnp.broadcast_to(part[:, 3 * rank + 1 : 3 * rank + 2], (8, 128))
            valid = jnp.broadcast_to(part[:, 3 * rank + 2 : 3 * rank + 3], (8, 128)) > 0.5
            for u in range(3):
                for v in range(3):
                    hit = (lane == 2.0 * col + v) & valid
                    blocks.append(jnp.where(hit, 2.0 * row + u, -1.0))
    key = jnp.concatenate(blocks, axis=0)
    key_ref[...] = key

    def step(o, total):
        pick = (key == o.astype(F32)).astype(F32).astype(BF16)
        return total + nt(pick, cot_ref[o].astype(BF16))

    total = lax.fori_loop(
        0, out_rows, step, jnp.zeros((key.shape[0], cot_ref.shape[1]), F32), unroll=4
    )
    pick = (key == float(out_rows)).astype(F32).astype(BF16)
    total = total + nt(pick, below_ref[...])
    total = total.astype(BF16)
    all_ref[...] = total
    half = total.shape[0] // CAP
    first = chan_ref[0] == 0
    low, high = total[:half].astype(F32), total[half:].astype(F32)
    own_ref[...] = jnp.where(first, low, high).astype(BF16)
    send_ref[...] = jnp.where(first, high, low).astype(BF16)


def center_of(values):
    center = values - jnp.mean(values, axis=-1, keepdims=True)
    rstd = lax.rsqrt(jnp.mean(center * center, axis=-1, keepdims=True) + 1e-06)
    return center * rstd, rstd


def fill_padded(padded_ref, pixels_ref, channels):
    padded_ref[...] = jnp.zeros_like(padded_ref)
    for i in range(SIDE):
        for j in range(SIDE):
            at = (i * SIDE + j) * channels
            padded_ref[i + 3, j + 3] = pixels_ref[:, at : at + channels].astype(F32)


def stem_kernel(
    pixels_ref, dw_ref, gain_ref, up_ref, proj_ref, scale_ref, ds_gain_ref, ds_ref,
    feat_ref, hat1_ref, rstd1_ref, hat2_ref, rstd2_ref, hidden_ref, slope_ref,
    padded_ref, spatial_ref, low_ref,
):
    channels = dw_ref.shape[1]
    fill_padded(padded_ref, pixels_ref, channels)

    def row_step(i, carry):
        total = jnp.zeros((SIDE, 8, channels), F32)
        for a in range(7):
            for b in range(7):
                weight = dw_ref[pl.ds(7 * a + b, 1), :].reshape(1, 1, channels)
                total = total + weight * padded_ref[i + a, b : b + SIDE]
        spatial_ref[i] = total
        return carry

    lax.fori_loop(0, SIDE, row_step, 0)
    hat1, rstd1 = center_of(spatial_ref[...].reshape(PIX * 8, channels))
    hat1_ref[...] = hat1
    rstd1_ref[...] = rstd1
    normed = (hat1 * gain_ref[...]).astype(BF16)
    before = nn(normed, up_ref[...])
    cdf = 0.5 * (1.0 + lax.erf(before * math.sqrt(0.5)))
    pdf = jnp.exp(-0.5 * before * before) * (1.0 / math.sqrt(2.0 * math.pi))
    hidden = (before * cdf).astype(BF16)
    hidden_ref[...] = hidden
    slope_ref[...] = cdf + before * pdf
    branch = nn(hidden, proj_ref[...])
    inputs = padded_ref[3 : 3 + SIDE, 3 : 3 + SIDE].reshape(PIX * 8, channels)
    hat2, rstd2 = center_of(inputs + scale_ref[...] * branch)
    hat2_ref[...] = hat2
    rstd2_ref[...] = rstd2
    low_ref[...] = (hat2 * ds_gain_ref[...]).reshape(low_ref.shape)
    half = SIDE // 2
    total = jnp.zeros((half * half * 8, ds_ref.shape[1]), F32)
    for di in range(2):
        for dj in range(2):
            part = low_ref[:, di, :, dj].reshape(half * half * 8, channels).astype(BF16)
            at = (2 * di + dj) * channels
            total = total + nn(part, ds_ref[at : at + channels])
    feat_ref[...] = total.astype(BF16)


def back_kernel(
    chan_ref, own_ref, peer_ref, w_own_ref, w_peer_ref, pixels_ref,
    hat1_ref, rstd1_ref, hat2_ref, rstd2_ref, hidden_ref, slope_ref,
    gain_ref, up_ref, proj_ref, scale_ref, ds_gain_ref, ds_ref,
    keep_ref, send_ref,
    padded_ref, low_ref, dlow_ref, dspatial_ref, dw_ref, ds_acc, up_acc, proj_acc, pack_ref,
    *, scale,
):
    channels = gain_ref.shape[1]
    width = w_own_ref.shape[1]
    half = SIDE // 2
    step = pl.program_id(0)

    @pl.when(step == 0)
    def _():
        dw_ref[...] = jnp.zeros_like(dw_ref)
        ds_acc[...] = jnp.zeros_like(ds_acc)
        up_acc[...] = jnp.zeros_like(up_acc)
        proj_acc[...] = jnp.zeros_like(proj_acc)

    own = own_ref[...].astype(F32).reshape(9, 8, own_ref.shape[1])
    peer = peer_ref[...].astype(F32).reshape(9, 8, peer_ref.shape[1])
    grads = {}
    for a in range(3):
        for b in range(3):
            places = [(u, v) for u in reach(a) for v in reach(b)]
            left_own = jnp.concatenate([own[3 * u + v] for u, v in places], axis=0).astype(BF16)
            left_peer = jnp.concatenate([peer[3 * u + v] for u, v in places], axis=0).astype(BF16)
            out = nt(left_own, w_own_ref[3 * a + b]) + nt(left_peer, w_peer_ref[3 * a + b])
            for n, (u, v) in enumerate(places):
                at = (2 * u + a - 1) * half + 2 * v + b - 1
                piece = out[8 * n : 8 * n + 8]
                grads[at] = grads[at] + piece if at in grads else piece
    dfeat = jnp.concatenate([grads[at] for at in range(half * half)], axis=0) * scale
    dfeat = dfeat.astype(BF16)

    hat2 = hat2_ref[...]
    low_ref[...] = (hat2 * ds_gain_ref[...]).reshape(low_ref.shape)
    for di in range(2):
        for dj in range(2):
            at = (2 * di + dj) * channels
            part = low_ref[:, di, :, dj].reshape(half * half * 8, channels).astype(BF16)
            ds_acc[at : at + channels, :] += tn(part, dfeat)
            back = nt(dfeat, ds_ref[at : at + channels])
            dlow_ref[:, di, :, dj] = back.reshape(half, half, 8, channels)
    dhat2 = dlow_ref[...].reshape(PIX * 8, channels) * ds_gain_ref[...]
    mean_a = jnp.mean(dhat2, axis=-1, keepdims=True)
    mean_b = jnp.mean(dhat2 * hat2, axis=-1, keepdims=True)
    dmixed = rstd2_ref[...] * (dhat2 - mean_a - hat2 * mean_b)
    dbranch = (dmixed * scale_ref[...]).astype(BF16)
    proj_acc[...] += tn(hidden_ref[...], dbranch)
    dhidden = nt(dbranch, proj_ref[...])
    dbefore = (dhidden * slope_ref[...]).astype(BF16)
    hat1 = hat1_ref[...]
    normed = (hat1 * gain_ref[...]).astype(BF16)
    up_acc[...] += tn(normed, dbefore)
    dhat1 = nt(dbefore, up_ref[...]) * gain_ref[...]
    mean_a = jnp.mean(dhat1, axis=-1, keepdims=True)
    mean_b = jnp.mean(dhat1 * hat1, axis=-1, keepdims=True)
    dspatial = rstd1_ref[...] * (dhat1 - mean_a - hat1 * mean_b)
    dspatial_ref[...] = dspatial.reshape(SIDE, SIDE, 8, channels)
    fill_padded(padded_ref, pixels_ref, channels)

    def tap_step(a, carry):
        totals = [jnp.zeros((8, channels), F32) for _ in range(7)]
        for i in range(SIDE):
            grad = dspatial_ref[i]
            for b in range(7):
                product = padded_ref[i + a, b : b + SIDE] * grad
                totals[b] = totals[b] + jnp.sum(product, axis=0)
        for b in range(7):
            dw_ref[a, b] += totals[b]
        return carry

    lax.fori_loop(0, 7, tap_step, 0)

    @pl.when(step == pl.num_programs(0) - 1)
    def _():
        pack_ref[...] = jnp.zeros_like(pack_ref)
        pack_ref[0:384, :] = ds_acc[:, 0:128]
        pack_ref[384:576, 0:64] = ds_acc[0:192, 128:192]
        pack_ref[384:576, 64:128] = ds_acc[192:384, 128:192]
        for n in range(3):
            pack_ref[576 + 96 * n : 672 + 96 * n, :] = up_acc[:, 128 * n : 128 * n + 128]
        pack_ref[864:1248, 0:channels] = proj_acc[...]
        pack_ref[1248:1297, 0:channels] = jnp.sum(dw_ref[...], axis=2).reshape(49, channels)
        mine = pl.multiple_of(chan_ref[0] * HALF_ROWS, 8)
        other = pl.multiple_of((1 - chan_ref[0]) * HALF_ROWS, 8)
        keep_ref[...] = pack_ref[pl.ds(mine, HALF_ROWS), :]
        send_ref[...] = pack_ref[pl.ds(other, HALF_ROWS), :].astype(BF16)


def unpack_kernel(pack_ref, dw_ref, up_ref, proj_ref, ds_ref):
    channels = dw_ref.shape[1]
    ds_ref[:, 0:128] = pack_ref[0:384, :]
    ds_ref[0:192, 128:192] = pack_ref[384:576, 0:64]
    ds_ref[192:384, 128:192] = pack_ref[384:576, 64:128]
    for n in range(3):
        up_ref[:, 128 * n : 128 * n + 128] = pack_ref[576 + 96 * n : 672 + 96 * n, :]
    proj_ref[...] = pack_ref[864:1248, 0:channels]
    dw_ref[...] = pack_ref[1248:1297, 0:channels]


def spread_kernel(feat_ref, w_ref, key_ref, y_ref, below_ref, *, last):
    width = feat_ref.shape[1]
    feats = feat_ref[...].astype(F32).reshape(16, 8, width)
    outs = {}
    for a in range(3):
        for b in range(3):
            places = [(u, v) for u in reach(a) for v in reach(b)]
            left = jnp.concatenate(
                [feats[(2 * u + a - 1) * 4 + 2 * v + b - 1] for u, v in places], axis=0
            ).astype(BF16)
            out = nn(left, w_ref[3 * a + b])
            for n, (u, v) in enumerate(places):
                piece = out[8 * n : 8 * n + 8]
                at = 3 * u + v
                outs[at] = outs[at] + piece if at in outs else piece
    total = jnp.concatenate([outs[at] for at in range(9)], axis=0)
    y_ref[...] = total
    pick = (key_ref[...] == float(last)).astype(F32).astype(BF16)
    high = total.astype(BF16)
    rest = (total - high.astype(F32)).astype(BF16)

    @pl.when(pl.program_id(0) == 0)
    def _():
        below_ref[...] = jnp.zeros_like(below_ref)

    below_ref[...] += tn(high, pick) + tn(rest, pick)


def map_kernel(y_ref, key_ref, above_ref, out_ref):
    out_rows, width, _ = out_ref.shape
    turned = y_ref[...].T
    high = turned.astype(BF16)
    rest = (turned - high.astype(F32)).astype(BF16)
    key = key_ref[...]

    def row_of(o):
        pick = (key == o).astype(F32).astype(BF16)
        return nn(high, pick) + nn(rest, pick)

    out_ref[0] = (row_of(0.0) + above_ref[...]).astype(BF16)

    def step(o, carry):
        out_ref[o] = row_of(o.astype(F32)).astype(BF16)
        return carry

    lax.fori_loop(1, out_rows, step, 0)


def weight_kernel(feat_ref, cot_ref, out_ref, feat_t_ref, cot_t_ref, *, scale):
    blocks = feat_ref.shape[0]
    width = feat_ref.shape[2]
    step = pl.program_id(0)

    @pl.when(step == 0)
    def _():
        out_ref[...] = jnp.zeros_like(out_ref)

    for n in range(blocks):
        feats = feat_ref[n].astype(F32).reshape(16, 8, width)
        cots = cot_ref[n].astype(F32).reshape(9, 8, cot_ref.shape[2])
        feat_t_ref[:, 8 * n : 8 * n + 8] = feats
        cot_t_ref[:, 8 * n : 8 * n + 8] = cots
    turned = [feat_t_ref[p].T.astype(BF16) for p in range(16)]
    cots = [cot_t_ref[p].astype(BF16) for p in range(9)]
    for a in range(3):
        for b in range(3):
            total = None
            for u in reach(a):
                for v in reach(b):
                    p = (2 * u + a - 1) * 4 + 2 * v + b - 1
                    piece = nn(turned[p], cots[3 * u + v])
                    total = piece if total is None else total + piece
            out_ref[3 * a + b] += total * scale


def whole(shape):
    return pl.BlockSpec(shape, lambda g: (0,) * len(shape))


def on_device(
    tile_pixels, tile_cell, agg_cot, dw_weight, norm_gain, up_weight, proj_weight,
    layer_scale, ds_gain, ds_weight, agg_weight,
):
    channels = dw_weight.shape[1]
    hid = up_weight.shape[1]
    width = ds_weight.shape[1]
    bands = lax.axis_size("slide")
    sources = bands * lax.axis_size("chan")
    chunks = sources // 8
    pixch = tile_pixels.shape[2]
    out_rows = agg_cot.shape[1]
    e_half = agg_weight.shape[2]
    cols = agg_cot.shape[3]
    blocks = CAP * chunks
    total_rows = out_rows * bands * lax.axis_size("rep") * cols
    loss_scale = 1.0 / math.sqrt(total_rows)
    chan = lax.axis_index("chan").astype(jnp.int32)[None]
    gain = norm_gain[None]
    scale = layer_scale[None]
    low_gain = ds_gain[None]

    peer_weight = swapped(agg_weight, "chan", 1)
    below_cot = shifted(agg_cot[0, 0].astype(BF16), "slide", -1)

    packed = pl.pallas_call(
        pack_kernel,
        out_shape=jax.ShapeDtypeStruct((sources, pixch + META), BF16),
        in_specs=[SMEM, VMEM],
        out_specs=VMEM,
        name="pack",
    )(tile_cell, tile_pixels[0])
    got = lax.all_to_all(packed, ("slide", "chan"), split_axis=0, concat_axis=0, tiled=True)

    key, cots_all, cots_own, cots_send = pl.pallas_call(
        patch_kernel,
        out_shape=(
            jax.ShapeDtypeStruct((blocks * 72, cols), F32),
            jax.ShapeDtypeStruct((blocks * 72, e_half), BF16),
            jax.ShapeDtypeStruct((chunks * 72, e_half), BF16),
            jax.ShapeDtypeStruct((chunks * 72, e_half), BF16),
        ),
        in_specs=[
            SMEM,
            pl.BlockSpec((sources, META), lambda i: (0, pixch // META)),
            pl.BlockSpec((None, out_rows, e_half, cols), lambda i: (0, 0, 0, 0)),
            whole((e_half, cols)),
        ],
        out_specs=(
            whole((blocks * 72, cols)),
            whole((blocks * 72, e_half)),
            whole((chunks * 72, e_half)),
            whole((chunks * 72, e_half)),
        ),
        grid=(1,),
        compiler_params=params_of(),
        name="patch",
    )(chan, got, agg_cot, below_cot)
    cots_peer = swapped(cots_send, "chan", 1)

    rows = PIX * 8
    pixel_spec = pl.BlockSpec((8, pixch), lambda g: (g, 0))

    def chunk(*shape):
        return pl.BlockSpec((None,) + shape, lambda g: (g,) + (0,) * len(shape))

    feats, hat1, rstd1, hat2, rstd2, hidden, slope = pl.pallas_call(
        stem_kernel,
        grid=(chunks,),
        out_shape=(
            jax.ShapeDtypeStruct((chunks, 128, width), BF16),
            jax.ShapeDtypeStruct((chunks, rows, channels), F32),
            jax.ShapeDtypeStruct((chunks, rows, 1), F32),
            jax.ShapeDtypeStruct((chunks, rows, channels), F32),
            jax.ShapeDtypeStruct((chunks, rows, 1), F32),
            jax.ShapeDtypeStruct((chunks, rows, hid), BF16),
            jax.ShapeDtypeStruct((chunks, rows, hid), F32),
        ),
        in_specs=[
            pixel_spec,
            whole(dw_weight.shape), whole((1, channels)), whole(up_weight.shape),
            whole(proj_weight.shape), whole((1, channels)), whole((1, channels)),
            whole(ds_weight.shape),
        ],
        out_specs=(
            chunk(128, width), chunk(rows, channels), chunk(rows, 1), chunk(rows, channels),
            chunk(rows, 1), chunk(rows, hid), chunk(rows, hid),
        ),
        scratch_shapes=[
            pltpu.VMEM((SIDE + 6, SIDE + 6, 8, channels), F32),
            pltpu.VMEM((SIDE, SIDE, 8, channels), F32),
            pltpu.VMEM((SIDE // 2, 2, SIDE // 2, 2, 8, channels), F32),
        ],
        compiler_params=params_of(),
        name="stem",
    )(got, dw_weight, gain, up_weight, proj_weight, scale, low_gain, ds_weight)

    feats_band = lax.all_gather(feats, "chan", axis=0, tiled=True)

    keep, send = pl.pallas_call(
        lambda *refs: back_kernel(*refs, scale=loss_scale),
        grid=(chunks,),
        out_shape=(
            jax.ShapeDtypeStruct((HALF_ROWS, 128), F32),
            jax.ShapeDtypeStruct((HALF_ROWS, 128), BF16),
        ),
        in_specs=[
            SMEM, chunk(72, e_half), chunk(72, e_half),
            whole(agg_weight.shape), whole(agg_weight.shape), pixel_spec,
            chunk(rows, channels), chunk(rows, 1), chunk(rows, channels), chunk(rows, 1),
            chunk(rows, hid), chunk(rows, hid),
            whole((1, channels)), whole(up_weight.shape), whole(proj_weight.shape),
            whole((1, channels)), whole((1, channels)), whole(ds_weight.shape),
        ],
        out_specs=(whole((HALF_ROWS, 128)), whole((HALF_ROWS, 128))),
        scratch_shapes=[
            pltpu.VMEM((SIDE + 6, SIDE + 6, 8, channels), F32),
            pltpu.VMEM((SIDE // 2, 2, SIDE // 2, 2, 8, channels), F32),
            pltpu.VMEM((SIDE // 2, 2, SIDE // 2, 2, 8, channels), F32),
            pltpu.VMEM((SIDE, SIDE, 8, channels), F32),
            pltpu.VMEM((7, 7, 8, channels), F32),
            pltpu.VMEM(ds_weight.shape, F32),
            pltpu.VMEM(up_weight.shape, F32),
            pltpu.VMEM(proj_weight.shape, F32),
            pltpu.VMEM((2 * HALF_ROWS, 128), F32),
        ],
        compiler_params=params_of(),
        name="stem_back",
    )(
        chan, cots_own.reshape(chunks, 72, e_half), cots_peer.reshape(chunks, 72, e_half),
        agg_weight, peer_weight, got, hat1, rstd1, hat2, rstd2, hidden, slope,
        gain, up_weight, proj_weight, scale, low_gain, ds_weight,
    )

    spread, below = pl.pallas_call(
        lambda *refs: spread_kernel(*refs, last=out_rows),
        grid=(blocks,),
        out_shape=(
            jax.ShapeDtypeStruct((blocks * 72, e_half), F32),
            jax.ShapeDtypeStruct((e_half, cols), F32),
        ),
        in_specs=[
            chunk(128, width), whole(agg_weight.shape),
            pl.BlockSpec((72, cols), lambda g: (g, 0)),
        ],
        out_specs=(pl.BlockSpec((72, e_half), lambda g: (g, 0)), whole((e_half, cols))),
        compiler_params=params_of(),
        name="spread",
    )(feats_band, agg_weight, key)
    above = shifted(below, "slide", 1)
    agg_map = pl.pallas_call(
        map_kernel,
        out_shape=jax.ShapeDtypeStruct((out_rows, e_half, cols), BF16),
        in_specs=[VMEM, VMEM, VMEM],
        out_specs=VMEM,
        compiler_params=pltpu.CompilerParams(vmem_limit_bytes=48 << 20),
        name="agg_map",
    )(spread, key, above)[None]

    cots_blocks = cots_all.reshape(blocks, 72, e_half)
    members = bands * lax.axis_size("rep")
    gather = members * blocks * 128 * width * 2 <= GATHER_LIMIT
    feats_in, cots_in = feats_band, cots_blocks
    if gather:
        feats_in = lax.all_gather(feats_band, ("slide", "rep"), axis=0, tiled=True)
        cots_in = lax.all_gather(cots_blocks, ("slide", "rep"), axis=0, tiled=True)
    count = feats_in.shape[0]
    per = min(count, 16)
    agg_grad = pl.pallas_call(
        lambda *refs: weight_kernel(*refs, scale=loss_scale),
        grid=(count // per,),
        out_shape=jax.ShapeDtypeStruct((9, width, e_half), F32),
        in_specs=[
            pl.BlockSpec((per, 128, width), lambda g: (g, 0, 0)),
            pl.BlockSpec((per, 72, e_half), lambda g: (g, 0, 0)),
        ],
        out_specs=whole((9, width, e_half)),
        scratch_shapes=[
            pltpu.VMEM((16, per * 8, width), F32),
            pltpu.VMEM((9, per * 8, e_half), F32),
        ],
        compiler_params=params_of(),
        name="agg_weight_grad",
    )(feats_in, cots_in)
    if not gather:
        agg_grad = lax.psum(agg_grad, ("slide", "rep"))

    part = keep + swapped(send, "chan", 1).astype(F32)
    for axis in ("rep", "slide"):
        step = 1
        while step < lax.axis_size(axis):
            wire = part.astype(BF16)
            part = wire.astype(F32) + swapped(wire, axis, step).astype(F32)
            step *= 2
    full = lax.all_gather(part, "chan", axis=0, tiled=True)
    dw_grad, up_grad, proj_grad, ds_grad = pl.pallas_call(
        unpack_kernel,
        out_shape=(
            jax.ShapeDtypeStruct(dw_weight.shape, F32),
            jax.ShapeDtypeStruct(up_weight.shape, F32),
            jax.ShapeDtypeStruct(proj_weight.shape, F32),
            jax.ShapeDtypeStruct(ds_weight.shape, F32),
        ),
        in_specs=[VMEM],
        out_specs=(VMEM, VMEM, VMEM, VMEM),
        name="unpack",
    )(full)
    return (agg_map, agg_grad, dw_grad, up_grad, proj_grad, ds_grad)


def solution(mesh):
    in_specs = (
        P(("groups", "rep"), ("slide", "chan"), None),
        P(("groups", "rep"), ("slide", "chan")),
        P(("groups", "rep"), "slide", "chan", None),
        P(), P(), P(), P(), P(), P(), P(),
        P(None, None, "chan"),
    )
    out_specs = (
        P(("groups", "rep"), "slide", "chan", None),
        P("groups", None, "chan"),
        P("groups", None),
        P("groups", None),
        P("groups", None),
        P("groups", None),
    )
    return jax.shard_map(
        on_device, mesh=mesh, in_specs=in_specs, out_specs=out_specs, check_vma=False
    )
```

time: 869 us -> 122 us (0.14)
  local copies, waits for them, and re-layouts: 628 us -> 5.94 us
  other arithmetic: 44.9 us -> 1.74 us
  waiting for transfers between devices: 54.1 us -> 13.9 us
  matrix products: 32.1 us -> 0 us
  Pallas kernels: 0 us -> 17.4 us
  between operations: 16 us -> 0.9 us
    pad x9 -> x0, local copies, waits for them, and re-layouts: 276 us -> none  [aggregate(): padded[row_tap:row_tap + 2 * out_rows - 1:2, col_tap:col_tap + 2 * out_co...]
    slice x9 -> x0, local copies, waits for them, and re-layouts: 257 us -> none  [aggregate(): padded[row_tap:row_tap + 2 * out_rows - 1:2, col_tap:col_tap + 2 * out_co...]
    all_gather x1 -> x4, blocking collectives: 2.01 us -> 67.2 us  [the longest x1 32.1 us: on_device(): feats_in = lax.all_gather(feats_band, ('slide', 'rep'), axis=0, tiled=True)]
    psum x1 -> x0, blocking collectives: 62.6 us -> none  [on_device(): lax.psum((dw_term, up_term, proj_term, ds_term, embedded), ('slide', 'rep...]
    reshape x21 -> x0, local copies, waits for them, and re-layouts: 47.4 us -> none  [the longest x2 13 us: on_device(): band_grid = band_grid.reshape(GR * feat_side, GW * feat_side, -1)]
    psum x1 -> x0, waiting for transfers between devices: 36.1 us -> none  [on_device(): lax.psum((dw_term, up_term, proj_term, ds_term, embedded), ('slide', 'rep...]
    dot_general x37 -> x0, matrix products: 32.1 us -> none  [the longest x27 20.7 us: aggregate(): jnp.dot(window.reshape(out_rows * out_cols, padded.shape[2]), weight_half...]
    pallas_call x0 -> x8, Pallas kernels: none -> 17.4 us  [the longest x1 3.6 us: on_device(): pl.pallas_call(lambda *refs: back_kernel(*refs, scale=loss_scale), grid=(...]
  transfers between devices with their start and end apart: 7 -> 9, of which waited for: 3 -> 4; matrix products, arithmetic and copies ran while one was open for 42% -> 3% of each run, Pallas kernels for 0% -> 10%
where the time goes in v1:
time: 122 us
  blocking collectives  67.2 us (55%)
  Pallas kernels  17.4 us (14%)
  starting transfers between devices  14.5 us (12%)
  waiting for transfers between devices  13.9 us (11%)
  local copies, waits for them, and re-layouts  5.94 us (5%)
  other arithmetic  1.74 us (1%)
    all_gather x1, blocking collectives, on_device(): feats_in = lax.all_gather(feats_band, ('slide', 'rep'), axis=0, tiled=True)  32.1 us
    all_gather x1, blocking collectives, on_device(): cots_in = lax.all_gather(cots_blocks, ('slide', 'rep'), axis=0, tiled=True)  30.9 us
    ppermute x6, waiting for transfers between devices, swapped(): lax.ppermute(value, axis, [(place, place ^ step) for place in range(count)])  8.77 us
    all_to_all x1, starting transfers between devices, on_device(): lax.all_to_all(packed, ('slide', 'chan'), split_axis=0, concat_axis=0, ti...  6 us
    ppermute x6, starting transfers between devices, swapped(): lax.ppermute(value, axis, [(place, place ^ step) for place in range(count)])  5.92 us
    all_to_all x1, waiting for transfers between devices, on_device(): lax.all_to_all(packed, ('slide', 'chan'), split_axis=0, concat_axis=0, ti...  5.09 us
    unnamed x27, local copies, waits for them, and re-layouts  4.69 us
    pallas_call x1, Pallas kernels, on_device(): pl.pallas_call(lambda *refs: back_kernel(*refs, scale=loss_scale), grid=(...  3.6 us
  transfers between devices with their start and end apart: 9, of which 4 were waited for; matrix products, arithmetic and copies ran while one was open for 3% of the time, Pallas kernels for 10%

profile of v1, /device:TPU:0, one launch (start us, length us, event | category | flops | bytes accessed | tf_op | source)
XLA Modules:
  0.0 121.6 jit_solution(16536326886742763356)
XLA Ops:
  0.6 0.5 collective-permute-start.3
  1.2 1.8 %pack.1 = bf16[8,6272]{1,0:T(8,128)(2,1)} custom-call(s32[1,8]{1,0:T(1,128)} %cells_ref.1, bf16[8,6144]{1,0:T(8,128)(2,1)} %bitcast.29), custom_call_target="tpu_custom_call" | custom-call | tf_op jit(solution)/shard_map/pack/pallas_call | solution.py:394
  3.0 0.5 broadcast
  3.5 1.6 %reduce = bf16[8,6272]{1,0:T(8,128)(2,1)S(1)} reduce(bf16[8,1,6272]{2,0,1:T(8,128)(2,1)} %bitcast.27, bf16[]{:T(256)} %broadcast), dimensions={1}, to_apply=%copy.33.reduce_sub_computation | reduce | bytes 200706 | tf_op jit(solution)/shard_map/all_to_all | solution.py:401
  5.0 0.8 reshape.27
  5.8 6.0 %all-to-all-start = ((bf16[8,2,3136]{2,1,0:T(2,128)(2,1)}), bf16[8,2,3136]{2,1,0:T(2,128)(2,1)S(1)}, u32[]{:S(2)}, u32[]{:S(2)}) async-start(bf16[8,2,3136]{2,1,0:T(2,128)(2,1)} %reshape.27), calls=%async_computation | async-start | bytes 204800 | tf_op jit(solution)/shard_map/all_to_all | solution.py:401
  11.9 1.3 %collective-permute-start = (bf16[96,128]{1,0:T(8,128)(2,1)S(1)}, bf16[96,128]{1,0:T(8,128)(2,1)S(1)}, u32[]{:S(2)}, u32[]{:S(2)}) collective-permute-start(bf16[96,128]{1,0:T(8,128)(2,1)S(1)} %fusion), channel_id=1, source_target_pairs={{4,0},{8,4},{12,8},{5,1},{9,5},{13,9},{6,2},{10,6},{14,10},{7,3},{... | collective-permute-start | bytes 73736 | tf_op jit(solution)/shard_map/ppermute | solution.py:45
  13.2 5.1 %all-to-all-done = bf16[8,2,3136]{2,1,0:T(2,128)(2,1)S(1)} async-done(((bf16[8,2,3136]{2,1,0:T(2,128)(2,1)}), bf16[8,2,3136]{2,1,0:T(2,128)(2,1)S(1)}, u32[]{:S(2)}, u32[]{:S(2)}) %all-to-all-start) | async-done | bytes 100384 | tf_op jit(solution)/shard_map/all_to_all | solution.py:401
  18.2 0.2 reshape.28
  18.4 0.0 collective-permute-done.below_ref
  18.5 0.0 copy-start.8
  18.5 0.0 copy-start.9
  18.5 0.0 copy-start.3
  18.5 1.2 patch.1
  19.7 0.0 copy-start
  19.7 0.1 collective-permute-start.2
  19.8 0.1 copy.35.ds_ref.refs_17_
  19.9 0.0 copy-start.2
  20.0 0.1 copy.34.proj_ref.refs_14_
  20.1 0.0 copy-start.4
  20.1 0.0 copy-start.5
  20.1 0.0 copy-start.6
  20.1 0.7 copy-done.2
  20.8 2.6 %stem.1 = (bf16[1,128,192]{2,1,0:T(8,128)(2,1)S(1)}, f32[1,512,96]{2,1,0:T(8,128)S(1)}, f32[1,512,1]{2,1,0:T(8,128)S(1)}, f32[1,512,96]{2,1,0:T(8,128)S(1)}, f32...) custom-call(bf16[8,6272]{1,0:T(8,128)(2,1)S(1)} %bitcast.16, ...), custom_call_target="tpu_custom_call" | custom-call | tf_op jit(solution)/shard_map/stem/pallas_call | solution.py:435
  23.4 0.0 collective-permute-done.2
  23.4 0.0 collective-permute-done.3.refs_4_
  23.4 3.6 %stem_back.1 = (f32[656,128]{1,0:T(8,128)S(1)}, bf16[656,128]{1,0:T(8,128)(2,1)S(1)}) custom-call(s32[1]{0:T(128)} %bitcast.5.chan_ref.refs_0_, bf16[1,72,96]{2,1,0:T(8,128)(2,1)S(1)} %bitcast.19, bf16[1,72,96]{2,1,0:T(8,128)(2,1)S(1)} %bitcast.20, bf16[9,192,96]{2,1,0:T(8,128)(2,1)S(1)} %copy-done, bf16[9,192,96]{2,1,0:T(8,128)(2,1)S(1)} %collective-permute-done.3.refs_4_, ...), custom_call_target="tpu_custom_call" | custom-call | tf_op jit(solution)/shard_map/stem_back/pallas_call | solution.py:468
  27.0 0.6 collective-permute-start.4
  27.6 1.0 collective-permute-done.4
  28.7 1.6 %collective-permute-start.5 = (bf16[656,128]{1,0:T(8,128)(2,1)S(1)}, bf16[656,128]{1,0:T(8,128)(2,1)S(1)}, u32[]{:S(2)}, u32[]{:S(2)}) collective-permute-start(bf16[656,128]{1,0:T(8,128)(2,1)S(1)} %add_convert_fusion.2), channel_id=1, source_target_pairs={{0,2},{2,0},{1,3},{3,1},{4,6},{6,4},{5,7},{7,5},{8,10},{10,8},{9,1... | collective-permute-start | bytes 503816 | tf_op jit(solution)/shard_map/ppermute | solution.py:50
  30.2 5.1 %collective-permute-done.5 = bf16[656,128]{1,0:T(8,128)(2,1)S(1)} collective-permute-done((bf16[656,128]{1,0:T(8,128)(2,1)S(1)}, bf16[656,128]{1,0:T(8,128)(2,1)S(1)}, u32[]{:S(2)}, u32[]{:S(2)}) %collective-permute-start.5) | collective-permute-done | bytes 167968 | tf_op jit(solution)/shard_map/ppermute | solution.py:50
  35.4 1.2 collective-permute-start.6
  36.5 0.1 copy.36
  36.6 1.9 %all_gather.12 = bf16[2,128,192]{1,2,0:T(8,128)(2,1)S(1)} all-gather(bf16[1,128,192]{1,2,0:T(8,128)(2,1)S(1)} %copy.36), channel_id=1, replica_groups=mesh['groups'=2,'slide'=4,'rep'=2,'chan'=2] {'chan'}, dimensions={0}, use_global_device_ids=true | all-gather | bytes 147456 | tf_op jit(solution)/shard_map/all_gather | solution.py:466
  38.5 2.7 %collective-permute-done.6 = bf16[656,128]{1,0:T(8,128)(2,1)S(1)} collective-permute-done((bf16[656,128]{1,0:T(8,128)(2,1)S(1)}, bf16[656,128]{1,0:T(8,128)(2,1)S(1)}, u32[]{:S(2)}, u32[]{:S(2)}) %collective-permute-start.6) | collective-permute-done | bytes 167968 | tf_op jit(solution)/shard_map/ppermute | solution.py:50
  41.2 2.1 %collective-permute-start.7 = (bf16[656,128]{1,0:T(8,128)(2,1)S(1)}, bf16[656,128]{1,0:T(8,128)(2,1)S(1)}, u32[]{:S(2)}, u32[]{:S(2)}) collective-permute-start(bf16[656,128]{1,0:T(8,128)(2,1)S(1)} %add_convert_fusion), channel_id=1, source_target_pairs={{0,8},{4,12},{8,0},{12,4},{1,9},{5,13},{9,1},{13,5},{2,10},{6,14},... | collective-permute-start | bytes 503816 | tf_op jit(solution)/shard_map/ppermute | solution.py:50
  43.3 32.1 %all_gather.13 = bf16[16,128,192]{1,2,0:T(8,128)(2,1)S(1)} all-gather(bf16[2,128,192]{1,2,0:T(8,128)(2,1)S(1)} %all_gather.12), channel_id=1, replica_groups=mesh['groups'=2,'slide'=4,'rep'=2,'chan'=2] {'slide','rep'}, dimensions={0}, use_global_device_ids=true | all-gather | bytes 884736 | tf_op jit(solution)/shard_map/all_gather | solution.py:533
  75.3 0.1 copy.37.refs_0_
  75.4 1.0 spread.1
  76.5 1.3 %collective-permute-start.1 = (f32[96,128]{1,0:T(8,128)S(1)}, f32[96,128]{1,0:T(8,128)S(1)}, u32[]{:S(2)}, u32[]{:S(2)}) collective-permute-start(f32[96,128]{1,0:T(8,128)S(1)} %get-tuple-element.28), channel_id=1, source_target_pairs={{0,4},{4,8},{8,12},{1,5},{5,9},{9,13},{2,6},{6,10},{10,14},{3,7},{... | collective-permute-start | bytes 147464 | tf_op jit(solution)/shard_map/ppermute | solution.py:45
  77.8 0.5 copy.38.refs_0_
  78.3 30.9 %all_gather.14.refs_1_ = bf16[16,72,96]{2,1,0:T(8,128)(2,1)S(1)} all-gather(bf16[2,72,96]{2,1,0:T(8,128)(2,1)S(1)} %bitcast.18), channel_id=1, replica_groups=mesh['groups'=2,'slide'=4,'rep'=2,'chan'=2] {'slide','rep'}, dimensions={0}, use_global_device_ids=true | all-gather | bytes 248832 | tf_op jit(solution)/shard_map/all_gather | solution.py:534
  109.2 1.8 %agg_weight_grad.1 = f32[9,192,96]{2,1,0:T(8,128)} custom-call(bf16[16,128,192]{2,1,0:T(8,128)(2,1)S(1)} %copy.38.refs_0_, bf16[16,72,96]{2,1,0:T(8,128)(2,1)S(1)} %all_gather.14.refs_1_), custom_call_target="tpu_custom_call" | custom-call | tf_op jit(solution)/shard_map/agg_weight_grad/pallas_call | solution.py:537
  110.9 3.5 %agg_map.1 = bf16[16,96,128]{2,1,0:T(8,128)(2,1)} custom-call(f32[144,96]{1,0:T(8,128)S(1)} %get-tuple-element.27.y_ref, f32[144,128]{1,0:T(8,128)S(1)} %get-tuple-element.26.refs_2_.key_ref, f32[96,128]{1,0:T(8,128)S(1)} %collective-permute-done.1.above_ref), custom_call_target="tpu_custom_call" | custom-call | tf_op jit(solution)/shard_map/agg_map/pallas_call | solution.py:519
  114.5 2.4 %all_gather.15.pack_ref = f32[1312,128]{1,0:T(8,128)} all-gather(f32[656,128]{1,0:T(8,128)S(1)} %convert_add_fusion), channel_id=1, replica_groups=mesh['groups'=2,'slide'=4,'rep'=2,'chan'=2] {'chan'}, dimensions={0}, use_global_device_ids=true | all-gather | bytes 1007616 | tf_op jit(solution)/shard_map/all_gather | solution.py:563
  116.9 2.0 %unpack.1 = (f32[49,96]{1,0:T(8,128)}, f32[96,384]{1,0:T(8,128)}, f32[384,96]{1,0:T(8,128)}, f32[384,192]{1,0:T(8,128)}) custom-call(f32[1312,128]{1,0:T(8,128)} %all_gather.15.pack_ref), custom_call_target="tpu_custom_call" | custom-call | tf_op jit(solution)/shard_map/unpack/pallas_call | solution.py:564
  118.9 1.9 %copy.42 = f32[384,192]{0,1:T(8,128)} copy(f32[384,192]{1,0:T(8,128)} %get-tuple-element.61) | data formatting | bytes 589824
  120.8 0.8 copy.41
  (19 shorter events, 0.2 us)
Async XLA Ops:
  0.6 11.2 %copy-start.1 = (f32[1,16,96,128]{3,2,1,0:T(8,128)S(1)}, f32[1,16,96,128]{3,2,1,0:T(8,128)}, u32[]{:S(2)}) copy-start(f32[1,16,96,128]{3,2,1,0:T(8,128)} %cot_ref.1) | copy-start | bytes 2359300
  0.6 22.8 %collective-permute-start.3 = (bf16[9,192,96]{2,1,0:T(8,128)(2,1)}, bf16[9,192,96]{2,1,0:T(8,128)(2,1)S(1)}, u32[]{:S(2)}, u32[]{:S(2)}) collective-permute-start(bf16[9,192,96]{2,1,0:T(8,128)(2,1)} %refs_3_.1), channel_id=1, source_target_pairs={{0,1},{1,0},{2,3},{3,2},{4,5},{5,4},{6,7},{7,6},{8,9},{9,8},{10,11... | collective-permute-start | bytes 995336 | tf_op jit(solution)/shard_map/ppermute | solution.py:50
  5.8 12.4 %all-to-all-start = ((bf16[8,2,3136]{2,1,0:T(2,128)(2,1)}), bf16[8,2,3136]{2,1,0:T(2,128)(2,1)S(1)}, u32[]{:S(2)}, u32[]{:S(2)}) async-start(bf16[8,2,3136]{2,1,0:T(2,128)(2,1)} %reshape.27), calls=%async_computation | async-start | bytes 204800 | tf_op jit(solution)/shard_map/all_to_all | solution.py:401
  11.9 6.6 %collective-permute-start = (bf16[96,128]{1,0:T(8,128)(2,1)S(1)}, bf16[96,128]{1,0:T(8,128)(2,1)S(1)}, u32[]{:S(2)}, u32[]{:S(2)}) collective-permute-start(bf16[96,128]{1,0:T(8,128)(2,1)S(1)} %fusion), channel_id=1, source_target_pairs={{4,0},{8,4},{12,8},{5,1},{9,5},{13,9},{6,2},{10,6},{14,10},{7,3},{... | collective-permute-start | bytes 73736 | tf_op jit(solution)/shard_map/ppermute | solution.py:45
  18.5 1.3 %copy-start.8 = (bf16[384,192]{0,1:T(8,128)(2,1)S(1)}, bf16[384,192]{0,1:T(8,128)(2,1)}, u32[]{:S(2)}) copy-start(bf16[384,192]{0,1:T(8,128)(2,1)} %param.20) | copy-start | bytes 442372
  18.5 1.5 %copy-start.9 = (bf16[384,96]{0,1:T(8,128)(2,1)S(1)}, bf16[384,96]{0,1:T(8,128)(2,1)}, u32[]{:S(2)}) copy-start(bf16[384,96]{0,1:T(8,128)(2,1)} %param.17) | copy-start | bytes 221188
  18.5 1.6 %copy-start.3 = (f32[49,96]{1,0:T(8,128)S(1)}, f32[49,96]{1,0:T(8,128)}, u32[]{:S(2)}) copy-start(f32[49,96]{1,0:T(8,128)} %dw_ref.1) | copy-start | bytes 56452
  19.7 3.7 %copy-start = (bf16[9,192,96]{2,1,0:T(8,128)(2,1)S(1)}, bf16[9,192,96]{2,1,0:T(8,128)(2,1)}, u32[]{:S(2)}) copy-start(bf16[9,192,96]{2,1,0:T(8,128)(2,1)} %refs_3_.1) | copy-start | bytes 995332
  19.7 3.7 %collective-permute-start.2 = (bf16[72,96]{1,0:T(8,128)(2,1)S(1)}, bf16[72,96]{1,0:T(8,128)(2,1)S(1)}, u32[]{:S(2)}, u32[]{:S(2)}) collective-permute-start(bf16[72,96]{1,0:T(8,128)(2,1)S(1)} %get-tuple-element.31), channel_id=1, source_target_pairs={{0,1},{1,0},{2,3},{3,2},{4,5},{5,4},{6,7},{7,6},{8,9},{9,8},{10,11... | collective-permute-start | bytes 41480 | tf_op jit(solution)/shard_map/ppermute | solution.py:50
  19.9 0.9 copy-start.2
  20.1 0.8 copy-start.4
  20.1 0.7 copy-start.5
  20.1 0.7 copy-start.6
  27.0 1.6 %collective-permute-start.4 = (bf16[656,128]{1,0:T(8,128)(2,1)S(1)}, bf16[656,128]{1,0:T(8,128)(2,1)S(1)}, u32[]{:S(2)}, u32[]{:S(2)}) collective-permute-start(bf16[656,128]{1,0:T(8,128)(2,1)S(1)} %get-tuple-element.39), channel_id=1, source_target_pairs={{0,1},{1,0},{2,3},{3,2},{4,5},{5,4},{6,7},{7,6},{8,9},{9,8},{10,11... | collective-permute-start | bytes 503816 | tf_op jit(solution)/shard_map/ppermute | solution.py:50
  28.7 6.6 %collective-permute-start.5 = (bf16[656,128]{1,0:T(8,128)(2,1)S(1)}, bf16[656,128]{1,0:T(8,128)(2,1)S(1)}, u32[]{:S(2)}, u32[]{:S(2)}) collective-permute-start(bf16[656,128]{1,0:T(8,128)(2,1)S(1)} %add_convert_fusion.2), channel_id=1, source_target_pairs={{0,2},{2,0},{1,3},{3,1},{4,6},{6,4},{5,7},{7,5},{8,10},{10,8},{9,1... | collective-permute-start | bytes 503816 | tf_op jit(solution)/shard_map/ppermute | solution.py:50
  35.4 5.8 %collective-permute-start.6 = (bf16[656,128]{1,0:T(8,128)(2,1)S(1)}, bf16[656,128]{1,0:T(8,128)(2,1)S(1)}, u32[]{:S(2)}, u32[]{:S(2)}) collective-permute-start(bf16[656,128]{1,0:T(8,128)(2,1)S(1)} %add_convert_fusion.1), channel_id=1, source_target_pairs={{0,4},{4,0},{8,12},{12,8},{1,5},{5,1},{9,13},{13,9},{2,6},{6,2},{1... | collective-permute-start | bytes 503816 | tf_op jit(solution)/shard_map/ppermute | solution.py:50
  41.2 73.2 %collective-permute-start.7 = (bf16[656,128]{1,0:T(8,128)(2,1)S(1)}, bf16[656,128]{1,0:T(8,128)(2,1)S(1)}, u32[]{:S(2)}, u32[]{:S(2)}) collective-permute-start(bf16[656,128]{1,0:T(8,128)(2,1)S(1)} %add_convert_fusion), channel_id=1, source_target_pairs={{0,8},{4,12},{8,0},{12,4},{1,9},{5,13},{9,1},{13,5},{2,10},{6,14},... | collective-permute-start | bytes 503816 | tf_op jit(solution)/shard_map/ppermute | solution.py:50
  76.5 34.5 %collective-permute-start.1 = (f32[96,128]{1,0:T(8,128)S(1)}, f32[96,128]{1,0:T(8,128)S(1)}, u32[]{:S(2)}, u32[]{:S(2)}) collective-permute-start(f32[96,128]{1,0:T(8,128)S(1)} %get-tuple-element.28), channel_id=1, source_target_pairs={{0,4},{4,8},{8,12},{1,5},{5,9},{9,13},{2,6},{6,10},{10,14},{3,7},{... | collective-permute-start | bytes 147464 | tf_op jit(solution)/shard_map/ppermute | solution.py:45
  118.9 1.9 %copy-start.7 = (f32[384,96]{1,0:T(8,128)S(1)}, f32[384,96]{1,0:T(8,128)}, u32[]{:S(2)}) copy-start(f32[384,96]{1,0:T(8,128)} %get-tuple-element.60) | copy-start | bytes 442372

commit v2 on v1

--- a/solution.py
+++ b/solution.py
@@ -13,8 +13,10 @@
 BAND_CELLS = 512
 PIX = SIDE * SIDE
 META = 128
-HALF_ROWS = 656
-GATHER_LIMIT = 16 << 20
+HALF_ROWS = 608
+FEAT_ROWS = 192
+COT_ROWS = 72
+BLOCK_ROWS = FEAT_ROWS + 2 * COT_ROWS
 F32 = jnp.float32
 BF16 = jnp.bfloat16
 VMEM = pl.BlockSpec(memory_space=pltpu.VMEM)
@@ -88,22 +90,25 @@
     out_ref[:, pixch:] = notes.astype(BF16)
 
 
-def patch_kernel(chan_ref, meta_ref, cot_ref, below_ref, key_ref, all_ref, own_ref, send_ref):
+def patch_kernel(chan_ref, meta_ref, cot_ref, below_ref, key_ref, own_ref, send_ref):
     sources = meta_ref.shape[0]
     chunks = sources // 8
-    out_rows = cot_ref.shape[0]
+    out_rows, e_half, _ = cot_ref.shape
     meta = meta_ref[...].astype(F32)
+    first = chan_ref[0] == 0
     lane = lax.broadcasted_iota(jnp.int32, (8, 128), 1).astype(F32)
     blocks = []
-    for rank in range(CAP):
+    for mine in (True, False):
         for chunk in range(chunks):
             part = meta[chunk * 8 : chunk * 8 + 8]
-            row = jnp.broadcast_to(part[:, 3 * rank : 3 * rank + 1], (8, 128))
-            col = jnp.broadcast_to(part[:, 3 * rank + 1 : 3 * rank + 2], (8, 128))
-            valid = jnp.broadcast_to(part[:, 3 * rank + 2 : 3 * rank + 3], (8, 128)) > 0.5
+            low = [jnp.broadcast_to(part[:, n : n + 1], (8, 128)) for n in range(3)]
+            high = [jnp.broadcast_to(part[:, n : n + 1], (8, 128)) for n in range(3, 6)]
+            row, col, valid = (
+                jnp.where(first == mine, one, two) for one, two in zip(low, high)
+            )
             for u in range(3):
                 for v in range(3):
-                    hit = (lane == 2.0 * col + v) & valid
+                    hit = (lane == 2.0 * col + v) & (valid > 0.5)
                     blocks.append(jnp.where(hit, 2.0 * row + u, -1.0))
     key = jnp.concatenate(blocks, axis=0)
     key_ref[...] = key
@@ -113,17 +118,15 @@
         return total + nt(pick, cot_ref[o].astype(BF16))
 
     total = lax.fori_loop(
-        0, out_rows, step, jnp.zeros((key.shape[0], cot_ref.shape[1]), F32), unroll=4
+        0, out_rows, step, jnp.zeros((key.shape[0], e_half), F32), unroll=4
     )
     pick = (key == float(out_rows)).astype(F32).astype(BF16)
     total = total + nt(pick, below_ref[...])
-    total = total.astype(BF16)
-    all_ref[...] = total
-    half = total.shape[0] // CAP
-    first = chan_ref[0] == 0
-    low, high = total[:half].astype(F32), total[half:].astype(F32)
-    own_ref[...] = jnp.where(first, low, high).astype(BF16)
-    send_ref[...] = jnp.where(first, high, low).astype(BF16)
+    half = total.shape[0] // 2
+    own_ref[...] = jnp.zeros_like(own_ref)
+    send_ref[...] = jnp.zeros_like(send_ref)
+    own_ref[:, :e_half] = total[:half].astype(BF16)
+    send_ref[:, :e_half] = total[half:].astype(BF16)
 
 
 def center_of(values):
@@ -142,8 +145,8 @@
 
 def stem_kernel(
     pixels_ref, dw_ref, gain_ref, up_ref, proj_ref, scale_ref, ds_gain_ref, ds_ref,
-    feat_ref, hat1_ref, rstd1_ref, hat2_ref, rstd2_ref, hidden_ref, slope_ref,
-    padded_ref, spatial_ref, low_ref,
+    feat_ref, hat1_ref, rstd1_ref, hat2_ref, rstd2_ref, hidden_ref, slope_ref, patch_ref,
+    padded_ref, spatial_ref, low_ref, wide_ref,
 ):
     channels = dw_ref.shape[1]
     fill_padded(padded_ref, pixels_ref, channels)
@@ -168,32 +171,43 @@
     hidden = (before * cdf).astype(BF16)
     hidden_ref[...] = hidden
     slope_ref[...] = cdf + before * pdf
-    branch = nn(hidden, proj_ref[...])
+    branch = nt(hidden, proj_ref[...])
     inputs = padded_ref[3 : 3 + SIDE, 3 : 3 + SIDE].reshape(PIX * 8, channels)
     hat2, rstd2 = center_of(inputs + scale_ref[...] * branch)
     hat2_ref[...] = hat2
     rstd2_ref[...] = rstd2
     low_ref[...] = (hat2 * ds_gain_ref[...]).reshape(low_ref.shape)
     half = SIDE // 2
-    total = jnp.zeros((half * half * 8, ds_ref.shape[1]), F32)
     for di in range(2):
         for dj in range(2):
-            part = low_ref[:, di, :, dj].reshape(half * half * 8, channels).astype(BF16)
             at = (2 * di + dj) * channels
-            total = total + nn(part, ds_ref[at : at + channels])
-    feat_ref[...] = total.astype(BF16)
+            wide_ref[:, at : at + channels] = low_ref[:, di, :, dj].reshape(-1, channels)
+    patches = wide_ref[...].astype(BF16)
+    patch_ref[...] = patches
+    total = nt(patches, ds_ref[...])
+    rows = total.shape[0]
+    feat_ref[0:rows] = total[:, 0:128].astype(BF16)
+    rest = jnp.concatenate([total[: rows // 2, 128:192], total[rows // 2 :, 128:192]], axis=1)
+    feat_ref[rows:] = rest.astype(BF16)
+
+
+def unfold(block):
+    rest = block[128:]
+    return jnp.concatenate(
+        [block[:128], jnp.concatenate([rest[:, :64], rest[:, 64:]], axis=0)], axis=1
+    )
 
 
 def back_kernel(
     chan_ref, own_ref, peer_ref, w_own_ref, w_peer_ref, pixels_ref,
-    hat1_ref, rstd1_ref, hat2_ref, rstd2_ref, hidden_ref, slope_ref,
+    hat1_ref, rstd1_ref, hat2_ref, rstd2_ref, hidden_ref, slope_ref, patch_ref,
     gain_ref, up_ref, proj_ref, scale_ref, ds_gain_ref, ds_ref,
     keep_ref, send_ref,
-    padded_ref, low_ref, dlow_ref, dspatial_ref, dw_ref, ds_acc, up_acc, proj_acc, pack_ref,
+    padded_ref, dlow_ref, dspatial_ref, dw_ref, ds_acc, up_acc, proj_acc, pack_ref,
     *, scale,
 ):
     channels = gain_ref.shape[1]
-    width = w_own_ref.shape[1]
+    e_half = w_own_ref.shape[2]
     half = SIDE // 2
     step = pl.program_id(0)
 
@@ -204,8 +218,8 @@
         up_acc[...] = jnp.zeros_like(up_acc)
         proj_acc[...] = jnp.zeros_like(proj_acc)
 
-    own = own_ref[...].astype(F32).reshape(9, 8, own_ref.shape[1])
-    peer = peer_ref[...].astype(F32).reshape(9, 8, peer_ref.shape[1])
+    own = own_ref[...].astype(F32)[:, :e_half].reshape(9, 8, e_half)
+    peer = peer_ref[...].astype(F32)[:, :e_half].reshape(9, 8, e_half)
     grads = {}
     for a in range(3):
         for b in range(3):
@@ -221,21 +235,19 @@
     dfeat = dfeat.astype(BF16)
 
     hat2 = hat2_ref[...]
-    low_ref[...] = (hat2 * ds_gain_ref[...]).reshape(low_ref.shape)
+    ds_acc[...] += tn(dfeat, patch_ref[...])
+    back = nn(dfeat, ds_ref[...])
     for di in range(2):
         for dj in range(2):
             at = (2 * di + dj) * channels
-            part = low_ref[:, di, :, dj].reshape(half * half * 8, channels).astype(BF16)
-            ds_acc[at : at + channels, :] += tn(part, dfeat)
-            back = nt(dfeat, ds_ref[at : at + channels])
-            dlow_ref[:, di, :, dj] = back.reshape(half, half, 8, channels)
+            dlow_ref[:, di, :, dj] = back[:, at : at + channels].reshape(half, half, 8, channels)
     dhat2 = dlow_ref[...].reshape(PIX * 8, channels) * ds_gain_ref[...]
     mean_a = jnp.mean(dhat2, axis=-1, keepdims=True)
     mean_b = jnp.mean(dhat2 * hat2, axis=-1, keepdims=True)
     dmixed = rstd2_ref[...] * (dhat2 - mean_a - hat2 * mean_b)
     dbranch = (dmixed * scale_ref[...]).astype(BF16)
-    proj_acc[...] += tn(hidden_ref[...], dbranch)
-    dhidden = nt(dbranch, proj_ref[...])
+    proj_acc[...] += tn(dbranch, hidden_ref[...])
+    dhidden = nn(dbranch, proj_ref[...])
     dbefore = (dhidden * slope_ref[...]).astype(BF16)
     hat1 = hat1_ref[...]
     normed = (hat1 * gain_ref[...]).astype(BF16)
@@ -263,33 +275,35 @@
     @pl.when(step == pl.num_programs(0) - 1)
     def _():
         pack_ref[...] = jnp.zeros_like(pack_ref)
-        pack_ref[0:384, :] = ds_acc[:, 0:128]
-        pack_ref[384:576, 0:64] = ds_acc[0:192, 128:192]
-        pack_ref[384:576, 64:128] = ds_acc[192:384, 128:192]
         for n in range(3):
-            pack_ref[576 + 96 * n : 672 + 96 * n, :] = up_acc[:, 128 * n : 128 * n + 128]
-        pack_ref[864:1248, 0:channels] = proj_acc[...]
-        pack_ref[1248:1297, 0:channels] = jnp.sum(dw_ref[...], axis=2).reshape(49, channels)
+            lanes = slice(128 * n, 128 * n + 128)
+            pack_ref[192 * n : 192 * n + 192, :] = ds_acc[:, lanes]
+            pack_ref[576 + 96 * n : 672 + 96 * n, :] = up_acc[:, lanes]
+            pack_ref[864 + 96 * n : 960 + 96 * n, :] = proj_acc[:, lanes]
+        pack_ref[1152:1201, 0:channels] = jnp.sum(dw_ref[...], axis=2).reshape(49, channels)
         mine = pl.multiple_of(chan_ref[0] * HALF_ROWS, 8)
         other = pl.multiple_of((1 - chan_ref[0]) * HALF_ROWS, 8)
         keep_ref[...] = pack_ref[pl.ds(mine, HALF_ROWS), :]
         send_ref[...] = pack_ref[pl.ds(other, HALF_ROWS), :].astype(BF16)
 
 
-def unpack_kernel(pack_ref, dw_ref, up_ref, proj_ref, ds_ref):
+def unpack_kernel(chan_ref, own_ref, peer_ref, dw_ref, up_ref, proj_ref, ds_ref, pack_ref):
     channels = dw_ref.shape[1]
-    ds_ref[:, 0:128] = pack_ref[0:384, :]
-    ds_ref[0:192, 128:192] = pack_ref[384:576, 0:64]
-    ds_ref[192:384, 128:192] = pack_ref[384:576, 64:128]
+    mine = pl.multiple_of(chan_ref[0] * HALF_ROWS, 8)
+    other = pl.multiple_of((1 - chan_ref[0]) * HALF_ROWS, 8)
+    pack_ref[pl.ds(mine, HALF_ROWS), :] = own_ref[...]
+    pack_ref[pl.ds(other, HALF_ROWS), :] = peer_ref[...]
     for n in range(3):
-        up_ref[:, 128 * n : 128 * n + 128] = pack_ref[576 + 96 * n : 672 + 96 * n, :]
-    proj_ref[...] = pack_ref[864:1248, 0:channels]
-    dw_ref[...] = pack_ref[1248:1297, 0:channels]
+        lanes = slice(128 * n, 128 * n + 128)
+        ds_ref[:, lanes] = pack_ref[192 * n : 192 * n + 192, :]
+        up_ref[:, lanes] = pack_ref[576 + 96 * n : 672 + 96 * n, :]
+        proj_ref[:, lanes] = pack_ref[864 + 96 * n : 960 + 96 * n, :]
+    dw_ref[...] = pack_ref[1152:1201, 0:channels]
 
 
 def spread_kernel(feat_ref, w_ref, key_ref, y_ref, below_ref, *, last):
-    width = feat_ref.shape[1]
-    feats = feat_ref[...].astype(F32).reshape(16, 8, width)
+    width = w_ref.shape[1]
+    feats = unfold(feat_ref[...].astype(F32)).reshape(16, 8, width)
     outs = {}
     for a in range(3):
         for b in range(3):
@@ -335,31 +349,48 @@
     lax.fori_loop(1, out_rows, step, 0)
 
 
-def weight_kernel(feat_ref, cot_ref, out_ref, feat_t_ref, cot_t_ref, *, scale):
-    blocks = feat_ref.shape[0]
-    width = feat_ref.shape[2]
+def weight_kernel(place_ref, near_ref, far_ref, keep_ref, send_ref, feat_ref, cot_ref, *, scale):
+    near = near_ref.shape[0]
+    members = feat_ref.shape[1] // 8
+    width, e_half = keep_ref.shape[1:]
     step = pl.program_id(0)
 
     @pl.when(step == 0)
     def _():
-        out_ref[...] = jnp.zeros_like(out_ref)
-
-    for n in range(blocks):
-        feats = feat_ref[n].astype(F32).reshape(16, 8, width)
-        cots = cot_ref[n].astype(F32).reshape(9, 8, cot_ref.shape[2])
-        feat_t_ref[:, 8 * n : 8 * n + 8] = feats
-        cot_t_ref[:, 8 * n : 8 * n + 8] = cots
-    turned = [feat_t_ref[p].T.astype(BF16) for p in range(16)]
-    cots = [cot_t_ref[p].astype(BF16) for p in range(9)]
+        keep_ref[...] = jnp.zeros_like(keep_ref)
+        send_ref[...] = jnp.zeros_like(send_ref)
+
+    def take(member, block):
+        block = block.astype(F32)
+        feat_ref[:, 8 * member : 8 * member + 8] = unfold(block[:FEAT_ROWS]).reshape(16, 8, width)
+        own = block[FEAT_ROWS : FEAT_ROWS + COT_ROWS].reshape(9, 8, 128)
+        peer = block[FEAT_ROWS + COT_ROWS :].reshape(9, 8, 128)
+        cot_ref[:, 8 * member : 8 * member + 8, 0:128] = own
+        cot_ref[:, 8 * member : 8 * member + 8, 128:256] = peer
+
+    for member in range(members):
+        at = place_ref[0] ^ member
+
+        @pl.when(at < near)
+        def _():
+            take(member, near_ref[jnp.minimum(at, near - 1)])
+
+        if members > near:
+
+            @pl.when(at >= near)
+            def _():
+                take(member, far_ref[jnp.maximum(at - near, 0)])
+
     for a in range(3):
         for b in range(3):
-            total = None
-            for u in reach(a):
-                for v in reach(b):
-                    p = (2 * u + a - 1) * 4 + 2 * v + b - 1
-                    piece = nn(turned[p], cots[3 * u + v])
-                    total = piece if total is None else total + piece
-            out_ref[3 * a + b] += total * scale
+            places = [(u, v) for u in reach(a) for v in reach(b)]
+            left = jnp.concatenate(
+                [feat_ref[(2 * u + a - 1) * 4 + 2 * v + b - 1] for u, v in places], axis=0
+            ).astype(BF16)
+            right = jnp.concatenate([cot_ref[3 * u + v] for u, v in places], axis=0).astype(BF16)
+            total = tn(left, right) * scale
+            keep_ref[3 * a + b] += total[:, :e_half]
+            send_ref[3 * a + b] += total[:, 128 : 128 + e_half]
 
 
 def whole(shape):
@@ -387,6 +418,8 @@
     gain = norm_gain[None]
     scale = layer_scale[None]
     low_gain = ds_gain[None]
+    proj_turned = proj_weight.T
+    ds_turned = ds_weight.T
 
     peer_weight = swapped(agg_weight, "chan", 1)
     below_cot = shifted(agg_cot[0, 0].astype(BF16), "slide", -1)
@@ -400,13 +433,12 @@
     )(tile_cell, tile_pixels[0])
     got = lax.all_to_all(packed, ("slide", "chan"), split_axis=0, concat_axis=0, tiled=True)
 
-    key, cots_all, cots_own, cots_send = pl.pallas_call(
+    key, cots_own, cots_send = pl.pallas_call(
         patch_kernel,
         out_shape=(
-            jax.ShapeDtypeStruct((blocks * 72, cols), F32),
-            jax.ShapeDtypeStruct((blocks * 72, e_half), BF16),
-            jax.ShapeDtypeStruct((chunks * 72, e_half), BF16),
-            jax.ShapeDtypeStruct((chunks * 72, e_half), BF16),
+            jax.ShapeDtypeStruct((blocks * COT_ROWS, cols), F32),
+            jax.ShapeDtypeStruct((chunks * COT_ROWS, 128), BF16),
+            jax.ShapeDtypeStruct((chunks * COT_ROWS, 128), BF16),
         ),
         in_specs=[
             SMEM,
@@ -415,16 +447,17 @@
             whole((e_half, cols)),
         ],
         out_specs=(
-            whole((blocks * 72, cols)),
-            whole((blocks * 72, e_half)),
-            whole((chunks * 72, e_half)),
-            whole((chunks * 72, e_half)),
+            whole((blocks * COT_ROWS, cols)),
+            whole((chunks * COT_ROWS, 128)),
+            whole((chunks * COT_ROWS, 128)),
         ),
         grid=(1,),
         compiler_params=params_of(),
         name="patch",
     )(chan, got, agg_cot, below_cot)
     cots_peer = swapped(cots_send, "chan", 1)
+    cots_own = cots_own.reshape(chunks, COT_ROWS, 128)
+    cots_peer = cots_peer.reshape(chunks, COT_ROWS, 128)
 
     rows = PIX * 8
     pixel_spec = pl.BlockSpec((8, pixch), lambda g: (g, 0))
@@ -432,38 +465,51 @@
     def chunk(*shape):
         return pl.BlockSpec((None,) + shape, lambda g: (g,) + (0,) * len(shape))
 
-    feats, hat1, rstd1, hat2, rstd2, hidden, slope = pl.pallas_call(
+    feats, hat1, rstd1, hat2, rstd2, hidden, slope, patches = pl.pallas_call(
         stem_kernel,
         grid=(chunks,),
         out_shape=(
-            jax.ShapeDtypeStruct((chunks, 128, width), BF16),
+            jax.ShapeDtypeStruct((chunks, FEAT_ROWS, 128), BF16),
             jax.ShapeDtypeStruct((chunks, rows, channels), F32),
             jax.ShapeDtypeStruct((chunks, rows, 1), F32),
             jax.ShapeDtypeStruct((chunks, rows, channels), F32),
             jax.ShapeDtypeStruct((chunks, rows, 1), F32),
             jax.ShapeDtypeStruct((chunks, rows, hid), BF16),
             jax.ShapeDtypeStruct((chunks, rows, hid), F32),
+            jax.ShapeDtypeStruct((chunks, 128, 4 * channels), BF16),
         ),
         in_specs=[
             pixel_spec,
             whole(dw_weight.shape), whole((1, channels)), whole(up_weight.shape),
-            whole(proj_weight.shape), whole((1, channels)), whole((1, channels)),
-            whole(ds_weight.shape),
+            whole(proj_turned.shape), whole((1, channels)), whole((1, channels)),
+            whole(ds_turned.shape),
         ],
         out_specs=(
-            chunk(128, width), chunk(rows, channels), chunk(rows, 1), chunk(rows, channels),
-            chunk(rows, 1), chunk(rows, hid), chunk(rows, hid),
+            chunk(FEAT_ROWS, 128), chunk(rows, channels), chunk(rows, 1), chunk(rows, channels),
+            chunk(rows, 1), chunk(rows, hid), chunk(rows, hid), chunk(128, 4 * channels),
         ),
         scratch_shapes=[
             pltpu.VMEM((SIDE + 6, SIDE + 6, 8, channels), F32),
             pltpu.VMEM((SIDE, SIDE, 8, channels), F32),
             pltpu.VMEM((SIDE // 2, 2, SIDE // 2, 2, 8, channels), F32),
+            pltpu.VMEM((128, 4 * channels), F32),
         ],
         compiler_params=params_of(),
         name="stem",
-    )(got, dw_weight, gain, up_weight, proj_weight, scale, low_gain, ds_weight)
-
-    feats_band = lax.all_gather(feats, "chan", axis=0, tiled=True)
+    )(got, dw_weight, gain, up_weight, proj_turned, scale, low_gain, ds_turned)
+
+    tile_blocks = jnp.concatenate([feats, cots_own, cots_peer], axis=1)
+    gather = chunks == 1
+    near = far = tile_blocks
+    place = jnp.zeros((1,), jnp.int32)
+    if gather:
+        spans = [("slide", 1 << n) for n in reversed(range(bands.bit_length() - 1))]
+        spans += [("rep", 1 << n) for n in range(lax.axis_size("rep").bit_length() - 1)]
+        for n, (axis, step) in enumerate(spans):
+            near = far if n == 0 else jnp.concatenate([near, far], axis=0)
+            far = swapped(near, axis, step)
+            bit = (lax.axis_index(axis).astype(jnp.int32) // step) % 2
+            place = place + bit * (1 << n)
 
     keep, send = pl.pallas_call(
         lambda *refs: back_kernel(*refs, scale=loss_scale),
@@ -473,33 +519,33 @@
             jax.ShapeDtypeStruct((HALF_ROWS, 128), BF16),
         ),
         in_specs=[
-            SMEM, chunk(72, e_half), chunk(72, e_half),
+            SMEM, chunk(COT_ROWS, 128), chunk(COT_ROWS, 128),
             whole(agg_weight.shape), whole(agg_weight.shape), pixel_spec,
             chunk(rows, channels), chunk(rows, 1), chunk(rows, channels), chunk(rows, 1),
-            chunk(rows, hid), chunk(rows, hid),
-            whole((1, channels)), whole(up_weight.shape), whole(proj_weight.shape),
-            whole((1, channels)), whole((1, channels)), whole(ds_weight.shape),
+            chunk(rows, hid), chunk(rows, hid), chunk(128, 4 * channels),
+            whole((1, channels)), whole(up_weight.shape), whole(proj_turned.shape),
+            whole((1, channels)), whole((1, channels)), whole(ds_turned.shape),
         ],
         out_specs=(whole((HALF_ROWS, 128)), whole((HALF_ROWS, 128))),
         scratch_shapes=[
             pltpu.VMEM((SIDE + 6, SIDE + 6, 8, channels), F32),
             pltpu.VMEM((SIDE // 2, 2, SIDE // 2, 2, 8, channels), F32),
-            pltpu.VMEM((SIDE // 2, 2, SIDE // 2, 2, 8, channels), F32),
             pltpu.VMEM((SIDE, SIDE, 8, channels), F32),
             pltpu.VMEM((7, 7, 8, channels), F32),
-            pltpu.VMEM(ds_weight.shape, F32),
+            pltpu.VMEM(ds_turned.shape, F32),
             pltpu.VMEM(up_weight.shape, F32),
-            pltpu.VMEM(proj_weight.shape, F32),
+            pltpu.VMEM(proj_turned.shape, F32),
             pltpu.VMEM((2 * HALF_ROWS, 128), F32),
         ],
         compiler_params=params_of(),
         name="stem_back",
     )(
-        chan, cots_own.reshape(chunks, 72, e_half), cots_peer.reshape(chunks, 72, e_half),
-        agg_weight, peer_weight, got, hat1, rstd1, hat2, rstd2, hidden, slope,
-        gain, up_weight, proj_weight, scale, low_gain, ds_weight,
+        chan, cots_own, cots_peer, agg_weight, peer_weight, got,
+        hat1, rstd1, hat2, rstd2, hidden, slope, patches,
+        gain, up_weight, proj_turned, scale, low_gain, ds_turned,
     )
 
+    feats_band = jnp.concatenate([feats, swapped(feats, "chan", 1)], axis=0)
     spread, below = pl.pallas_call(
         lambda *refs: spread_kernel(*refs, last=out_rows),
         grid=(blocks,),
@@ -508,7 +554,7 @@
             jax.ShapeDtypeStruct((e_half, cols), F32),
         ),
         in_specs=[
-            chunk(128, width), whole(agg_weight.shape),
+            chunk(FEAT_ROWS, 128), whole(agg_weight.shape),
             pl.BlockSpec((72, cols), lambda g: (g, 0)),
         ],
         out_specs=(pl.BlockSpec((72, e_half), lambda g: (g, 0)), whole((e_half, cols))),
@@ -525,31 +571,30 @@
         name="agg_map",
     )(spread, key, above)[None]
 
-    cots_blocks = cots_all.reshape(blocks, 72, e_half)
-    members = bands * lax.axis_size("rep")
-    gather = members * blocks * 128 * width * 2 <= GATHER_LIMIT
-    feats_in, cots_in = feats_band, cots_blocks
-    if gather:
-        feats_in = lax.all_gather(feats_band, ("slide", "rep"), axis=0, tiled=True)
-        cots_in = lax.all_gather(cots_blocks, ("slide", "rep"), axis=0, tiled=True)
-    count = feats_in.shape[0]
-    per = min(count, 16)
-    agg_grad = pl.pallas_call(
+    count = 2 * near.shape[0] if gather else chunks
+    per = count if gather else 1
+    near_count = near.shape[0] if gather else 1
+    agg_keep, agg_send = pl.pallas_call(
         lambda *refs: weight_kernel(*refs, scale=loss_scale),
         grid=(count // per,),
-        out_shape=jax.ShapeDtypeStruct((9, width, e_half), F32),
+        out_shape=(
+            jax.ShapeDtypeStruct((9, width, e_half), F32),
+            jax.ShapeDtypeStruct((9, width, e_half), F32),
+        ),
         in_specs=[
-            pl.BlockSpec((per, 128, width), lambda g: (g, 0, 0)),
-            pl.BlockSpec((per, 72, e_half), lambda g: (g, 0, 0)),
-        ],
-        out_specs=whole((9, width, e_half)),
+            SMEM,
+            pl.BlockSpec((near_count, BLOCK_ROWS, 128), lambda g: (g, 0, 0)),
+            pl.BlockSpec((near_count, BLOCK_ROWS, 128), lambda g: (g, 0, 0)),
+        ],
+        out_specs=(whole((9, width, e_half)), whole((9, width, e_half))),
         scratch_shapes=[
             pltpu.VMEM((16, per * 8, width), F32),
-            pltpu.VMEM((9, per * 8, e_half), F32),
+            pltpu.VMEM((9, per * 8, 256), F32),
         ],
         compiler_params=params_of(),
         name="agg_weight_grad",
-    )(feats_in, cots_in)
+    )(place, near, far)
+    agg_grad = agg_keep + swapped(agg_send.astype(BF16), "chan", 1).astype(F32)
     if not gather:
         agg_grad = lax.psum(agg_grad, ("slide", "rep"))
 
@@ -560,19 +605,21 @@
             wire = part.astype(BF16)
             part = wire.astype(F32) + swapped(wire, axis, step).astype(F32)
             step *= 2
-    full = lax.all_gather(part, "chan", axis=0, tiled=True)
     dw_grad, up_grad, proj_grad, ds_grad = pl.pallas_call(
         unpack_kernel,
         out_shape=(
             jax.ShapeDtypeStruct(dw_weight.shape, F32),
             jax.ShapeDtypeStruct(up_weight.shape, F32),
-            jax.ShapeDtypeStruct(proj_weight.shape, F32),
-            jax.ShapeDtypeStruct(ds_weight.shape, F32),
-        ),
-        in_specs=[VMEM],
+            jax.ShapeDtypeStruct(proj_turned.shape, F32),
+            jax.ShapeDtypeStruct(ds_turned.shape, F32),
+        ),
+        in_specs=[SMEM, VMEM, VMEM],
         out_specs=(VMEM, VMEM, VMEM, VMEM),
+        scratch_shapes=[pltpu.VMEM((2 * HALF_ROWS, 128), F32)],
         name="unpack",
-    )(full)
+    )(chan, part, swapped(part, "chan", 1))
+    proj_grad = proj_grad.T
+    ds_grad = ds_grad.T
     return (agg_map, agg_grad, dw_grad, up_grad, proj_grad, ds_grad)
 
 

time: 122 us -> 63.1 us (0.52)
  blocking collectives: 67.2 us -> 0 us
  waiting for transfers between devices: 13.9 us -> 21.4 us
  local copies, waits for them, and re-layouts: 5.94 us -> 2.28 us
  starting transfers between devices: 14.5 us -> 17.9 us
    all_gather x4 -> x0, blocking collectives: 67.2 us -> none  [the longest x1 32.1 us: on_device(): feats_in = lax.all_gather(feats_band, ('slide', 'rep'), axis=0, tiled=True)]
    ppermute x6 -> x12, waiting for transfers between devices: 8.77 us -> 14.9 us  [swapped(): lax.ppermute(value, axis, [(place, place ^ step) for place in range(count)])]
    unnamed x27 -> x25, local copies, waits for them, and re-layouts: 4.69 us -> 1.77 us
    ppermute x6 -> x12, starting transfers between devices: 5.92 us -> 8.32 us  [swapped(): lax.ppermute(value, axis, [(place, place ^ step) for place in range(count)])]
    ppermute x2, waiting for transfers between devices: 0.01 us -> 1.4 us  [shifted(): lax.ppermute(value, axis, [(source, source + steps) for source in range(f...]
  transfers between devices with their start and end apart: 9 -> 15, of which waited for: 4 -> 7; matrix products, arithmetic and copies ran while one was open for 3% -> 7% of each run, Pallas kernels for 10% -> 18%
where the time goes in v2:
time: 63.1 us; the launch traced here: 62.7 us
  waiting for transfers between devices  21.4 us (34%)
  starting transfers between devices  17.9 us (28%)
  Pallas kernels  17.3 us (27%)
  other arithmetic  2.87 us (5%)
  local copies, waits for them, and re-layouts  2.28 us (4%)
  between operations  1 us (2%)
    ppermute x12, waiting for transfers between devices, swapped(): lax.ppermute(value, axis, [(place, place ^ step) for place in range(count)])  14.9 us
    ppermute x12, starting transfers between devices, swapped(): lax.ppermute(value, axis, [(place, place ^ step) for place in range(count)])  8.32 us
    all_to_all x1, starting transfers between devices, on_device(): lax.all_to_all(packed, ('slide', 'chan'), split_axis=0, concat_axis=0, ti...  6 us
    all_to_all x1, waiting for transfers between devices, on_device(): lax.all_to_all(packed, ('slide', 'chan'), split_axis=0, concat_axis=0, ti...  5.08 us
    pallas_call x1, Pallas kernels, on_device(): pl.pallas_call(lambda *refs: back_kernel(*refs, scale=loss_scale), grid=(...  3.77 us
    ppermute x2, starting transfers between devices, shifted(): lax.ppermute(value, axis, [(source, source + steps) for source in range(f...  3.59 us
    pallas_call x1, Pallas kernels, on_device(): pl.pallas_call(map_kernel, out_shape=jax.ShapeDtypeStruct((out_rows, e_ha...  3.49 us
    pallas_call x1, Pallas kernels, on_device(): pl.pallas_call(stem_kernel, grid=(chunks,), out_shape=(jax.ShapeDtypeStru...  2.72 us
  transfers between devices with their start and end apart: 15, of which 7 were waited for; matrix products, arithmetic and copies ran while one was open for 7% of the time, Pallas kernels for 18%

profile of v2, /device:TPU:0, one launch (start us, length us, event | category | flops | bytes accessed | tf_op | source)
XLA Modules:
  0.0 62.7 jit_solution(4939106073315135601)
XLA Ops:
  0.6 0.5 collective-permute-start.8
  1.2 1.8 %pack.1 = bf16[8,6272]{1,0:T(8,128)(2,1)} custom-call(s32[1,8]{1,0:T(1,128)} %cells_ref.1, bf16[8,6144]{1,0:T(8,128)(2,1)} %bitcast.42), custom_call_target="tpu_custom_call" | custom-call | tf_op jit(solution)/shard_map/pack/pallas_call | solution.py:427
  3.0 0.5 broadcast.6
  3.5 1.6 %reduce = bf16[8,6272]{1,0:T(8,128)(2,1)S(1)} reduce(bf16[8,1,6272]{2,0,1:T(8,128)(2,1)} %bitcast.40, bf16[]{:T(256)} %broadcast.6), dimensions={1}, to_apply=%copy.18.reduce_sub_computation | reduce | bytes 200706 | tf_op jit(solution)/shard_map/all_to_all | solution.py:434
  5.0 0.8 %reshape.25 = bf16[8,2,3136]{2,1,0:T(2,128)(2,1)} reshape(bf16[8,6272]{1,0:T(8,128)(2,1)S(1)} %reduce) | data formatting | bytes 200704
  5.8 6.0 %all-to-all-start = ((bf16[8,2,3136]{2,1,0:T(2,128)(2,1)}), bf16[8,2,3136]{2,1,0:T(2,128)(2,1)S(1)}, u32[]{:S(2)}, u32[]{:S(2)}) async-start(bf16[8,2,3136]{2,1,0:T(2,128)(2,1)} %reshape.25), calls=%async_computation | async-start | bytes 204800 | tf_op jit(solution)/shard_map/all_to_all | solution.py:434
  11.9 1.3 %collective-permute-start.1 = (bf16[96,128]{1,0:T(8,128)(2,1)S(1)}, bf16[96,128]{1,0:T(8,128)(2,1)S(1)}, u32[]{:S(2)}, u32[]{:S(2)}) collective-permute-start(bf16[96,128]{1,0:T(8,128)(2,1)S(1)} %fusion), channel_id=1, source_target_pairs={{4,0},{8,4},{12,8},{5,1},{9,5},{13,9},{6,2},{10,6},{14,10},{7,3},{... | collective-permute-start | bytes 73736 | tf_op jit(solution)/shard_map/ppermute | solution.py:47
  13.2 5.1 %all-to-all-done = bf16[8,2,3136]{2,1,0:T(2,128)(2,1)S(1)} async-done(((bf16[8,2,3136]{2,1,0:T(2,128)(2,1)}), bf16[8,2,3136]{2,1,0:T(2,128)(2,1)S(1)}, u32[]{:S(2)}, u32[]{:S(2)}) %all-to-all-start) | async-done | bytes 100384 | tf_op jit(solution)/shard_map/all_to_all | solution.py:434
  18.2 0.2 reshape.26
  18.4 0.0 collective-permute-done.1.below_ref
  18.5 0.0 copy-start.2
  18.5 0.0 copy-start.3
  18.5 0.0 copy-start.4
  18.5 0.0 copy-start.5
  18.5 0.0 copy-start.6
  18.5 0.0 copy-start.7
  18.5 0.0 copy-start.8
  18.5 1.2 %patch.1 = (f32[144,128]{1,0:T(8,128)S(1)}, bf16[72,128]{1,0:T(8,128)(2,1)S(1)}, bf16[72,128]{1,0:T(8,128)(2,1)S(1)}) custom-call(s32[1]{0:T(128)} %bitcast.7.chan_ref.refs_0_, bf16[8,6272]{1,0:T(8,128)(2,1)S(1)} %bitcast.19, f32[1,16,96,128]{3,2,1,0:T(8,128)S(1)} %copy-done.1, bf16[96,128]{1,0:T(8,128)(2,1)S(1)} %collective-permute-done.1.below_ref), custom_call_target="tpu_custom_call" | custom-call | tf_op jit(solution)/shard_map/patch/pallas_call | solution.py:436
  19.7 0.0 copy-start
  19.7 0.1 collective-permute-start.3
  19.9 2.7 %stem.1 = (bf16[1,192,128]{2,1,0:T(8,128)(2,1)S(1)}, f32[1,512,96]{2,1,0:T(8,128)S(1)}, f32[1,512,1]{2,1,0:T(8,128)S(1)}, f32[1,512,96]{2,1,0:T(8,128)S(1)}, f32...) custom-call(bf16[8,6272]{1,0:T(8,128)(2,1)S(1)} %bitcast.20, ...), custom_call_target="tpu_custom_call" | custom-call | tf_op jit(solution)/shard_map/stem/pallas_call | solution.py:468
  22.6 0.0 copy-done
  22.6 3.8 %stem_back.1 = (f32[608,128]{1,0:T(8,128)S(1)}, bf16[608,128]{1,0:T(8,128)(2,1)S(1)}) custom-call(s32[1]{0:T(128)} %bitcast.7.chan_ref.refs_0_, bf16[1,72,128]{2,1,0:T(8,128)(2,1)S(1)} %bitcast.24, bf16[1,72,128]{2,1,0:T(8,128)(2,1)S(1)} %bitcast.28, bf16[9,192,96]{2,1,0:T(8,128)(2,1)S(1)} %copy-done, ...), custom_call_target="tpu_custom_call" | custom-call | tf_op jit(solution)/shard_map/stem_back/pallas_call | solution.py:514
  26.4 0.5 collective-permute-start.9
  26.9 2.0 %collective-permute-start.4 = (bf16[1,336,128]{2,1,0:T(8,128)(2,1)S(1)}, bf16[1,336,128]{2,1,0:T(8,128)(2,1)S(1)}, u32[]{:S(2)}, u32[]{:S(2)}) collective-permute-start(bf16[1,336,128]{2,1,0:T(8,128)(2,1)S(1)} %pad_maximum_fusion.3), channel_id=1, source_target_pairs={{0,8},{4,12},{8,0},{12,4},{1,9},{5,13},{9,1},{13,5},{2,10},{6,14},... | collective-permute-start | bytes 258056 | tf_op jit(solution)/shard_map/ppermute | solution.py:52
  28.9 0.0 collective-permute-done.9
  29.0 1.6 %collective-permute-start.10 = (bf16[608,128]{1,0:T(8,128)(2,1)S(1)}, bf16[608,128]{1,0:T(8,128)(2,1)S(1)}, u32[]{:S(2)}, u32[]{:S(2)}) collective-permute-start(bf16[608,128]{1,0:T(8,128)(2,1)S(1)} %add_convert_fusion.2), channel_id=1, source_target_pairs={{0,2},{2,0},{1,3},{3,1},{4,6},{6,4},{5,7},{7,5},{8,10},{10,8},{9,1... | collective-permute-start | bytes 466952 | tf_op jit(solution)/shard_map/ppermute | solution.py:52
  30.6 3.7 %collective-permute-done.4 = bf16[1,336,128]{2,1,0:T(8,128)(2,1)S(1)} collective-permute-done((bf16[1,336,128]{2,1,0:T(8,128)(2,1)S(1)}, bf16[1,336,128]{2,1,0:T(8,128)(2,1)S(1)}, u32[]{:S(2)}, u32[]{:S(2)}) %collective-permute-start.4) | collective-permute-done | bytes 86048 | tf_op jit(solution)/shard_map/ppermute | solution.py:52
  34.2 0.1 collective-permute-start.5
  34.3 0.5 collective-permute-done.10
  34.9 1.6 %collective-permute-start.11 = (bf16[608,128]{1,0:T(8,128)(2,1)S(1)}, bf16[608,128]{1,0:T(8,128)(2,1)S(1)}, u32[]{:S(2)}, u32[]{:S(2)}) collective-permute-start(bf16[608,128]{1,0:T(8,128)(2,1)S(1)} %add_convert_fusion.1), channel_id=1, source_target_pairs={{0,4},{4,0},{8,12},{12,8},{1,5},{5,1},{9,13},{13,9},{2,6},{6,2},{1... | collective-permute-start | bytes 466952 | tf_op jit(solution)/shard_map/ppermute | solution.py:52
  36.5 5.2 %collective-permute-done.5 = bf16[2,336,128]{2,1,0:T(8,128)(2,1)S(1)} collective-permute-done((bf16[2,336,128]{2,1,0:T(8,128)(2,1)S(1)}, bf16[2,336,128]{2,1,0:T(8,128)(2,1)S(1)}, u32[]{:S(2)}, u32[]{:S(2)}) %collective-permute-start.5) | collective-permute-done | bytes 172064 | tf_op jit(solution)/shard_map/ppermute | solution.py:52
  41.6 1.6 %collective-permute-start.6 = (bf16[4,336,128]{2,1,0:T(8,128)(2,1)S(1)}, bf16[4,336,128]{2,1,0:T(8,128)(2,1)S(1)}, u32[]{:S(2)}, u32[]{:S(2)}) collective-permute-start(bf16[4,336,128]{2,1,0:T(8,128)(2,1)S(1)} %pad_maximum_fusion.refs_1_), channel_id=1, source_target_pairs={{0,2},{2,0},{1,3},{3,1},{4,6},{6,4},{5,7},{7,5},{8,10},{10,8},{9,1... | collective-permute-start | bytes 1032200 | tf_op jit(solution)/shard_map/ppermute | solution.py:52
  43.2 0.0 collective-permute-start
  43.2 0.2 collective-permute-done.11
  43.5 0.1 collective-permute-start.12
  43.6 5.4 %collective-permute-done.6.refs_2_ = bf16[4,336,128]{2,1,0:T(8,128)(2,1)S(1)} collective-permute-done((bf16[4,336,128]{2,1,0:T(8,128)(2,1)S(1)}, bf16[4,336,128]{2,1,0:T(8,128)(2,1)S(1)}, u32[]{:S(2)}, u32[]{:S(2)}) %collective-permute-start.6) | collective-permute-done | bytes 344096 | tf_op jit(solution)/shard_map/ppermute | solution.py:52
  49.0 1.3 %agg_weight_grad.1 = (f32[9,192,96]{2,1,0:T(8,128)S(1)}, f32[9,192,96]{2,1,0:T(8,128)S(1)}) custom-call(s32[1]{0:T(128)} %bitcast.10.refs_0_, bf16[4,336,128]{2,1,0:T(8,128)(2,1)S(1)} %pad_maximum_fusion.refs_1_, bf16[4,336,128]{2,1,0:T(8,128)(2,1)S(1)} %collective-permute-done.6.refs_2_), custom_call_target="tpu_custom_call" | custom-call | tf_op jit(solution)/shard_map/agg_weight_grad/pallas_call | solution.py:577
  50.3 0.1 convert_element_type.41
  50.4 0.1 collective-permute-start.7
  50.5 1.0 %spread.1 = (f32[144,96]{1,0:T(8,128)S(1)}, f32[96,128]{1,0:T(8,128)S(1)}) custom-call(bf16[2,192,128]{2,1,0:T(8,128)(2,1)S(1)} %pad_maximum_fusion.2.refs_0_, bf16[9,192,96]{2,1,0:T(8,128)(2,1)S(1)} %copy-done, f32[144,128]{1,0:T(8,128)S(1)} %get-tuple-element.28.refs_2_.key_ref), custom_call_target="tpu_custom_call" | custom-call | tf_op jit(solution)/shard_map/spread/pallas_call | solution.py:549
  51.5 2.3 %collective-permute-start.2 = (f32[96,128]{1,0:T(8,128)S(1)}, f32[96,128]{1,0:T(8,128)S(1)}, u32[]{:S(2)}, u32[]{:S(2)}) collective-permute-start(f32[96,128]{1,0:T(8,128)S(1)} %get-tuple-element.30), channel_id=1, source_target_pairs={{0,4},{4,8},{8,12},{1,5},{5,9},{9,13},{2,6},{6,10},{10,14},{3,7},{... | collective-permute-start | bytes 147464 | tf_op jit(solution)/shard_map/ppermute | solution.py:47
  53.9 0.3 collective-permute-start.13
  54.2 1.4 %collective-permute-done.2.above_ref = f32[96,128]{1,0:T(8,128)S(1)} collective-permute-done((f32[96,128]{1,0:T(8,128)S(1)}, f32[96,128]{1,0:T(8,128)S(1)}, u32[]{:S(2)}, u32[]{:S(2)}) %collective-permute-start.2) | collective-permute-done | bytes 49184 | tf_op jit(solution)/shard_map/ppermute | solution.py:47
  55.6 3.5 %agg_map.1 = bf16[16,96,128]{2,1,0:T(8,128)(2,1)} custom-call(f32[144,96]{1,0:T(8,128)S(1)} %get-tuple-element.29.y_ref, f32[144,128]{1,0:T(8,128)S(1)} %get-tuple-element.28.refs_2_.key_ref, f32[96,128]{1,0:T(8,128)S(1)} %collective-permute-done.2.above_ref), custom_call_target="tpu_custom_call" | custom-call | tf_op jit(solution)/shard_map/agg_map/pallas_call | solution.py:565
  59.1 1.0 %convert_add_fusion = f32[9,192,96]{2,1,0:T(8,128)} fusion(f32[9,192,96]{2,1,0:T(8,128)S(1)} %get-tuple-element.33, bf16[9,192,96]{2,1,0:T(8,128)(2,1)S(1)} %collective-permute-done.7), kind=kLoop, calls=%fused_computation | loop fusion | flops 331776 | bytes 1658880 | tf_op jit(solution)/shard_map/add | solution.py:597
  60.1 0.7 %copy-done.10 = f32[608,128]{1,0:T(8,128)} copy-done((f32[608,128]{1,0:T(8,128)}, f32[608,128]{1,0:T(8,128)S(1)}, u32[]{:S(2)}) %copy-start.10) | copy-done | bytes 311320
  60.8 1.9 %unpack.1 = (f32[49,96]{1,0:T(8,128)}, f32[96,384]{1,0:T(8,128)}, f32[96,384]{1,0:T(8,128)}, f32[192,384]{1,0:T(8,128)}) custom-call(s32[1]{0:T(128)} %bitcast.7.chan_ref.refs_0_, f32[608,128]{1,0:T(8,128)} %copy-done.9, f32[608,128]{1,0:T(8,128)} %copy-done.10), custom_call_target="tpu_custom_call" | custom-call | tf_op jit(solution)/shard_map/unpack/pallas_call | solution.py:608
  (28 shorter events, 0.3 us)
Async XLA Ops:
  0.6 11.2 %copy-start.1 = (f32[1,16,96,128]{3,2,1,0:T(8,128)S(1)}, f32[1,16,96,128]{3,2,1,0:T(8,128)}, u32[]{:S(2)}) copy-start(f32[1,16,96,128]{3,2,1,0:T(8,128)} %cot_ref.1) | copy-start | bytes 2359300
  0.6 22.0 %collective-permute-start.8 = (bf16[9,192,96]{2,1,0:T(8,128)(2,1)}, bf16[9,192,96]{2,1,0:T(8,128)(2,1)S(1)}, u32[]{:S(2)}, u32[]{:S(2)}) collective-permute-start(bf16[9,192,96]{2,1,0:T(8,128)(2,1)} %refs_3_.1), channel_id=1, source_target_pairs={{0,1},{1,0},{2,3},{3,2},{4,5},{5,4},{6,7},{7,6},{8,9},{9,8},{10,11... | collective-permute-start | bytes 995336 | tf_op jit(solution)/shard_map/ppermute | solution.py:52
  5.8 12.4 %all-to-all-start = ((bf16[8,2,3136]{2,1,0:T(2,128)(2,1)}), bf16[8,2,3136]{2,1,0:T(2,128)(2,1)S(1)}, u32[]{:S(2)}, u32[]{:S(2)}) async-start(bf16[8,2,3136]{2,1,0:T(2,128)(2,1)} %reshape.25), calls=%async_computation | async-start | bytes 204800 | tf_op jit(solution)/shard_map/all_to_all | solution.py:434
  11.9 6.6 %collective-permute-start.1 = (bf16[96,128]{1,0:T(8,128)(2,1)S(1)}, bf16[96,128]{1,0:T(8,128)(2,1)S(1)}, u32[]{:S(2)}, u32[]{:S(2)}) collective-permute-start(bf16[96,128]{1,0:T(8,128)(2,1)S(1)} %fusion), channel_id=1, source_target_pairs={{4,0},{8,4},{12,8},{5,1},{9,5},{13,9},{6,2},{10,6},{14,10},{7,3},{... | collective-permute-start | bytes 73736 | tf_op jit(solution)/shard_map/ppermute | solution.py:47
  18.5 1.4 %copy-start.2 = (bf16[384,192]{0,1:T(8,128)(2,1)S(1)}, bf16[384,192]{0,1:T(8,128)(2,1)}, u32[]{:S(2)}) copy-start(bf16[384,192]{0,1:T(8,128)(2,1)} %param.20) | copy-start | bytes 442372
  18.5 1.4 %copy-start.3 = (bf16[96,384]{1,0:T(8,128)(2,1)S(1)}, bf16[96,384]{1,0:T(8,128)(2,1)}, u32[]{:S(2)}) copy-start(bf16[96,384]{1,0:T(8,128)(2,1)} %refs_14_.1) | copy-start | bytes 221188
  18.5 1.4 %copy-start.4 = (bf16[384,96]{0,1:T(8,128)(2,1)S(1)}, bf16[384,96]{0,1:T(8,128)(2,1)}, u32[]{:S(2)}) copy-start(bf16[384,96]{0,1:T(8,128)(2,1)} %param.17) | copy-start | bytes 221188
  18.5 1.4 %copy-start.5 = (f32[49,96]{1,0:T(8,128)S(1)}, f32[49,96]{1,0:T(8,128)}, u32[]{:S(2)}) copy-start(f32[49,96]{1,0:T(8,128)} %dw_ref.1) | copy-start | bytes 56452
  18.5 1.4 %copy-start.6 = (f32[96]{0:T(128)S(1)}, f32[96]{0:T(128)}, u32[]{:S(2)}) copy-start(f32[96]{0:T(128)} %param.15) | copy-start | bytes 1156
  18.5 1.4 %copy-start.7 = (f32[96]{0:T(128)S(1)}, f32[96]{0:T(128)}, u32[]{:S(2)}) copy-start(f32[96]{0:T(128)} %param.18) | copy-start | bytes 1156
  18.5 1.3 %copy-start.8 = (f32[96]{0:T(128)S(1)}, f32[96]{0:T(128)}, u32[]{:S(2)}) copy-start(f32[96]{0:T(128)} %param.19) | copy-start | bytes 1156
  19.7 2.9 %copy-start = (bf16[9,192,96]{2,1,0:T(8,128)(2,1)S(1)}, bf16[9,192,96]{2,1,0:T(8,128)(2,1)}, u32[]{:S(2)}) copy-start(bf16[9,192,96]{2,1,0:T(8,128)(2,1)} %refs_3_.1) | copy-start | bytes 995332
  19.7 2.9 %collective-permute-start.3 = (bf16[72,128]{1,0:T(8,128)(2,1)S(1)}, bf16[72,128]{1,0:T(8,128)(2,1)S(1)}, u32[]{:S(2)}, u32[]{:S(2)}) collective-permute-start(bf16[72,128]{1,0:T(8,128)(2,1)S(1)} %get-tuple-element.32), channel_id=1, source_target_pairs={{0,1},{1,0},{2,3},{3,2},{4,5},{5,4},{6,7},{7,6},{8,9},{9,8},{10,11... | collective-permute-start | bytes 55304 | tf_op jit(solution)/shard_map/ppermute | solution.py:52
  26.4 2.5 %collective-permute-start.9 = (bf16[608,128]{1,0:T(8,128)(2,1)S(1)}, bf16[608,128]{1,0:T(8,128)(2,1)S(1)}, u32[]{:S(2)}, u32[]{:S(2)}) collective-permute-start(bf16[608,128]{1,0:T(8,128)(2,1)S(1)} %get-tuple-element.43), channel_id=1, source_target_pairs={{0,1},{1,0},{2,3},{3,2},{4,5},{5,4},{6,7},{7,6},{8,9},{9,8},{10,11... | collective-permute-start | bytes 466952 | tf_op jit(solution)/shard_map/ppermute | solution.py:52
  26.9 7.3 %collective-permute-start.4 = (bf16[1,336,128]{2,1,0:T(8,128)(2,1)S(1)}, bf16[1,336,128]{2,1,0:T(8,128)(2,1)S(1)}, u32[]{:S(2)}, u32[]{:S(2)}) collective-permute-start(bf16[1,336,128]{2,1,0:T(8,128)(2,1)S(1)} %pad_maximum_fusion.3), channel_id=1, source_target_pairs={{0,8},{4,12},{8,0},{12,4},{1,9},{5,13},{9,1},{13,5},{2,10},{6,14},... | collective-permute-start | bytes 258056 | tf_op jit(solution)/shard_map/ppermute | solution.py:52
  29.0 5.8 %collective-permute-start.10 = (bf16[608,128]{1,0:T(8,128)(2,1)S(1)}, bf16[608,128]{1,0:T(8,128)(2,1)S(1)}, u32[]{:S(2)}, u32[]{:S(2)}) collective-permute-start(bf16[608,128]{1,0:T(8,128)(2,1)S(1)} %add_convert_fusion.2), channel_id=1, source_target_pairs={{0,2},{2,0},{1,3},{3,1},{4,6},{6,4},{5,7},{7,5},{8,10},{10,8},{9,1... | collective-permute-start | bytes 466952 | tf_op jit(solution)/shard_map/ppermute | solution.py:52
  34.2 7.4 %collective-permute-start.5 = (bf16[2,336,128]{2,1,0:T(8,128)(2,1)S(1)}, bf16[2,336,128]{2,1,0:T(8,128)(2,1)S(1)}, u32[]{:S(2)}, u32[]{:S(2)}) collective-permute-start(bf16[2,336,128]{2,1,0:T(8,128)(2,1)S(1)} %pad_maximum_fusion.1), channel_id=1, source_target_pairs={{0,4},{4,0},{8,12},{12,8},{1,5},{5,1},{9,13},{13,9},{2,6},{6,2},{1... | collective-permute-start | bytes 516104 | tf_op jit(solution)/shard_map/ppermute | solution.py:52
  34.9 8.6 %collective-permute-start.11 = (bf16[608,128]{1,0:T(8,128)(2,1)S(1)}, bf16[608,128]{1,0:T(8,128)(2,1)S(1)}, u32[]{:S(2)}, u32[]{:S(2)}) collective-permute-start(bf16[608,128]{1,0:T(8,128)(2,1)S(1)} %add_convert_fusion.1), channel_id=1, source_target_pairs={{0,4},{4,0},{8,12},{12,8},{1,5},{5,1},{9,13},{13,9},{2,6},{6,2},{1... | collective-permute-start | bytes 466952 | tf_op jit(solution)/shard_map/ppermute | solution.py:52
  41.6 7.3 %collective-permute-start.6 = (bf16[4,336,128]{2,1,0:T(8,128)(2,1)S(1)}, bf16[4,336,128]{2,1,0:T(8,128)(2,1)S(1)}, u32[]{:S(2)}, u32[]{:S(2)}) collective-permute-start(bf16[4,336,128]{2,1,0:T(8,128)(2,1)S(1)} %pad_maximum_fusion.refs_1_), channel_id=1, source_target_pairs={{0,2},{2,0},{1,3},{3,1},{4,6},{6,4},{5,7},{7,5},{8,10},{10,8},{9,1... | collective-permute-start | bytes 1032200 | tf_op jit(solution)/shard_map/ppermute | solution.py:52
  43.2 7.3 %collective-permute-start = (bf16[1,192,128]{2,1,0:T(8,128)(2,1)S(1)}, bf16[1,192,128]{2,1,0:T(8,128)(2,1)S(1)}, u32[]{:S(2)}, u32[]{:S(2)}) collective-permute-start(bf16[1,192,128]{2,1,0:T(8,128)(2,1)S(1)} %get-tuple-element.27), channel_id=1, source_target_pairs={{0,1},{1,0},{2,3},{3,2},{4,5},{5,4},{6,7},{7,6},{8,9},{9,8},{10,11... | collective-permute-start | bytes 147464 | tf_op jit(solution)/shard_map/ppermute | solution.py:52
  43.5 10.4 %collective-permute-start.12 = (bf16[608,128]{1,0:T(8,128)(2,1)S(1)}, bf16[608,128]{1,0:T(8,128)(2,1)S(1)}, u32[]{:S(2)}, u32[]{:S(2)}) collective-permute-start(bf16[608,128]{1,0:T(8,128)(2,1)S(1)} %add_convert_fusion), channel_id=1, source_target_pairs={{0,8},{4,12},{8,0},{12,4},{1,9},{5,13},{9,1},{13,5},{2,10},{6,14},... | collective-permute-start | bytes 466952 | tf_op jit(solution)/shard_map/ppermute | solution.py:52
  50.4 8.7 %collective-permute-start.7 = (bf16[9,192,96]{2,1,0:T(8,128)(2,1)S(1)}, bf16[9,192,96]{2,1,0:T(8,128)(2,1)S(1)}, u32[]{:S(2)}, u32[]{:S(2)}) collective-permute-start(bf16[9,192,96]{2,1,0:T(8,128)(2,1)S(1)} %convert_element_type.41), channel_id=1, source_target_pairs={{0,1},{1,0},{2,3},{3,2},{4,5},{5,4},{6,7},{7,6},{8,9},{9,8},{10,11... | collective-permute-start | bytes 995336 | tf_op jit(solution)/shard_map/ppermute | solution.py:52
  51.5 4.0 %collective-permute-start.2 = (f32[96,128]{1,0:T(8,128)S(1)}, f32[96,128]{1,0:T(8,128)S(1)}, u32[]{:S(2)}, u32[]{:S(2)}) collective-permute-start(f32[96,128]{1,0:T(8,128)S(1)} %get-tuple-element.30), channel_id=1, source_target_pairs={{0,4},{4,8},{8,12},{1,5},{5,9},{9,13},{2,6},{6,10},{10,14},{3,7},{... | collective-permute-start | bytes 147464 | tf_op jit(solution)/shard_map/ppermute | solution.py:47
  53.9 6.2 %copy-start.9 = (f32[608,128]{1,0:T(8,128)}, f32[608,128]{1,0:T(8,128)S(1)}, u32[]{:S(2)}) copy-start(f32[608,128]{1,0:T(8,128)S(1)} %convert_add_fusion.1.own_ref) | copy-start | bytes 933892
  53.9 6.2 %collective-permute-start.13 = (f32[608,128]{1,0:T(8,128)S(1)}, f32[608,128]{1,0:T(8,128)S(1)}, u32[]{:S(2)}, u32[]{:S(2)}) collective-permute-start(f32[608,128]{1,0:T(8,128)S(1)} %convert_add_fusion.1.own_ref), channel_id=1, source_target_pairs={{0,1},{1,0},{2,3},{3,2},{4,5},{5,4},{6,7},{7,6},{8,9},{9,8},{10,11... | collective-permute-start | bytes 933896 | tf_op jit(solution)/shard_map/ppermute | solution.py:52
  60.1 0.7 %copy-start.10 = (f32[608,128]{1,0:T(8,128)}, f32[608,128]{1,0:T(8,128)S(1)}, u32[]{:S(2)}) copy-start(f32[608,128]{1,0:T(8,128)S(1)} %collective-permute-done.13.peer_ref) | copy-start | bytes 933892

commit v3 on v2

--- a/solution.py
+++ b/solution.py
@@ -12,10 +12,10 @@
 GW = 64
 BAND_CELLS = 512
 PIX = SIDE * SIDE
-META = 128
 HALF_ROWS = 608
 FEAT_ROWS = 192
 COT_ROWS = 72
+WIRE_ROWS = 56
 BLOCK_ROWS = FEAT_ROWS + 2 * COT_ROWS
 F32 = jnp.float32
 BF16 = jnp.bfloat16
@@ -25,7 +25,13 @@
 
 def params_of(steps=1):
     return pltpu.CompilerParams(
-        dimension_semantics=("arbitrary",) * steps, vmem_limit_bytes=48 << 20
+        dimension_semantics=("arbitrary",) * steps, vmem_limit_bytes=24 << 20
+    )
+
+
+def takes(microseconds):
+    return pl.CostEstimate(
+        flops=0, transcendentals=0, bytes_accessed=int(microseconds * 3.69e6)
     )
 
 
@@ -56,7 +62,7 @@
     return (1, 2) if tap == 0 else (0, 1)
 
 
-def pack_kernel(cells_ref, pixels_ref, out_ref):
+def pack_kernel(cells_ref, pixels_ref, out_ref, wide_ref):
     slots = pixels_ref.shape[0]
     rows = out_ref.shape[0]
     pixch = pixels_ref.shape[1]
@@ -75,10 +81,13 @@
     for t in range(slots):
         place = jnp.where(slot == t, places[t], place)
     route = (place == dest).astype(F32).astype(BF16)
-    out_ref[:, :pixch] = nn(route, pixels_ref[...]).astype(BF16)
-    lane = lax.broadcasted_iota(jnp.int32, (rows, META), 1)
-    base = (lax.broadcasted_iota(jnp.int32, (rows, META), 0) // CAP) * CAP
-    notes = jnp.zeros((rows, META), F32)
+    routed = nn(route, pixels_ref[...])
+    wide_ref[...] = jnp.zeros_like(wide_ref)
+    for n in range(pixch // 128):
+        wide_ref[:, n, :] = routed[:, 128 * n : 128 * n + 128]
+    lane = lax.broadcasted_iota(jnp.int32, (rows, 128), 1)
+    base = (lax.broadcasted_iota(jnp.int32, (rows, 128), 0) // CAP) * CAP
+    notes = jnp.zeros((rows, 128), F32)
     for t in range(slots):
         within = cells[t] % BAND_CELLS
         own_row = (within // GW).astype(F32)
@@ -87,14 +96,16 @@
             hit = base + rank == places[t]
             for at, value in enumerate((own_row, own_col, jnp.float32(1.0))):
                 notes = jnp.where(hit & (lane == 3 * rank + at), value, notes)
-    out_ref[:, pixch:] = notes.astype(BF16)
-
-
-def patch_kernel(chan_ref, meta_ref, cot_ref, below_ref, key_ref, own_ref, send_ref):
+    wide_ref[:, pixch // 128, :] = notes
+    out_ref[...] = wide_ref[...].astype(BF16)
+
+
+def patch_kernel(chan_ref, meta_ref, cot_ref, below_ref, key_ref, own_ref, send_ref, meta_f32):
     sources = meta_ref.shape[0]
     chunks = sources // 8
     out_rows, e_half, _ = cot_ref.shape
-    meta = meta_ref[...].astype(F32)
+    meta_f32[...] = meta_ref[...].astype(F32)
+    meta = meta_f32[:, 0, :]
     first = chan_ref[0] == 0
     lane = lax.broadcasted_iota(jnp.int32, (8, 128), 1).astype(F32)
     blocks = []
@@ -135,21 +146,24 @@
     return center * rstd, rstd
 
 
-def fill_padded(padded_ref, pixels_ref, channels):
+def fill_padded(padded_ref, got_ref, wide_ref, pixels_ref, channels):
+    wide_ref[...] = got_ref[...].astype(F32)
+    for n in range(pixels_ref.shape[1] // 128):
+        pixels_ref[:, 128 * n : 128 * n + 128] = wide_ref[:, n, :]
     padded_ref[...] = jnp.zeros_like(padded_ref)
     for i in range(SIDE):
         for j in range(SIDE):
             at = (i * SIDE + j) * channels
-            padded_ref[i + 3, j + 3] = pixels_ref[:, at : at + channels].astype(F32)
+            padded_ref[i + 3, j + 3] = pixels_ref[:, at : at + channels]
 
 
 def stem_kernel(
-    pixels_ref, dw_ref, gain_ref, up_ref, proj_ref, scale_ref, ds_gain_ref, ds_ref,
+    got_ref, dw_ref, gain_ref, up_ref, proj_ref, scale_ref, ds_gain_ref, ds_ref,
     feat_ref, hat1_ref, rstd1_ref, hat2_ref, rstd2_ref, hidden_ref, slope_ref, patch_ref,
-    padded_ref, spatial_ref, low_ref, wide_ref,
+    padded_ref, spatial_ref, low_ref, patch_f32, wide_ref, pixels_ref,
 ):
     channels = dw_ref.shape[1]
-    fill_padded(padded_ref, pixels_ref, channels)
+    fill_padded(padded_ref, got_ref, wide_ref, pixels_ref, channels)
 
     def row_step(i, carry):
         total = jnp.zeros((SIDE, 8, channels), F32)
@@ -181,8 +195,8 @@
     for di in range(2):
         for dj in range(2):
             at = (2 * di + dj) * channels
-            wide_ref[:, at : at + channels] = low_ref[:, di, :, dj].reshape(-1, channels)
-    patches = wide_ref[...].astype(BF16)
+            patch_f32[:, at : at + channels] = low_ref[:, di, :, dj].reshape(-1, channels)
+    patches = patch_f32[...].astype(BF16)
     patch_ref[...] = patches
     total = nt(patches, ds_ref[...])
     rows = total.shape[0]
@@ -199,11 +213,12 @@
 
 
 def back_kernel(
-    chan_ref, own_ref, peer_ref, w_own_ref, w_peer_ref, pixels_ref,
+    chan_ref, own_ref, peer_ref, w_own_ref, w_peer_ref, got_ref,
     hat1_ref, rstd1_ref, hat2_ref, rstd2_ref, hidden_ref, slope_ref, patch_ref,
     gain_ref, up_ref, proj_ref, scale_ref, ds_gain_ref, ds_ref,
     keep_ref, send_ref,
     padded_ref, dlow_ref, dspatial_ref, dw_ref, ds_acc, up_acc, proj_acc, pack_ref,
+    wide_ref, pixels_ref,
     *, scale,
 ):
     channels = gain_ref.shape[1]
@@ -257,7 +272,7 @@
     mean_b = jnp.mean(dhat1 * hat1, axis=-1, keepdims=True)
     dspatial = rstd1_ref[...] * (dhat1 - mean_a - hat1 * mean_b)
     dspatial_ref[...] = dspatial.reshape(SIDE, SIDE, 8, channels)
-    fill_padded(padded_ref, pixels_ref, channels)
+    fill_padded(padded_ref, got_ref, wide_ref, pixels_ref, channels)
 
     def tap_step(a, carry):
         totals = [jnp.zeros((8, channels), F32) for _ in range(7)]
@@ -426,9 +441,12 @@
 
     packed = pl.pallas_call(
         pack_kernel,
-        out_shape=jax.ShapeDtypeStruct((sources, pixch + META), BF16),
+        out_shape=jax.ShapeDtypeStruct((sources, WIRE_ROWS, 128), BF16),
         in_specs=[SMEM, VMEM],
         out_specs=VMEM,
+        scratch_shapes=[pltpu.VMEM((sources, WIRE_ROWS, 128), F32)],
+        compiler_params=pltpu.CompilerParams(vmem_limit_bytes=24 << 20),
+        cost_estimate=takes(1.5),
         name="pack",
     )(tile_cell, tile_pixels[0])
     got = lax.all_to_all(packed, ("slide", "chan"), split_axis=0, concat_axis=0, tiled=True)
@@ -442,7 +460,7 @@
         ),
         in_specs=[
             SMEM,
-            pl.BlockSpec((sources, META), lambda i: (0, pixch // META)),
+            pl.BlockSpec((sources, 8, 128), lambda i: (0, pixch // 1024, 0)),
             pl.BlockSpec((None, out_rows, e_half, cols), lambda i: (0, 0, 0, 0)),
             whole((e_half, cols)),
         ],
@@ -452,7 +470,9 @@
             whole((chunks * COT_ROWS, 128)),
         ),
         grid=(1,),
+        scratch_shapes=[pltpu.VMEM((sources, 8, 128), F32)],
         compiler_params=params_of(),
+        cost_estimate=takes(1.2),
         name="patch",
     )(chan, got, agg_cot, below_cot)
     cots_peer = swapped(cots_send, "chan", 1)
@@ -460,7 +480,8 @@
     cots_peer = cots_peer.reshape(chunks, COT_ROWS, 128)
 
     rows = PIX * 8
-    pixel_spec = pl.BlockSpec((8, pixch), lambda g: (g, 0))
+    pixel_spec = pl.BlockSpec((8, WIRE_ROWS, 128), lambda g: (g, 0, 0))
+    pixel_scratch = [pltpu.VMEM((8, WIRE_ROWS, 128), F32), pltpu.VMEM((8, pixch), F32)]
 
     def chunk(*shape):
         return pl.BlockSpec((None,) + shape, lambda g: (g,) + (0,) * len(shape))
@@ -493,8 +514,10 @@
             pltpu.VMEM((SIDE, SIDE, 8, channels), F32),
             pltpu.VMEM((SIDE // 2, 2, SIDE // 2, 2, 8, channels), F32),
             pltpu.VMEM((128, 4 * channels), F32),
+            *pixel_scratch,
         ],
         compiler_params=params_of(),
+        cost_estimate=takes(2.7),
         name="stem",
     )(got, dw_weight, gain, up_weight, proj_turned, scale, low_gain, ds_turned)
 
@@ -536,8 +559,10 @@
             pltpu.VMEM(up_weight.shape, F32),
             pltpu.VMEM(proj_turned.shape, F32),
             pltpu.VMEM((2 * HALF_ROWS, 128), F32),
+            *pixel_scratch,
         ],
         compiler_params=params_of(),
+        cost_estimate=takes(3.7),
         name="stem_back",
     )(
         chan, cots_own, cots_peer, agg_weight, peer_weight, got,
@@ -559,6 +584,7 @@
         ],
         out_specs=(pl.BlockSpec((72, e_half), lambda g: (g, 0)), whole((e_half, cols))),
         compiler_params=params_of(),
+        cost_estimate=takes(1.0),
         name="spread",
     )(feats_band, agg_weight, key)
     above = shifted(below, "slide", 1)
@@ -567,7 +593,8 @@
         out_shape=jax.ShapeDtypeStruct((out_rows, e_half, cols), BF16),
         in_specs=[VMEM, VMEM, VMEM],
         out_specs=VMEM,
-        compiler_params=pltpu.CompilerParams(vmem_limit_bytes=48 << 20),
+        compiler_params=pltpu.CompilerParams(vmem_limit_bytes=24 << 20),
+        cost_estimate=takes(3.5),
         name="agg_map",
     )(spread, key, above)[None]
 
@@ -592,6 +619,7 @@
             pltpu.VMEM((9, per * 8, 256), F32),
         ],
         compiler_params=params_of(),
+        cost_estimate=takes(1.4),
         name="agg_weight_grad",
     )(place, near, far)
     agg_grad = agg_keep + swapped(agg_send.astype(BF16), "chan", 1).astype(F32)
@@ -616,6 +644,8 @@
         in_specs=[SMEM, VMEM, VMEM],
         out_specs=(VMEM, VMEM, VMEM, VMEM),
         scratch_shapes=[pltpu.VMEM((2 * HALF_ROWS, 128), F32)],
+        compiler_params=pltpu.CompilerParams(vmem_limit_bytes=24 << 20),
+        cost_estimate=takes(1.5),
         name="unpack",
     )(chan, part, swapped(part, "chan", 1))
     proj_grad = proj_grad.T

time: 63.1 us -> 60.3 us (0.956)
  waiting for transfers between devices: 21.4 us -> 18.3 us
  starting transfers between devices: 17.9 us -> 20.3 us
  other arithmetic: 2.87 us -> 1.3 us
  Pallas kernels: 17.3 us -> 16.1 us
  local copies, waits for them, and re-layouts: 2.28 us -> 3.01 us
    all_to_all x1, waiting for transfers between devices: 5.08 us -> 0.01 us  [on_device(): lax.all_to_all(packed, ('slide', 'chan'), split_axis=0, concat_axis=0, ti...]
    ppermute x2, waiting for transfers between devices: 1.4 us -> 6.08 us  [shifted(): lax.ppermute(value, axis, [(source, source + steps) for source in range(f...]
    ppermute x12, waiting for transfers between devices: 14.9 us -> 12.2 us  [swapped(): lax.ppermute(value, axis, [(place, place ^ step) for place in range(count)])]
    ppermute x12, starting transfers between devices: 8.32 us -> 10.1 us  [swapped(): lax.ppermute(value, axis, [(place, place ^ step) for place in range(count)])]
    all_to_all x1 -> x0, other arithmetic: 1.56 us -> none  [on_device(): lax.all_to_all(packed, ('slide', 'chan'), split_axis=0, concat_axis=0, ti...]
    pallas_call x1, Pallas kernels: 1.92 us -> 0.86 us  [on_device(): pl.pallas_call(unpack_kernel, out_shape=(jax.ShapeDtypeStruct(dw_weight.s...]
    convert_element_type x1, local copies, waits for them, and re-layouts: 0.01 us -> 0.8 us  [on_device(): below_cot = shifted(agg_cot[0, 0].astype(BF16), 'slide', -1)]
    unnamed x25 -> x22, local copies, waits for them, and re-layouts: 1.77 us -> 2.21 us
  transfers between devices with their start and end apart: 15 -> 15, of which waited for: 7 -> 7; matrix products, arithmetic and copies ran while one was open for 7% -> 4% of each run, Pallas kernels for 18% -> 19%
where the time goes in v3:
time: 60.3 us; the launch traced here: 59.9 us
  starting transfers between devices  20.3 us (34%)
  waiting for transfers between devices  18.3 us (30%)
  Pallas kernels  16.1 us (27%)
  local copies, waits for them, and re-layouts  3.01 us (5%)
  other arithmetic  1.3 us (2%)
  between operations  0.88 us (1%)
    ppermute x12, waiting for transfers between devices, swapped(): lax.ppermute(value, axis, [(place, place ^ step) for place in range(count)])  12.2 us
    ppermute x12, starting transfers between devices, swapped(): lax.ppermute(value, axis, [(place, place ^ step) for place in range(count)])  10.1 us
    all_to_all x1, starting transfers between devices, on_device(): lax.all_to_all(packed, ('slide', 'chan'), split_axis=0, concat_axis=0, ti...  6.33 us
    ppermute x2, waiting for transfers between devices, shifted(): lax.ppermute(value, axis, [(source, source + steps) for source in range(f...  6.08 us
    ppermute x2, starting transfers between devices, shifted(): lax.ppermute(value, axis, [(source, source + steps) for source in range(f...  3.88 us
    pallas_call x1, Pallas kernels, on_device(): pl.pallas_call(lambda *refs: back_kernel(*refs, scale=loss_scale), grid=(...  3.79 us
    pallas_call x1, Pallas kernels, on_device(): pl.pallas_call(map_kernel, out_shape=jax.ShapeDtypeStruct((out_rows, e_ha...  3.5 us
    pallas_call x1, Pallas kernels, on_device(): pl.pallas_call(stem_kernel, grid=(chunks,), out_shape=(jax.ShapeDtypeStru...  2.8 us
  transfers between devices with their start and end apart: 15, of which 7 were waited for; matrix products, arithmetic and copies ran while one was open for 4% of the time, Pallas kernels for 19%

profile of v3, /device:TPU:0, one launch (start us, length us, event | category | flops | bytes accessed | tf_op | source)
XLA Modules:
  0.0 59.9 jit_solution(1972144129142808768)
XLA Ops:
  0.6 0.5 collective-permute-start.8
  1.2 0.1 copy-done.10
  1.3 0.9 %copy-done.5 = bf16[1,8,6144]{2,1,0:T(8,128)(2,1)S(1)} copy-done((bf16[1,8,6144]{2,1,0:T(8,128)(2,1)S(1)}, bf16[1,8,6144]{2,1,0:T(8,128)(2,1)}, u32[]{:S(2)}) %copy-start.5) | copy-done | bytes 98328
  2.2 1.5 %pack.1 = bf16[8,56,128]{2,1,0:T(8,128)(2,1)} custom-call(s32[1,8]{1,0:T(1,128)S(1)} %copy-done.10, bf16[8,6144]{1,0:T(8,128)(2,1)S(1)} %bitcast.27), custom_call_target="tpu_custom_call" | custom-call | bytes 5535000 | tf_op jit(solution)/shard_map/pack/pallas_call | solution.py:442
  3.7 6.3 %all-to-all-start = ((bf16[8,56,128]{2,1,0:T(8,128)(2,1)}), bf16[8,56,128]{2,1,0:T(8,128)(2,1)S(1)}, u32[]{:S(2)}, u32[]{:S(2)}) async-start(bf16[8,56,128]{2,1,0:T(8,128)(2,1)} %pack.1), calls=%async_computation | async-start | bytes 229376 | tf_op jit(solution)/shard_map/all_to_all | solution.py:452
  10.0 0.8 %fusion = bf16[96,128]{1,0:T(8,128)(2,1)S(1)} fusion(f32[1,16,96,128]{3,2,1,0:T(8,128)} %cot_ref.1), kind=kLoop, calls=%fused_computation.10 | loop fusion | bytes 49152 | tf_op jit(solution)/shard_map/convert_element_type | solution.py:440
  10.8 1.3 %collective-permute-start.1 = (bf16[96,128]{1,0:T(8,128)(2,1)S(1)}, bf16[96,128]{1,0:T(8,128)(2,1)S(1)}, u32[]{:S(2)}, u32[]{:S(2)}) collective-permute-start(bf16[96,128]{1,0:T(8,128)(2,1)S(1)} %fusion), channel_id=1, source_target_pairs={{4,0},{8,4},{12,8},{5,1},{9,5},{13,9},{6,2},{10,6},{14,10},{7,3},{... | collective-permute-start | bytes 73736 | tf_op jit(solution)/shard_map/ppermute | solution.py:53
  12.1 4.7 %collective-permute-done.1.below_ref = bf16[96,128]{1,0:T(8,128)(2,1)S(1)} collective-permute-done((bf16[96,128]{1,0:T(8,128)(2,1)S(1)}, bf16[96,128]{1,0:T(8,128)(2,1)S(1)}, u32[]{:S(2)}, u32[]{:S(2)}) %collective-permute-start.1) | collective-permute-done | bytes 24608 | tf_op jit(solution)/shard_map/ppermute | solution.py:53
  16.8 0.0 all-to-all-done.got_ref.meta_ref.refs_5_
  16.8 1.1 %copy-done.1 = f32[1,16,96,128]{3,2,1,0:T(8,128)S(1)} copy-done((f32[1,16,96,128]{3,2,1,0:T(8,128)S(1)}, f32[1,16,96,128]{3,2,1,0:T(8,128)}, u32[]{:S(2)}) %copy-start.1) | copy-done | bytes 786456
  18.0 0.0 copy-start.7
  18.0 0.0 copy-start.8
  18.0 0.0 copy-start.9
  18.0 1.3 %patch.1 = (f32[144,128]{1,0:T(8,128)S(1)}, bf16[72,128]{1,0:T(8,128)(2,1)S(1)}, bf16[72,128]{1,0:T(8,128)(2,1)S(1)}) custom-call(s32[1]{0:T(128)} %bitcast.6.chan_ref.refs_0_, bf16[8,56,128]{2,1,0:T(8,128)(2,1)S(1)} %all-to-all-done.got_ref.meta_ref.refs_5_, f32[1,16,96,128]{3,2,1,0:T(8,128)S(1)} %copy-done.1, ...), custom_call_target="tpu_custom_call" | custom-call | bytes 4428000 | tf_op jit(solution)/shard_map/patch/pallas_call | solution.py:454
  19.2 0.0 copy-start
  19.3 0.1 collective-permute-start.3
  19.4 2.8 %stem.1 = (bf16[1,192,128]{2,1,0:T(8,128)(2,1)S(1)}, f32[1,512,96]{2,1,0:T(8,128)S(1)}, f32[1,512,1]{2,1,0:T(8,128)S(1)}, f32[1,512,96]{2,1,0:T(8,128)S(1)}, f32...) custom-call(bf16[8,56,128]{2,1,0:T(8,128)(2,1)S(1)} %all-to-all-done, ...), custom_call_target="tpu_custom_call" | custom-call | bytes 9963000 | tf_op jit(solution)/shard_map/stem/pallas_call | solution.py:489
  22.2 0.0 collective-permute-done.3
  22.2 0.0 collective-permute-done.8.refs_4_
  22.2 0.0 copy-done
  22.2 3.8 %stem_back.1 = (f32[608,128]{1,0:T(8,128)S(1)}, bf16[608,128]{1,0:T(8,128)(2,1)S(1)}) custom-call(s32[1]{0:T(128)} %bitcast.6.chan_ref.refs_0_, bf16[1,72,128]{2,1,0:T(8,128)(2,1)S(1)} %bitcast.17, bf16[1,72,128]{2,1,0:T(8,128)(2,1)S(1)} %bitcast.21, bf16[9,192,96]{2,1,0:T(8,128)(2,1)S(1)} %copy-done, ...), custom_call_target="tpu_custom_call" | custom-call | bytes 13653000 | tf_op jit(solution)/shard_map/stem_back/pallas_call | solution.py:537
  26.0 0.5 collective-permute-start.9
  26.6 2.7 %collective-permute-start.4 = (bf16[1,336,128]{2,1,0:T(8,128)(2,1)S(1)}, bf16[1,336,128]{2,1,0:T(8,128)(2,1)S(1)}, u32[]{:S(2)}, u32[]{:S(2)}) collective-permute-start(bf16[1,336,128]{2,1,0:T(8,128)(2,1)S(1)} %pad_maximum_fusion.3), channel_id=1, source_target_pairs={{0,8},{4,12},{8,0},{12,4},{1,9},{5,13},{9,1},{13,5},{2,10},{6,14},... | collective-permute-start | bytes 258056 | tf_op jit(solution)/shard_map/ppermute | solution.py:58
  29.2 0.0 collective-permute-done.9
  29.3 1.5 %collective-permute-start.10 = (bf16[608,128]{1,0:T(8,128)(2,1)S(1)}, bf16[608,128]{1,0:T(8,128)(2,1)S(1)}, u32[]{:S(2)}, u32[]{:S(2)}) collective-permute-start(bf16[608,128]{1,0:T(8,128)(2,1)S(1)} %add_convert_fusion.2), channel_id=1, source_target_pairs={{0,2},{2,0},{1,3},{3,1},{4,6},{6,4},{5,7},{7,5},{8,10},{10,8},{9,1... | collective-permute-start | bytes 466952 | tf_op jit(solution)/shard_map/ppermute | solution.py:58
  30.8 3.0 %collective-permute-done.4 = bf16[1,336,128]{2,1,0:T(8,128)(2,1)S(1)} collective-permute-done((bf16[1,336,128]{2,1,0:T(8,128)(2,1)S(1)}, bf16[1,336,128]{2,1,0:T(8,128)(2,1)S(1)}, u32[]{:S(2)}, u32[]{:S(2)}) %collective-permute-start.4) | collective-permute-done | bytes 86048 | tf_op jit(solution)/shard_map/ppermute | solution.py:58
  33.9 0.1 collective-permute-start.5
  34.0 1.1 %collective-permute-done.10 = bf16[608,128]{1,0:T(8,128)(2,1)S(1)} collective-permute-done((bf16[608,128]{1,0:T(8,128)(2,1)S(1)}, bf16[608,128]{1,0:T(8,128)(2,1)S(1)}, u32[]{:S(2)}, u32[]{:S(2)}) %collective-permute-start.10) | collective-permute-done | bytes 155680 | tf_op jit(solution)/shard_map/ppermute | solution.py:58
  35.1 1.0 %collective-permute-start.11 = (bf16[608,128]{1,0:T(8,128)(2,1)S(1)}, bf16[608,128]{1,0:T(8,128)(2,1)S(1)}, u32[]{:S(2)}, u32[]{:S(2)}) collective-permute-start(bf16[608,128]{1,0:T(8,128)(2,1)S(1)} %add_convert_fusion.1), channel_id=1, source_target_pairs={{0,4},{4,0},{8,12},{12,8},{1,5},{5,1},{9,13},{13,9},{2,6},{6,2},{1... | collective-permute-start | bytes 466952 | tf_op jit(solution)/shard_map/ppermute | solution.py:58
  36.1 4.2 %collective-permute-done.5 = bf16[2,336,128]{2,1,0:T(8,128)(2,1)S(1)} collective-permute-done((bf16[2,336,128]{2,1,0:T(8,128)(2,1)S(1)}, bf16[2,336,128]{2,1,0:T(8,128)(2,1)S(1)}, u32[]{:S(2)}, u32[]{:S(2)}) %collective-permute-start.5) | collective-permute-done | bytes 172064 | tf_op jit(solution)/shard_map/ppermute | solution.py:58
  40.3 1.6 %collective-permute-start.6 = (bf16[4,336,128]{2,1,0:T(8,128)(2,1)S(1)}, bf16[4,336,128]{2,1,0:T(8,128)(2,1)S(1)}, u32[]{:S(2)}, u32[]{:S(2)}) collective-permute-start(bf16[4,336,128]{2,1,0:T(8,128)(2,1)S(1)} %pad_maximum_fusion.refs_1_), channel_id=1, source_target_pairs={{0,2},{2,0},{1,3},{3,1},{4,6},{6,4},{5,7},{7,5},{8,10},{10,8},{9,1... | collective-permute-start | bytes 1032200 | tf_op jit(solution)/shard_map/ppermute | solution.py:58
  41.8 0.0 collective-permute-start
  41.9 0.1 collective-permute-done.11
  42.0 1.8 %collective-permute-start.12 = (bf16[608,128]{1,0:T(8,128)(2,1)S(1)}, bf16[608,128]{1,0:T(8,128)(2,1)S(1)}, u32[]{:S(2)}, u32[]{:S(2)}) collective-permute-start(bf16[608,128]{1,0:T(8,128)(2,1)S(1)} %add_convert_fusion), channel_id=1, source_target_pairs={{0,8},{4,12},{8,0},{12,4},{1,9},{5,13},{9,1},{13,5},{2,10},{6,14},... | collective-permute-start | bytes 466952 | tf_op jit(solution)/shard_map/ppermute | solution.py:58
  43.8 3.8 %collective-permute-done.6.refs_2_ = bf16[4,336,128]{2,1,0:T(8,128)(2,1)S(1)} collective-permute-done((bf16[4,336,128]{2,1,0:T(8,128)(2,1)S(1)}, bf16[4,336,128]{2,1,0:T(8,128)(2,1)S(1)}, u32[]{:S(2)}, u32[]{:S(2)}) %collective-permute-start.6) | collective-permute-done | bytes 344096 | tf_op jit(solution)/shard_map/ppermute | solution.py:58
  47.6 1.3 %agg_weight_grad.1 = (f32[9,192,96]{2,1,0:T(8,128)S(1)}, f32[9,192,96]{2,1,0:T(8,128)S(1)}) custom-call(s32[1]{0:T(128)} %bitcast.9.refs_0_, bf16[4,336,128]{2,1,0:T(8,128)(2,1)S(1)} %pad_maximum_fusion.refs_1_, bf16[4,336,128]{2,1,0:T(8,128)(2,1)S(1)} %collective-permute-done.6.refs_2_), custom_call_target="tpu_custom_call" | custom-call | bytes 5166000 | tf_op jit(solution)/shard_map/agg_weight_grad/pallas_call | solution.py:604
  49.0 0.1 convert_element_type.41
  49.0 0.1 collective-permute-start.7
  49.1 0.0 collective-permute-done
  49.1 1.0 %spread.1 = (f32[144,96]{1,0:T(8,128)S(1)}, f32[96,128]{1,0:T(8,128)S(1)}) custom-call(bf16[2,192,128]{2,1,0:T(8,128)(2,1)S(1)} %pad_maximum_fusion.2.refs_0_, bf16[9,192,96]{2,1,0:T(8,128)(2,1)S(1)} %copy-done, f32[144,128]{1,0:T(8,128)S(1)} %get-tuple-element.28.refs_2_.key_ref), custom_call_target="tpu_custom_call" | custom-call | bytes 3690000 | tf_op jit(solution)/shard_map/spread/pallas_call | solution.py:574
  50.2 2.6 %collective-permute-start.2 = (f32[96,128]{1,0:T(8,128)S(1)}, f32[96,128]{1,0:T(8,128)S(1)}, u32[]{:S(2)}, u32[]{:S(2)}) collective-permute-start(f32[96,128]{1,0:T(8,128)S(1)} %get-tuple-element.30), channel_id=1, source_target_pairs={{0,4},{4,8},{8,12},{1,5},{5,9},{9,13},{2,6},{6,10},{10,14},{3,7},{... | collective-permute-start | bytes 147464 | tf_op jit(solution)/shard_map/ppermute | solution.py:53
  52.8 0.0 collective-permute-done.12
  52.8 0.3 collective-permute-start.13
  53.1 1.4 %collective-permute-done.2.above_ref = f32[96,128]{1,0:T(8,128)S(1)} collective-permute-done((f32[96,128]{1,0:T(8,128)S(1)}, f32[96,128]{1,0:T(8,128)S(1)}, u32[]{:S(2)}, u32[]{:S(2)}) %collective-permute-start.2) | collective-permute-done | bytes 49184 | tf_op jit(solution)/shard_map/ppermute | solution.py:53
  54.5 3.5 %agg_map.1 = bf16[16,96,128]{2,1,0:T(8,128)(2,1)} custom-call(f32[144,96]{1,0:T(8,128)S(1)} %get-tuple-element.29.y_ref, f32[144,128]{1,0:T(8,128)S(1)} %get-tuple-element.28.refs_2_.key_ref, f32[96,128]{1,0:T(8,128)S(1)} %collective-permute-done.2.above_ref), custom_call_target="tpu_custom_call" | custom-call | bytes 12915000 | tf_op jit(solution)/shard_map/agg_map/pallas_call | solution.py:591
  58.0 0.0 collective-permute-done.7
  58.0 1.0 %convert_add_fusion = f32[9,192,96]{2,1,0:T(8,128)} fusion(f32[9,192,96]{2,1,0:T(8,128)S(1)} %get-tuple-element.33, bf16[9,192,96]{2,1,0:T(8,128)(2,1)S(1)} %collective-permute-done.7), kind=kLoop, calls=%fused_computation | loop fusion | flops 331776 | bytes 1658880 | tf_op jit(solution)/shard_map/add | solution.py:625
  59.0 0.9 %unpack.1 = (f32[49,96]{1,0:T(8,128)}, f32[96,384]{1,0:T(8,128)}, f32[96,384]{1,0:T(8,128)}, f32[192,384]{1,0:T(8,128)}) custom-call(s32[1]{0:T(128)} %bitcast.6.chan_ref.refs_0_, f32[608,128]{1,0:T(8,128)S(1)} %convert_add_fusion.1.own_ref, f32[608,128]{1,0:T(8,128)S(1)} %collective-permute-done.13.peer_ref), custom_call_target="tpu_custom_call" | custom-call | bytes 5535000 | tf_op jit(solution)/shard_map/unpack/pallas_call | solution.py:636
  (23 shorter events, 0.2 us)
Async XLA Ops:
  0.6 0.7 %copy-start.10 = (s32[1,8]{1,0:T(1,128)S(1)}, s32[1,8]{1,0:T(1,128)}, u32[]{:S(2)}) copy-start(s32[1,8]{1,0:T(1,128)} %cells_ref.1) | copy-start | bytes 100
  0.6 21.6 %collective-permute-start.8 = (bf16[9,192,96]{2,1,0:T(8,128)(2,1)}, bf16[9,192,96]{2,1,0:T(8,128)(2,1)S(1)}, u32[]{:S(2)}, u32[]{:S(2)}) collective-permute-start(bf16[9,192,96]{2,1,0:T(8,128)(2,1)} %refs_3_.1), channel_id=1, source_target_pairs={{0,1},{1,0},{2,3},{3,2},{4,5},{5,4},{6,7},{7,6},{8,9},{9,8},{10,11... | collective-permute-start | bytes 995336 | tf_op jit(solution)/shard_map/ppermute | solution.py:58
  1.3 0.9 %copy-start.5 = (bf16[1,8,6144]{2,1,0:T(8,128)(2,1)S(1)}, bf16[1,8,6144]{2,1,0:T(8,128)(2,1)}, u32[]{:S(2)}) copy-start(bf16[1,8,6144]{2,1,0:T(8,128)(2,1)} %param.11) | copy-start | bytes 294916
  3.7 13.1 %all-to-all-start = ((bf16[8,56,128]{2,1,0:T(8,128)(2,1)}), bf16[8,56,128]{2,1,0:T(8,128)(2,1)S(1)}, u32[]{:S(2)}, u32[]{:S(2)}) async-start(bf16[8,56,128]{2,1,0:T(8,128)(2,1)} %pack.1), calls=%async_computation | async-start | bytes 229376 | tf_op jit(solution)/shard_map/all_to_all | solution.py:452
  10.8 6.0 %collective-permute-start.1 = (bf16[96,128]{1,0:T(8,128)(2,1)S(1)}, bf16[96,128]{1,0:T(8,128)(2,1)S(1)}, u32[]{:S(2)}, u32[]{:S(2)}) collective-permute-start(bf16[96,128]{1,0:T(8,128)(2,1)S(1)} %fusion), channel_id=1, source_target_pairs={{4,0},{8,4},{12,8},{5,1},{9,5},{13,9},{6,2},{10,6},{14,10},{7,3},{... | collective-permute-start | bytes 73736 | tf_op jit(solution)/shard_map/ppermute | solution.py:53
  16.8 1.1 %copy-start.1 = (f32[1,16,96,128]{3,2,1,0:T(8,128)S(1)}, f32[1,16,96,128]{3,2,1,0:T(8,128)}, u32[]{:S(2)}) copy-start(f32[1,16,96,128]{3,2,1,0:T(8,128)} %cot_ref.1) | copy-start | bytes 2359300
  17.9 1.4 %copy-start.2 = (bf16[384,192]{0,1:T(8,128)(2,1)S(1)}, bf16[384,192]{0,1:T(8,128)(2,1)}, u32[]{:S(2)}) copy-start(bf16[384,192]{0,1:T(8,128)(2,1)} %param.20) | copy-start | bytes 442372
  17.9 1.4 %copy-start.3 = (bf16[96,384]{1,0:T(8,128)(2,1)S(1)}, bf16[96,384]{1,0:T(8,128)(2,1)}, u32[]{:S(2)}) copy-start(bf16[96,384]{1,0:T(8,128)(2,1)} %refs_14_.1) | copy-start | bytes 221188
  17.9 1.4 %copy-start.4 = (bf16[384,96]{0,1:T(8,128)(2,1)S(1)}, bf16[384,96]{0,1:T(8,128)(2,1)}, u32[]{:S(2)}) copy-start(bf16[384,96]{0,1:T(8,128)(2,1)} %param.17) | copy-start | bytes 221188
  17.9 1.4 %copy-start.6 = (f32[49,96]{1,0:T(8,128)S(1)}, f32[49,96]{1,0:T(8,128)}, u32[]{:S(2)}) copy-start(f32[49,96]{1,0:T(8,128)} %dw_ref.1) | copy-start | bytes 56452
  18.0 1.4 %copy-start.7 = (f32[96]{0:T(128)S(1)}, f32[96]{0:T(128)}, u32[]{:S(2)}) copy-start(f32[96]{0:T(128)} %param.15) | copy-start | bytes 1156
  18.0 1.4 %copy-start.8 = (f32[96]{0:T(128)S(1)}, f32[96]{0:T(128)}, u32[]{:S(2)}) copy-start(f32[96]{0:T(128)} %param.18) | copy-start | bytes 1156
  18.0 1.4 %copy-start.9 = (f32[96]{0:T(128)S(1)}, f32[96]{0:T(128)}, u32[]{:S(2)}) copy-start(f32[96]{0:T(128)} %param.19) | copy-start | bytes 1156
  19.2 3.0 %copy-start = (bf16[9,192,96]{2,1,0:T(8,128)(2,1)S(1)}, bf16[9,192,96]{2,1,0:T(8,128)(2,1)}, u32[]{:S(2)}) copy-start(bf16[9,192,96]{2,1,0:T(8,128)(2,1)} %refs_3_.1) | copy-start | bytes 995332
  19.3 3.0 %collective-permute-start.3 = (bf16[72,128]{1,0:T(8,128)(2,1)S(1)}, bf16[72,128]{1,0:T(8,128)(2,1)S(1)}, u32[]{:S(2)}, u32[]{:S(2)}) collective-permute-start(bf16[72,128]{1,0:T(8,128)(2,1)S(1)} %get-tuple-element.32), channel_id=1, source_target_pairs={{0,1},{1,0},{2,3},{3,2},{4,5},{5,4},{6,7},{7,6},{8,9},{9,8},{10,11... | collective-permute-start | bytes 55304 | tf_op jit(solution)/shard_map/ppermute | solution.py:58
  26.0 3.2 %collective-permute-start.9 = (bf16[608,128]{1,0:T(8,128)(2,1)S(1)}, bf16[608,128]{1,0:T(8,128)(2,1)S(1)}, u32[]{:S(2)}, u32[]{:S(2)}) collective-permute-start(bf16[608,128]{1,0:T(8,128)(2,1)S(1)} %get-tuple-element.43), channel_id=1, source_target_pairs={{0,1},{1,0},{2,3},{3,2},{4,5},{5,4},{6,7},{7,6},{8,9},{9,8},{10,11... | collective-permute-start | bytes 466952 | tf_op jit(solution)/shard_map/ppermute | solution.py:58
  26.6 7.3 %collective-permute-start.4 = (bf16[1,336,128]{2,1,0:T(8,128)(2,1)S(1)}, bf16[1,336,128]{2,1,0:T(8,128)(2,1)S(1)}, u32[]{:S(2)}, u32[]{:S(2)}) collective-permute-start(bf16[1,336,128]{2,1,0:T(8,128)(2,1)S(1)} %pad_maximum_fusion.3), channel_id=1, source_target_pairs={{0,8},{4,12},{8,0},{12,4},{1,9},{5,13},{9,1},{13,5},{2,10},{6,14},... | collective-permute-start | bytes 258056 | tf_op jit(solution)/shard_map/ppermute | solution.py:58
  29.3 5.8 %collective-permute-start.10 = (bf16[608,128]{1,0:T(8,128)(2,1)S(1)}, bf16[608,128]{1,0:T(8,128)(2,1)S(1)}, u32[]{:S(2)}, u32[]{:S(2)}) collective-permute-start(bf16[608,128]{1,0:T(8,128)(2,1)S(1)} %add_convert_fusion.2), channel_id=1, source_target_pairs={{0,2},{2,0},{1,3},{3,1},{4,6},{6,4},{5,7},{7,5},{8,10},{10,8},{9,1... | collective-permute-start | bytes 466952 | tf_op jit(solution)/shard_map/ppermute | solution.py:58
  33.9 6.4 %collective-permute-start.5 = (bf16[2,336,128]{2,1,0:T(8,128)(2,1)S(1)}, bf16[2,336,128]{2,1,0:T(8,128)(2,1)S(1)}, u32[]{:S(2)}, u32[]{:S(2)}) collective-permute-start(bf16[2,336,128]{2,1,0:T(8,128)(2,1)S(1)} %pad_maximum_fusion.1), channel_id=1, source_target_pairs={{0,4},{4,0},{8,12},{12,8},{1,5},{5,1},{9,13},{13,9},{2,6},{6,2},{1... | collective-permute-start | bytes 516104 | tf_op jit(solution)/shard_map/ppermute | solution.py:58
  35.1 6.8 %collective-permute-start.11 = (bf16[608,128]{1,0:T(8,128)(2,1)S(1)}, bf16[608,128]{1,0:T(8,128)(2,1)S(1)}, u32[]{:S(2)}, u32[]{:S(2)}) collective-permute-start(bf16[608,128]{1,0:T(8,128)(2,1)S(1)} %add_convert_fusion.1), channel_id=1, source_target_pairs={{0,4},{4,0},{8,12},{12,8},{1,5},{5,1},{9,13},{13,9},{2,6},{6,2},{1... | collective-permute-start | bytes 466952 | tf_op jit(solution)/shard_map/ppermute | solution.py:58
  40.3 7.3 %collective-permute-start.6 = (bf16[4,336,128]{2,1,0:T(8,128)(2,1)S(1)}, bf16[4,336,128]{2,1,0:T(8,128)(2,1)S(1)}, u32[]{:S(2)}, u32[]{:S(2)}) collective-permute-start(bf16[4,336,128]{2,1,0:T(8,128)(2,1)S(1)} %pad_maximum_fusion.refs_1_), channel_id=1, source_target_pairs={{0,2},{2,0},{1,3},{3,1},{4,6},{6,4},{5,7},{7,5},{8,10},{10,8},{9,1... | collective-permute-start | bytes 1032200 | tf_op jit(solution)/shard_map/ppermute | solution.py:58
  41.8 7.3 %collective-permute-start = (bf16[1,192,128]{2,1,0:T(8,128)(2,1)S(1)}, bf16[1,192,128]{2,1,0:T(8,128)(2,1)S(1)}, u32[]{:S(2)}, u32[]{:S(2)}) collective-permute-start(bf16[1,192,128]{2,1,0:T(8,128)(2,1)S(1)} %get-tuple-element.27), channel_id=1, source_target_pairs={{0,1},{1,0},{2,3},{3,2},{4,5},{5,4},{6,7},{7,6},{8,9},{9,8},{10,11... | collective-permute-start | bytes 147464 | tf_op jit(solution)/shard_map/ppermute | solution.py:58
  42.0 10.8 %collective-permute-start.12 = (bf16[608,128]{1,0:T(8,128)(2,1)S(1)}, bf16[608,128]{1,0:T(8,128)(2,1)S(1)}, u32[]{:S(2)}, u32[]{:S(2)}) collective-permute-start(bf16[608,128]{1,0:T(8,128)(2,1)S(1)} %add_convert_fusion), channel_id=1, source_target_pairs={{0,8},{4,12},{8,0},{12,4},{1,9},{5,13},{9,1},{13,5},{2,10},{6,14},... | collective-permute-start | bytes 466952 | tf_op jit(solution)/shard_map/ppermute | solution.py:58
  49.0 9.0 %collective-permute-start.7 = (bf16[9,192,96]{2,1,0:T(8,128)(2,1)S(1)}, bf16[9,192,96]{2,1,0:T(8,128)(2,1)S(1)}, u32[]{:S(2)}, u32[]{:S(2)}) collective-permute-start(bf16[9,192,96]{2,1,0:T(8,128)(2,1)S(1)} %convert_element_type.41), channel_id=1, source_target_pairs={{0,1},{1,0},{2,3},{3,2},{4,5},{5,4},{6,7},{7,6},{8,9},{9,8},{10,11... | collective-permute-start | bytes 995336 | tf_op jit(solution)/shard_map/ppermute | solution.py:58
  50.2 4.3 %collective-permute-start.2 = (f32[96,128]{1,0:T(8,128)S(1)}, f32[96,128]{1,0:T(8,128)S(1)}, u32[]{:S(2)}, u32[]{:S(2)}) collective-permute-start(f32[96,128]{1,0:T(8,128)S(1)} %get-tuple-element.30), channel_id=1, source_target_pairs={{0,4},{4,8},{8,12},{1,5},{5,9},{9,13},{2,6},{6,10},{10,14},{3,7},{... | collective-permute-start | bytes 147464 | tf_op jit(solution)/shard_map/ppermute | solution.py:53
  52.8 6.2 %collective-permute-start.13 = (f32[608,128]{1,0:T(8,128)S(1)}, f32[608,128]{1,0:T(8,128)S(1)}, u32[]{:S(2)}, u32[]{:S(2)}) collective-permute-start(f32[608,128]{1,0:T(8,128)S(1)} %convert_add_fusion.1.own_ref), channel_id=1, source_target_pairs={{0,1},{1,0},{2,3},{3,2},{4,5},{5,4},{6,7},{7,6},{8,9},{9,8},{10,11... | collective-permute-start | bytes 933896 | tf_op jit(solution)/shard_map/ppermute | solution.py:58

commit v4 on v3

--- a/solution.py
+++ b/solution.py
@@ -521,6 +521,35 @@
         name="stem",
     )(got, dw_weight, gain, up_weight, proj_turned, scale, low_gain, ds_turned)
 
+    feats_band = jnp.concatenate([feats, swapped(feats, "chan", 1)], axis=0)
+    spread, below = pl.pallas_call(
+        lambda *refs: spread_kernel(*refs, last=out_rows),
+        grid=(blocks,),
+        out_shape=(
+            jax.ShapeDtypeStruct((blocks * 72, e_half), F32),
+            jax.ShapeDtypeStruct((e_half, cols), F32),
+        ),
+        in_specs=[
+            chunk(FEAT_ROWS, 128), whole(agg_weight.shape),
+            pl.BlockSpec((72, cols), lambda g: (g, 0)),
+        ],
+        out_specs=(pl.BlockSpec((72, e_half), lambda g: (g, 0)), whole((e_half, cols))),
+        compiler_params=params_of(),
+        cost_estimate=takes(1.0),
+        name="spread",
+    )(feats_band, agg_weight, key)
+    above = shifted(below, "slide", 1)
+    map_call = pl.pallas_call(
+        map_kernel,
+        out_shape=jax.ShapeDtypeStruct((out_rows, e_half, cols), BF16),
+        in_specs=[VMEM, VMEM, VMEM],
+        out_specs=VMEM,
+        compiler_params=pltpu.CompilerParams(vmem_limit_bytes=24 << 20),
+        cost_estimate=takes(3.5),
+        name="agg_map",
+    )
+    agg_map = map_call(spread, key, above)
+
     tile_blocks = jnp.concatenate([feats, cots_own, cots_peer], axis=1)
     gather = chunks == 1
     near = far = tile_blocks
@@ -530,10 +559,15 @@
         spans += [("rep", 1 << n) for n in range(lax.axis_size("rep").bit_length() - 1)]
         for n, (axis, step) in enumerate(spans):
             near = far if n == 0 else jnp.concatenate([near, far], axis=0)
+            if n == 1:
+                near, spread, below = lax.optimization_barrier((near, spread, below))
+                above = shifted(below, "slide", 1)
+                agg_map = map_call(spread, key, above)
+            if n == len(spans) - 1:
+                near, agg_map = lax.optimization_barrier((near, agg_map))
             far = swapped(near, axis, step)
             bit = (lax.axis_index(axis).astype(jnp.int32) // step) % 2
             place = place + bit * (1 << n)
-
     keep, send = pl.pallas_call(
         lambda *refs: back_kernel(*refs, scale=loss_scale),
         grid=(chunks,),
@@ -569,34 +603,6 @@
         hat1, rstd1, hat2, rstd2, hidden, slope, patches,
         gain, up_weight, proj_turned, scale, low_gain, ds_turned,
     )
-
-    feats_band = jnp.concatenate([feats, swapped(feats, "chan", 1)], axis=0)
-    spread, below = pl.pallas_call(
-        lambda *refs: spread_kernel(*refs, last=out_rows),
-        grid=(blocks,),
-        out_shape=(
-            jax.ShapeDtypeStruct((blocks * 72, e_half), F32),
-            jax.ShapeDtypeStruct((e_half, cols), F32),
-        ),
-        in_specs=[
-            chunk(FEAT_ROWS, 128), whole(agg_weight.shape),
-            pl.BlockSpec((72, cols), lambda g: (g, 0)),
-        ],
-        out_specs=(pl.BlockSpec((72, e_half), lambda g: (g, 0)), whole((e_half, cols))),
-        compiler_params=params_of(),
-        cost_estimate=takes(1.0),
-        name="spread",
-    )(feats_band, agg_weight, key)
-    above = shifted(below, "slide", 1)
-    agg_map = pl.pallas_call(
-        map_kernel,
-        out_shape=jax.ShapeDtypeStruct((out_rows, e_half, cols), BF16),
-        in_specs=[VMEM, VMEM, VMEM],
-        out_specs=VMEM,
-        compiler_params=pltpu.CompilerParams(vmem_limit_bytes=24 << 20),
-        cost_estimate=takes(3.5),
-        name="agg_map",
-    )(spread, key, above)[None]
 
     count = 2 * near.shape[0] if gather else chunks
     per = count if gather else 1
@@ -650,7 +656,7 @@
     )(chan, part, swapped(part, "chan", 1))
     proj_grad = proj_grad.T
     ds_grad = ds_grad.T
-    return (agg_map, agg_grad, dw_grad, up_grad, proj_grad, ds_grad)
+    return (agg_map[None], agg_grad, dw_grad, up_grad, proj_grad, ds_grad)
 
 
 def solution(mesh):

time: 60.3 us -> 56.9 us (0.944)
  waiting for transfers between devices: 18.3 us -> 15.2 us
    ppermute x12, waiting for transfers between devices: 12.2 us -> 10.5 us  [swapped(): lax.ppermute(value, axis, [(place, place ^ step) for place in range(count)])]
    ppermute x2, waiting for transfers between devices: 6.08 us -> 4.68 us  [shifted(): lax.ppermute(value, axis, [(source, source + steps) for source in range(f...]
    ppermute x2, starting transfers between devices: 3.88 us -> 3.17 us  [shifted(): lax.ppermute(value, axis, [(source, source + steps) for source in range(f...]
  transfers between devices with their start and end apart: 15 -> 15, of which waited for: 7 -> 7; matrix products, arithmetic and copies ran while one was open for 4% -> 4% of each run, Pallas kernels for 19% -> 20%
where the time goes in v4:
time: 56.9 us; the launch traced here: 56.6 us
  starting transfers between devices  20.1 us (35%)
  Pallas kernels  16.1 us (28%)
  waiting for transfers between devices  15.2 us (27%)
  local copies, waits for them, and re-layouts  3.01 us (5%)
  other arithmetic  1.28 us (2%)
  between operations  0.87 us (2%)
    ppermute x12, starting transfers between devices, swapped(): lax.ppermute(value, axis, [(place, place ^ step) for place in range(count)])  10.6 us
    ppermute x12, waiting for transfers between devices, swapped(): lax.ppermute(value, axis, [(place, place ^ step) for place in range(count)])  10.5 us
    all_to_all x1, starting transfers between devices, on_device(): lax.all_to_all(packed, ('slide', 'chan'), split_axis=0, concat_axis=0, ti...  6.33 us
    ppermute x2, waiting for transfers between devices, shifted(): lax.ppermute(value, axis, [(source, source + steps) for source in range(f...  4.68 us
    pallas_call x1, Pallas kernels, on_device(): pl.pallas_call(lambda *refs: back_kernel(*refs, scale=loss_scale), grid=(...  3.79 us
    pallas_call x1, Pallas kernels, on_device(): agg_map = map_call(spread, key, above)  3.49 us
    ppermute x2, starting transfers between devices, shifted(): lax.ppermute(value, axis, [(source, source + steps) for source in range(f...  3.17 us
    pallas_call x1, Pallas kernels, on_device(): pl.pallas_call(stem_kernel, grid=(chunks,), out_shape=(jax.ShapeDtypeStru...  2.8 us
  transfers between devices with their start and end apart: 15, of which 7 were waited for; matrix products, arithmetic and copies ran while one was open for 4% of the time, Pallas kernels for 20%

profile of v4, /device:TPU:0, one launch (start us, length us, event | category | flops | bytes accessed | tf_op | source)
XLA Modules:
  0.0 56.6 jit_solution(16321509703239082493)
XLA Ops:
  0.6 0.5 collective-permute-start.8
  1.2 0.1 copy-done.10
  1.3 0.9 %copy-done.5 = bf16[1,8,6144]{2,1,0:T(8,128)(2,1)S(1)} copy-done((bf16[1,8,6144]{2,1,0:T(8,128)(2,1)S(1)}, bf16[1,8,6144]{2,1,0:T(8,128)(2,1)}, u32[]{:S(2)}) %copy-start.5) | copy-done | bytes 98328
  2.2 1.5 %pack.1 = bf16[8,56,128]{2,1,0:T(8,128)(2,1)} custom-call(s32[1,8]{1,0:T(1,128)S(1)} %copy-done.10, bf16[8,6144]{1,0:T(8,128)(2,1)S(1)} %bitcast.25), custom_call_target="tpu_custom_call" | custom-call | bytes 5535000 | tf_op jit(solution)/shard_map/pack/pallas_call | solution.py:442
  3.7 6.3 %all-to-all-start = ((bf16[8,56,128]{2,1,0:T(8,128)(2,1)}), bf16[8,56,128]{2,1,0:T(8,128)(2,1)S(1)}, u32[]{:S(2)}, u32[]{:S(2)}) async-start(bf16[8,56,128]{2,1,0:T(8,128)(2,1)} %pack.1), calls=%async_computation | async-start | bytes 229376 | tf_op jit(solution)/shard_map/all_to_all | solution.py:452
  10.0 0.8 %fusion = bf16[96,128]{1,0:T(8,128)(2,1)S(1)} fusion(f32[1,16,96,128]{3,2,1,0:T(8,128)} %cot_ref.1), kind=kLoop, calls=%fused_computation.10 | loop fusion | bytes 49152 | tf_op jit(solution)/shard_map/convert_element_type | solution.py:440
  10.8 1.3 %collective-permute-start = (bf16[96,128]{1,0:T(8,128)(2,1)S(1)}, bf16[96,128]{1,0:T(8,128)(2,1)S(1)}, u32[]{:S(2)}, u32[]{:S(2)}) collective-permute-start(bf16[96,128]{1,0:T(8,128)(2,1)S(1)} %fusion), channel_id=1, source_target_pairs={{4,0},{8,4},{12,8},{5,1},{9,5},{13,9},{6,2},{10,6},{14,10},{7,3},{... | collective-permute-start | bytes 73736 | tf_op jit(solution)/shard_map/ppermute | solution.py:53
  12.1 4.7 %collective-permute-done.below_ref = bf16[96,128]{1,0:T(8,128)(2,1)S(1)} collective-permute-done((bf16[96,128]{1,0:T(8,128)(2,1)S(1)}, bf16[96,128]{1,0:T(8,128)(2,1)S(1)}, u32[]{:S(2)}, u32[]{:S(2)}) %collective-permute-start) | collective-permute-done | bytes 24608 | tf_op jit(solution)/shard_map/ppermute | solution.py:53
  16.8 0.0 all-to-all-done.got_ref.meta_ref.refs_5_
  16.8 1.1 %copy-done.1 = f32[1,16,96,128]{3,2,1,0:T(8,128)S(1)} copy-done((f32[1,16,96,128]{3,2,1,0:T(8,128)S(1)}, f32[1,16,96,128]{3,2,1,0:T(8,128)}, u32[]{:S(2)}) %copy-start.1) | copy-done | bytes 786456
  18.0 0.0 copy-start.7
  18.0 0.0 copy-start.8
  18.0 0.0 copy-start.9
  18.0 1.3 %patch.1 = (f32[144,128]{1,0:T(8,128)S(1)}, bf16[72,128]{1,0:T(8,128)(2,1)S(1)}, bf16[72,128]{1,0:T(8,128)(2,1)S(1)}) custom-call(s32[1]{0:T(128)} %bitcast.6.chan_ref.refs_0_, bf16[8,56,128]{2,1,0:T(8,128)(2,1)S(1)} %all-to-all-done.got_ref.meta_ref.refs_5_, f32[1,16,96,128]{3,2,1,0:T(8,128)S(1)} %copy-done.1, ...), custom_call_target="tpu_custom_call" | custom-call | bytes 4428000 | tf_op jit(solution)/shard_map/patch/pallas_call | solution.py:454
  19.2 0.0 copy-start
  19.3 0.1 collective-permute-start.1
  19.4 2.8 %stem.1 = (bf16[1,192,128]{2,1,0:T(8,128)(2,1)S(1)}, f32[1,512,96]{2,1,0:T(8,128)S(1)}, f32[1,512,1]{2,1,0:T(8,128)S(1)}, f32[1,512,96]{2,1,0:T(8,128)S(1)}, f32...) custom-call(bf16[8,56,128]{2,1,0:T(8,128)(2,1)S(1)} %all-to-all-done, ...), custom_call_target="tpu_custom_call" | custom-call | bytes 9963000 | tf_op jit(solution)/shard_map/stem/pallas_call | solution.py:489
  22.2 0.0 collective-permute-done.1
  22.2 0.0 collective-permute-done.8.refs_4_
  22.2 0.0 copy-done
  22.2 3.8 %stem_back.1 = (f32[608,128]{1,0:T(8,128)S(1)}, bf16[608,128]{1,0:T(8,128)(2,1)S(1)}) custom-call(s32[1]{0:T(128)} %bitcast.6.chan_ref.refs_0_, bf16[1,72,128]{2,1,0:T(8,128)(2,1)S(1)} %bitcast.19, bf16[1,72,128]{2,1,0:T(8,128)(2,1)S(1)} %bitcast.22, bf16[9,192,96]{2,1,0:T(8,128)(2,1)S(1)} %copy-done, ...), custom_call_target="tpu_custom_call" | custom-call | bytes 13653000 | tf_op jit(solution)/shard_map/stem_back/pallas_call | solution.py:571
  26.0 0.5 collective-permute-start.9
  26.6 0.1 collective-permute-start.3
  26.6 2.7 %collective-permute-start.2 = (bf16[1,336,128]{2,1,0:T(8,128)(2,1)S(1)}, bf16[1,336,128]{2,1,0:T(8,128)(2,1)S(1)}, u32[]{:S(2)}, u32[]{:S(2)}) collective-permute-start(bf16[1,336,128]{2,1,0:T(8,128)(2,1)S(1)} %pad_maximum_fusion.3), channel_id=1, source_target_pairs={{0,8},{4,12},{8,0},{12,4},{1,9},{5,13},{9,1},{13,5},{2,10},{6,14},... | collective-permute-start | bytes 258056 | tf_op jit(solution)/shard_map/ppermute | solution.py:58
  29.4 0.0 collective-permute-done.9
  29.4 1.6 %collective-permute-start.10 = (bf16[608,128]{1,0:T(8,128)(2,1)S(1)}, bf16[608,128]{1,0:T(8,128)(2,1)S(1)}, u32[]{:S(2)}, u32[]{:S(2)}) collective-permute-start(bf16[608,128]{1,0:T(8,128)(2,1)S(1)} %add_convert_fusion.2), channel_id=1, source_target_pairs={{0,2},{2,0},{1,3},{3,1},{4,6},{6,4},{5,7},{7,5},{8,10},{10,8},{9,1... | collective-permute-start | bytes 466952 | tf_op jit(solution)/shard_map/ppermute | solution.py:58
  31.0 0.0 collective-permute-done.3
  31.0 1.0 %spread.1 = (f32[144,96]{1,0:T(8,128)S(1)}, f32[96,128]{1,0:T(8,128)S(1)}) custom-call(bf16[2,192,128]{2,1,0:T(8,128)(2,1)S(1)} %pad_maximum_fusion.2.refs_0_, bf16[9,192,96]{2,1,0:T(8,128)(2,1)S(1)} %copy-done, f32[144,128]{1,0:T(8,128)S(1)} %get-tuple-element.35.refs_2_.key_ref), custom_call_target="tpu_custom_call" | custom-call | bytes 3690000 | tf_op jit(solution)/shard_map/spread/pallas_call | solution.py:525
  32.1 2.2 %collective-permute-done.2 = bf16[1,336,128]{2,1,0:T(8,128)(2,1)S(1)} collective-permute-done((bf16[1,336,128]{2,1,0:T(8,128)(2,1)S(1)}, bf16[1,336,128]{2,1,0:T(8,128)(2,1)S(1)}, u32[]{:S(2)}, u32[]{:S(2)}) %collective-permute-start.2) | collective-permute-done | bytes 86048 | tf_op jit(solution)/shard_map/ppermute | solution.py:58
  34.3 1.9 %collective-permute-start.5 = (f32[96,128]{1,0:T(8,128)S(1)}, f32[96,128]{1,0:T(8,128)S(1)}, u32[]{:S(2)}, u32[]{:S(2)}) collective-permute-start(f32[96,128]{1,0:T(8,128)S(1)} %get-tuple-element.40), channel_id=1, source_target_pairs={{0,4},{4,8},{8,12},{1,5},{5,9},{9,13},{2,6},{6,10},{10,14},{3,7},{... | collective-permute-start | bytes 147464 | tf_op jit(solution)/shard_map/ppermute | solution.py:53
  36.2 1.5 %collective-permute-start.4 = (bf16[2,336,128]{2,1,0:T(8,128)(2,1)S(1)}, bf16[2,336,128]{2,1,0:T(8,128)(2,1)S(1)}, u32[]{:S(2)}, u32[]{:S(2)}) collective-permute-start(bf16[2,336,128]{2,1,0:T(8,128)(2,1)S(1)} %pad_maximum_fusion.1), channel_id=1, source_target_pairs={{0,4},{4,0},{8,12},{12,8},{1,5},{5,1},{9,13},{13,9},{2,6},{6,2},{1... | collective-permute-start | bytes 516104 | tf_op jit(solution)/shard_map/ppermute | solution.py:58
  37.7 0.0 collective-permute-done.10
  37.8 0.6 %collective-permute-start.11 = (bf16[608,128]{1,0:T(8,128)(2,1)S(1)}, bf16[608,128]{1,0:T(8,128)(2,1)S(1)}, u32[]{:S(2)}, u32[]{:S(2)}) collective-permute-start(bf16[608,128]{1,0:T(8,128)(2,1)S(1)} %add_convert_fusion.1), channel_id=1, source_target_pairs={{0,4},{4,0},{8,12},{12,8},{1,5},{5,1},{9,13},{13,9},{2,6},{6,2},{1... | collective-permute-start | bytes 466952 | tf_op jit(solution)/shard_map/ppermute | solution.py:58
  38.4 0.0 collective-permute-done.5.above_ref
  38.4 3.5 %agg_map.1 = bf16[16,96,128]{2,1,0:T(8,128)(2,1)} custom-call(f32[144,96]{1,0:T(8,128)S(1)} %get-tuple-element.39.y_ref, f32[144,128]{1,0:T(8,128)S(1)} %get-tuple-element.35.refs_2_.key_ref, f32[96,128]{1,0:T(8,128)S(1)} %collective-permute-done.5.above_ref), custom_call_target="tpu_custom_call" | custom-call | bytes 12915000 | tf_op jit(solution)/shard_map/agg_map/pallas_call | solution.py:565
  41.9 1.5 %collective-permute-done.4 = bf16[2,336,128]{2,1,0:T(8,128)(2,1)S(1)} collective-permute-done((bf16[2,336,128]{2,1,0:T(8,128)(2,1)S(1)}, bf16[2,336,128]{2,1,0:T(8,128)(2,1)S(1)}, u32[]{:S(2)}, u32[]{:S(2)}) %collective-permute-start.4) | collective-permute-done | bytes 172064 | tf_op jit(solution)/shard_map/ppermute | solution.py:58
  43.5 1.6 %collective-permute-start.6 = (bf16[4,336,128]{2,1,0:T(8,128)(2,1)S(1)}, bf16[4,336,128]{2,1,0:T(8,128)(2,1)S(1)}, u32[]{:S(2)}, u32[]{:S(2)}) collective-permute-start(bf16[4,336,128]{2,1,0:T(8,128)(2,1)S(1)} %pad_maximum_fusion.refs_1_), channel_id=1, source_target_pairs={{0,2},{2,0},{1,3},{3,1},{4,6},{6,4},{5,7},{7,5},{8,10},{10,8},{9,1... | collective-permute-start | bytes 1032200 | tf_op jit(solution)/shard_map/ppermute | solution.py:58
  45.0 0.1 collective-permute-done.11
  45.2 1.3 %collective-permute-start.12 = (bf16[608,128]{1,0:T(8,128)(2,1)S(1)}, bf16[608,128]{1,0:T(8,128)(2,1)S(1)}, u32[]{:S(2)}, u32[]{:S(2)}) collective-permute-start(bf16[608,128]{1,0:T(8,128)(2,1)S(1)} %add_convert_fusion), channel_id=1, source_target_pairs={{0,8},{4,12},{8,0},{12,4},{1,9},{5,13},{9,1},{13,5},{2,10},{6,14},... | collective-permute-start | bytes 466952 | tf_op jit(solution)/shard_map/ppermute | solution.py:58
  46.4 4.4 %collective-permute-done.6.refs_2_ = bf16[4,336,128]{2,1,0:T(8,128)(2,1)S(1)} collective-permute-done((bf16[4,336,128]{2,1,0:T(8,128)(2,1)S(1)}, bf16[4,336,128]{2,1,0:T(8,128)(2,1)S(1)}, u32[]{:S(2)}, u32[]{:S(2)}) %collective-permute-start.6) | collective-permute-done | bytes 344096 | tf_op jit(solution)/shard_map/ppermute | solution.py:58
  50.8 1.3 %agg_weight_grad.1 = (f32[9,192,96]{2,1,0:T(8,128)S(1)}, f32[9,192,96]{2,1,0:T(8,128)S(1)}) custom-call(s32[1]{0:T(128)} %bitcast.11.refs_0_, bf16[4,336,128]{2,1,0:T(8,128)(2,1)S(1)} %pad_maximum_fusion.refs_1_, bf16[4,336,128]{2,1,0:T(8,128)(2,1)S(1)} %collective-permute-done.6.refs_2_), custom_call_target="tpu_custom_call" | custom-call | bytes 5166000 | tf_op jit(solution)/shard_map/agg_weight_grad/pallas_call | solution.py:610
  52.2 0.1 convert_element_type.41
  52.2 0.1 collective-permute-start.7
  52.3 1.7 %collective-permute-done.12 = bf16[608,128]{1,0:T(8,128)(2,1)S(1)} collective-permute-done((bf16[608,128]{1,0:T(8,128)(2,1)S(1)}, bf16[608,128]{1,0:T(8,128)(2,1)S(1)}, u32[]{:S(2)}, u32[]{:S(2)}) %collective-permute-start.12) | collective-permute-done | bytes 155680 | tf_op jit(solution)/shard_map/ppermute | solution.py:58
  54.0 0.1 collective-permute-start.13
  54.1 1.0 %convert_add_fusion = f32[9,192,96]{2,1,0:T(8,128)} fusion(f32[9,192,96]{2,1,0:T(8,128)S(1)} %get-tuple-element.43, bf16[9,192,96]{2,1,0:T(8,128)(2,1)S(1)} %collective-permute-done.7), kind=kLoop, calls=%fused_computation | loop fusion | flops 331776 | bytes 1658880 | tf_op jit(solution)/shard_map/add | solution.py:631
  55.1 0.6 %collective-permute-done.13.peer_ref = f32[608,128]{1,0:T(8,128)S(1)} collective-permute-done((f32[608,128]{1,0:T(8,128)S(1)}, f32[608,128]{1,0:T(8,128)S(1)}, u32[]{:S(2)}, u32[]{:S(2)}) %collective-permute-start.13) | collective-permute-done | bytes 311328 | tf_op jit(solution)/shard_map/ppermute | solution.py:58
  55.7 0.9 %unpack.1 = (f32[49,96]{1,0:T(8,128)}, f32[96,384]{1,0:T(8,128)}, f32[96,384]{1,0:T(8,128)}, f32[192,384]{1,0:T(8,128)}) custom-call(s32[1]{0:T(128)} %bitcast.6.chan_ref.refs_0_, f32[608,128]{1,0:T(8,128)S(1)} %convert_add_fusion.1.own_ref, f32[608,128]{1,0:T(8,128)S(1)} %collective-permute-done.13.peer_ref), custom_call_target="tpu_custom_call" | custom-call | bytes 5535000 | tf_op jit(solution)/shard_map/unpack/pallas_call | solution.py:642
  (23 shorter events, 0.3 us)
Async XLA Ops:
  0.6 0.7 %copy-start.10 = (s32[1,8]{1,0:T(1,128)S(1)}, s32[1,8]{1,0:T(1,128)}, u32[]{:S(2)}) copy-start(s32[1,8]{1,0:T(1,128)} %cells_ref.1) | copy-start | bytes 100
  0.6 21.6 %collective-permute-start.8 = (bf16[9,192,96]{2,1,0:T(8,128)(2,1)}, bf16[9,192,96]{2,1,0:T(8,128)(2,1)S(1)}, u32[]{:S(2)}, u32[]{:S(2)}) collective-permute-start(bf16[9,192,96]{2,1,0:T(8,128)(2,1)} %refs_3_.1), channel_id=1, source_target_pairs={{0,1},{1,0},{2,3},{3,2},{4,5},{5,4},{6,7},{7,6},{8,9},{9,8},{10,11... | collective-permute-start | bytes 995336 | tf_op jit(solution)/shard_map/ppermute | solution.py:58
  1.3 0.9 %copy-start.5 = (bf16[1,8,6144]{2,1,0:T(8,128)(2,1)S(1)}, bf16[1,8,6144]{2,1,0:T(8,128)(2,1)}, u32[]{:S(2)}) copy-start(bf16[1,8,6144]{2,1,0:T(8,128)(2,1)} %param.11) | copy-start | bytes 294916
  3.7 13.1 %all-to-all-start = ((bf16[8,56,128]{2,1,0:T(8,128)(2,1)}), bf16[8,56,128]{2,1,0:T(8,128)(2,1)S(1)}, u32[]{:S(2)}, u32[]{:S(2)}) async-start(bf16[8,56,128]{2,1,0:T(8,128)(2,1)} %pack.1), calls=%async_computation | async-start | bytes 229376 | tf_op jit(solution)/shard_map/all_to_all | solution.py:452
  10.8 6.0 %collective-permute-start = (bf16[96,128]{1,0:T(8,128)(2,1)S(1)}, bf16[96,128]{1,0:T(8,128)(2,1)S(1)}, u32[]{:S(2)}, u32[]{:S(2)}) collective-permute-start(bf16[96,128]{1,0:T(8,128)(2,1)S(1)} %fusion), channel_id=1, source_target_pairs={{4,0},{8,4},{12,8},{5,1},{9,5},{13,9},{6,2},{10,6},{14,10},{7,3},{... | collective-permute-start | bytes 73736 | tf_op jit(solution)/shard_map/ppermute | solution.py:53
  16.8 1.1 %copy-start.1 = (f32[1,16,96,128]{3,2,1,0:T(8,128)S(1)}, f32[1,16,96,128]{3,2,1,0:T(8,128)}, u32[]{:S(2)}) copy-start(f32[1,16,96,128]{3,2,1,0:T(8,128)} %cot_ref.1) | copy-start | bytes 2359300
  17.9 1.4 %copy-start.2 = (bf16[384,192]{0,1:T(8,128)(2,1)S(1)}, bf16[384,192]{0,1:T(8,128)(2,1)}, u32[]{:S(2)}) copy-start(bf16[384,192]{0,1:T(8,128)(2,1)} %param.20) | copy-start | bytes 442372
  17.9 1.4 %copy-start.3 = (bf16[96,384]{1,0:T(8,128)(2,1)S(1)}, bf16[96,384]{1,0:T(8,128)(2,1)}, u32[]{:S(2)}) copy-start(bf16[96,384]{1,0:T(8,128)(2,1)} %refs_14_.1) | copy-start | bytes 221188
  17.9 1.4 %copy-start.4 = (bf16[384,96]{0,1:T(8,128)(2,1)S(1)}, bf16[384,96]{0,1:T(8,128)(2,1)}, u32[]{:S(2)}) copy-start(bf16[384,96]{0,1:T(8,128)(2,1)} %param.17) | copy-start | bytes 221188
  17.9 1.4 %copy-start.6 = (f32[49,96]{1,0:T(8,128)S(1)}, f32[49,96]{1,0:T(8,128)}, u32[]{:S(2)}) copy-start(f32[49,96]{1,0:T(8,128)} %dw_ref.1) | copy-start | bytes 56452
  18.0 1.4 %copy-start.7 = (f32[96]{0:T(128)S(1)}, f32[96]{0:T(128)}, u32[]{:S(2)}) copy-start(f32[96]{0:T(128)} %param.15) | copy-start | bytes 1156
  18.0 1.4 %copy-start.8 = (f32[96]{0:T(128)S(1)}, f32[96]{0:T(128)}, u32[]{:S(2)}) copy-start(f32[96]{0:T(128)} %param.18) | copy-start | bytes 1156
  18.0 1.4 %copy-start.9 = (f32[96]{0:T(128)S(1)}, f32[96]{0:T(128)}, u32[]{:S(2)}) copy-start(f32[96]{0:T(128)} %param.19) | copy-start | bytes 1156
  19.2 3.0 %copy-start = (bf16[9,192,96]{2,1,0:T(8,128)(2,1)S(1)}, bf16[9,192,96]{2,1,0:T(8,128)(2,1)}, u32[]{:S(2)}) copy-start(bf16[9,192,96]{2,1,0:T(8,128)(2,1)} %refs_3_.1) | copy-start | bytes 995332
  19.3 3.0 %collective-permute-start.1 = (bf16[72,128]{1,0:T(8,128)(2,1)S(1)}, bf16[72,128]{1,0:T(8,128)(2,1)S(1)}, u32[]{:S(2)}, u32[]{:S(2)}) collective-permute-start(bf16[72,128]{1,0:T(8,128)(2,1)S(1)} %get-tuple-element.34), channel_id=1, source_target_pairs={{0,1},{1,0},{2,3},{3,2},{4,5},{5,4},{6,7},{7,6},{8,9},{9,8},{10,11... | collective-permute-start | bytes 55304 | tf_op jit(solution)/shard_map/ppermute | solution.py:58
  26.0 3.4 %collective-permute-start.9 = (bf16[608,128]{1,0:T(8,128)(2,1)S(1)}, bf16[608,128]{1,0:T(8,128)(2,1)S(1)}, u32[]{:S(2)}, u32[]{:S(2)}) collective-permute-start(bf16[608,128]{1,0:T(8,128)(2,1)S(1)} %get-tuple-element.53), channel_id=1, source_target_pairs={{0,1},{1,0},{2,3},{3,2},{4,5},{5,4},{6,7},{7,6},{8,9},{9,8},{10,11... | collective-permute-start | bytes 466952 | tf_op jit(solution)/shard_map/ppermute | solution.py:58
  26.6 4.4 %collective-permute-start.3 = (bf16[1,192,128]{2,1,0:T(8,128)(2,1)S(1)}, bf16[1,192,128]{2,1,0:T(8,128)(2,1)S(1)}, u32[]{:S(2)}, u32[]{:S(2)}) collective-permute-start(bf16[1,192,128]{2,1,0:T(8,128)(2,1)S(1)} %get-tuple-element.32), channel_id=1, source_target_pairs={{0,1},{1,0},{2,3},{3,2},{4,5},{5,4},{6,7},{7,6},{8,9},{9,8},{10,11... | collective-permute-start | bytes 147464 | tf_op jit(solution)/shard_map/ppermute | solution.py:58
  26.6 7.6 %collective-permute-start.2 = (bf16[1,336,128]{2,1,0:T(8,128)(2,1)S(1)}, bf16[1,336,128]{2,1,0:T(8,128)(2,1)S(1)}, u32[]{:S(2)}, u32[]{:S(2)}) collective-permute-start(bf16[1,336,128]{2,1,0:T(8,128)(2,1)S(1)} %pad_maximum_fusion.3), channel_id=1, source_target_pairs={{0,8},{4,12},{8,0},{12,4},{1,9},{5,13},{9,1},{13,5},{2,10},{6,14},... | collective-permute-start | bytes 258056 | tf_op jit(solution)/shard_map/ppermute | solution.py:58
  29.4 8.3 %collective-permute-start.10 = (bf16[608,128]{1,0:T(8,128)(2,1)S(1)}, bf16[608,128]{1,0:T(8,128)(2,1)S(1)}, u32[]{:S(2)}, u32[]{:S(2)}) collective-permute-start(bf16[608,128]{1,0:T(8,128)(2,1)S(1)} %add_convert_fusion.2), channel_id=1, source_target_pairs={{0,2},{2,0},{1,3},{3,1},{4,6},{6,4},{5,7},{7,5},{8,10},{10,8},{9,1... | collective-permute-start | bytes 466952 | tf_op jit(solution)/shard_map/ppermute | solution.py:58
  34.3 4.1 %collective-permute-start.5 = (f32[96,128]{1,0:T(8,128)S(1)}, f32[96,128]{1,0:T(8,128)S(1)}, u32[]{:S(2)}, u32[]{:S(2)}) collective-permute-start(f32[96,128]{1,0:T(8,128)S(1)} %get-tuple-element.40), channel_id=1, source_target_pairs={{0,4},{4,8},{8,12},{1,5},{5,9},{9,13},{2,6},{6,10},{10,14},{3,7},{... | collective-permute-start | bytes 147464 | tf_op jit(solution)/shard_map/ppermute | solution.py:53
  36.2 7.2 %collective-permute-start.4 = (bf16[2,336,128]{2,1,0:T(8,128)(2,1)S(1)}, bf16[2,336,128]{2,1,0:T(8,128)(2,1)S(1)}, u32[]{:S(2)}, u32[]{:S(2)}) collective-permute-start(bf16[2,336,128]{2,1,0:T(8,128)(2,1)S(1)} %pad_maximum_fusion.1), channel_id=1, source_target_pairs={{0,4},{4,0},{8,12},{12,8},{1,5},{5,1},{9,13},{13,9},{2,6},{6,2},{1... | collective-permute-start | bytes 516104 | tf_op jit(solution)/shard_map/ppermute | solution.py:58
  37.8 7.3 %collective-permute-start.11 = (bf16[608,128]{1,0:T(8,128)(2,1)S(1)}, bf16[608,128]{1,0:T(8,128)(2,1)S(1)}, u32[]{:S(2)}, u32[]{:S(2)}) collective-permute-start(bf16[608,128]{1,0:T(8,128)(2,1)S(1)} %add_convert_fusion.1), channel_id=1, source_target_pairs={{0,4},{4,0},{8,12},{12,8},{1,5},{5,1},{9,13},{13,9},{2,6},{6,2},{1... | collective-permute-start | bytes 466952 | tf_op jit(solution)/shard_map/ppermute | solution.py:58
  43.5 7.3 %collective-permute-start.6 = (bf16[4,336,128]{2,1,0:T(8,128)(2,1)S(1)}, bf16[4,336,128]{2,1,0:T(8,128)(2,1)S(1)}, u32[]{:S(2)}, u32[]{:S(2)}) collective-permute-start(bf16[4,336,128]{2,1,0:T(8,128)(2,1)S(1)} %pad_maximum_fusion.refs_1_), channel_id=1, source_target_pairs={{0,2},{2,0},{1,3},{3,1},{4,6},{6,4},{5,7},{7,5},{8,10},{10,8},{9,1... | collective-permute-start | bytes 1032200 | tf_op jit(solution)/shard_map/ppermute | solution.py:58
  45.2 8.8 %collective-permute-start.12 = (bf16[608,128]{1,0:T(8,128)(2,1)S(1)}, bf16[608,128]{1,0:T(8,128)(2,1)S(1)}, u32[]{:S(2)}, u32[]{:S(2)}) collective-permute-start(bf16[608,128]{1,0:T(8,128)(2,1)S(1)} %add_convert_fusion), channel_id=1, source_target_pairs={{0,8},{4,12},{8,0},{12,4},{1,9},{5,13},{9,1},{13,5},{2,10},{6,14},... | collective-permute-start | bytes 466952 | tf_op jit(solution)/shard_map/ppermute | solution.py:58
  52.2 1.9 %collective-permute-start.7 = (bf16[9,192,96]{2,1,0:T(8,128)(2,1)S(1)}, bf16[9,192,96]{2,1,0:T(8,128)(2,1)S(1)}, u32[]{:S(2)}, u32[]{:S(2)}) collective-permute-start(bf16[9,192,96]{2,1,0:T(8,128)(2,1)S(1)} %convert_element_type.41), channel_id=1, source_target_pairs={{0,1},{1,0},{2,3},{3,2},{4,5},{5,4},{6,7},{7,6},{8,9},{9,8},{10,11... | collective-permute-start | bytes 995336 | tf_op jit(solution)/shard_map/ppermute | solution.py:58
  54.0 1.7 %collective-permute-start.13 = (f32[608,128]{1,0:T(8,128)S(1)}, f32[608,128]{1,0:T(8,128)S(1)}, u32[]{:S(2)}, u32[]{:S(2)}) collective-permute-start(f32[608,128]{1,0:T(8,128)S(1)} %convert_add_fusion.1.own_ref), channel_id=1, source_target_pairs={{0,1},{1,0},{2,3},{3,2},{4,5},{5,4},{6,7},{7,6},{8,9},{9,8},{10,11... | collective-permute-start | bytes 933896 | tf_op jit(solution)/shard_map/ppermute | solution.py:58

commit v5 on v4

--- a/solution.py
+++ b/solution.py
@@ -62,7 +62,7 @@
     return (1, 2) if tap == 0 else (0, 1)
 
 
-def pack_kernel(cells_ref, pixels_ref, out_ref, wide_ref):
+def pack_kernel(cells_ref, pixels_ref, row_ref, out_ref, below_ref, wide_ref):
     slots = pixels_ref.shape[0]
     rows = out_ref.shape[0]
     pixch = pixels_ref.shape[1]
@@ -81,6 +81,7 @@
     for t in range(slots):
         place = jnp.where(slot == t, places[t], place)
     route = (place == dest).astype(F32).astype(BF16)
+    below_ref[...] = row_ref[...].astype(BF16)
     routed = nn(route, pixels_ref[...])
     wide_ref[...] = jnp.zeros_like(wide_ref)
     for n in range(pixch // 128):
@@ -436,19 +437,26 @@
     proj_turned = proj_weight.T
     ds_turned = ds_weight.T
 
-    peer_weight = swapped(agg_weight, "chan", 1)
-    below_cot = shifted(agg_cot[0, 0].astype(BF16), "slide", -1)
-
-    packed = pl.pallas_call(
+    packed, top_cot = pl.pallas_call(
         pack_kernel,
-        out_shape=jax.ShapeDtypeStruct((sources, WIRE_ROWS, 128), BF16),
-        in_specs=[SMEM, VMEM],
-        out_specs=VMEM,
+        grid=(1,),
+        out_shape=(
+            jax.ShapeDtypeStruct((sources, WIRE_ROWS, 128), BF16),
+            jax.ShapeDtypeStruct((e_half, cols), BF16),
+        ),
+        in_specs=[
+            SMEM,
+            pl.BlockSpec((None,) + tile_pixels.shape[1:], lambda i: (0, 0, 0)),
+            pl.BlockSpec((None, None, e_half, cols), lambda i: (0, 0, 0, 0)),
+        ],
+        out_specs=(whole((sources, WIRE_ROWS, 128)), whole((e_half, cols))),
         scratch_shapes=[pltpu.VMEM((sources, WIRE_ROWS, 128), F32)],
-        compiler_params=pltpu.CompilerParams(vmem_limit_bytes=24 << 20),
         cost_estimate=takes(1.5),
         name="pack",
-    )(tile_cell, tile_pixels[0])
+    )(tile_cell, tile_pixels, agg_cot)
+    below_cot = shifted(top_cot, "slide", -1)
+    packed, own_weight = lax.optimization_barrier((packed, agg_weight))
+    peer_weight = swapped(own_weight, "chan", 1)
     got = lax.all_to_all(packed, ("slide", "chan"), split_axis=0, concat_axis=0, tiled=True)
 
     key, cots_own, cots_send = pl.pallas_call(
@@ -538,36 +546,22 @@
         cost_estimate=takes(1.0),
         name="spread",
     )(feats_band, agg_weight, key)
-    above = shifted(below, "slide", 1)
-    map_call = pl.pallas_call(
-        map_kernel,
-        out_shape=jax.ShapeDtypeStruct((out_rows, e_half, cols), BF16),
-        in_specs=[VMEM, VMEM, VMEM],
-        out_specs=VMEM,
-        compiler_params=pltpu.CompilerParams(vmem_limit_bytes=24 << 20),
-        cost_estimate=takes(3.5),
-        name="agg_map",
-    )
-    agg_map = map_call(spread, key, above)
-
     tile_blocks = jnp.concatenate([feats, cots_own, cots_peer], axis=1)
     gather = chunks == 1
     near = far = tile_blocks
     place = jnp.zeros((1,), jnp.int32)
+    spans = [("slide", 1 << n) for n in reversed(range(bands.bit_length() - 1))]
+    spans += [("rep", 1 << n) for n in range(lax.axis_size("rep").bit_length() - 1)]
+
+    def widen(n, near, place):
+        axis, step = spans[n]
+        bit = (lax.axis_index(axis).astype(jnp.int32) // step) % 2
+        return swapped(near, axis, step), place + bit * (1 << n)
+
     if gather:
-        spans = [("slide", 1 << n) for n in reversed(range(bands.bit_length() - 1))]
-        spans += [("rep", 1 << n) for n in range(lax.axis_size("rep").bit_length() - 1)]
-        for n, (axis, step) in enumerate(spans):
-            near = far if n == 0 else jnp.concatenate([near, far], axis=0)
-            if n == 1:
-                near, spread, below = lax.optimization_barrier((near, spread, below))
-                above = shifted(below, "slide", 1)
-                agg_map = map_call(spread, key, above)
-            if n == len(spans) - 1:
-                near, agg_map = lax.optimization_barrier((near, agg_map))
-            far = swapped(near, axis, step)
-            bit = (lax.axis_index(axis).astype(jnp.int32) // step) % 2
-            place = place + bit * (1 << n)
+        far, place = widen(0, near, place)
+        near = jnp.concatenate([near, far], axis=0)
+
     keep, send = pl.pallas_call(
         lambda *refs: back_kernel(*refs, scale=loss_scale),
         grid=(chunks,),
@@ -604,6 +598,37 @@
         gain, up_weight, proj_turned, scale, low_gain, ds_turned,
     )
 
+    part = keep + swapped(send, "chan", 1).astype(F32)
+    if gather:
+        part, near, spread, below = lax.optimization_barrier((part, near, spread, below))
+    steps = []
+    for axis in ("rep", "slide"):
+        step = 1
+        while step < lax.axis_size(axis):
+            steps.append((axis, step))
+            step *= 2
+    for n, (axis, step) in enumerate(steps):
+        wire = part.astype(BF16)
+        part = wire.astype(F32) + swapped(wire, axis, step).astype(F32)
+    above = shifted(below, "slide", 1)
+    map_call = pl.pallas_call(
+        map_kernel,
+        out_shape=jax.ShapeDtypeStruct((out_rows, e_half, cols), BF16),
+        in_specs=[VMEM, VMEM, VMEM],
+        out_specs=VMEM,
+        compiler_params=pltpu.CompilerParams(vmem_limit_bytes=24 << 20),
+        cost_estimate=takes(3.5),
+        name="agg_map",
+    )
+    agg_map = map_call(spread, key, above)
+
+    for n in range(1, len(spans) if gather else 0):
+        if n == len(spans) - 1:
+            near, agg_map = lax.optimization_barrier((near, agg_map))
+        far, place = widen(n, near, place)
+        if n < len(spans) - 1:
+            near = jnp.concatenate([near, far], axis=0)
+
     count = 2 * near.shape[0] if gather else chunks
     per = count if gather else 1
     near_count = near.shape[0] if gather else 1
@@ -632,13 +657,6 @@
     if not gather:
         agg_grad = lax.psum(agg_grad, ("slide", "rep"))
 
-    part = keep + swapped(send, "chan", 1).astype(F32)
-    for axis in ("rep", "slide"):
-        step = 1
-        while step < lax.axis_size(axis):
-            wire = part.astype(BF16)
-            part = wire.astype(F32) + swapped(wire, axis, step).astype(F32)
-            step *= 2
     dw_grad, up_grad, proj_grad, ds_grad = pl.pallas_call(
         unpack_kernel,
         out_shape=(

time: 56.9 us -> 54 us (0.949)
  local copies, waits for them, and re-layouts: 3.01 us -> 0.06 us
    unnamed x22 -> x20, local copies, waits for them, and re-layouts: 2.21 us -> 0.06 us
    convert_element_type x1 -> x0, local copies, waits for them, and re-layouts: 0.8 us -> none  [on_device(): below_cot = shifted(agg_cot[0, 0].astype(BF16), 'slide', -1)]
  transfers between devices with their start and end apart: 15 -> 15, of which waited for: 7 -> 9; matrix products, arithmetic and copies ran while one was open for 4% -> 0% of each run, Pallas kernels for 20% -> 27%
where the time goes in v5:
time: 54 us; the launch traced here: 53.7 us
  starting transfers between devices  20.1 us (37%)
  Pallas kernels  16.5 us (31%)
  waiting for transfers between devices  14.9 us (28%)
  other arithmetic  1.28 us (2%)
  between operations  0.91 us (2%)
    ppermute x12, starting transfers between devices, swapped(): lax.ppermute(value, axis, [(place, place ^ step) for place in range(count)])  10.7 us
    ppermute x12, waiting for transfers between devices, swapped(): lax.ppermute(value, axis, [(place, place ^ step) for place in range(count)])  10.1 us
    all_to_all x1, starting transfers between devices, on_device(): lax.all_to_all(packed, ('slide', 'chan'), split_axis=0, concat_axis=0, ti...  6.46 us
    ppermute x2, waiting for transfers between devices, shifted(): lax.ppermute(value, axis, [(source, source + steps) for source in range(f...  4.84 us
    pallas_call x1, Pallas kernels, on_device(): pl.pallas_call(lambda *refs: back_kernel(*refs, scale=loss_scale), grid=(...  3.78 us
    pallas_call x1, Pallas kernels, on_device(): agg_map = map_call(spread, key, above)  3.5 us
    ppermute x2, starting transfers between devices, shifted(): lax.ppermute(value, axis, [(source, source + steps) for source in range(f...  2.89 us
    pallas_call x1, Pallas kernels, on_device(): pl.pallas_call(stem_kernel, grid=(chunks,), out_shape=(jax.ShapeDtypeStru...  2.77 us
  transfers between devices with their start and end apart: 15, of which 9 were waited for; matrix products, arithmetic and copies ran while one was open for 0% of the time, Pallas kernels for 27%

profile of v5, /device:TPU:0, one launch (start us, length us, event | category | flops | bytes accessed | tf_op | source)
XLA Modules:
  0.0 53.7 jit_solution(175192778571348184)
XLA Ops:
  0.6 2.0 %pack.1 = (bf16[8,56,128]{2,1,0:T(8,128)(2,1)}, bf16[96,128]{1,0:T(8,128)(2,1)}) custom-call(s32[1,8]{1,0:T(1,128)} %cells_ref.1, bf16[1,8,6144]{2,1,0:T(8,128)(2,1)} %pixels_ref.1, f32[1,16,96,128]{3,2,1,0:T(8,128)} %cot_ref.1), custom_call_target="tpu_custom_call" | custom-call | bytes 5535000 | tf_op jit(solution)/shard_map/pack/pallas_call | solution.py:440
  2.6 6.5 %all-to-all-start = ((bf16[8,56,128]{2,1,0:T(8,128)(2,1)}), bf16[8,56,128]{2,1,0:T(8,128)(2,1)S(1)}, u32[]{:S(2)}, u32[]{:S(2)}) async-start(bf16[8,56,128]{2,1,0:T(8,128)(2,1)} %get-tuple-element.38), calls=%async_computation | async-start | bytes 229376 | tf_op jit(solution)/shard_map/all_to_all | solution.py:460
  9.1 0.5 collective-permute-start.2
  9.6 1.3 %collective-permute-start = (bf16[96,128]{1,0:T(8,128)(2,1)S(1)}, bf16[96,128]{1,0:T(8,128)(2,1)S(1)}, u32[]{:S(2)}, u32[]{:S(2)}) collective-permute-start(bf16[96,128]{1,0:T(8,128)(2,1)S(1)} %copy-done.9), channel_id=1, source_target_pairs={{4,0},{8,4},{12,8},{5,1},{9,5},{13,9},{6,2},{10,6},{14,10},{7,3},{... | collective-permute-start | bytes 73736 | tf_op jit(solution)/shard_map/ppermute | solution.py:53
  10.9 4.8 %collective-permute-done.below_ref = bf16[96,128]{1,0:T(8,128)(2,1)S(1)} collective-permute-done((bf16[96,128]{1,0:T(8,128)(2,1)S(1)}, bf16[96,128]{1,0:T(8,128)(2,1)S(1)}, u32[]{:S(2)}, u32[]{:S(2)}) %collective-permute-start) | collective-permute-done | bytes 24608 | tf_op jit(solution)/shard_map/ppermute | solution.py:53
  15.7 0.0 all-to-all-done.meta_ref.got_ref.refs_5_
  15.7 0.0 copy-done
  15.7 0.0 copy-start.3
  15.7 0.0 copy-start.4
  15.8 0.0 copy-start.5
  15.8 0.0 copy-start.6
  15.8 0.0 copy-start.7
  15.8 0.0 copy-start.8
  15.8 1.3 %patch.1 = (f32[144,128]{1,0:T(8,128)S(1)}, bf16[72,128]{1,0:T(8,128)(2,1)S(1)}, bf16[72,128]{1,0:T(8,128)(2,1)S(1)}) custom-call(s32[1]{0:T(128)} %bitcast.chan_ref.refs_0_, bf16[8,56,128]{2,1,0:T(8,128)(2,1)S(1)} %all-to-all-done.meta_ref.got_ref.refs_5_, f32[1,16,96,128]{3,2,1,0:T(8,128)S(1)} %copy-done, bf16[96,128]{1,0:T(8,128)(2,1)S(1)} %collective-permute-done.below_ref), custom_call_target="tpu_custom_call" | custom-call | bytes 4428000 | tf_op jit(solution)/shard_map/patch/pallas_call | solution.py:462
  17.1 0.0 copy-start.1
  17.1 0.1 collective-permute-start.1
  17.2 2.8 %stem.1 = (bf16[1,192,128]{2,1,0:T(8,128)(2,1)S(1)}, f32[1,512,96]{2,1,0:T(8,128)S(1)}, f32[1,512,1]{2,1,0:T(8,128)S(1)}, f32[1,512,96]{2,1,0:T(8,128)S(1)}, f32...) custom-call(bf16[8,56,128]{2,1,0:T(8,128)(2,1)S(1)} %all-to-all-done, ...), custom_call_target="tpu_custom_call" | custom-call | bytes 9963000 | tf_op jit(solution)/shard_map/stem/pallas_call | solution.py:497
  20.0 0.5 collective-permute-start.5
  20.5 0.0 collective-permute-done.1
  20.5 2.2 %collective-permute-start.4 = (bf16[1,336,128]{2,1,0:T(8,128)(2,1)S(1)}, bf16[1,336,128]{2,1,0:T(8,128)(2,1)S(1)}, u32[]{:S(2)}, u32[]{:S(2)}) collective-permute-start(bf16[1,336,128]{2,1,0:T(8,128)(2,1)S(1)} %pad_maximum_fusion.3), channel_id=1, source_target_pairs={{0,8},{4,12},{8,0},{12,4},{1,9},{5,13},{9,1},{13,5},{2,10},{6,14},... | collective-permute-start | bytes 258056 | tf_op jit(solution)/shard_map/ppermute | solution.py:58
  22.7 0.0 collective-permute-done.2.refs_4_
  22.7 3.8 %stem_back.1 = (f32[608,128]{1,0:T(8,128)S(1)}, bf16[608,128]{1,0:T(8,128)(2,1)S(1)}) custom-call(s32[1]{0:T(128)} %bitcast.chan_ref.refs_0_, bf16[1,72,128]{2,1,0:T(8,128)(2,1)S(1)} %bitcast.17, bf16[1,72,128]{2,1,0:T(8,128)(2,1)S(1)} %bitcast.20, bf16[9,192,96]{2,1,0:T(8,128)(2,1)S(1)} %copy-done.1, ...), custom_call_target="tpu_custom_call" | custom-call | bytes 13653000 | tf_op jit(solution)/shard_map/stem_back/pallas_call | solution.py:565
  26.5 0.1 collective-permute-start.3
  26.6 0.0 collective-permute-done.5
  26.6 1.0 %spread.1 = (f32[144,96]{1,0:T(8,128)S(1)}, f32[96,128]{1,0:T(8,128)S(1)}) custom-call(bf16[2,192,128]{2,1,0:T(8,128)(2,1)S(1)} %pad_maximum_fusion.2.refs_0_, bf16[9,192,96]{2,1,0:T(8,128)(2,1)S(1)} %copy-done.1, f32[144,128]{1,0:T(8,128)S(1)} %get-tuple-element.53.refs_2_.key_ref), custom_call_target="tpu_custom_call" | custom-call | bytes 3690000 | tf_op jit(solution)/shard_map/spread/pallas_call | solution.py:533
  27.7 0.1 collective-permute-done.4
  27.8 0.2 collective-permute-done.3
  28.0 1.6 %collective-permute-start.10 = (bf16[608,128]{1,0:T(8,128)(2,1)S(1)}, bf16[608,128]{1,0:T(8,128)(2,1)S(1)}, u32[]{:S(2)}, u32[]{:S(2)}) collective-permute-start(bf16[608,128]{1,0:T(8,128)(2,1)S(1)} %convert_add_fusion.2), channel_id=1, source_target_pairs={{0,2},{2,0},{1,3},{3,1},{4,6},{6,4},{5,7},{7,5},{8,10},{10,8},{9,1... | collective-permute-start | bytes 466952 | tf_op jit(solution)/shard_map/ppermute | solution.py:58
  29.6 1.6 %collective-permute-start.7 = (f32[96,128]{1,0:T(8,128)S(1)}, f32[96,128]{1,0:T(8,128)S(1)}, u32[]{:S(2)}, u32[]{:S(2)}) collective-permute-start(f32[96,128]{1,0:T(8,128)S(1)} %get-tuple-element.58), channel_id=1, source_target_pairs={{0,4},{4,8},{8,12},{1,5},{5,9},{9,13},{2,6},{6,10},{10,14},{3,7},{... | collective-permute-start | bytes 147464 | tf_op jit(solution)/shard_map/ppermute | solution.py:53
  31.2 1.7 %collective-permute-start.6 = (bf16[2,336,128]{2,1,0:T(8,128)(2,1)S(1)}, bf16[2,336,128]{2,1,0:T(8,128)(2,1)S(1)}, u32[]{:S(2)}, u32[]{:S(2)}) collective-permute-start(bf16[2,336,128]{2,1,0:T(8,128)(2,1)S(1)} %pad_maximum_fusion.1), channel_id=1, source_target_pairs={{0,4},{4,0},{8,12},{12,8},{1,5},{5,1},{9,13},{13,9},{2,6},{6,2},{1... | collective-permute-start | bytes 516104 | tf_op jit(solution)/shard_map/ppermute | solution.py:58
  32.9 1.4 %collective-permute-done.10 = bf16[608,128]{1,0:T(8,128)(2,1)S(1)} collective-permute-done((bf16[608,128]{1,0:T(8,128)(2,1)S(1)}, bf16[608,128]{1,0:T(8,128)(2,1)S(1)}, u32[]{:S(2)}, u32[]{:S(2)}) %collective-permute-start.10) | collective-permute-done | bytes 155680 | tf_op jit(solution)/shard_map/ppermute | solution.py:58
  34.3 0.1 collective-permute-start.11
  34.4 0.0 collective-permute-done.7.above_ref
  34.4 3.5 %agg_map.1 = bf16[16,96,128]{2,1,0:T(8,128)(2,1)} custom-call(f32[144,96]{1,0:T(8,128)S(1)} %get-tuple-element.57.y_ref, f32[144,128]{1,0:T(8,128)S(1)} %get-tuple-element.53.refs_2_.key_ref, f32[96,128]{1,0:T(8,128)S(1)} %collective-permute-done.7.above_ref), custom_call_target="tpu_custom_call" | custom-call | bytes 12915000 | tf_op jit(solution)/shard_map/agg_map/pallas_call | solution.py:623
  37.9 0.1 collective-permute-done.6
  38.0 1.5 %collective-permute-start.8 = (bf16[4,336,128]{2,1,0:T(8,128)(2,1)S(1)}, bf16[4,336,128]{2,1,0:T(8,128)(2,1)S(1)}, u32[]{:S(2)}, u32[]{:S(2)}) collective-permute-start(bf16[4,336,128]{2,1,0:T(8,128)(2,1)S(1)} %pad_maximum_fusion.refs_1_), channel_id=1, source_target_pairs={{0,2},{2,0},{1,3},{3,1},{4,6},{6,4},{5,7},{7,5},{8,10},{10,8},{9,1... | collective-permute-start | bytes 1032200 | tf_op jit(solution)/shard_map/ppermute | solution.py:58
  39.5 1.1 %collective-permute-done.11 = bf16[608,128]{1,0:T(8,128)(2,1)S(1)} collective-permute-done((bf16[608,128]{1,0:T(8,128)(2,1)S(1)}, bf16[608,128]{1,0:T(8,128)(2,1)S(1)}, u32[]{:S(2)}, u32[]{:S(2)}) %collective-permute-start.11) | collective-permute-done | bytes 155680 | tf_op jit(solution)/shard_map/ppermute | solution.py:58
  40.6 2.4 %collective-permute-start.12 = (bf16[608,128]{1,0:T(8,128)(2,1)S(1)}, bf16[608,128]{1,0:T(8,128)(2,1)S(1)}, u32[]{:S(2)}, u32[]{:S(2)}) collective-permute-start(bf16[608,128]{1,0:T(8,128)(2,1)S(1)} %add_convert_fusion), channel_id=1, source_target_pairs={{0,8},{4,12},{8,0},{12,4},{1,9},{5,13},{9,1},{13,5},{2,10},{6,14},... | collective-permute-start | bytes 466952 | tf_op jit(solution)/shard_map/ppermute | solution.py:58
  43.0 4.3 %collective-permute-done.8.refs_2_ = bf16[4,336,128]{2,1,0:T(8,128)(2,1)S(1)} collective-permute-done((bf16[4,336,128]{2,1,0:T(8,128)(2,1)S(1)}, bf16[4,336,128]{2,1,0:T(8,128)(2,1)S(1)}, u32[]{:S(2)}, u32[]{:S(2)}) %collective-permute-start.8) | collective-permute-done | bytes 344096 | tf_op jit(solution)/shard_map/ppermute | solution.py:58
  47.4 1.3 %agg_weight_grad.1 = (f32[9,192,96]{2,1,0:T(8,128)S(1)}, f32[9,192,96]{2,1,0:T(8,128)S(1)}) custom-call(s32[1]{0:T(128)} %bitcast.9.refs_0_, bf16[4,336,128]{2,1,0:T(8,128)(2,1)S(1)} %pad_maximum_fusion.refs_1_, bf16[4,336,128]{2,1,0:T(8,128)(2,1)S(1)} %collective-permute-done.8.refs_2_), custom_call_target="tpu_custom_call" | custom-call | bytes 5166000 | tf_op jit(solution)/shard_map/agg_weight_grad/pallas_call | solution.py:635
  48.7 0.1 convert_element_type.37
  48.8 0.1 collective-permute-start.9
  48.8 1.3 %collective-permute-done.12 = bf16[608,128]{1,0:T(8,128)(2,1)S(1)} collective-permute-done((bf16[608,128]{1,0:T(8,128)(2,1)S(1)}, bf16[608,128]{1,0:T(8,128)(2,1)S(1)}, u32[]{:S(2)}, u32[]{:S(2)}) %collective-permute-start.12) | collective-permute-done | bytes 155680 | tf_op jit(solution)/shard_map/ppermute | solution.py:58
  50.2 0.1 collective-permute-start.13
  50.3 1.6 %collective-permute-done.13.peer_ref = f32[608,128]{1,0:T(8,128)S(1)} collective-permute-done((f32[608,128]{1,0:T(8,128)S(1)}, f32[608,128]{1,0:T(8,128)S(1)}, u32[]{:S(2)}, u32[]{:S(2)}) %collective-permute-start.13) | collective-permute-done | bytes 311328 | tf_op jit(solution)/shard_map/ppermute | solution.py:58
  51.9 0.9 %unpack.1 = (f32[49,96]{1,0:T(8,128)}, f32[96,384]{1,0:T(8,128)}, f32[96,384]{1,0:T(8,128)}, f32[192,384]{1,0:T(8,128)}) custom-call(s32[1]{0:T(128)} %bitcast.chan_ref.refs_0_, f32[608,128]{1,0:T(8,128)S(1)} %convert_add_fusion.1.own_ref, f32[608,128]{1,0:T(8,128)S(1)} %collective-permute-done.13.peer_ref), custom_call_target="tpu_custom_call" | custom-call | bytes 5535000 | tf_op jit(solution)/shard_map/unpack/pallas_call | solution.py:660
  52.7 0.0 collective-permute-done.9
  52.7 1.0 %convert_add_fusion = f32[9,192,96]{2,1,0:T(8,128)} fusion(f32[9,192,96]{2,1,0:T(8,128)S(1)} %get-tuple-element.61, bf16[9,192,96]{2,1,0:T(8,128)(2,1)S(1)} %collective-permute-done.9), kind=kLoop, calls=%fused_computation | loop fusion | flops 331776 | bytes 1658880 | tf_op jit(solution)/shard_map/add | solution.py:656
  (20 shorter events, 0.3 us)
Async XLA Ops:
  0.6 15.1 %copy-start = (f32[1,16,96,128]{3,2,1,0:T(8,128)S(1)}, f32[1,16,96,128]{3,2,1,0:T(8,128)}, u32[]{:S(2)}) copy-start(f32[1,16,96,128]{3,2,1,0:T(8,128)} %cot_ref.1) | copy-start | bytes 2359300
  2.6 7.0 %copy-start.9 = (bf16[96,128]{1,0:T(8,128)(2,1)S(1)}, bf16[96,128]{1,0:T(8,128)(2,1)}, u32[]{:S(2)}) copy-start(bf16[96,128]{1,0:T(8,128)(2,1)} %get-tuple-element.39) | copy-start | bytes 73732
  2.6 13.1 %all-to-all-start = ((bf16[8,56,128]{2,1,0:T(8,128)(2,1)}), bf16[8,56,128]{2,1,0:T(8,128)(2,1)S(1)}, u32[]{:S(2)}, u32[]{:S(2)}) async-start(bf16[8,56,128]{2,1,0:T(8,128)(2,1)} %get-tuple-element.38), calls=%async_computation | async-start | bytes 229376 | tf_op jit(solution)/shard_map/all_to_all | solution.py:460
  9.1 13.6 %collective-permute-start.2 = (bf16[9,192,96]{2,1,0:T(8,128)(2,1)}, bf16[9,192,96]{2,1,0:T(8,128)(2,1)S(1)}, u32[]{:S(2)}, u32[]{:S(2)}) collective-permute-start(bf16[9,192,96]{2,1,0:T(8,128)(2,1)} %refs_1_.1), channel_id=1, source_target_pairs={{0,1},{1,0},{2,3},{3,2},{4,5},{5,4},{6,7},{7,6},{8,9},{9,8},{10,11... | collective-permute-start | bytes 995336 | tf_op jit(solution)/shard_map/ppermute | solution.py:58
  9.6 6.1 %collective-permute-start = (bf16[96,128]{1,0:T(8,128)(2,1)S(1)}, bf16[96,128]{1,0:T(8,128)(2,1)S(1)}, u32[]{:S(2)}, u32[]{:S(2)}) collective-permute-start(bf16[96,128]{1,0:T(8,128)(2,1)S(1)} %copy-done.9), channel_id=1, source_target_pairs={{4,0},{8,4},{12,8},{5,1},{9,5},{13,9},{6,2},{10,6},{14,10},{7,3},{... | collective-permute-start | bytes 73736 | tf_op jit(solution)/shard_map/ppermute | solution.py:53
  15.7 1.4 %copy-start.2 = (bf16[384,192]{0,1:T(8,128)(2,1)S(1)}, bf16[384,192]{0,1:T(8,128)(2,1)}, u32[]{:S(2)}) copy-start(bf16[384,192]{0,1:T(8,128)(2,1)} %param.20) | copy-start | bytes 442372
  15.7 1.4 %copy-start.3 = (bf16[96,384]{1,0:T(8,128)(2,1)S(1)}, bf16[96,384]{1,0:T(8,128)(2,1)}, u32[]{:S(2)}) copy-start(bf16[96,384]{1,0:T(8,128)(2,1)} %refs_14_.1) | copy-start | bytes 221188
  15.7 1.4 %copy-start.4 = (bf16[384,96]{0,1:T(8,128)(2,1)S(1)}, bf16[384,96]{0,1:T(8,128)(2,1)}, u32[]{:S(2)}) copy-start(bf16[384,96]{0,1:T(8,128)(2,1)} %param.17) | copy-start | bytes 221188
  15.8 1.4 %copy-start.5 = (f32[49,96]{1,0:T(8,128)S(1)}, f32[49,96]{1,0:T(8,128)}, u32[]{:S(2)}) copy-start(f32[49,96]{1,0:T(8,128)} %dw_ref.1) | copy-start | bytes 56452
  15.8 1.4 %copy-start.6 = (f32[96]{0:T(128)S(1)}, f32[96]{0:T(128)}, u32[]{:S(2)}) copy-start(f32[96]{0:T(128)} %param.15) | copy-start | bytes 1156
  15.8 1.4 %copy-start.7 = (f32[96]{0:T(128)S(1)}, f32[96]{0:T(128)}, u32[]{:S(2)}) copy-start(f32[96]{0:T(128)} %param.18) | copy-start | bytes 1156
  15.8 1.4 %copy-start.8 = (f32[96]{0:T(128)S(1)}, f32[96]{0:T(128)}, u32[]{:S(2)}) copy-start(f32[96]{0:T(128)} %param.19) | copy-start | bytes 1156
  17.1 5.7 %copy-start.1 = (bf16[9,192,96]{2,1,0:T(8,128)(2,1)S(1)}, bf16[9,192,96]{2,1,0:T(8,128)(2,1)}, u32[]{:S(2)}) copy-start(bf16[9,192,96]{2,1,0:T(8,128)(2,1)} %refs_1_.1) | copy-start | bytes 995332
  17.1 3.4 %collective-permute-start.1 = (bf16[72,128]{1,0:T(8,128)(2,1)S(1)}, bf16[72,128]{1,0:T(8,128)(2,1)S(1)}, u32[]{:S(2)}, u32[]{:S(2)}) collective-permute-start(bf16[72,128]{1,0:T(8,128)(2,1)S(1)} %get-tuple-element.41), channel_id=1, source_target_pairs={{0,1},{1,0},{2,3},{3,2},{4,5},{5,4},{6,7},{7,6},{8,9},{9,8},{10,11... | collective-permute-start | bytes 55304 | tf_op jit(solution)/shard_map/ppermute | solution.py:58
  20.0 6.6 %collective-permute-start.5 = (bf16[1,192,128]{2,1,0:T(8,128)(2,1)S(1)}, bf16[1,192,128]{2,1,0:T(8,128)(2,1)S(1)}, u32[]{:S(2)}, u32[]{:S(2)}) collective-permute-start(bf16[1,192,128]{2,1,0:T(8,128)(2,1)S(1)} %get-tuple-element.52), channel_id=1, source_target_pairs={{0,1},{1,0},{2,3},{3,2},{4,5},{5,4},{6,7},{7,6},{8,9},{9,8},{10,11... | collective-permute-start | bytes 147464 | tf_op jit(solution)/shard_map/ppermute | solution.py:58
  20.5 7.3 %collective-permute-start.4 = (bf16[1,336,128]{2,1,0:T(8,128)(2,1)S(1)}, bf16[1,336,128]{2,1,0:T(8,128)(2,1)S(1)}, u32[]{:S(2)}, u32[]{:S(2)}) collective-permute-start(bf16[1,336,128]{2,1,0:T(8,128)(2,1)S(1)} %pad_maximum_fusion.3), channel_id=1, source_target_pairs={{0,8},{4,12},{8,0},{12,4},{1,9},{5,13},{9,1},{13,5},{2,10},{6,14},... | collective-permute-start | bytes 258056 | tf_op jit(solution)/shard_map/ppermute | solution.py:58
  26.5 1.4 %collective-permute-start.3 = (bf16[608,128]{1,0:T(8,128)(2,1)S(1)}, bf16[608,128]{1,0:T(8,128)(2,1)S(1)}, u32[]{:S(2)}, u32[]{:S(2)}) collective-permute-start(bf16[608,128]{1,0:T(8,128)(2,1)S(1)} %get-tuple-element.51), channel_id=1, source_target_pairs={{0,1},{1,0},{2,3},{3,2},{4,5},{5,4},{6,7},{7,6},{8,9},{9,8},{10,11... | collective-permute-start | bytes 466952 | tf_op jit(solution)/shard_map/ppermute | solution.py:58
  28.0 6.2 %collective-permute-start.10 = (bf16[608,128]{1,0:T(8,128)(2,1)S(1)}, bf16[608,128]{1,0:T(8,128)(2,1)S(1)}, u32[]{:S(2)}, u32[]{:S(2)}) collective-permute-start(bf16[608,128]{1,0:T(8,128)(2,1)S(1)} %convert_add_fusion.2), channel_id=1, source_target_pairs={{0,2},{2,0},{1,3},{3,1},{4,6},{6,4},{5,7},{7,5},{8,10},{10,8},{9,1... | collective-permute-start | bytes 466952 | tf_op jit(solution)/shard_map/ppermute | solution.py:58
  29.6 4.8 %collective-permute-start.7 = (f32[96,128]{1,0:T(8,128)S(1)}, f32[96,128]{1,0:T(8,128)S(1)}, u32[]{:S(2)}, u32[]{:S(2)}) collective-permute-start(f32[96,128]{1,0:T(8,128)S(1)} %get-tuple-element.58), channel_id=1, source_target_pairs={{0,4},{4,8},{8,12},{1,5},{5,9},{9,13},{2,6},{6,10},{10,14},{3,7},{... | collective-permute-start | bytes 147464 | tf_op jit(solution)/shard_map/ppermute | solution.py:53
  31.2 6.8 %collective-permute-start.6 = (bf16[2,336,128]{2,1,0:T(8,128)(2,1)S(1)}, bf16[2,336,128]{2,1,0:T(8,128)(2,1)S(1)}, u32[]{:S(2)}, u32[]{:S(2)}) collective-permute-start(bf16[2,336,128]{2,1,0:T(8,128)(2,1)S(1)} %pad_maximum_fusion.1), channel_id=1, source_target_pairs={{0,4},{4,0},{8,12},{12,8},{1,5},{5,1},{9,13},{13,9},{2,6},{6,2},{1... | collective-permute-start | bytes 516104 | tf_op jit(solution)/shard_map/ppermute | solution.py:58
  34.3 6.3 %collective-permute-start.11 = (bf16[608,128]{1,0:T(8,128)(2,1)S(1)}, bf16[608,128]{1,0:T(8,128)(2,1)S(1)}, u32[]{:S(2)}, u32[]{:S(2)}) collective-permute-start(bf16[608,128]{1,0:T(8,128)(2,1)S(1)} %add_convert_fusion.1), channel_id=1, source_target_pairs={{0,4},{4,0},{8,12},{12,8},{1,5},{5,1},{9,13},{13,9},{2,6},{6,2},{1... | collective-permute-start | bytes 466952 | tf_op jit(solution)/shard_map/ppermute | solution.py:58
  38.0 9.4 %collective-permute-start.8 = (bf16[4,336,128]{2,1,0:T(8,128)(2,1)S(1)}, bf16[4,336,128]{2,1,0:T(8,128)(2,1)S(1)}, u32[]{:S(2)}, u32[]{:S(2)}) collective-permute-start(bf16[4,336,128]{2,1,0:T(8,128)(2,1)S(1)} %pad_maximum_fusion.refs_1_), channel_id=1, source_target_pairs={{0,2},{2,0},{1,3},{3,1},{4,6},{6,4},{5,7},{7,5},{8,10},{10,8},{9,1... | collective-permute-start | bytes 1032200 | tf_op jit(solution)/shard_map/ppermute | solution.py:58
  40.6 9.6 %collective-permute-start.12 = (bf16[608,128]{1,0:T(8,128)(2,1)S(1)}, bf16[608,128]{1,0:T(8,128)(2,1)S(1)}, u32[]{:S(2)}, u32[]{:S(2)}) collective-permute-start(bf16[608,128]{1,0:T(8,128)(2,1)S(1)} %add_convert_fusion), channel_id=1, source_target_pairs={{0,8},{4,12},{8,0},{12,4},{1,9},{5,13},{9,1},{13,5},{2,10},{6,14},... | collective-permute-start | bytes 466952 | tf_op jit(solution)/shard_map/ppermute | solution.py:58
  48.8 4.0 %collective-permute-start.9 = (bf16[9,192,96]{2,1,0:T(8,128)(2,1)S(1)}, bf16[9,192,96]{2,1,0:T(8,128)(2,1)S(1)}, u32[]{:S(2)}, u32[]{:S(2)}) collective-permute-start(bf16[9,192,96]{2,1,0:T(8,128)(2,1)S(1)} %convert_element_type.37), channel_id=1, source_target_pairs={{0,1},{1,0},{2,3},{3,2},{4,5},{5,4},{6,7},{7,6},{8,9},{9,8},{10,11... | collective-permute-start | bytes 995336 | tf_op jit(solution)/shard_map/ppermute | solution.py:58
  50.2 1.7 %collective-permute-start.13 = (f32[608,128]{1,0:T(8,128)S(1)}, f32[608,128]{1,0:T(8,128)S(1)}, u32[]{:S(2)}, u32[]{:S(2)}) collective-permute-start(f32[608,128]{1,0:T(8,128)S(1)} %convert_add_fusion.1.own_ref), channel_id=1, source_target_pairs={{0,1},{1,0},{2,3},{3,2},{4,5},{5,4},{6,7},{7,6},{8,9},{9,8},{10,11... | collective-permute-start | bytes 933896 | tf_op jit(solution)/shard_map/ppermute | solution.py:58

commit v6 on v5

--- a/solution.py
+++ b/solution.py
@@ -307,8 +307,8 @@
     channels = dw_ref.shape[1]
     mine = pl.multiple_of(chan_ref[0] * HALF_ROWS, 8)
     other = pl.multiple_of((1 - chan_ref[0]) * HALF_ROWS, 8)
-    pack_ref[pl.ds(mine, HALF_ROWS), :] = own_ref[...]
-    pack_ref[pl.ds(other, HALF_ROWS), :] = peer_ref[...]
+    pack_ref[pl.ds(mine, HALF_ROWS), :] = own_ref[...].astype(F32)
+    pack_ref[pl.ds(other, HALF_ROWS), :] = peer_ref[...].astype(F32)
     for n in range(3):
         lanes = slice(128 * n, 128 * n + 128)
         ds_ref[:, lanes] = pack_ref[192 * n : 192 * n + 192, :]
@@ -365,7 +365,9 @@
     lax.fori_loop(1, out_rows, step, 0)
 
 
-def weight_kernel(place_ref, near_ref, far_ref, keep_ref, send_ref, feat_ref, cot_ref, *, scale):
+def weight_kernel(
+    place_ref, near_ref, far_ref, keep_ref, send_ref, feat_ref, cot_ref, send_acc, *, scale
+):
     near = near_ref.shape[0]
     members = feat_ref.shape[1] // 8
     width, e_half = keep_ref.shape[1:]
@@ -374,7 +376,7 @@
     @pl.when(step == 0)
     def _():
         keep_ref[...] = jnp.zeros_like(keep_ref)
-        send_ref[...] = jnp.zeros_like(send_ref)
+        send_acc[...] = jnp.zeros_like(send_acc)
 
     def take(member, block):
         block = block.astype(F32)
@@ -406,7 +408,11 @@
             right = jnp.concatenate([cot_ref[3 * u + v] for u, v in places], axis=0).astype(BF16)
             total = tn(left, right) * scale
             keep_ref[3 * a + b] += total[:, :e_half]
-            send_ref[3 * a + b] += total[:, 128 : 128 + e_half]
+            send_acc[3 * a + b] += total[:, 128 : 128 + e_half]
+
+    @pl.when(step == pl.num_programs(0) - 1)
+    def _():
+        send_ref[...] = send_acc[...].astype(BF16)
 
 
 def whole(shape):
@@ -609,6 +615,8 @@
             step *= 2
     for n, (axis, step) in enumerate(steps):
         wire = part.astype(BF16)
+        if n == 1:
+            wire, below = lax.optimization_barrier((wire, below))
         part = wire.astype(F32) + swapped(wire, axis, step).astype(F32)
     above = shifted(below, "slide", 1)
     map_call = pl.pallas_call(
@@ -623,12 +631,12 @@
     agg_map = map_call(spread, key, above)
 
     for n in range(1, len(spans) if gather else 0):
-        if n == len(spans) - 1:
-            near, agg_map = lax.optimization_barrier((near, agg_map))
         far, place = widen(n, near, place)
         if n < len(spans) - 1:
             near = jnp.concatenate([near, far], axis=0)
 
+    if gather:
+        far, agg_map = lax.optimization_barrier((far, agg_map))
     count = 2 * near.shape[0] if gather else chunks
     per = count if gather else 1
     near_count = near.shape[0] if gather else 1
@@ -637,7 +645,7 @@
         grid=(count // per,),
         out_shape=(
             jax.ShapeDtypeStruct((9, width, e_half), F32),
-            jax.ShapeDtypeStruct((9, width, e_half), F32),
+            jax.ShapeDtypeStruct((9, width, e_half), BF16),
         ),
         in_specs=[
             SMEM,
@@ -648,15 +656,19 @@
         scratch_shapes=[
             pltpu.VMEM((16, per * 8, width), F32),
             pltpu.VMEM((9, per * 8, 256), F32),
+            pltpu.VMEM((9, width, e_half), F32),
         ],
         compiler_params=params_of(),
         cost_estimate=takes(1.4),
         name="agg_weight_grad",
     )(place, near, far)
-    agg_grad = agg_keep + swapped(agg_send.astype(BF16), "chan", 1).astype(F32)
+    agg_grad = agg_keep + swapped(agg_send, "chan", 1).astype(F32)
     if not gather:
         agg_grad = lax.psum(agg_grad, ("slide", "rep"))
 
+    part = part.astype(BF16)
+    peer_part = swapped(part, "chan", 1)
+    part, agg_grad = lax.optimization_barrier((part, agg_grad))
     dw_grad, up_grad, proj_grad, ds_grad = pl.pallas_call(
         unpack_kernel,
         out_shape=(
@@ -671,7 +683,7 @@
         compiler_params=pltpu.CompilerParams(vmem_limit_bytes=24 << 20),
         cost_estimate=takes(1.5),
         name="unpack",
-    )(chan, part, swapped(part, "chan", 1))
+    )(chan, part, peer_part)
     proj_grad = proj_grad.T
     ds_grad = ds_grad.T
     return (agg_map[None], agg_grad, dw_grad, up_grad, proj_grad, ds_grad)

time: 54 us -> 55.4 us (1.026)
  the two profiles are of different devices: /device:TPU:0 before, /device:TPU:23 now
where the time goes in v6:
time: 55.4 us; the launch traced here: 55.1 us
  starting transfers between devices  19.7 us (36%)
  Pallas kernels  16.6 us (30%)
  waiting for transfers between devices  16.6 us (30%)
  other arithmetic  1.2 us (2%)
  between operations  0.89 us (2%)
    ppermute x12, starting transfers between devices, swapped(): lax.ppermute(value, axis, [(place, place ^ step) for place in range(count)])  9.69 us
    ppermute x12, waiting for transfers between devices, swapped(): lax.ppermute(value, axis, [(place, place ^ step) for place in range(count)])  8.31 us
    ppermute x2, waiting for transfers between devices, shifted(): lax.ppermute(value, axis, [(source, source + steps) for source in range(f...  8.3 us
    all_to_all x1, starting transfers between devices, on_device(): lax.all_to_all(packed, ('slide', 'chan'), split_axis=0, concat_axis=0, ti...  5.66 us
    ppermute x2, starting transfers between devices, shifted(): lax.ppermute(value, axis, [(source, source + steps) for source in range(f...  4.39 us
    pallas_call x1, Pallas kernels, on_device(): pl.pallas_call(lambda *refs: back_kernel(*refs, scale=loss_scale), grid=(...  3.77 us
    pallas_call x1, Pallas kernels, on_device(): agg_map = map_call(spread, key, above)  3.5 us
    pallas_call x1, Pallas kernels, on_device(): pl.pallas_call(stem_kernel, grid=(chunks,), out_shape=(jax.ShapeDtypeStru...  2.77 us
  transfers between devices with their start and end apart: 15, of which 5 were waited for; matrix products, arithmetic and copies ran while one was open for 2% of the time, Pallas kernels for 25%

profile of v6, /device:TPU:23, one launch (start us, length us, event | category | flops | bytes accessed | tf_op | source)
XLA Modules:
  0.0 55.1 jit_solution(5456239557713104955)
XLA Ops:
  0.6 2.0 %pack.1 = (bf16[8,56,128]{2,1,0:T(8,128)(2,1)}, bf16[96,128]{1,0:T(8,128)(2,1)}) custom-call(s32[1,8]{1,0:T(1,128)} %cells_ref.1, bf16[1,8,6144]{2,1,0:T(8,128)(2,1)} %pixels_ref.1, f32[1,16,96,128]{3,2,1,0:T(8,128)} %cot_ref.1), custom_call_target="tpu_custom_call" | custom-call | bytes 5535000 | tf_op jit(solution)/shard_map/pack/pallas_call | solution.py:446
  2.6 5.7 %all-to-all-start = ((bf16[8,56,128]{2,1,0:T(8,128)(2,1)}), bf16[8,56,128]{2,1,0:T(8,128)(2,1)S(1)}, u32[]{:S(2)}, u32[]{:S(2)}) async-start(bf16[8,56,128]{2,1,0:T(8,128)(2,1)} %get-tuple-element.42), calls=%async_computation | async-start | bytes 229376 | tf_op jit(solution)/shard_map/all_to_all | solution.py:466
  8.3 0.4 collective-permute-start.2
  8.6 2.2 %collective-permute-start = (bf16[96,128]{1,0:T(8,128)(2,1)S(1)}, bf16[96,128]{1,0:T(8,128)(2,1)S(1)}, u32[]{:S(2)}, u32[]{:S(2)}) collective-permute-start(bf16[96,128]{1,0:T(8,128)(2,1)S(1)} %copy-done.9), channel_id=1, source_target_pairs={{4,0},{8,4},{12,8},{5,1},{9,5},{13,9},{6,2},{10,6},{14,10},{7,3},{... | collective-permute-start | bytes 73736 | tf_op jit(solution)/shard_map/ppermute | solution.py:53
  10.8 2.4 %collective-permute-done.below_ref = bf16[96,128]{1,0:T(8,128)(2,1)S(1)} collective-permute-done((bf16[96,128]{1,0:T(8,128)(2,1)S(1)}, bf16[96,128]{1,0:T(8,128)(2,1)S(1)}, u32[]{:S(2)}, u32[]{:S(2)}) %collective-permute-start) | collective-permute-done | bytes 24608 | tf_op jit(solution)/shard_map/ppermute | solution.py:53
  13.2 0.0 all-to-all-done.meta_ref.got_ref.refs_5_
  13.2 0.0 copy-done
  13.2 0.0 copy-start.3
  13.2 0.0 copy-start.4
  13.2 0.0 copy-start.5
  13.2 0.0 copy-start.6
  13.3 0.0 copy-start.7
  13.3 0.0 copy-start.8
  13.3 1.2 %patch.1 = (f32[144,128]{1,0:T(8,128)S(1)}, bf16[72,128]{1,0:T(8,128)(2,1)S(1)}, bf16[72,128]{1,0:T(8,128)(2,1)S(1)}) custom-call(s32[1]{0:T(128)} %bitcast.chan_ref.refs_0_, bf16[8,56,128]{2,1,0:T(8,128)(2,1)S(1)} %all-to-all-done.meta_ref.got_ref.refs_5_, f32[1,16,96,128]{3,2,1,0:T(8,128)S(1)} %copy-done, bf16[96,128]{1,0:T(8,128)(2,1)S(1)} %collective-permute-done.below_ref), custom_call_target="tpu_custom_call" | custom-call | bytes 4428000 | tf_op jit(solution)/shard_map/patch/pallas_call | solution.py:468
  14.5 0.0 copy-start.1
  14.5 1.4 %collective-permute-start.1 = (bf16[72,128]{1,0:T(8,128)(2,1)S(1)}, bf16[72,128]{1,0:T(8,128)(2,1)S(1)}, u32[]{:S(2)}, u32[]{:S(2)}) collective-permute-start(bf16[72,128]{1,0:T(8,128)(2,1)S(1)} %get-tuple-element.45), channel_id=1, source_target_pairs={{0,1},{1,0},{2,3},{3,2},{4,5},{5,4},{6,7},{7,6},{8,9},{9,8},{10,11... | collective-permute-start | bytes 55304 | tf_op jit(solution)/shard_map/ppermute | solution.py:58
  15.9 0.0 copy-done.5
  16.0 2.8 %stem.1 = (bf16[1,192,128]{2,1,0:T(8,128)(2,1)S(1)}, f32[1,512,96]{2,1,0:T(8,128)S(1)}, f32[1,512,1]{2,1,0:T(8,128)S(1)}, f32[1,512,96]{2,1,0:T(8,128)S(1)}, f32...) custom-call(bf16[8,56,128]{2,1,0:T(8,128)(2,1)S(1)} %all-to-all-done, ...), custom_call_target="tpu_custom_call" | custom-call | bytes 9963000 | tf_op jit(solution)/shard_map/stem/pallas_call | solution.py:503
  18.7 0.1 collective-permute-start.5
  18.8 0.0 collective-permute-done.1
  18.8 0.6 %collective-permute-start.4 = (bf16[1,336,128]{2,1,0:T(8,128)(2,1)S(1)}, bf16[1,336,128]{2,1,0:T(8,128)(2,1)S(1)}, u32[]{:S(2)}, u32[]{:S(2)}) collective-permute-start(bf16[1,336,128]{2,1,0:T(8,128)(2,1)S(1)} %pad_maximum_fusion.2), channel_id=1, source_target_pairs={{0,8},{4,12},{8,0},{12,4},{1,9},{5,13},{9,1},{13,5},{2,10},{6,14},... | collective-permute-start | bytes 258056 | tf_op jit(solution)/shard_map/ppermute | solution.py:58
  19.4 0.0 collective-permute-done.2.refs_4_
  19.4 3.8 %stem_back.1 = (f32[608,128]{1,0:T(8,128)S(1)}, bf16[608,128]{1,0:T(8,128)(2,1)S(1)}) custom-call(s32[1]{0:T(128)} %bitcast.chan_ref.refs_0_, bf16[1,72,128]{2,1,0:T(8,128)(2,1)S(1)} %bitcast.17, bf16[1,72,128]{2,1,0:T(8,128)(2,1)S(1)} %bitcast.20, bf16[9,192,96]{2,1,0:T(8,128)(2,1)S(1)} %copy-done.1, ...), custom_call_target="tpu_custom_call" | custom-call | bytes 13653000 | tf_op jit(solution)/shard_map/stem_back/pallas_call | solution.py:571
  23.2 0.8 %collective-permute-start.3 = (bf16[608,128]{1,0:T(8,128)(2,1)S(1)}, bf16[608,128]{1,0:T(8,128)(2,1)S(1)}, u32[]{:S(2)}, u32[]{:S(2)}) collective-permute-start(bf16[608,128]{1,0:T(8,128)(2,1)S(1)} %get-tuple-element.55), channel_id=1, source_target_pairs={{0,1},{1,0},{2,3},{3,2},{4,5},{5,4},{6,7},{7,6},{8,9},{9,8},{10,11... | collective-permute-start | bytes 466952 | tf_op jit(solution)/shard_map/ppermute | solution.py:58
  24.0 0.0 collective-permute-done.5
  24.0 1.0 %spread.1 = (f32[144,96]{1,0:T(8,128)S(1)}, f32[96,128]{1,0:T(8,128)S(1)}) custom-call(bf16[2,192,128]{2,1,0:T(8,128)(2,1)S(1)} %pad_maximum_fusion.1.refs_0_, bf16[9,192,96]{2,1,0:T(8,128)(2,1)S(1)} %copy-done.1, f32[144,128]{1,0:T(8,128)S(1)} %get-tuple-element.57.refs_2_.key_ref), custom_call_target="tpu_custom_call" | custom-call | bytes 3690000 | tf_op jit(solution)/shard_map/spread/pallas_call | solution.py:539
  25.1 0.0 collective-permute-done.4
  25.1 0.0 collective-permute-done.3
  25.2 0.3 collective-permute-start.8
  25.5 1.0 %collective-permute-start.6 = (bf16[2,336,128]{2,1,0:T(8,128)(2,1)S(1)}, bf16[2,336,128]{2,1,0:T(8,128)(2,1)S(1)}, u32[]{:S(2)}, u32[]{:S(2)}) collective-permute-start(bf16[2,336,128]{2,1,0:T(8,128)(2,1)S(1)} %pad_maximum_fusion), channel_id=1, source_target_pairs={{0,4},{4,0},{8,12},{12,8},{1,5},{5,1},{9,13},{13,9},{2,6},{6,2},{1... | collective-permute-start | bytes 516104 | tf_op jit(solution)/shard_map/ppermute | solution.py:58
  26.5 4.1 %collective-permute-done.8 = bf16[608,128]{1,0:T(8,128)(2,1)S(1)} collective-permute-done((bf16[608,128]{1,0:T(8,128)(2,1)S(1)}, bf16[608,128]{1,0:T(8,128)(2,1)S(1)}, u32[]{:S(2)}, u32[]{:S(2)}) %collective-permute-start.8) | collective-permute-done | bytes 155680 | tf_op jit(solution)/shard_map/ppermute | solution.py:58
  30.6 1.1 %collective-permute-start.10 = (bf16[608,128]{1,0:T(8,128)(2,1)S(1)}, bf16[608,128]{1,0:T(8,128)(2,1)S(1)}, u32[]{:S(2)}, u32[]{:S(2)}) collective-permute-start(bf16[608,128]{1,0:T(8,128)(2,1)S(1)} %add_convert_fusion.2), channel_id=1, source_target_pairs={{0,4},{4,0},{8,12},{12,8},{1,5},{5,1},{9,13},{13,9},{2,6},{6,2},{1... | collective-permute-start | bytes 466952 | tf_op jit(solution)/shard_map/ppermute | solution.py:58
  31.7 0.0 collective-permute-done.6
  31.8 0.4 collective-permute-start.7
  32.2 3.0 %collective-permute-done.10 = bf16[608,128]{1,0:T(8,128)(2,1)S(1)} collective-permute-done((bf16[608,128]{1,0:T(8,128)(2,1)S(1)}, bf16[608,128]{1,0:T(8,128)(2,1)S(1)}, u32[]{:S(2)}, u32[]{:S(2)}) %collective-permute-start.10) | collective-permute-done | bytes 155680 | tf_op jit(solution)/shard_map/ppermute | solution.py:58
  35.2 1.9 %collective-permute-start.11 = (bf16[608,128]{1,0:T(8,128)(2,1)S(1)}, bf16[608,128]{1,0:T(8,128)(2,1)S(1)}, u32[]{:S(2)}, u32[]{:S(2)}) collective-permute-start(bf16[608,128]{1,0:T(8,128)(2,1)S(1)} %add_convert_fusion.1), channel_id=1, source_target_pairs={{0,8},{4,12},{8,0},{12,4},{1,9},{5,13},{9,1},{13,5},{2,10},{6,14},... | collective-permute-start | bytes 466952 | tf_op jit(solution)/shard_map/ppermute | solution.py:58
  37.1 2.2 %collective-permute-start.9 = (f32[96,128]{1,0:T(8,128)S(1)}, f32[96,128]{1,0:T(8,128)S(1)}, u32[]{:S(2)}, u32[]{:S(2)}) collective-permute-start(f32[96,128]{1,0:T(8,128)S(1)} %get-tuple-element.64), channel_id=1, source_target_pairs={{0,4},{4,8},{8,12},{1,5},{5,9},{9,13},{2,6},{6,10},{10,14},{3,7},{... | collective-permute-start | bytes 147464 | tf_op jit(solution)/shard_map/ppermute | solution.py:53
  39.4 5.9 %collective-permute-done.9.above_ref = f32[96,128]{1,0:T(8,128)S(1)} collective-permute-done((f32[96,128]{1,0:T(8,128)S(1)}, f32[96,128]{1,0:T(8,128)S(1)}, u32[]{:S(2)}, u32[]{:S(2)}) %collective-permute-start.9) | collective-permute-done | bytes 49184 | tf_op jit(solution)/shard_map/ppermute | solution.py:53
  45.3 3.5 %agg_map.1 = bf16[16,96,128]{2,1,0:T(8,128)(2,1)} custom-call(f32[144,96]{1,0:T(8,128)S(1)} %get-tuple-element.61.y_ref, f32[144,128]{1,0:T(8,128)S(1)} %get-tuple-element.57.refs_2_.key_ref, f32[96,128]{1,0:T(8,128)S(1)} %collective-permute-done.9.above_ref), custom_call_target="tpu_custom_call" | custom-call | bytes 12915000 | tf_op jit(solution)/shard_map/agg_map/pallas_call | solution.py:631
  48.8 0.0 collective-permute-done.7.refs_2_
  48.8 1.4 %agg_weight_grad.1 = (f32[9,192,96]{2,1,0:T(8,128)S(1)}, bf16[9,192,96]{2,1,0:T(8,128)(2,1)S(1)}) custom-call(s32[1]{0:T(128)} %bitcast.9.refs_0_, bf16[4,336,128]{2,1,0:T(8,128)(2,1)S(1)} %constant_dynamic-update-slice_fusion.refs_1_, bf16[4,336,128]{2,1,0:T(8,128)(2,1)S(1)} %collective-permute-done.7.refs_2_), custom_call_target="tpu_custom_call" | custom-call | bytes 5166000 | tf_op jit(solution)/shard_map/agg_weight_grad/pallas_call | solution.py:643
  50.2 1.6 %collective-permute-start.12 = (bf16[9,192,96]{2,1,0:T(8,128)(2,1)S(1)}, bf16[9,192,96]{2,1,0:T(8,128)(2,1)S(1)}, u32[]{:S(2)}, u32[]{:S(2)}) collective-permute-start(bf16[9,192,96]{2,1,0:T(8,128)(2,1)S(1)} %get-tuple-element.69), channel_id=1, source_target_pairs={{0,1},{1,0},{2,3},{3,2},{4,5},{5,4},{6,7},{7,6},{8,9},{9,8},{10,11... | collective-permute-start | bytes 995336 | tf_op jit(solution)/shard_map/ppermute | solution.py:58
  51.9 0.0 collective-permute-done.11
  51.9 0.1 collective-permute-start.13
  52.0 1.3 %collective-permute-done.12 = bf16[9,192,96]{2,1,0:T(8,128)(2,1)S(1)} collective-permute-done((bf16[9,192,96]{2,1,0:T(8,128)(2,1)S(1)}, bf16[9,192,96]{2,1,0:T(8,128)(2,1)S(1)}, u32[]{:S(2)}, u32[]{:S(2)}) %collective-permute-start.12) | collective-permute-done | bytes 331808 | tf_op jit(solution)/shard_map/ppermute | solution.py:58
  53.3 1.0 %convert_add_fusion = f32[9,192,96]{2,1,0:T(8,128)} fusion(f32[9,192,96]{2,1,0:T(8,128)S(1)} %get-tuple-element.68, bf16[9,192,96]{2,1,0:T(8,128)(2,1)S(1)} %collective-permute-done.12), kind=kLoop, calls=%fused_computation | loop fusion | flops 331776 | bytes 1658880 | tf_op jit(solution)/shard_map/add | solution.py:665
  54.3 0.0 collective-permute-done.13.peer_ref
  54.3 0.9 %unpack.1 = (f32[49,96]{1,0:T(8,128)}, f32[96,384]{1,0:T(8,128)}, f32[96,384]{1,0:T(8,128)}, f32[192,384]{1,0:T(8,128)}) custom-call(s32[1]{0:T(128)} %bitcast.chan_ref.refs_0_, bf16[608,128]{1,0:T(8,128)(2,1)S(1)} %add_convert_fusion.own_ref, bf16[608,128]{1,0:T(8,128)(2,1)S(1)} %collective-permute-done.13.peer_ref), custom_call_target="tpu_custom_call" | custom-call | bytes 5535000 | tf_op jit(solution)/shard_map/unpack/pallas_call | solution.py:672
  (20 shorter events, 0.3 us)
Async XLA Ops:
  0.6 12.6 %copy-start = (f32[1,16,96,128]{3,2,1,0:T(8,128)S(1)}, f32[1,16,96,128]{3,2,1,0:T(8,128)}, u32[]{:S(2)}) copy-start(f32[1,16,96,128]{3,2,1,0:T(8,128)} %cot_ref.1) | copy-start | bytes 2359300
  2.6 6.0 %copy-start.9 = (bf16[96,128]{1,0:T(8,128)(2,1)S(1)}, bf16[96,128]{1,0:T(8,128)(2,1)}, u32[]{:S(2)}) copy-start(bf16[96,128]{1,0:T(8,128)(2,1)} %get-tuple-element.43) | copy-start | bytes 73732
  2.6 10.6 %all-to-all-start = ((bf16[8,56,128]{2,1,0:T(8,128)(2,1)}), bf16[8,56,128]{2,1,0:T(8,128)(2,1)S(1)}, u32[]{:S(2)}, u32[]{:S(2)}) async-start(bf16[8,56,128]{2,1,0:T(8,128)(2,1)} %get-tuple-element.42), calls=%async_computation | async-start | bytes 229376 | tf_op jit(solution)/shard_map/all_to_all | solution.py:466
  8.3 11.1 %collective-permute-start.2 = (bf16[9,192,96]{2,1,0:T(8,128)(2,1)}, bf16[9,192,96]{2,1,0:T(8,128)(2,1)S(1)}, u32[]{:S(2)}, u32[]{:S(2)}) collective-permute-start(bf16[9,192,96]{2,1,0:T(8,128)(2,1)} %refs_1_.1), channel_id=1, source_target_pairs={{0,1},{1,0},{2,3},{3,2},{4,5},{5,4},{6,7},{7,6},{8,9},{9,8},{10,11... | collective-permute-start | bytes 995336 | tf_op jit(solution)/shard_map/ppermute | solution.py:58
  8.6 4.6 %collective-permute-start = (bf16[96,128]{1,0:T(8,128)(2,1)S(1)}, bf16[96,128]{1,0:T(8,128)(2,1)S(1)}, u32[]{:S(2)}, u32[]{:S(2)}) collective-permute-start(bf16[96,128]{1,0:T(8,128)(2,1)S(1)} %copy-done.9), channel_id=1, source_target_pairs={{4,0},{8,4},{12,8},{5,1},{9,5},{13,9},{6,2},{10,6},{14,10},{7,3},{... | collective-permute-start | bytes 73736 | tf_op jit(solution)/shard_map/ppermute | solution.py:53
  13.2 2.7 %copy-start.2 = (bf16[384,192]{0,1:T(8,128)(2,1)S(1)}, bf16[384,192]{0,1:T(8,128)(2,1)}, u32[]{:S(2)}) copy-start(bf16[384,192]{0,1:T(8,128)(2,1)} %param.20) | copy-start | bytes 442372
  13.2 2.7 %copy-start.3 = (bf16[96,384]{1,0:T(8,128)(2,1)S(1)}, bf16[96,384]{1,0:T(8,128)(2,1)}, u32[]{:S(2)}) copy-start(bf16[96,384]{1,0:T(8,128)(2,1)} %refs_14_.1) | copy-start | bytes 221188
  13.2 2.7 %copy-start.4 = (bf16[384,96]{0,1:T(8,128)(2,1)S(1)}, bf16[384,96]{0,1:T(8,128)(2,1)}, u32[]{:S(2)}) copy-start(bf16[384,96]{0,1:T(8,128)(2,1)} %param.17) | copy-start | bytes 221188
  13.2 2.7 %copy-start.5 = (f32[49,96]{1,0:T(8,128)S(1)}, f32[49,96]{1,0:T(8,128)}, u32[]{:S(2)}) copy-start(f32[49,96]{1,0:T(8,128)} %dw_ref.1) | copy-start | bytes 56452
  13.2 2.7 %copy-start.6 = (f32[96]{0:T(128)S(1)}, f32[96]{0:T(128)}, u32[]{:S(2)}) copy-start(f32[96]{0:T(128)} %param.15) | copy-start | bytes 1156
  13.3 2.7 %copy-start.7 = (f32[96]{0:T(128)S(1)}, f32[96]{0:T(128)}, u32[]{:S(2)}) copy-start(f32[96]{0:T(128)} %param.18) | copy-start | bytes 1156
  13.3 2.7 %copy-start.8 = (f32[96]{0:T(128)S(1)}, f32[96]{0:T(128)}, u32[]{:S(2)}) copy-start(f32[96]{0:T(128)} %param.19) | copy-start | bytes 1156
  14.5 4.9 %copy-start.1 = (bf16[9,192,96]{2,1,0:T(8,128)(2,1)S(1)}, bf16[9,192,96]{2,1,0:T(8,128)(2,1)}, u32[]{:S(2)}) copy-start(bf16[9,192,96]{2,1,0:T(8,128)(2,1)} %refs_1_.1) | copy-start | bytes 995332
  14.5 4.3 %collective-permute-start.1 = (bf16[72,128]{1,0:T(8,128)(2,1)S(1)}, bf16[72,128]{1,0:T(8,128)(2,1)S(1)}, u32[]{:S(2)}, u32[]{:S(2)}) collective-permute-start(bf16[72,128]{1,0:T(8,128)(2,1)S(1)} %get-tuple-element.45), channel_id=1, source_target_pairs={{0,1},{1,0},{2,3},{3,2},{4,5},{5,4},{6,7},{7,6},{8,9},{9,8},{10,11... | collective-permute-start | bytes 55304 | tf_op jit(solution)/shard_map/ppermute | solution.py:58
  18.7 5.3 %collective-permute-start.5 = (bf16[1,192,128]{2,1,0:T(8,128)(2,1)S(1)}, bf16[1,192,128]{2,1,0:T(8,128)(2,1)S(1)}, u32[]{:S(2)}, u32[]{:S(2)}) collective-permute-start(bf16[1,192,128]{2,1,0:T(8,128)(2,1)S(1)} %get-tuple-element.56), channel_id=1, source_target_pairs={{0,1},{1,0},{2,3},{3,2},{4,5},{5,4},{6,7},{7,6},{8,9},{9,8},{10,11... | collective-permute-start | bytes 147464 | tf_op jit(solution)/shard_map/ppermute | solution.py:58
  18.8 6.2 %collective-permute-start.4 = (bf16[1,336,128]{2,1,0:T(8,128)(2,1)S(1)}, bf16[1,336,128]{2,1,0:T(8,128)(2,1)S(1)}, u32[]{:S(2)}, u32[]{:S(2)}) collective-permute-start(bf16[1,336,128]{2,1,0:T(8,128)(2,1)S(1)} %pad_maximum_fusion.2), channel_id=1, source_target_pairs={{0,8},{4,12},{8,0},{12,4},{1,9},{5,13},{9,1},{13,5},{2,10},{6,14},... | collective-permute-start | bytes 258056 | tf_op jit(solution)/shard_map/ppermute | solution.py:58
  23.2 1.9 %collective-permute-start.3 = (bf16[608,128]{1,0:T(8,128)(2,1)S(1)}, bf16[608,128]{1,0:T(8,128)(2,1)S(1)}, u32[]{:S(2)}, u32[]{:S(2)}) collective-permute-start(bf16[608,128]{1,0:T(8,128)(2,1)S(1)} %get-tuple-element.55), channel_id=1, source_target_pairs={{0,1},{1,0},{2,3},{3,2},{4,5},{5,4},{6,7},{7,6},{8,9},{9,8},{10,11... | collective-permute-start | bytes 466952 | tf_op jit(solution)/shard_map/ppermute | solution.py:58
  25.2 5.4 %collective-permute-start.8 = (bf16[608,128]{1,0:T(8,128)(2,1)S(1)}, bf16[608,128]{1,0:T(8,128)(2,1)S(1)}, u32[]{:S(2)}, u32[]{:S(2)}) collective-permute-start(bf16[608,128]{1,0:T(8,128)(2,1)S(1)} %convert_add_fusion.1), channel_id=1, source_target_pairs={{0,2},{2,0},{1,3},{3,1},{4,6},{6,4},{5,7},{7,5},{8,10},{10,8},{9,1... | collective-permute-start | bytes 466952 | tf_op jit(solution)/shard_map/ppermute | solution.py:58
  25.5 6.3 %collective-permute-start.6 = (bf16[2,336,128]{2,1,0:T(8,128)(2,1)S(1)}, bf16[2,336,128]{2,1,0:T(8,128)(2,1)S(1)}, u32[]{:S(2)}, u32[]{:S(2)}) collective-permute-start(bf16[2,336,128]{2,1,0:T(8,128)(2,1)S(1)} %pad_maximum_fusion), channel_id=1, source_target_pairs={{0,4},{4,0},{8,12},{12,8},{1,5},{5,1},{9,13},{13,9},{2,6},{6,2},{1... | collective-permute-start | bytes 516104 | tf_op jit(solution)/shard_map/ppermute | solution.py:58
  30.6 4.5 %collective-permute-start.10 = (bf16[608,128]{1,0:T(8,128)(2,1)S(1)}, bf16[608,128]{1,0:T(8,128)(2,1)S(1)}, u32[]{:S(2)}, u32[]{:S(2)}) collective-permute-start(bf16[608,128]{1,0:T(8,128)(2,1)S(1)} %add_convert_fusion.2), channel_id=1, source_target_pairs={{0,4},{4,0},{8,12},{12,8},{1,5},{5,1},{9,13},{13,9},{2,6},{6,2},{1... | collective-permute-start | bytes 466952 | tf_op jit(solution)/shard_map/ppermute | solution.py:58
  31.8 17.1 %collective-permute-start.7 = (bf16[4,336,128]{2,1,0:T(8,128)(2,1)S(1)}, bf16[4,336,128]{2,1,0:T(8,128)(2,1)S(1)}, u32[]{:S(2)}, u32[]{:S(2)}) collective-permute-start(bf16[4,336,128]{2,1,0:T(8,128)(2,1)S(1)} %constant_dynamic-update-slice_fusion.refs_1_), channel_id=1, source_target_pairs={{0,2},{2,0},{1,3},{3,1},{4,6},{6,4},{5,7},{7,5},{8,10},{10,8},{9,1... | collective-permute-start | bytes 1032200 | tf_op jit(solution)/shard_map/ppermute | solution.py:58
  35.2 16.7 %collective-permute-start.11 = (bf16[608,128]{1,0:T(8,128)(2,1)S(1)}, bf16[608,128]{1,0:T(8,128)(2,1)S(1)}, u32[]{:S(2)}, u32[]{:S(2)}) collective-permute-start(bf16[608,128]{1,0:T(8,128)(2,1)S(1)} %add_convert_fusion.1), channel_id=1, source_target_pairs={{0,8},{4,12},{8,0},{12,4},{1,9},{5,13},{9,1},{13,5},{2,10},{6,14},... | collective-permute-start | bytes 466952 | tf_op jit(solution)/shard_map/ppermute | solution.py:58
  37.1 8.2 %collective-permute-start.9 = (f32[96,128]{1,0:T(8,128)S(1)}, f32[96,128]{1,0:T(8,128)S(1)}, u32[]{:S(2)}, u32[]{:S(2)}) collective-permute-start(f32[96,128]{1,0:T(8,128)S(1)} %get-tuple-element.64), channel_id=1, source_target_pairs={{0,4},{4,8},{8,12},{1,5},{5,9},{9,13},{2,6},{6,10},{10,14},{3,7},{... | collective-permute-start | bytes 147464 | tf_op jit(solution)/shard_map/ppermute | solution.py:53
  50.2 3.0 %collective-permute-start.12 = (bf16[9,192,96]{2,1,0:T(8,128)(2,1)S(1)}, bf16[9,192,96]{2,1,0:T(8,128)(2,1)S(1)}, u32[]{:S(2)}, u32[]{:S(2)}) collective-permute-start(bf16[9,192,96]{2,1,0:T(8,128)(2,1)S(1)} %get-tuple-element.69), channel_id=1, source_target_pairs={{0,1},{1,0},{2,3},{3,2},{4,5},{5,4},{6,7},{7,6},{8,9},{9,8},{10,11... | collective-permute-start | bytes 995336 | tf_op jit(solution)/shard_map/ppermute | solution.py:58
  51.9 2.4 %collective-permute-start.13 = (bf16[608,128]{1,0:T(8,128)(2,1)S(1)}, bf16[608,128]{1,0:T(8,128)(2,1)S(1)}, u32[]{:S(2)}, u32[]{:S(2)}) collective-permute-start(bf16[608,128]{1,0:T(8,128)(2,1)S(1)} %add_convert_fusion.own_ref), channel_id=1, source_target_pairs={{0,1},{1,0},{2,3},{3,2},{4,5},{5,4},{6,7},{7,6},{8,9},{9,8},{10,11... | collective-permute-start | bytes 466952 | tf_op jit(solution)/shard_map/ppermute | solution.py:58

commit v7 on v6

--- a/solution.py
+++ b/solution.py
@@ -607,6 +607,7 @@
     part = keep + swapped(send, "chan", 1).astype(F32)
     if gather:
         part, near, spread, below = lax.optimization_barrier((part, near, spread, below))
+    above = shifted(below, "slide", 1)
     steps = []
     for axis in ("rep", "slide"):
         step = 1
@@ -616,9 +617,8 @@
     for n, (axis, step) in enumerate(steps):
         wire = part.astype(BF16)
         if n == 1:
-            wire, below = lax.optimization_barrier((wire, below))
+            wire, above = lax.optimization_barrier((wire, above))
         part = wire.astype(F32) + swapped(wire, axis, step).astype(F32)
-    above = shifted(below, "slide", 1)
     map_call = pl.pallas_call(
         map_kernel,
         out_shape=jax.ShapeDtypeStruct((out_rows, e_half, cols), BF16),

time: 55.4 us -> 52.9 us (0.955)
  the two profiles are of different devices: /device:TPU:23 before, /device:TPU:0 now
where the time goes in v7:
time: 52.9 us; the launch traced here: 52.5 us
  starting transfers between devices  20 us (38%)
  Pallas kernels  16.6 us (31%)
  waiting for transfers between devices  13.7 us (26%)
  other arithmetic  1.2 us (2%)
  between operations  0.9 us (2%)
    ppermute x12, starting transfers between devices, swapped(): lax.ppermute(value, axis, [(place, place ^ step) for place in range(count)])  10.6 us
    ppermute x12, waiting for transfers between devices, swapped(): lax.ppermute(value, axis, [(place, place ^ step) for place in range(count)])  8.9 us
    all_to_all x1, starting transfers between devices, on_device(): lax.all_to_all(packed, ('slide', 'chan'), split_axis=0, concat_axis=0, ti...  6.46 us
    ppermute x2, waiting for transfers between devices, shifted(): lax.ppermute(value, axis, [(source, source + steps) for source in range(f...  4.84 us
    pallas_call x1, Pallas kernels, on_device(): pl.pallas_call(lambda *refs: back_kernel(*refs, scale=loss_scale), grid=(...  3.79 us
    pallas_call x1, Pallas kernels, on_device(): agg_map = map_call(spread, key, above)  3.5 us
    ppermute x2, starting transfers between devices, shifted(): lax.ppermute(value, axis, [(source, source + steps) for source in range(f...  2.89 us
    pallas_call x1, Pallas kernels, on_device(): pl.pallas_call(stem_kernel, grid=(chunks,), out_shape=(jax.ShapeDtypeStru...  2.77 us
  transfers between devices with their start and end apart: 15, of which 8 were waited for; matrix products, arithmetic and copies ran while one was open for 2% of the time, Pallas kernels for 26%

profile of v7, /device:TPU:0, one launch (start us, length us, event | category | flops | bytes accessed | tf_op | source)
XLA Modules:
  0.0 52.5 jit_solution(10566587708144407403)
XLA Ops:
  0.6 0.0 copy-start
  0.6 2.0 %pack.1 = (bf16[8,56,128]{2,1,0:T(8,128)(2,1)}, bf16[96,128]{1,0:T(8,128)(2,1)}) custom-call(s32[1,8]{1,0:T(1,128)} %cells_ref.1, bf16[1,8,6144]{2,1,0:T(8,128)(2,1)} %pixels_ref.1, f32[1,16,96,128]{3,2,1,0:T(8,128)} %cot_ref.1), custom_call_target="tpu_custom_call" | custom-call | bytes 5535000 | tf_op jit(solution)/shard_map/pack/pallas_call | solution.py:446
  2.6 6.5 %all-to-all-start = ((bf16[8,56,128]{2,1,0:T(8,128)(2,1)}), bf16[8,56,128]{2,1,0:T(8,128)(2,1)S(1)}, u32[]{:S(2)}, u32[]{:S(2)}) async-start(bf16[8,56,128]{2,1,0:T(8,128)(2,1)} %get-tuple-element.42), calls=%async_computation | async-start | bytes 229376 | tf_op jit(solution)/shard_map/all_to_all | solution.py:466
  9.1 0.5 collective-permute-start.2
  9.6 1.3 %collective-permute-start = (bf16[96,128]{1,0:T(8,128)(2,1)S(1)}, bf16[96,128]{1,0:T(8,128)(2,1)S(1)}, u32[]{:S(2)}, u32[]{:S(2)}) collective-permute-start(bf16[96,128]{1,0:T(8,128)(2,1)S(1)} %copy-done.9), channel_id=1, source_target_pairs={{4,0},{8,4},{12,8},{5,1},{9,5},{13,9},{6,2},{10,6},{14,10},{7,3},{... | collective-permute-start | bytes 73736 | tf_op jit(solution)/shard_map/ppermute | solution.py:53
  10.9 4.8 %collective-permute-done.below_ref = bf16[96,128]{1,0:T(8,128)(2,1)S(1)} collective-permute-done((bf16[96,128]{1,0:T(8,128)(2,1)S(1)}, bf16[96,128]{1,0:T(8,128)(2,1)S(1)}, u32[]{:S(2)}, u32[]{:S(2)}) %collective-permute-start) | collective-permute-done | bytes 24608 | tf_op jit(solution)/shard_map/ppermute | solution.py:53
  15.7 0.0 all-to-all-done.meta_ref.got_ref.refs_5_
  15.7 0.0 copy-done
  15.7 0.0 copy-start.3
  15.7 0.0 copy-start.4
  15.8 0.0 copy-start.5
  15.8 0.0 copy-start.6
  15.8 0.0 copy-start.7
  15.8 0.0 copy-start.8
  15.8 1.3 %patch.1 = (f32[144,128]{1,0:T(8,128)S(1)}, bf16[72,128]{1,0:T(8,128)(2,1)S(1)}, bf16[72,128]{1,0:T(8,128)(2,1)S(1)}) custom-call(s32[1]{0:T(128)} %bitcast.chan_ref.refs_0_, bf16[8,56,128]{2,1,0:T(8,128)(2,1)S(1)} %all-to-all-done.meta_ref.got_ref.refs_5_, f32[1,16,96,128]{3,2,1,0:T(8,128)S(1)} %copy-done, bf16[96,128]{1,0:T(8,128)(2,1)S(1)} %collective-permute-done.below_ref), custom_call_target="tpu_custom_call" | custom-call | bytes 4428000 | tf_op jit(solution)/shard_map/patch/pallas_call | solution.py:468
  17.1 0.0 copy-start.1
  17.1 0.1 collective-permute-start.1
  17.2 2.8 %stem.1 = (bf16[1,192,128]{2,1,0:T(8,128)(2,1)S(1)}, f32[1,512,96]{2,1,0:T(8,128)S(1)}, f32[1,512,1]{2,1,0:T(8,128)S(1)}, f32[1,512,96]{2,1,0:T(8,128)S(1)}, f32...) custom-call(bf16[8,56,128]{2,1,0:T(8,128)(2,1)S(1)} %all-to-all-done, ...), custom_call_target="tpu_custom_call" | custom-call | bytes 9963000 | tf_op jit(solution)/shard_map/stem/pallas_call | solution.py:503
  20.0 0.5 collective-permute-start.5
  20.5 0.0 collective-permute-done.1
  20.5 2.2 %collective-permute-start.4 = (bf16[1,336,128]{2,1,0:T(8,128)(2,1)S(1)}, bf16[1,336,128]{2,1,0:T(8,128)(2,1)S(1)}, u32[]{:S(2)}, u32[]{:S(2)}) collective-permute-start(bf16[1,336,128]{2,1,0:T(8,128)(2,1)S(1)} %pad_maximum_fusion.2), channel_id=1, source_target_pairs={{0,8},{4,12},{8,0},{12,4},{1,9},{5,13},{9,1},{13,5},{2,10},{6,14},... | collective-permute-start | bytes 258056 | tf_op jit(solution)/shard_map/ppermute | solution.py:58
  22.7 0.0 collective-permute-done.2.refs_4_
  22.7 3.8 %stem_back.1 = (f32[608,128]{1,0:T(8,128)S(1)}, bf16[608,128]{1,0:T(8,128)(2,1)S(1)}) custom-call(s32[1]{0:T(128)} %bitcast.chan_ref.refs_0_, bf16[1,72,128]{2,1,0:T(8,128)(2,1)S(1)} %bitcast.17, bf16[1,72,128]{2,1,0:T(8,128)(2,1)S(1)} %bitcast.20, bf16[9,192,96]{2,1,0:T(8,128)(2,1)S(1)} %copy-done.1, ...), custom_call_target="tpu_custom_call" | custom-call | bytes 13653000 | tf_op jit(solution)/shard_map/stem_back/pallas_call | solution.py:571
  26.5 0.1 collective-permute-start.3
  26.6 0.0 collective-permute-done.5
  26.6 1.0 %spread.1 = (f32[144,96]{1,0:T(8,128)S(1)}, f32[96,128]{1,0:T(8,128)S(1)}) custom-call(bf16[2,192,128]{2,1,0:T(8,128)(2,1)S(1)} %pad_maximum_fusion.1.refs_0_, bf16[9,192,96]{2,1,0:T(8,128)(2,1)S(1)} %copy-done.1, f32[144,128]{1,0:T(8,128)S(1)} %get-tuple-element.57.refs_2_.key_ref), custom_call_target="tpu_custom_call" | custom-call | bytes 3690000 | tf_op jit(solution)/shard_map/spread/pallas_call | solution.py:539
  27.7 0.1 collective-permute-done.4
  27.8 0.2 collective-permute-done.3
  28.0 1.6 %collective-permute-start.8 = (bf16[608,128]{1,0:T(8,128)(2,1)S(1)}, bf16[608,128]{1,0:T(8,128)(2,1)S(1)}, u32[]{:S(2)}, u32[]{:S(2)}) collective-permute-start(bf16[608,128]{1,0:T(8,128)(2,1)S(1)} %convert_add_fusion.1), channel_id=1, source_target_pairs={{0,2},{2,0},{1,3},{3,1},{4,6},{6,4},{5,7},{7,5},{8,10},{10,8},{9,1... | collective-permute-start | bytes 466952 | tf_op jit(solution)/shard_map/ppermute | solution.py:58
  29.6 1.6 %collective-permute-start.9 = (f32[96,128]{1,0:T(8,128)S(1)}, f32[96,128]{1,0:T(8,128)S(1)}, u32[]{:S(2)}, u32[]{:S(2)}) collective-permute-start(f32[96,128]{1,0:T(8,128)S(1)} %get-tuple-element.63), channel_id=1, source_target_pairs={{0,4},{4,8},{8,12},{1,5},{5,9},{9,13},{2,6},{6,10},{10,14},{3,7},{... | collective-permute-start | bytes 147464 | tf_op jit(solution)/shard_map/ppermute | solution.py:53
  31.2 1.7 %collective-permute-start.6 = (bf16[2,336,128]{2,1,0:T(8,128)(2,1)S(1)}, bf16[2,336,128]{2,1,0:T(8,128)(2,1)S(1)}, u32[]{:S(2)}, u32[]{:S(2)}) collective-permute-start(bf16[2,336,128]{2,1,0:T(8,128)(2,1)S(1)} %pad_maximum_fusion), channel_id=1, source_target_pairs={{0,4},{4,0},{8,12},{12,8},{1,5},{5,1},{9,13},{13,9},{2,6},{6,2},{1... | collective-permute-start | bytes 516104 | tf_op jit(solution)/shard_map/ppermute | solution.py:58
  32.9 1.4 %collective-permute-done.8 = bf16[608,128]{1,0:T(8,128)(2,1)S(1)} collective-permute-done((bf16[608,128]{1,0:T(8,128)(2,1)S(1)}, bf16[608,128]{1,0:T(8,128)(2,1)S(1)}, u32[]{:S(2)}, u32[]{:S(2)}) %collective-permute-start.8) | collective-permute-done | bytes 155680 | tf_op jit(solution)/shard_map/ppermute | solution.py:58
  34.3 0.0 collective-permute-done.9.above_ref
  34.3 1.1 %collective-permute-start.10 = (bf16[608,128]{1,0:T(8,128)(2,1)S(1)}, bf16[608,128]{1,0:T(8,128)(2,1)S(1)}, u32[]{:S(2)}, u32[]{:S(2)}) collective-permute-start(bf16[608,128]{1,0:T(8,128)(2,1)S(1)} %add_convert_fusion.2), channel_id=1, source_target_pairs={{0,4},{4,0},{8,12},{12,8},{1,5},{5,1},{9,13},{13,9},{2,6},{6,2},{1... | collective-permute-start | bytes 466952 | tf_op jit(solution)/shard_map/ppermute | solution.py:58
  35.5 2.5 %collective-permute-done.6 = bf16[2,336,128]{2,1,0:T(8,128)(2,1)S(1)} collective-permute-done((bf16[2,336,128]{2,1,0:T(8,128)(2,1)S(1)}, bf16[2,336,128]{2,1,0:T(8,128)(2,1)S(1)}, u32[]{:S(2)}, u32[]{:S(2)}) %collective-permute-start.6) | collective-permute-done | bytes 172064 | tf_op jit(solution)/shard_map/ppermute | solution.py:58
  38.0 0.3 collective-permute-start.7
  38.3 2.2 %collective-permute-done.10 = bf16[608,128]{1,0:T(8,128)(2,1)S(1)} collective-permute-done((bf16[608,128]{1,0:T(8,128)(2,1)S(1)}, bf16[608,128]{1,0:T(8,128)(2,1)S(1)}, u32[]{:S(2)}, u32[]{:S(2)}) %collective-permute-start.10) | collective-permute-done | bytes 155680 | tf_op jit(solution)/shard_map/ppermute | solution.py:58
  40.6 2.4 %collective-permute-start.11 = (bf16[608,128]{1,0:T(8,128)(2,1)S(1)}, bf16[608,128]{1,0:T(8,128)(2,1)S(1)}, u32[]{:S(2)}, u32[]{:S(2)}) collective-permute-start(bf16[608,128]{1,0:T(8,128)(2,1)S(1)} %add_convert_fusion.1), channel_id=1, source_target_pairs={{0,8},{4,12},{8,0},{12,4},{1,9},{5,13},{9,1},{13,5},{2,10},{6,14},... | collective-permute-start | bytes 466952 | tf_op jit(solution)/shard_map/ppermute | solution.py:58
  43.0 3.5 %agg_map.1 = bf16[16,96,128]{2,1,0:T(8,128)(2,1)} custom-call(f32[144,96]{1,0:T(8,128)S(1)} %get-tuple-element.61.y_ref, f32[144,128]{1,0:T(8,128)S(1)} %get-tuple-element.57.refs_2_.key_ref, f32[96,128]{1,0:T(8,128)S(1)} %collective-permute-done.9.above_ref), custom_call_target="tpu_custom_call" | custom-call | bytes 12915000 | tf_op jit(solution)/shard_map/agg_map/pallas_call | solution.py:631
  46.5 0.0 collective-permute-done.7.refs_2_
  46.5 1.4 %agg_weight_grad.1 = (f32[9,192,96]{2,1,0:T(8,128)S(1)}, bf16[9,192,96]{2,1,0:T(8,128)(2,1)S(1)}) custom-call(s32[1]{0:T(128)} %bitcast.9.refs_0_, bf16[4,336,128]{2,1,0:T(8,128)(2,1)S(1)} %constant_dynamic-update-slice_fusion.refs_1_, bf16[4,336,128]{2,1,0:T(8,128)(2,1)S(1)} %collective-permute-done.7.refs_2_), custom_call_target="tpu_custom_call" | custom-call | bytes 5166000 | tf_op jit(solution)/shard_map/agg_weight_grad/pallas_call | solution.py:643
  48.0 0.1 collective-permute-start.12
  48.0 2.1 %collective-permute-done.11 = bf16[608,128]{1,0:T(8,128)(2,1)S(1)} collective-permute-done((bf16[608,128]{1,0:T(8,128)(2,1)S(1)}, bf16[608,128]{1,0:T(8,128)(2,1)S(1)}, u32[]{:S(2)}, u32[]{:S(2)}) %collective-permute-start.11) | collective-permute-done | bytes 155680 | tf_op jit(solution)/shard_map/ppermute | solution.py:58
  50.2 0.1 collective-permute-start.13
  50.3 0.0 collective-permute-done.12
  50.3 1.0 %convert_add_fusion = f32[9,192,96]{2,1,0:T(8,128)} fusion(f32[9,192,96]{2,1,0:T(8,128)S(1)} %get-tuple-element.68, bf16[9,192,96]{2,1,0:T(8,128)(2,1)S(1)} %collective-permute-done.12), kind=kLoop, calls=%fused_computation | loop fusion | flops 331776 | bytes 1658880 | tf_op jit(solution)/shard_map/add | solution.py:665
  51.3 0.4 collective-permute-done.13.peer_ref
  51.7 0.9 %unpack.1 = (f32[49,96]{1,0:T(8,128)}, f32[96,384]{1,0:T(8,128)}, f32[96,384]{1,0:T(8,128)}, f32[192,384]{1,0:T(8,128)}) custom-call(s32[1]{0:T(128)} %bitcast.chan_ref.refs_0_, bf16[608,128]{1,0:T(8,128)(2,1)S(1)} %add_convert_fusion.own_ref, bf16[608,128]{1,0:T(8,128)(2,1)S(1)} %collective-permute-done.13.peer_ref), custom_call_target="tpu_custom_call" | custom-call | bytes 5535000 | tf_op jit(solution)/shard_map/unpack/pallas_call | solution.py:672
  (20 shorter events, 0.3 us)
Async XLA Ops:
  0.6 15.1 %copy-start = (f32[1,16,96,128]{3,2,1,0:T(8,128)S(1)}, f32[1,16,96,128]{3,2,1,0:T(8,128)}, u32[]{:S(2)}) copy-start(f32[1,16,96,128]{3,2,1,0:T(8,128)} %cot_ref.1) | copy-start | bytes 2359300
  2.6 7.0 %copy-start.9 = (bf16[96,128]{1,0:T(8,128)(2,1)S(1)}, bf16[96,128]{1,0:T(8,128)(2,1)}, u32[]{:S(2)}) copy-start(bf16[96,128]{1,0:T(8,128)(2,1)} %get-tuple-element.43) | copy-start | bytes 73732
  2.6 13.1 %all-to-all-start = ((bf16[8,56,128]{2,1,0:T(8,128)(2,1)}), bf16[8,56,128]{2,1,0:T(8,128)(2,1)S(1)}, u32[]{:S(2)}, u32[]{:S(2)}) async-start(bf16[8,56,128]{2,1,0:T(8,128)(2,1)} %get-tuple-element.42), calls=%async_computation | async-start | bytes 229376 | tf_op jit(solution)/shard_map/all_to_all | solution.py:466
  9.1 13.6 %collective-permute-start.2 = (bf16[9,192,96]{2,1,0:T(8,128)(2,1)}, bf16[9,192,96]{2,1,0:T(8,128)(2,1)S(1)}, u32[]{:S(2)}, u32[]{:S(2)}) collective-permute-start(bf16[9,192,96]{2,1,0:T(8,128)(2,1)} %refs_1_.1), channel_id=1, source_target_pairs={{0,1},{1,0},{2,3},{3,2},{4,5},{5,4},{6,7},{7,6},{8,9},{9,8},{10,11... | collective-permute-start | bytes 995336 | tf_op jit(solution)/shard_map/ppermute | solution.py:58
  9.6 6.1 %collective-permute-start = (bf16[96,128]{1,0:T(8,128)(2,1)S(1)}, bf16[96,128]{1,0:T(8,128)(2,1)S(1)}, u32[]{:S(2)}, u32[]{:S(2)}) collective-permute-start(bf16[96,128]{1,0:T(8,128)(2,1)S(1)} %copy-done.9), channel_id=1, source_target_pairs={{4,0},{8,4},{12,8},{5,1},{9,5},{13,9},{6,2},{10,6},{14,10},{7,3},{... | collective-permute-start | bytes 73736 | tf_op jit(solution)/shard_map/ppermute | solution.py:53
  15.7 1.4 %copy-start.2 = (bf16[384,192]{0,1:T(8,128)(2,1)S(1)}, bf16[384,192]{0,1:T(8,128)(2,1)}, u32[]{:S(2)}) copy-start(bf16[384,192]{0,1:T(8,128)(2,1)} %param.20) | copy-start | bytes 442372
  15.7 1.4 %copy-start.3 = (bf16[96,384]{1,0:T(8,128)(2,1)S(1)}, bf16[96,384]{1,0:T(8,128)(2,1)}, u32[]{:S(2)}) copy-start(bf16[96,384]{1,0:T(8,128)(2,1)} %refs_14_.1) | copy-start | bytes 221188
  15.7 1.4 %copy-start.4 = (bf16[384,96]{0,1:T(8,128)(2,1)S(1)}, bf16[384,96]{0,1:T(8,128)(2,1)}, u32[]{:S(2)}) copy-start(bf16[384,96]{0,1:T(8,128)(2,1)} %param.17) | copy-start | bytes 221188
  15.8 1.4 %copy-start.5 = (f32[49,96]{1,0:T(8,128)S(1)}, f32[49,96]{1,0:T(8,128)}, u32[]{:S(2)}) copy-start(f32[49,96]{1,0:T(8,128)} %dw_ref.1) | copy-start | bytes 56452
  15.8 1.4 %copy-start.6 = (f32[96]{0:T(128)S(1)}, f32[96]{0:T(128)}, u32[]{:S(2)}) copy-start(f32[96]{0:T(128)} %param.15) | copy-start | bytes 1156
  15.8 1.4 %copy-start.7 = (f32[96]{0:T(128)S(1)}, f32[96]{0:T(128)}, u32[]{:S(2)}) copy-start(f32[96]{0:T(128)} %param.18) | copy-start | bytes 1156
  15.8 1.4 %copy-start.8 = (f32[96]{0:T(128)S(1)}, f32[96]{0:T(128)}, u32[]{:S(2)}) copy-start(f32[96]{0:T(128)} %param.19) | copy-start | bytes 1156
  17.1 5.7 %copy-start.1 = (bf16[9,192,96]{2,1,0:T(8,128)(2,1)S(1)}, bf16[9,192,96]{2,1,0:T(8,128)(2,1)}, u32[]{:S(2)}) copy-start(bf16[9,192,96]{2,1,0:T(8,128)(2,1)} %refs_1_.1) | copy-start | bytes 995332
  17.1 3.4 %collective-permute-start.1 = (bf16[72,128]{1,0:T(8,128)(2,1)S(1)}, bf16[72,128]{1,0:T(8,128)(2,1)S(1)}, u32[]{:S(2)}, u32[]{:S(2)}) collective-permute-start(bf16[72,128]{1,0:T(8,128)(2,1)S(1)} %get-tuple-element.45), channel_id=1, source_target_pairs={{0,1},{1,0},{2,3},{3,2},{4,5},{5,4},{6,7},{7,6},{8,9},{9,8},{10,11... | collective-permute-start | bytes 55304 | tf_op jit(solution)/shard_map/ppermute | solution.py:58
  20.0 6.6 %collective-permute-start.5 = (bf16[1,192,128]{2,1,0:T(8,128)(2,1)S(1)}, bf16[1,192,128]{2,1,0:T(8,128)(2,1)S(1)}, u32[]{:S(2)}, u32[]{:S(2)}) collective-permute-start(bf16[1,192,128]{2,1,0:T(8,128)(2,1)S(1)} %get-tuple-element.56), channel_id=1, source_target_pairs={{0,1},{1,0},{2,3},{3,2},{4,5},{5,4},{6,7},{7,6},{8,9},{9,8},{10,11... | collective-permute-start | bytes 147464 | tf_op jit(solution)/shard_map/ppermute | solution.py:58
  20.5 7.3 %collective-permute-start.4 = (bf16[1,336,128]{2,1,0:T(8,128)(2,1)S(1)}, bf16[1,336,128]{2,1,0:T(8,128)(2,1)S(1)}, u32[]{:S(2)}, u32[]{:S(2)}) collective-permute-start(bf16[1,336,128]{2,1,0:T(8,128)(2,1)S(1)} %pad_maximum_fusion.2), channel_id=1, source_target_pairs={{0,8},{4,12},{8,0},{12,4},{1,9},{5,13},{9,1},{13,5},{2,10},{6,14},... | collective-permute-start | bytes 258056 | tf_op jit(solution)/shard_map/ppermute | solution.py:58
  26.5 1.4 %collective-permute-start.3 = (bf16[608,128]{1,0:T(8,128)(2,1)S(1)}, bf16[608,128]{1,0:T(8,128)(2,1)S(1)}, u32[]{:S(2)}, u32[]{:S(2)}) collective-permute-start(bf16[608,128]{1,0:T(8,128)(2,1)S(1)} %get-tuple-element.55), channel_id=1, source_target_pairs={{0,1},{1,0},{2,3},{3,2},{4,5},{5,4},{6,7},{7,6},{8,9},{9,8},{10,11... | collective-permute-start | bytes 466952 | tf_op jit(solution)/shard_map/ppermute | solution.py:58
  28.0 6.2 %collective-permute-start.8 = (bf16[608,128]{1,0:T(8,128)(2,1)S(1)}, bf16[608,128]{1,0:T(8,128)(2,1)S(1)}, u32[]{:S(2)}, u32[]{:S(2)}) collective-permute-start(bf16[608,128]{1,0:T(8,128)(2,1)S(1)} %convert_add_fusion.1), channel_id=1, source_target_pairs={{0,2},{2,0},{1,3},{3,1},{4,6},{6,4},{5,7},{7,5},{8,10},{10,8},{9,1... | collective-permute-start | bytes 466952 | tf_op jit(solution)/shard_map/ppermute | solution.py:58
  29.6 4.7 %collective-permute-start.9 = (f32[96,128]{1,0:T(8,128)S(1)}, f32[96,128]{1,0:T(8,128)S(1)}, u32[]{:S(2)}, u32[]{:S(2)}) collective-permute-start(f32[96,128]{1,0:T(8,128)S(1)} %get-tuple-element.63), channel_id=1, source_target_pairs={{0,4},{4,8},{8,12},{1,5},{5,9},{9,13},{2,6},{6,10},{10,14},{3,7},{... | collective-permute-start | bytes 147464 | tf_op jit(solution)/shard_map/ppermute | solution.py:53
  31.2 6.8 %collective-permute-start.6 = (bf16[2,336,128]{2,1,0:T(8,128)(2,1)S(1)}, bf16[2,336,128]{2,1,0:T(8,128)(2,1)S(1)}, u32[]{:S(2)}, u32[]{:S(2)}) collective-permute-start(bf16[2,336,128]{2,1,0:T(8,128)(2,1)S(1)} %pad_maximum_fusion), channel_id=1, source_target_pairs={{0,4},{4,0},{8,12},{12,8},{1,5},{5,1},{9,13},{13,9},{2,6},{6,2},{1... | collective-permute-start | bytes 516104 | tf_op jit(solution)/shard_map/ppermute | solution.py:58
  34.3 6.2 %collective-permute-start.10 = (bf16[608,128]{1,0:T(8,128)(2,1)S(1)}, bf16[608,128]{1,0:T(8,128)(2,1)S(1)}, u32[]{:S(2)}, u32[]{:S(2)}) collective-permute-start(bf16[608,128]{1,0:T(8,128)(2,1)S(1)} %add_convert_fusion.2), channel_id=1, source_target_pairs={{0,4},{4,0},{8,12},{12,8},{1,5},{5,1},{9,13},{13,9},{2,6},{6,2},{1... | collective-permute-start | bytes 466952 | tf_op jit(solution)/shard_map/ppermute | solution.py:58
  38.0 8.5 %collective-permute-start.7 = (bf16[4,336,128]{2,1,0:T(8,128)(2,1)S(1)}, bf16[4,336,128]{2,1,0:T(8,128)(2,1)S(1)}, u32[]{:S(2)}, u32[]{:S(2)}) collective-permute-start(bf16[4,336,128]{2,1,0:T(8,128)(2,1)S(1)} %constant_dynamic-update-slice_fusion.refs_1_), channel_id=1, source_target_pairs={{0,2},{2,0},{1,3},{3,1},{4,6},{6,4},{5,7},{7,5},{8,10},{10,8},{9,1... | collective-permute-start | bytes 1032200 | tf_op jit(solution)/shard_map/ppermute | solution.py:58
  40.6 9.6 %collective-permute-start.11 = (bf16[608,128]{1,0:T(8,128)(2,1)S(1)}, bf16[608,128]{1,0:T(8,128)(2,1)S(1)}, u32[]{:S(2)}, u32[]{:S(2)}) collective-permute-start(bf16[608,128]{1,0:T(8,128)(2,1)S(1)} %add_convert_fusion.1), channel_id=1, source_target_pairs={{0,8},{4,12},{8,0},{12,4},{1,9},{5,13},{9,1},{13,5},{2,10},{6,14},... | collective-permute-start | bytes 466952 | tf_op jit(solution)/shard_map/ppermute | solution.py:58
  48.0 2.3 %collective-permute-start.12 = (bf16[9,192,96]{2,1,0:T(8,128)(2,1)S(1)}, bf16[9,192,96]{2,1,0:T(8,128)(2,1)S(1)}, u32[]{:S(2)}, u32[]{:S(2)}) collective-permute-start(bf16[9,192,96]{2,1,0:T(8,128)(2,1)S(1)} %get-tuple-element.69), channel_id=1, source_target_pairs={{0,1},{1,0},{2,3},{3,2},{4,5},{5,4},{6,7},{7,6},{8,9},{9,8},{10,11... | collective-permute-start | bytes 995336 | tf_op jit(solution)/shard_map/ppermute | solution.py:58
  50.2 1.4 %collective-permute-start.13 = (bf16[608,128]{1,0:T(8,128)(2,1)S(1)}, bf16[608,128]{1,0:T(8,128)(2,1)S(1)}, u32[]{:S(2)}, u32[]{:S(2)}) collective-permute-start(bf16[608,128]{1,0:T(8,128)(2,1)S(1)} %add_convert_fusion.own_ref), channel_id=1, source_target_pairs={{0,1},{1,0},{2,3},{3,2},{4,5},{5,4},{6,7},{7,6},{8,9},{9,8},{10,11... | collective-permute-start | bytes 466952 | tf_op jit(solution)/shard_map/ppermute | solution.py:58

commit v8 on v7

--- a/solution.py
+++ b/solution.py
@@ -62,7 +62,7 @@
     return (1, 2) if tap == 0 else (0, 1)
 
 
-def pack_kernel(cells_ref, pixels_ref, row_ref, out_ref, below_ref, wide_ref):
+def pack_kernel(cells_ref, pixels_ref, row_ref, out_ref, below_ref, wide_ref, note_ref):
     slots = pixels_ref.shape[0]
     rows = out_ref.shape[0]
     pixch = pixels_ref.shape[1]
@@ -75,17 +75,18 @@
         for s in range(t):
             rank = rank + ((bands[s] == bands[t]) & live[s]).astype(jnp.int32)
         places.append(jnp.where(live[t], bands[t] * CAP + rank, -1))
-    dest = lax.broadcasted_iota(jnp.int32, (rows, slots), 0)
-    slot = lax.broadcasted_iota(jnp.int32, (rows, slots), 1)
-    place = jnp.full((rows, slots), -1, jnp.int32)
+    below_ref[...] = row_ref[...].astype(BF16)
+    pixels = pixels_ref[...].astype(F32)
+    for n in range(pixch // 128):
+        wide_ref[:, n, :] = pixels[:, 128 * n : 128 * n + 128]
+    wide_ref[:, pixch // 128 :, :] = jnp.zeros_like(wide_ref[:, pixch // 128 :, :])
+    out_ref[...] = jnp.zeros_like(out_ref)
     for t in range(slots):
-        place = jnp.where(slot == t, places[t], place)
-    route = (place == dest).astype(F32).astype(BF16)
-    below_ref[...] = row_ref[...].astype(BF16)
-    routed = nn(route, pixels_ref[...])
-    wide_ref[...] = jnp.zeros_like(wide_ref)
-    for n in range(pixch // 128):
-        wide_ref[:, n, :] = routed[:, 128 * n : 128 * n + 128]
+
+        @pl.when(live[t])
+        def _():
+            out_ref[jnp.maximum(places[t], 0)] = wide_ref[t].astype(BF16)
+
     lane = lax.broadcasted_iota(jnp.int32, (rows, 128), 1)
     base = (lax.broadcasted_iota(jnp.int32, (rows, 128), 0) // CAP) * CAP
     notes = jnp.zeros((rows, 128), F32)
@@ -97,8 +98,9 @@
             hit = base + rank == places[t]
             for at, value in enumerate((own_row, own_col, jnp.float32(1.0))):
                 notes = jnp.where(hit & (lane == 3 * rank + at), value, notes)
-    wide_ref[:, pixch // 128, :] = notes
-    out_ref[...] = wide_ref[...].astype(BF16)
+    note_ref[...] = jnp.zeros_like(note_ref)
+    note_ref[:, 0, :] = notes
+    out_ref[:, pixch // 128 :, :] = note_ref[...].astype(BF16)
 
 
 def patch_kernel(chan_ref, meta_ref, cot_ref, below_ref, key_ref, own_ref, send_ref, meta_f32):
@@ -166,16 +168,13 @@
     channels = dw_ref.shape[1]
     fill_padded(padded_ref, got_ref, wide_ref, pixels_ref, channels)
 
-    def row_step(i, carry):
+    for i in range(SIDE):
         total = jnp.zeros((SIDE, 8, channels), F32)
-        for a in range(7):
+        for a in range(max(0, 3 - i), min(7, SIDE + 3 - i)):
             for b in range(7):
-                weight = dw_ref[pl.ds(7 * a + b, 1), :].reshape(1, 1, channels)
+                weight = dw_ref[7 * a + b : 7 * a + b + 1, :].reshape(1, 1, channels)
                 total = total + weight * padded_ref[i + a, b : b + SIDE]
         spatial_ref[i] = total
-        return carry
-
-    lax.fori_loop(0, SIDE, row_step, 0)
     hat1, rstd1 = center_of(spatial_ref[...].reshape(PIX * 8, channels))
     hat1_ref[...] = hat1
     rstd1_ref[...] = rstd1
@@ -219,11 +218,10 @@
     gain_ref, up_ref, proj_ref, scale_ref, ds_gain_ref, ds_ref,
     keep_ref, send_ref,
     padded_ref, dlow_ref, dspatial_ref, dw_ref, ds_acc, up_acc, proj_acc, pack_ref,
-    wide_ref, pixels_ref,
+    wide_ref, pixels_ref, w_ref,
     *, scale,
 ):
     channels = gain_ref.shape[1]
-    e_half = w_own_ref.shape[2]
     half = SIDE // 2
     step = pl.program_id(0)
 
@@ -234,19 +232,21 @@
         up_acc[...] = jnp.zeros_like(up_acc)
         proj_acc[...] = jnp.zeros_like(proj_acc)
 
-    own = own_ref[...].astype(F32)[:, :e_half].reshape(9, 8, e_half)
-    peer = peer_ref[...].astype(F32)[:, :e_half].reshape(9, 8, e_half)
+    e_half = w_own_ref.shape[2]
+    w_ref[...] = jnp.zeros_like(w_ref)
+    w_ref[:, :, 0:e_half] = w_own_ref[...]
+    w_ref[:, :, 128 : 128 + e_half] = w_peer_ref[...]
+    cots = jnp.concatenate([own_ref[...], peer_ref[...]], axis=1)
     grads = {}
     for a in range(3):
         for b in range(3):
-            places = [(u, v) for u in reach(a) for v in reach(b)]
-            left_own = jnp.concatenate([own[3 * u + v] for u, v in places], axis=0).astype(BF16)
-            left_peer = jnp.concatenate([peer[3 * u + v] for u, v in places], axis=0).astype(BF16)
-            out = nt(left_own, w_own_ref[3 * a + b]) + nt(left_peer, w_peer_ref[3 * a + b])
-            for n, (u, v) in enumerate(places):
-                at = (2 * u + a - 1) * half + 2 * v + b - 1
-                piece = out[8 * n : 8 * n + 8]
-                grads[at] = grads[at] + piece if at in grads else piece
+            out = nt(cots, w_ref[3 * a + b])
+            for u in reach(a):
+                for v in reach(b):
+                    at = (2 * u + a - 1) * half + 2 * v + b - 1
+                    row = 8 * (3 * u + v)
+                    piece = out[row : row + 8]
+                    grads[at] = grads[at] + piece if at in grads else piece
     dfeat = jnp.concatenate([grads[at] for at in range(half * half)], axis=0) * scale
     dfeat = dfeat.astype(BF16)
 
@@ -275,18 +275,15 @@
     dspatial_ref[...] = dspatial.reshape(SIDE, SIDE, 8, channels)
     fill_padded(padded_ref, got_ref, wide_ref, pixels_ref, channels)
 
-    def tap_step(a, carry):
+    for a in range(7):
         totals = [jnp.zeros((8, channels), F32) for _ in range(7)]
-        for i in range(SIDE):
-            grad = dspatial_ref[i]
+        for i in range(max(0, 3 - a), min(SIDE, SIDE + 3 - a)):
             for b in range(7):
-                product = padded_ref[i + a, b : b + SIDE] * grad
+                low, high = max(0, 3 - b), min(SIDE, SIDE + 3 - b)
+                product = padded_ref[i + a, b + low : b + high] * dspatial_ref[i, low:high]
                 totals[b] = totals[b] + jnp.sum(product, axis=0)
         for b in range(7):
             dw_ref[a, b] += totals[b]
-        return carry
-
-    lax.fori_loop(0, 7, tap_step, 0)
 
     @pl.when(step == pl.num_programs(0) - 1)
     def _():
@@ -456,7 +453,10 @@
             pl.BlockSpec((None, None, e_half, cols), lambda i: (0, 0, 0, 0)),
         ],
         out_specs=(whole((sources, WIRE_ROWS, 128)), whole((e_half, cols))),
-        scratch_shapes=[pltpu.VMEM((sources, WIRE_ROWS, 128), F32)],
+        scratch_shapes=[
+            pltpu.VMEM((tile_pixels.shape[1], WIRE_ROWS, 128), F32),
+            pltpu.VMEM((sources, 8, 128), F32),
+        ],
         cost_estimate=takes(1.5),
         name="pack",
     )(tile_cell, tile_pixels, agg_cot)
@@ -594,6 +594,7 @@
             pltpu.VMEM(proj_turned.shape, F32),
             pltpu.VMEM((2 * HALF_ROWS, 128), F32),
             *pixel_scratch,
+            pltpu.VMEM((9, width, 256), BF16),
         ],
         compiler_params=params_of(),
         cost_estimate=takes(3.7),

time: 52.9 us -> 51 us (0.964)
  Pallas kernels: 16.6 us -> 15.2 us
  waiting for transfers between devices: 13.7 us -> 13 us
    pallas_call x1, Pallas kernels: 3.79 us -> 2.95 us  [on_device(): pl.pallas_call(lambda *refs: back_kernel(*refs, scale=loss_scale), grid=(...]
    ppermute x12, waiting for transfers between devices: 8.9 us -> 8.13 us  [swapped(): lax.ppermute(value, axis, [(place, place ^ step) for place in range(count)])]
  transfers between devices with their start and end apart: 15 -> 15, of which waited for: 8 -> 7; matrix products, arithmetic and copies ran while one was open for 2% -> 2% of each run, Pallas kernels for 26% -> 24%
where the time goes in v8:
time: 51 us; the launch traced here: 50.7 us
  starting transfers between devices  20.3 us (40%)
  Pallas kernels  15.2 us (30%)
  waiting for transfers between devices  13 us (25%)
  other arithmetic  1.2 us (2%)
  between operations  0.93 us (2%)
    ppermute x12, starting transfers between devices, swapped(): lax.ppermute(value, axis, [(place, place ^ step) for place in range(count)])  11.1 us
    ppermute x12, waiting for transfers between devices, swapped(): lax.ppermute(value, axis, [(place, place ^ step) for place in range(count)])  8.13 us
    all_to_all x1, starting transfers between devices, on_device(): lax.all_to_all(packed, ('slide', 'chan'), split_axis=0, concat_axis=0, ti...  6.46 us
    ppermute x2, waiting for transfers between devices, shifted(): lax.ppermute(value, axis, [(source, source + steps) for source in range(f...  4.84 us
    pallas_call x1, Pallas kernels, on_device(): agg_map = map_call(spread, key, above)  3.5 us
    pallas_call x1, Pallas kernels, on_device(): pl.pallas_call(lambda *refs: back_kernel(*refs, scale=loss_scale), grid=(...  2.95 us
    ppermute x2, starting transfers between devices, shifted(): lax.ppermute(value, axis, [(source, source + steps) for source in range(f...  2.75 us
    pallas_call x1, Pallas kernels, on_device(): pl.pallas_call(stem_kernel, grid=(chunks,), out_shape=(jax.ShapeDtypeStru...  2.25 us
  transfers between devices with their start and end apart: 15, of which 7 were waited for; matrix products, arithmetic and copies ran while one was open for 2% of the time, Pallas kernels for 24%

profile of v8, /device:TPU:0, one launch (start us, length us, event | category | flops | bytes accessed | tf_op | source)
XLA Modules:
  0.0 50.7 jit_solution(10701779344556011282)
XLA Ops:
  0.6 0.0 copy-start
  0.6 1.9 %pack.1 = (bf16[8,56,128]{2,1,0:T(8,128)(2,1)}, bf16[96,128]{1,0:T(8,128)(2,1)}) custom-call(s32[1,8]{1,0:T(1,128)} %cells_ref.1, bf16[1,8,6144]{2,1,0:T(8,128)(2,1)} %pixels_ref.1, f32[1,16,96,128]{3,2,1,0:T(8,128)} %cot_ref.1), custom_call_target="tpu_custom_call" | custom-call | bytes 5535000 | tf_op jit(solution)/shard_map/pack/pallas_call | solution.py:443
  2.5 6.5 %all-to-all-start = ((bf16[8,56,128]{2,1,0:T(8,128)(2,1)}), bf16[8,56,128]{2,1,0:T(8,128)(2,1)S(1)}, u32[]{:S(2)}, u32[]{:S(2)}) async-start(bf16[8,56,128]{2,1,0:T(8,128)(2,1)} %get-tuple-element.42), calls=%async_computation | async-start | bytes 229376 | tf_op jit(solution)/shard_map/all_to_all | solution.py:466
  9.0 0.5 collective-permute-start.2
  9.5 0.0 copy-done.9
  9.5 1.3 %collective-permute-start = (bf16[96,128]{1,0:T(8,128)(2,1)S(1)}, bf16[96,128]{1,0:T(8,128)(2,1)S(1)}, u32[]{:S(2)}, u32[]{:S(2)}) collective-permute-start(bf16[96,128]{1,0:T(8,128)(2,1)S(1)} %copy-done.9), channel_id=1, source_target_pairs={{4,0},{8,4},{12,8},{5,1},{9,5},{13,9},{6,2},{10,6},{14,10},{7,3},{... | collective-permute-start | bytes 73736 | tf_op jit(solution)/shard_map/ppermute | solution.py:53
  10.8 4.8 %collective-permute-done.below_ref = bf16[96,128]{1,0:T(8,128)(2,1)S(1)} collective-permute-done((bf16[96,128]{1,0:T(8,128)(2,1)S(1)}, bf16[96,128]{1,0:T(8,128)(2,1)S(1)}, u32[]{:S(2)}, u32[]{:S(2)}) %collective-permute-start) | collective-permute-done | bytes 24608 | tf_op jit(solution)/shard_map/ppermute | solution.py:53
  15.6 0.0 all-to-all-done.meta_ref.got_ref.refs_5_
  15.6 0.0 copy-start.3
  15.7 0.0 copy-start.4
  15.7 0.0 copy-start.5
  15.7 0.0 copy-start.6
  15.7 0.0 copy-start.7
  15.7 0.0 copy-start.8
  15.7 1.2 %patch.1 = (f32[144,128]{1,0:T(8,128)S(1)}, bf16[72,128]{1,0:T(8,128)(2,1)S(1)}, bf16[72,128]{1,0:T(8,128)(2,1)S(1)}) custom-call(s32[1]{0:T(128)} %bitcast.chan_ref.refs_0_, bf16[8,56,128]{2,1,0:T(8,128)(2,1)S(1)} %all-to-all-done.meta_ref.got_ref.refs_5_, f32[1,16,96,128]{3,2,1,0:T(8,128)S(1)} %copy-done, bf16[96,128]{1,0:T(8,128)(2,1)S(1)} %collective-permute-done.below_ref), custom_call_target="tpu_custom_call" | custom-call | bytes 4428000 | tf_op jit(solution)/shard_map/patch/pallas_call | solution.py:468
  17.0 0.0 copy-start.1
  17.0 0.1 collective-permute-start.1
  17.1 2.2 %stem.1 = (bf16[1,192,128]{2,1,0:T(8,128)(2,1)S(1)}, f32[1,512,96]{2,1,0:T(8,128)S(1)}, f32[1,512,1]{2,1,0:T(8,128)S(1)}, f32[1,512,96]{2,1,0:T(8,128)S(1)}, f32...) custom-call(bf16[8,56,128]{2,1,0:T(8,128)(2,1)S(1)} %all-to-all-done, ...), custom_call_target="tpu_custom_call" | custom-call | bytes 9963000 | tf_op jit(solution)/shard_map/stem/pallas_call | solution.py:503
  19.4 0.5 %collective-permute-start.5 = (bf16[1,192,128]{2,1,0:T(8,128)(2,1)S(1)}, bf16[1,192,128]{2,1,0:T(8,128)(2,1)S(1)}, u32[]{:S(2)}, u32[]{:S(2)}) collective-permute-start(bf16[1,192,128]{2,1,0:T(8,128)(2,1)S(1)} %get-tuple-element.56), channel_id=1, source_target_pairs={{0,1},{1,0},{2,3},{3,2},{4,5},{5,4},{6,7},{7,6},{8,9},{9,8},{10,11... | collective-permute-start | bytes 147464 | tf_op jit(solution)/shard_map/ppermute | solution.py:58
  19.9 0.0 collective-permute-done.1
  19.9 2.2 %collective-permute-start.4 = (bf16[1,336,128]{2,1,0:T(8,128)(2,1)S(1)}, bf16[1,336,128]{2,1,0:T(8,128)(2,1)S(1)}, u32[]{:S(2)}, u32[]{:S(2)}) collective-permute-start(bf16[1,336,128]{2,1,0:T(8,128)(2,1)S(1)} %pad_maximum_fusion.2), channel_id=1, source_target_pairs={{0,8},{4,12},{8,0},{12,4},{1,9},{5,13},{9,1},{13,5},{2,10},{6,14},... | collective-permute-start | bytes 258056 | tf_op jit(solution)/shard_map/ppermute | solution.py:58
  22.1 0.0 collective-permute-done.2.refs_4_
  22.1 2.9 %stem_back.1 = (f32[608,128]{1,0:T(8,128)S(1)}, bf16[608,128]{1,0:T(8,128)(2,1)S(1)}) custom-call(s32[1]{0:T(128)} %bitcast.chan_ref.refs_0_, bf16[1,72,128]{2,1,0:T(8,128)(2,1)S(1)} %bitcast.17, bf16[1,72,128]{2,1,0:T(8,128)(2,1)S(1)} %bitcast.20, bf16[9,192,96]{2,1,0:T(8,128)(2,1)S(1)} %copy-done.1, ...), custom_call_target="tpu_custom_call" | custom-call | bytes 13653000 | tf_op jit(solution)/shard_map/stem_back/pallas_call | solution.py:571
  25.1 0.1 collective-permute-start.3
  25.2 0.0 collective-permute-done.5
  25.2 1.0 %spread.1 = (f32[144,96]{1,0:T(8,128)S(1)}, f32[96,128]{1,0:T(8,128)S(1)}) custom-call(bf16[2,192,128]{2,1,0:T(8,128)(2,1)S(1)} %pad_maximum_fusion.1.refs_0_, bf16[9,192,96]{2,1,0:T(8,128)(2,1)S(1)} %copy-done.1, f32[144,128]{1,0:T(8,128)S(1)} %get-tuple-element.57.refs_2_.key_ref), custom_call_target="tpu_custom_call" | custom-call | bytes 3690000 | tf_op jit(solution)/shard_map/spread/pallas_call | solution.py:539
  26.3 0.9 %collective-permute-done.4 = bf16[1,336,128]{2,1,0:T(8,128)(2,1)S(1)} collective-permute-done((bf16[1,336,128]{2,1,0:T(8,128)(2,1)S(1)}, bf16[1,336,128]{2,1,0:T(8,128)(2,1)S(1)}, u32[]{:S(2)}, u32[]{:S(2)}) %collective-permute-start.4) | collective-permute-done | bytes 86048 | tf_op jit(solution)/shard_map/ppermute | solution.py:58
  27.2 0.0 collective-permute-done.3
  27.3 1.6 %collective-permute-start.8 = (bf16[608,128]{1,0:T(8,128)(2,1)S(1)}, bf16[608,128]{1,0:T(8,128)(2,1)S(1)}, u32[]{:S(2)}, u32[]{:S(2)}) collective-permute-start(bf16[608,128]{1,0:T(8,128)(2,1)S(1)} %convert_add_fusion.1), channel_id=1, source_target_pairs={{0,2},{2,0},{1,3},{3,1},{4,6},{6,4},{5,7},{7,5},{8,10},{10,8},{9,1... | collective-permute-start | bytes 466952 | tf_op jit(solution)/shard_map/ppermute | solution.py:58
  28.8 1.5 %collective-permute-start.9 = (f32[96,128]{1,0:T(8,128)S(1)}, f32[96,128]{1,0:T(8,128)S(1)}, u32[]{:S(2)}, u32[]{:S(2)}) collective-permute-start(f32[96,128]{1,0:T(8,128)S(1)} %get-tuple-element.63), channel_id=1, source_target_pairs={{0,4},{4,8},{8,12},{1,5},{5,9},{9,13},{2,6},{6,10},{10,14},{3,7},{... | collective-permute-start | bytes 147464 | tf_op jit(solution)/shard_map/ppermute | solution.py:53
  30.3 1.5 %collective-permute-start.6 = (bf16[2,336,128]{2,1,0:T(8,128)(2,1)S(1)}, bf16[2,336,128]{2,1,0:T(8,128)(2,1)S(1)}, u32[]{:S(2)}, u32[]{:S(2)}) collective-permute-start(bf16[2,336,128]{2,1,0:T(8,128)(2,1)S(1)} %pad_maximum_fusion), channel_id=1, source_target_pairs={{0,4},{4,0},{8,12},{12,8},{1,5},{5,1},{9,13},{13,9},{2,6},{6,2},{1... | collective-permute-start | bytes 516104 | tf_op jit(solution)/shard_map/ppermute | solution.py:58
  31.8 1.0 %collective-permute-done.8 = bf16[608,128]{1,0:T(8,128)(2,1)S(1)} collective-permute-done((bf16[608,128]{1,0:T(8,128)(2,1)S(1)}, bf16[608,128]{1,0:T(8,128)(2,1)S(1)}, u32[]{:S(2)}, u32[]{:S(2)}) %collective-permute-start.8) | collective-permute-done | bytes 155680 | tf_op jit(solution)/shard_map/ppermute | solution.py:58
  32.9 0.0 collective-permute-done.9.above_ref
  32.9 2.0 %collective-permute-start.10 = (bf16[608,128]{1,0:T(8,128)(2,1)S(1)}, bf16[608,128]{1,0:T(8,128)(2,1)S(1)}, u32[]{:S(2)}, u32[]{:S(2)}) collective-permute-start(bf16[608,128]{1,0:T(8,128)(2,1)S(1)} %add_convert_fusion.2), channel_id=1, source_target_pairs={{0,4},{4,0},{8,12},{12,8},{1,5},{5,1},{9,13},{13,9},{2,6},{6,2},{1... | collective-permute-start | bytes 466952 | tf_op jit(solution)/shard_map/ppermute | solution.py:58
  34.9 2.5 %collective-permute-done.6 = bf16[2,336,128]{2,1,0:T(8,128)(2,1)S(1)} collective-permute-done((bf16[2,336,128]{2,1,0:T(8,128)(2,1)S(1)}, bf16[2,336,128]{2,1,0:T(8,128)(2,1)S(1)}, u32[]{:S(2)}, u32[]{:S(2)}) %collective-permute-start.6) | collective-permute-done | bytes 172064 | tf_op jit(solution)/shard_map/ppermute | solution.py:58
  37.4 0.1 collective-permute-start.7
  37.5 1.6 %collective-permute-done.10 = bf16[608,128]{1,0:T(8,128)(2,1)S(1)} collective-permute-done((bf16[608,128]{1,0:T(8,128)(2,1)S(1)}, bf16[608,128]{1,0:T(8,128)(2,1)S(1)}, u32[]{:S(2)}, u32[]{:S(2)}) %collective-permute-start.10) | collective-permute-done | bytes 155680 | tf_op jit(solution)/shard_map/ppermute | solution.py:58
  39.2 2.4 %collective-permute-start.11 = (bf16[608,128]{1,0:T(8,128)(2,1)S(1)}, bf16[608,128]{1,0:T(8,128)(2,1)S(1)}, u32[]{:S(2)}, u32[]{:S(2)}) collective-permute-start(bf16[608,128]{1,0:T(8,128)(2,1)S(1)} %add_convert_fusion.1), channel_id=1, source_target_pairs={{0,8},{4,12},{8,0},{12,4},{1,9},{5,13},{9,1},{13,5},{2,10},{6,14},... | collective-permute-start | bytes 466952 | tf_op jit(solution)/shard_map/ppermute | solution.py:58
  41.6 3.5 %agg_map.1 = bf16[16,96,128]{2,1,0:T(8,128)(2,1)} custom-call(f32[144,96]{1,0:T(8,128)S(1)} %get-tuple-element.61.y_ref, f32[144,128]{1,0:T(8,128)S(1)} %get-tuple-element.57.refs_2_.key_ref, f32[96,128]{1,0:T(8,128)S(1)} %collective-permute-done.9.above_ref), custom_call_target="tpu_custom_call" | custom-call | bytes 12915000 | tf_op jit(solution)/shard_map/agg_map/pallas_call | solution.py:632
  45.1 0.0 collective-permute-done.7.refs_2_
  45.1 1.4 %agg_weight_grad.1 = (f32[9,192,96]{2,1,0:T(8,128)S(1)}, bf16[9,192,96]{2,1,0:T(8,128)(2,1)S(1)}) custom-call(s32[1]{0:T(128)} %bitcast.9.refs_0_, bf16[4,336,128]{2,1,0:T(8,128)(2,1)S(1)} %constant_dynamic-update-slice_fusion.refs_1_, bf16[4,336,128]{2,1,0:T(8,128)(2,1)S(1)} %collective-permute-done.7.refs_2_), custom_call_target="tpu_custom_call" | custom-call | bytes 5166000 | tf_op jit(solution)/shard_map/agg_weight_grad/pallas_call | solution.py:644
  46.6 0.1 collective-permute-start.12
  46.6 1.7 %collective-permute-done.11 = bf16[608,128]{1,0:T(8,128)(2,1)S(1)} collective-permute-done((bf16[608,128]{1,0:T(8,128)(2,1)S(1)}, bf16[608,128]{1,0:T(8,128)(2,1)S(1)}, u32[]{:S(2)}, u32[]{:S(2)}) %collective-permute-start.11) | collective-permute-done | bytes 155680 | tf_op jit(solution)/shard_map/ppermute | solution.py:58
  48.3 0.1 collective-permute-start.13
  48.4 0.0 collective-permute-done.12
  48.4 1.0 %convert_add_fusion = f32[9,192,96]{2,1,0:T(8,128)} fusion(f32[9,192,96]{2,1,0:T(8,128)S(1)} %get-tuple-element.68, bf16[9,192,96]{2,1,0:T(8,128)(2,1)S(1)} %collective-permute-done.12), kind=kLoop, calls=%fused_computation | loop fusion | flops 331776 | bytes 1658880 | tf_op jit(solution)/shard_map/add | solution.py:666
  49.4 0.4 collective-permute-done.13.peer_ref
  49.8 0.9 %unpack.1 = (f32[49,96]{1,0:T(8,128)}, f32[96,384]{1,0:T(8,128)}, f32[96,384]{1,0:T(8,128)}, f32[192,384]{1,0:T(8,128)}) custom-call(s32[1]{0:T(128)} %bitcast.chan_ref.refs_0_, bf16[608,128]{1,0:T(8,128)(2,1)S(1)} %add_convert_fusion.own_ref, bf16[608,128]{1,0:T(8,128)(2,1)S(1)} %collective-permute-done.13.peer_ref), custom_call_target="tpu_custom_call" | custom-call | bytes 5535000 | tf_op jit(solution)/shard_map/unpack/pallas_call | solution.py:673
  (20 shorter events, 0.3 us)
Async XLA Ops:
  0.6 15.0 %copy-start = (f32[1,16,96,128]{3,2,1,0:T(8,128)S(1)}, f32[1,16,96,128]{3,2,1,0:T(8,128)}, u32[]{:S(2)}) copy-start(f32[1,16,96,128]{3,2,1,0:T(8,128)} %cot_ref.1) | copy-start | bytes 2359300
  2.5 7.0 %copy-start.9 = (bf16[96,128]{1,0:T(8,128)(2,1)S(1)}, bf16[96,128]{1,0:T(8,128)(2,1)}, u32[]{:S(2)}) copy-start(bf16[96,128]{1,0:T(8,128)(2,1)} %get-tuple-element.43) | copy-start | bytes 73732
  2.5 13.1 %all-to-all-start = ((bf16[8,56,128]{2,1,0:T(8,128)(2,1)}), bf16[8,56,128]{2,1,0:T(8,128)(2,1)S(1)}, u32[]{:S(2)}, u32[]{:S(2)}) async-start(bf16[8,56,128]{2,1,0:T(8,128)(2,1)} %get-tuple-element.42), calls=%async_computation | async-start | bytes 229376 | tf_op jit(solution)/shard_map/all_to_all | solution.py:466
  9.0 13.2 %collective-permute-start.2 = (bf16[9,192,96]{2,1,0:T(8,128)(2,1)}, bf16[9,192,96]{2,1,0:T(8,128)(2,1)S(1)}, u32[]{:S(2)}, u32[]{:S(2)}) collective-permute-start(bf16[9,192,96]{2,1,0:T(8,128)(2,1)} %refs_1_.1), channel_id=1, source_target_pairs={{0,1},{1,0},{2,3},{3,2},{4,5},{5,4},{6,7},{7,6},{8,9},{9,8},{10,11... | collective-permute-start | bytes 995336 | tf_op jit(solution)/shard_map/ppermute | solution.py:58
  9.5 6.1 %collective-permute-start = (bf16[96,128]{1,0:T(8,128)(2,1)S(1)}, bf16[96,128]{1,0:T(8,128)(2,1)S(1)}, u32[]{:S(2)}, u32[]{:S(2)}) collective-permute-start(bf16[96,128]{1,0:T(8,128)(2,1)S(1)} %copy-done.9), channel_id=1, source_target_pairs={{4,0},{8,4},{12,8},{5,1},{9,5},{13,9},{6,2},{10,6},{14,10},{7,3},{... | collective-permute-start | bytes 73736 | tf_op jit(solution)/shard_map/ppermute | solution.py:53
  15.6 1.4 %copy-start.2 = (bf16[384,192]{0,1:T(8,128)(2,1)S(1)}, bf16[384,192]{0,1:T(8,128)(2,1)}, u32[]{:S(2)}) copy-start(bf16[384,192]{0,1:T(8,128)(2,1)} %param.20) | copy-start | bytes 442372
  15.6 1.4 %copy-start.3 = (bf16[96,384]{1,0:T(8,128)(2,1)S(1)}, bf16[96,384]{1,0:T(8,128)(2,1)}, u32[]{:S(2)}) copy-start(bf16[96,384]{1,0:T(8,128)(2,1)} %refs_14_.1) | copy-start | bytes 221188
  15.7 1.4 %copy-start.4 = (bf16[384,96]{0,1:T(8,128)(2,1)S(1)}, bf16[384,96]{0,1:T(8,128)(2,1)}, u32[]{:S(2)}) copy-start(bf16[384,96]{0,1:T(8,128)(2,1)} %param.17) | copy-start | bytes 221188
  15.7 1.4 %copy-start.5 = (f32[49,96]{1,0:T(8,128)S(1)}, f32[49,96]{1,0:T(8,128)}, u32[]{:S(2)}) copy-start(f32[49,96]{1,0:T(8,128)} %dw_ref.1) | copy-start | bytes 56452
  15.7 1.4 %copy-start.6 = (f32[96]{0:T(128)S(1)}, f32[96]{0:T(128)}, u32[]{:S(2)}) copy-start(f32[96]{0:T(128)} %param.15) | copy-start | bytes 1156
  15.7 1.4 %copy-start.7 = (f32[96]{0:T(128)S(1)}, f32[96]{0:T(128)}, u32[]{:S(2)}) copy-start(f32[96]{0:T(128)} %param.18) | copy-start | bytes 1156
  15.7 1.4 %copy-start.8 = (f32[96]{0:T(128)S(1)}, f32[96]{0:T(128)}, u32[]{:S(2)}) copy-start(f32[96]{0:T(128)} %param.19) | copy-start | bytes 1156
  17.0 5.2 %copy-start.1 = (bf16[9,192,96]{2,1,0:T(8,128)(2,1)S(1)}, bf16[9,192,96]{2,1,0:T(8,128)(2,1)}, u32[]{:S(2)}) copy-start(bf16[9,192,96]{2,1,0:T(8,128)(2,1)} %refs_1_.1) | copy-start | bytes 995332
  17.0 2.9 %collective-permute-start.1 = (bf16[72,128]{1,0:T(8,128)(2,1)S(1)}, bf16[72,128]{1,0:T(8,128)(2,1)S(1)}, u32[]{:S(2)}, u32[]{:S(2)}) collective-permute-start(bf16[72,128]{1,0:T(8,128)(2,1)S(1)} %get-tuple-element.45), channel_id=1, source_target_pairs={{0,1},{1,0},{2,3},{3,2},{4,5},{5,4},{6,7},{7,6},{8,9},{9,8},{10,11... | collective-permute-start | bytes 55304 | tf_op jit(solution)/shard_map/ppermute | solution.py:58
  19.4 5.8 %collective-permute-start.5 = (bf16[1,192,128]{2,1,0:T(8,128)(2,1)S(1)}, bf16[1,192,128]{2,1,0:T(8,128)(2,1)S(1)}, u32[]{:S(2)}, u32[]{:S(2)}) collective-permute-start(bf16[1,192,128]{2,1,0:T(8,128)(2,1)S(1)} %get-tuple-element.56), channel_id=1, source_target_pairs={{0,1},{1,0},{2,3},{3,2},{4,5},{5,4},{6,7},{7,6},{8,9},{9,8},{10,11... | collective-permute-start | bytes 147464 | tf_op jit(solution)/shard_map/ppermute | solution.py:58
  19.9 7.3 %collective-permute-start.4 = (bf16[1,336,128]{2,1,0:T(8,128)(2,1)S(1)}, bf16[1,336,128]{2,1,0:T(8,128)(2,1)S(1)}, u32[]{:S(2)}, u32[]{:S(2)}) collective-permute-start(bf16[1,336,128]{2,1,0:T(8,128)(2,1)S(1)} %pad_maximum_fusion.2), channel_id=1, source_target_pairs={{0,8},{4,12},{8,0},{12,4},{1,9},{5,13},{9,1},{13,5},{2,10},{6,14},... | collective-permute-start | bytes 258056 | tf_op jit(solution)/shard_map/ppermute | solution.py:58
  25.1 2.1 %collective-permute-start.3 = (bf16[608,128]{1,0:T(8,128)(2,1)S(1)}, bf16[608,128]{1,0:T(8,128)(2,1)S(1)}, u32[]{:S(2)}, u32[]{:S(2)}) collective-permute-start(bf16[608,128]{1,0:T(8,128)(2,1)S(1)} %get-tuple-element.55), channel_id=1, source_target_pairs={{0,1},{1,0},{2,3},{3,2},{4,5},{5,4},{6,7},{7,6},{8,9},{9,8},{10,11... | collective-permute-start | bytes 466952 | tf_op jit(solution)/shard_map/ppermute | solution.py:58
  27.3 5.6 %collective-permute-start.8 = (bf16[608,128]{1,0:T(8,128)(2,1)S(1)}, bf16[608,128]{1,0:T(8,128)(2,1)S(1)}, u32[]{:S(2)}, u32[]{:S(2)}) collective-permute-start(bf16[608,128]{1,0:T(8,128)(2,1)S(1)} %convert_add_fusion.1), channel_id=1, source_target_pairs={{0,2},{2,0},{1,3},{3,1},{4,6},{6,4},{5,7},{7,5},{8,10},{10,8},{9,1... | collective-permute-start | bytes 466952 | tf_op jit(solution)/shard_map/ppermute | solution.py:58
  28.8 4.0 %collective-permute-start.9 = (f32[96,128]{1,0:T(8,128)S(1)}, f32[96,128]{1,0:T(8,128)S(1)}, u32[]{:S(2)}, u32[]{:S(2)}) collective-permute-start(f32[96,128]{1,0:T(8,128)S(1)} %get-tuple-element.63), channel_id=1, source_target_pairs={{0,4},{4,8},{8,12},{1,5},{5,9},{9,13},{2,6},{6,10},{10,14},{3,7},{... | collective-permute-start | bytes 147464 | tf_op jit(solution)/shard_map/ppermute | solution.py:53
  30.3 7.1 %collective-permute-start.6 = (bf16[2,336,128]{2,1,0:T(8,128)(2,1)S(1)}, bf16[2,336,128]{2,1,0:T(8,128)(2,1)S(1)}, u32[]{:S(2)}, u32[]{:S(2)}) collective-permute-start(bf16[2,336,128]{2,1,0:T(8,128)(2,1)S(1)} %pad_maximum_fusion), channel_id=1, source_target_pairs={{0,4},{4,0},{8,12},{12,8},{1,5},{5,1},{9,13},{13,9},{2,6},{6,2},{1... | collective-permute-start | bytes 516104 | tf_op jit(solution)/shard_map/ppermute | solution.py:58
  32.9 6.2 %collective-permute-start.10 = (bf16[608,128]{1,0:T(8,128)(2,1)S(1)}, bf16[608,128]{1,0:T(8,128)(2,1)S(1)}, u32[]{:S(2)}, u32[]{:S(2)}) collective-permute-start(bf16[608,128]{1,0:T(8,128)(2,1)S(1)} %add_convert_fusion.2), channel_id=1, source_target_pairs={{0,4},{4,0},{8,12},{12,8},{1,5},{5,1},{9,13},{13,9},{2,6},{6,2},{1... | collective-permute-start | bytes 466952 | tf_op jit(solution)/shard_map/ppermute | solution.py:58
  37.4 7.7 %collective-permute-start.7 = (bf16[4,336,128]{2,1,0:T(8,128)(2,1)S(1)}, bf16[4,336,128]{2,1,0:T(8,128)(2,1)S(1)}, u32[]{:S(2)}, u32[]{:S(2)}) collective-permute-start(bf16[4,336,128]{2,1,0:T(8,128)(2,1)S(1)} %constant_dynamic-update-slice_fusion.refs_1_), channel_id=1, source_target_pairs={{0,2},{2,0},{1,3},{3,1},{4,6},{6,4},{5,7},{7,5},{8,10},{10,8},{9,1... | collective-permute-start | bytes 1032200 | tf_op jit(solution)/shard_map/ppermute | solution.py:58
  39.2 9.1 %collective-permute-start.11 = (bf16[608,128]{1,0:T(8,128)(2,1)S(1)}, bf16[608,128]{1,0:T(8,128)(2,1)S(1)}, u32[]{:S(2)}, u32[]{:S(2)}) collective-permute-start(bf16[608,128]{1,0:T(8,128)(2,1)S(1)} %add_convert_fusion.1), channel_id=1, source_target_pairs={{0,8},{4,12},{8,0},{12,4},{1,9},{5,13},{9,1},{13,5},{2,10},{6,14},... | collective-permute-start | bytes 466952 | tf_op jit(solution)/shard_map/ppermute | solution.py:58
  46.6 1.9 %collective-permute-start.12 = (bf16[9,192,96]{2,1,0:T(8,128)(2,1)S(1)}, bf16[9,192,96]{2,1,0:T(8,128)(2,1)S(1)}, u32[]{:S(2)}, u32[]{:S(2)}) collective-permute-start(bf16[9,192,96]{2,1,0:T(8,128)(2,1)S(1)} %get-tuple-element.69), channel_id=1, source_target_pairs={{0,1},{1,0},{2,3},{3,2},{4,5},{5,4},{6,7},{7,6},{8,9},{9,8},{10,11... | collective-permute-start | bytes 995336 | tf_op jit(solution)/shard_map/ppermute | solution.py:58
  48.3 1.4 %collective-permute-start.13 = (bf16[608,128]{1,0:T(8,128)(2,1)S(1)}, bf16[608,128]{1,0:T(8,128)(2,1)S(1)}, u32[]{:S(2)}, u32[]{:S(2)}) collective-permute-start(bf16[608,128]{1,0:T(8,128)(2,1)S(1)} %add_convert_fusion.own_ref), channel_id=1, source_target_pairs={{0,1},{1,0},{2,3},{3,2},{4,5},{5,4},{6,7},{7,6},{8,9},{9,8},{10,11... | collective-permute-start | bytes 466952 | tf_op jit(solution)/shard_map/ppermute | solution.py:58

commit v9 on v8

--- a/solution.py
+++ b/solution.py
@@ -62,59 +62,80 @@
     return (1, 2) if tap == 0 else (0, 1)
 
 
-def pack_kernel(cells_ref, pixels_ref, row_ref, out_ref, below_ref, wide_ref, note_ref):
-    slots = pixels_ref.shape[0]
-    rows = out_ref.shape[0]
-    pixch = pixels_ref.shape[1]
+def pack_kernel(slide_ref, chan_ref, cells_ref, pixels_ref, row_ref, *refs):
+    out_refs, below_ref, packed_ref, wide_ref, note_ref = refs[:-4], *refs[-4:]
+    slots, pixch = pixels_ref.shape
+    rows = packed_ref.shape[0]
+    slide, chan = slide_ref[0], chan_ref[0]
     cells = [cells_ref[0, t] for t in range(slots)]
     live = [cell >= 0 for cell in cells]
     bands = [cell // BAND_CELLS for cell in cells]
-    places = []
-    for t in range(slots):
-        rank = jnp.int32(0)
-        for s in range(t):
-            rank = rank + ((bands[s] == bands[t]) & live[s]).astype(jnp.int32)
-        places.append(jnp.where(live[t], bands[t] * CAP + rank, -1))
     below_ref[...] = row_ref[...].astype(BF16)
     pixels = pixels_ref[...].astype(F32)
     for n in range(pixch // 128):
         wide_ref[:, n, :] = pixels[:, 128 * n : 128 * n + 128]
     wide_ref[:, pixch // 128 :, :] = jnp.zeros_like(wide_ref[:, pixch // 128 :, :])
-    out_ref[...] = jnp.zeros_like(out_ref)
+    packed_ref[...] = jnp.zeros_like(packed_ref)
+    lane = lax.broadcasted_iota(jnp.int32, (rows, 128), 1)
+    base = ((lax.broadcasted_iota(jnp.int32, (rows, 128), 0) // CAP) ^ slide) * CAP
+    notes = jnp.zeros((rows, 128), F32)
     for t in range(slots):
+        order = jnp.int32(0)
+        for s in range(t):
+            order = order + ((bands[s] == bands[t]) & live[s]).astype(jnp.int32)
+        band = jnp.maximum(bands[t], 0)
+        place = (band ^ slide) * CAP + (order ^ chan)
+        known = jnp.where(live[t], bands[t] * CAP + order, -1)
 
         @pl.when(live[t])
         def _():
-            out_ref[jnp.maximum(places[t], 0)] = wide_ref[t].astype(BF16)
-
-    lane = lax.broadcasted_iota(jnp.int32, (rows, 128), 1)
-    base = (lax.broadcasted_iota(jnp.int32, (rows, 128), 0) // CAP) * CAP
-    notes = jnp.zeros((rows, 128), F32)
-    for t in range(slots):
+            packed_ref[place] = wide_ref[t].astype(BF16)
+
         within = cells[t] % BAND_CELLS
         own_row = (within // GW).astype(F32)
         own_col = (within % GW).astype(F32)
         for rank in range(CAP):
-            hit = base + rank == places[t]
+            hit = base + rank == known
             for at, value in enumerate((own_row, own_col, jnp.float32(1.0))):
                 notes = jnp.where(hit & (lane == 3 * rank + at), value, notes)
     note_ref[...] = jnp.zeros_like(note_ref)
     note_ref[:, 0, :] = notes
-    out_ref[:, pixch // 128 :, :] = note_ref[...].astype(BF16)
-
-
-def patch_kernel(chan_ref, meta_ref, cot_ref, below_ref, key_ref, own_ref, send_ref, meta_f32):
-    sources = meta_ref.shape[0]
+    packed_ref[:, pixch // 128 :, :] = note_ref[...].astype(BF16)
+    count = rows // len(out_refs)
+    for n, out_ref in enumerate(out_refs):
+        out_ref[...] = packed_ref[count * n : count * n + count]
+
+
+def stack_kernel(*refs):
+    for n, part_ref in enumerate(refs[:-1]):
+        refs[-1][n] = part_ref[0]
+
+
+def gathered(target_ref, refs, other=False):
+    if len(refs) == 1:
+        target_ref[...] = refs[0][...].astype(F32)
+        return
+    half = len(refs) - 1
+    first, second = (half, 0) if other else (0, half)
+    for n in range(half):
+        target_ref[first + n] = refs[n][0].astype(F32)
+    target_ref[second : second + half] = refs[half][...].astype(F32)
+
+
+def patch_kernel(chan_ref, cot_ref, bottom_ref, *refs):
+    meta_refs, (key_ref, own_ref, send_ref, meta_f32, other_f32) = refs[:-5], refs[-5:]
+    sources = meta_f32.shape[0]
     chunks = sources // 8
     out_rows, e_half, _ = cot_ref.shape
-    meta_f32[...] = meta_ref[...].astype(F32)
-    meta = meta_f32[:, 0, :]
+    gathered(meta_f32, meta_refs)
+    gathered(other_f32, meta_refs, other=True)
+    metas = {True: meta_f32[:, 0, :], False: other_f32[:, 0, :]}
     first = chan_ref[0] == 0
     lane = lax.broadcasted_iota(jnp.int32, (8, 128), 1).astype(F32)
     blocks = []
     for mine in (True, False):
         for chunk in range(chunks):
-            part = meta[chunk * 8 : chunk * 8 + 8]
+            part = metas[mine][chunk * 8 : chunk * 8 + 8]
             low = [jnp.broadcast_to(part[:, n : n + 1], (8, 128)) for n in range(3)]
             high = [jnp.broadcast_to(part[:, n : n + 1], (8, 128)) for n in range(3, 6)]
             row, col, valid = (
@@ -135,7 +156,7 @@
         0, out_rows, step, jnp.zeros((key.shape[0], e_half), F32), unroll=4
     )
     pick = (key == float(out_rows)).astype(F32).astype(BF16)
-    total = total + nt(pick, below_ref[...])
+    total = total + nt(pick, bottom_ref[...])
     half = total.shape[0] // 2
     own_ref[...] = jnp.zeros_like(own_ref)
     send_ref[...] = jnp.zeros_like(send_ref)
@@ -149,8 +170,8 @@
     return center * rstd, rstd
 
 
-def fill_padded(padded_ref, got_ref, wide_ref, pixels_ref, channels):
-    wide_ref[...] = got_ref[...].astype(F32)
+def fill_padded(padded_ref, got_refs, wide_ref, pixels_ref, channels):
+    gathered(wide_ref, got_refs)
     for n in range(pixels_ref.shape[1] // 128):
         pixels_ref[:, 128 * n : 128 * n + 128] = wide_ref[:, n, :]
     padded_ref[...] = jnp.zeros_like(padded_ref)
@@ -161,12 +182,16 @@
 
 
 def stem_kernel(
-    got_ref, dw_ref, gain_ref, up_ref, proj_ref, scale_ref, ds_gain_ref, ds_ref,
+    *refs, parts
+):
+    got_refs = refs[:parts]
+    (
+    dw_ref, gain_ref, up_ref, proj_ref, scale_ref, ds_gain_ref, ds_ref,
     feat_ref, hat1_ref, rstd1_ref, hat2_ref, rstd2_ref, hidden_ref, slope_ref, patch_ref,
     padded_ref, spatial_ref, low_ref, patch_f32, wide_ref, pixels_ref,
-):
+    ) = refs[parts:]
     channels = dw_ref.shape[1]
-    fill_padded(padded_ref, got_ref, wide_ref, pixels_ref, channels)
+    fill_padded(padded_ref, got_refs, wide_ref, pixels_ref, channels)
 
     for i in range(SIDE):
         total = jnp.zeros((SIDE, 8, channels), F32)
@@ -212,15 +237,16 @@
     )
 
 
-def back_kernel(
-    chan_ref, own_ref, peer_ref, w_own_ref, w_peer_ref, got_ref,
+def back_kernel(*refs, parts, scale):
+    got_refs = refs[:parts]
+    (
+    chan_ref, own_ref, peer_ref, w_own_ref, w_peer_ref,
     hat1_ref, rstd1_ref, hat2_ref, rstd2_ref, hidden_ref, slope_ref, patch_ref,
     gain_ref, up_ref, proj_ref, scale_ref, ds_gain_ref, ds_ref,
     keep_ref, send_ref,
     padded_ref, dlow_ref, dspatial_ref, dw_ref, ds_acc, up_acc, proj_acc, pack_ref,
     wide_ref, pixels_ref, w_ref,
-    *, scale,
-):
+    ) = refs[parts:]
     channels = gain_ref.shape[1]
     half = SIDE // 2
     step = pl.program_id(0)
@@ -273,7 +299,7 @@
     mean_b = jnp.mean(dhat1 * hat1, axis=-1, keepdims=True)
     dspatial = rstd1_ref[...] * (dhat1 - mean_a - hat1 * mean_b)
     dspatial_ref[...] = dspatial.reshape(SIDE, SIDE, 8, channels)
-    fill_padded(padded_ref, got_ref, wide_ref, pixels_ref, channels)
+    fill_padded(padded_ref, got_refs, wide_ref, pixels_ref, channels)
 
     for a in range(7):
         totals = [jnp.zeros((8, channels), F32) for _ in range(7)]
@@ -440,30 +466,57 @@
     proj_turned = proj_weight.T
     ds_turned = ds_weight.T
 
-    packed, top_cot = pl.pallas_call(
+    paired = 1 < bands <= 4
+    pieces = bands if paired else 1
+    spot = (jnp.zeros((1,), jnp.int32),) * 2
+    if paired:
+        spot = (lax.axis_index("slide").astype(jnp.int32)[None], chan)
+    *packed, top_cot = pl.pallas_call(
         pack_kernel,
         grid=(1,),
         out_shape=(
-            jax.ShapeDtypeStruct((sources, WIRE_ROWS, 128), BF16),
+            *[jax.ShapeDtypeStruct((sources // pieces, WIRE_ROWS, 128), BF16)] * pieces,
             jax.ShapeDtypeStruct((e_half, cols), BF16),
         ),
         in_specs=[
+            SMEM,
+            SMEM,
             SMEM,
             pl.BlockSpec((None,) + tile_pixels.shape[1:], lambda i: (0, 0, 0)),
             pl.BlockSpec((None, None, e_half, cols), lambda i: (0, 0, 0, 0)),
         ],
-        out_specs=(whole((sources, WIRE_ROWS, 128)), whole((e_half, cols))),
+        out_specs=(*[whole((sources // pieces, WIRE_ROWS, 128))] * pieces, whole((e_half, cols))),
         scratch_shapes=[
+            pltpu.VMEM((sources, WIRE_ROWS, 128), BF16),
             pltpu.VMEM((tile_pixels.shape[1], WIRE_ROWS, 128), F32),
             pltpu.VMEM((sources, 8, 128), F32),
         ],
         cost_estimate=takes(1.5),
         name="pack",
-    )(tile_cell, tile_pixels, agg_cot)
+    )(*spot, tile_cell, tile_pixels, agg_cot)
     below_cot = shifted(top_cot, "slide", -1)
-    packed, own_weight = lax.optimization_barrier((packed, agg_weight))
+    packed[0], own_weight = lax.optimization_barrier((packed[0], agg_weight))
     peer_weight = swapped(own_weight, "chan", 1)
-    got = lax.all_to_all(packed, ("slide", "chan"), split_axis=0, concat_axis=0, tiled=True)
+    if paired:
+        got = [packed[0]] + [None] * (bands - 1)
+        for step in reversed(range(1, bands)):
+            got[step] = swapped(packed[step], "slide", step)
+        got[1], below_cot = lax.optimization_barrier((got[1], below_cot))
+        others = pl.pallas_call(
+            stack_kernel,
+            grid=(1,),
+            out_shape=jax.ShapeDtypeStruct((bands, WIRE_ROWS, 128), BF16),
+            in_specs=[pl.BlockSpec((1, WIRE_ROWS, 128), lambda i: (1, 0, 0))] * bands,
+            out_specs=whole((bands, WIRE_ROWS, 128)),
+            compiler_params=params_of(),
+            cost_estimate=takes(0.5),
+            name="stack",
+        )(*got)
+        got.append(swapped(others, "chan", 1))
+    else:
+        got = [
+            lax.all_to_all(packed[0], ("slide", "chan"), split_axis=0, concat_axis=0, tiled=True)
+        ]
 
     key, cots_own, cots_send = pl.pallas_call(
         patch_kernel,
@@ -474,9 +527,12 @@
         ),
         in_specs=[
             SMEM,
-            pl.BlockSpec((sources, 8, 128), lambda i: (0, pixch // 1024, 0)),
             pl.BlockSpec((None, out_rows, e_half, cols), lambda i: (0, 0, 0, 0)),
             whole((e_half, cols)),
+            *[
+                pl.BlockSpec((part.shape[0], 8, 128), lambda i: (0, pixch // 1024, 0))
+                for part in got
+            ],
         ],
         out_specs=(
             whole((blocks * COT_ROWS, cols)),
@@ -484,24 +540,26 @@
             whole((chunks * COT_ROWS, 128)),
         ),
         grid=(1,),
-        scratch_shapes=[pltpu.VMEM((sources, 8, 128), F32)],
+        scratch_shapes=[pltpu.VMEM((sources, 8, 128), F32)] * 2,
         compiler_params=params_of(),
         cost_estimate=takes(1.2),
         name="patch",
-    )(chan, got, agg_cot, below_cot)
+    )(chan, agg_cot, below_cot, *got)
     cots_peer = swapped(cots_send, "chan", 1)
     cots_own = cots_own.reshape(chunks, COT_ROWS, 128)
     cots_peer = cots_peer.reshape(chunks, COT_ROWS, 128)
 
     rows = PIX * 8
-    pixel_spec = pl.BlockSpec((8, WIRE_ROWS, 128), lambda g: (g, 0, 0))
+    pixel_specs = [pl.BlockSpec((8, WIRE_ROWS, 128), lambda g: (g, 0, 0))]
+    if paired:
+        pixel_specs = [whole(part.shape) for part in got]
     pixel_scratch = [pltpu.VMEM((8, WIRE_ROWS, 128), F32), pltpu.VMEM((8, pixch), F32)]
 
     def chunk(*shape):
         return pl.BlockSpec((None,) + shape, lambda g: (g,) + (0,) * len(shape))
 
     feats, hat1, rstd1, hat2, rstd2, hidden, slope, patches = pl.pallas_call(
-        stem_kernel,
+        lambda *refs: stem_kernel(*refs, parts=len(got)),
         grid=(chunks,),
         out_shape=(
             jax.ShapeDtypeStruct((chunks, FEAT_ROWS, 128), BF16),
@@ -514,7 +572,7 @@
             jax.ShapeDtypeStruct((chunks, 128, 4 * channels), BF16),
         ),
         in_specs=[
-            pixel_spec,
+            *pixel_specs,
             whole(dw_weight.shape), whole((1, channels)), whole(up_weight.shape),
             whole(proj_turned.shape), whole((1, channels)), whole((1, channels)),
             whole(ds_turned.shape),
@@ -533,7 +591,7 @@
         compiler_params=params_of(),
         cost_estimate=takes(2.7),
         name="stem",
-    )(got, dw_weight, gain, up_weight, proj_turned, scale, low_gain, ds_turned)
+    )(*got, dw_weight, gain, up_weight, proj_turned, scale, low_gain, ds_turned)
 
     feats_band = jnp.concatenate([feats, swapped(feats, "chan", 1)], axis=0)
     spread, below = pl.pallas_call(
@@ -569,15 +627,16 @@
         near = jnp.concatenate([near, far], axis=0)
 
     keep, send = pl.pallas_call(
-        lambda *refs: back_kernel(*refs, scale=loss_scale),
+        lambda *refs: back_kernel(*refs, parts=len(got), scale=loss_scale),
         grid=(chunks,),
         out_shape=(
             jax.ShapeDtypeStruct((HALF_ROWS, 128), F32),
             jax.ShapeDtypeStruct((HALF_ROWS, 128), BF16),
         ),
         in_specs=[
+            *pixel_specs,
             SMEM, chunk(COT_ROWS, 128), chunk(COT_ROWS, 128),
-            whole(agg_weight.shape), whole(agg_weight.shape), pixel_spec,
+            whole(agg_weight.shape), whole(agg_weight.shape),
             chunk(rows, channels), chunk(rows, 1), chunk(rows, channels), chunk(rows, 1),
             chunk(rows, hid), chunk(rows, hid), chunk(128, 4 * channels),
             whole((1, channels)), whole(up_weight.shape), whole(proj_turned.shape),
@@ -600,7 +659,7 @@
         cost_estimate=takes(3.7),
         name="stem_back",
     )(
-        chan, cots_own, cots_peer, agg_weight, peer_weight, got,
+        *got, chan, cots_own, cots_peer, agg_weight, peer_weight,
         hat1, rstd1, hat2, rstd2, hidden, slope, patches,
         gain, up_weight, proj_turned, scale, low_gain, ds_turned,
     )

time: 51 us -> 52.3 us (1.025)
  waiting for transfers between devices: 13 us -> 17.4 us
  starting transfers between devices: 20.3 us -> 16.5 us
  local copies, waits for them, and re-layouts: 0.09 us -> 0.83 us
    all_to_all x1 -> x0, starting transfers between devices: 6.46 us -> none  [on_device(): lax.all_to_all(packed, ('slide', 'chan'), split_axis=0, concat_axis=0, ti...]
    ppermute x12 -> x16, waiting for transfers between devices: 8.13 us -> 12.5 us  [swapped(): lax.ppermute(value, axis, [(place, place ^ step) for place in range(count)])]
    ppermute x12 -> x16, starting transfers between devices: 11.1 us -> 13.9 us  [swapped(): lax.ppermute(value, axis, [(place, place ^ step) for place in range(count)])]
    unnamed x21 -> x23, local copies, waits for them, and re-layouts: 0.07 us -> 0.81 us
    pallas_call x3 -> x4, Pallas kernels: 7.09 us -> 7.14 us  [the longest x1 2.89 us: on_device(): pl.pallas_call(lambda *refs: back_kernel(*refs, parts=len(got), scale=los...]
  transfers between devices with their start and end apart: 15 -> 18, of which waited for: 7 -> 9; matrix products, arithmetic and copies ran while one was open for 2% -> 2% of each run, Pallas kernels for 24% -> 24%
where the time goes in v9:
time: 52.3 us; the launch traced here: 52 us
  waiting for transfers between devices  17.4 us (33%)
  starting transfers between devices  16.5 us (32%)
  Pallas kernels  15.2 us (29%)
  other arithmetic  1.21 us (2%)
  between operations  0.9 us (2%)
  local copies, waits for them, and re-layouts  0.83 us (2%)
    ppermute x16, starting transfers between devices, swapped(): lax.ppermute(value, axis, [(place, place ^ step) for place in range(count)])  13.9 us
    ppermute x16, waiting for transfers between devices, swapped(): lax.ppermute(value, axis, [(place, place ^ step) for place in range(count)])  12.5 us
    ppermute x2, waiting for transfers between devices, shifted(): lax.ppermute(value, axis, [(source, source + steps) for source in range(f...  4.85 us
    pallas_call x1, Pallas kernels, on_device(): agg_map = map_call(spread, key, above)  3.5 us
    pallas_call x1, Pallas kernels, on_device(): pl.pallas_call(lambda *refs: back_kernel(*refs, parts=len(got), scale=los...  2.89 us
    ppermute x2, starting transfers between devices, shifted(): lax.ppermute(value, axis, [(source, source + steps) for source in range(f...  2.56 us
    pallas_call x1, Pallas kernels, on_device(): pl.pallas_call(lambda *refs: stem_kernel(*refs, parts=len(got)), grid=(ch...  2.3 us
    pallas_call x1, Pallas kernels, on_device(): pl.pallas_call(pack_kernel, grid=(1,), out_shape=(*[jax.ShapeDtypeStruct(...  1.93 us
  transfers between devices with their start and end apart: 18, of which 9 were waited for; matrix products, arithmetic and copies ran while one was open for 2% of the time, Pallas kernels for 24%

profile of v9, /device:TPU:0, one launch (start us, length us, event | category | flops | bytes accessed | tf_op | source)
XLA Modules:
  0.0 52.0 jit_solution(14533770102450143762)
XLA Ops:
  0.6 1.9 %pack.1 = (bf16[2,56,128]{2,1,0:T(8,128)(2,1)}, bf16[2,56,128]{2,1,0:T(8,128)(2,1)}, bf16[2,56,128]{2,1,0:T(8,128)(2,1)}, bf16[2,56,128]{2,1,0:T(8,128)(2,1)}, bf16[96,128]{1,0:T(8,128)(2,1)}) custom-call(s32[1]{0:T(128)} %bitcast.slide_ref, s32[1]{0:T(128)} %bitcast.1.chan_ref.refs_5_, s32[1,8]{1,0:T(1,128)} %cells_ref.1, bf16[1,8,6144]{2,1,0:T(8,128)(2,1)} %pixels_ref.1, ...), custom_call_target="tpu_custom_call" | custom-call | bytes 5535000 | tf_op jit(solution)/shard_map/pack/pallas_call | solution.py:474
  2.6 0.5 collective-permute-start.6
  3.0 2.6 %collective-permute-start = (bf16[2,56,128]{2,1,0:T(8,128)(2,1)}, bf16[2,56,128]{2,1,0:T(8,128)(2,1)S(1)}, u32[]{:S(2)}, u32[]{:S(2)}) collective-permute-start(bf16[2,56,128]{2,1,0:T(8,128)(2,1)} %get-tuple-element.48), channel_id=1, source_target_pairs={{0,4},{4,0},{8,12},{12,8},{1,5},{5,1},{9,13},{13,9},{2,6},{6,2},{1... | collective-permute-start | bytes 86024 | tf_op jit(solution)/shard_map/ppermute | solution.py:58
  5.6 2.6 %collective-permute-start.2 = (bf16[2,56,128]{2,1,0:T(8,128)(2,1)}, bf16[2,56,128]{2,1,0:T(8,128)(2,1)S(1)}, u32[]{:S(2)}, u32[]{:S(2)}) collective-permute-start(bf16[2,56,128]{2,1,0:T(8,128)(2,1)} %get-tuple-element.51), channel_id=1, source_target_pairs={{0,8},{4,12},{8,0},{12,4},{1,9},{5,13},{9,1},{13,5},{2,10},{6,14},... | collective-permute-start | bytes 86024 | tf_op jit(solution)/shard_map/ppermute | solution.py:58
  8.2 0.0 collective-permute-start.3
  8.2 1.3 %collective-permute-start.1 = (bf16[96,128]{1,0:T(8,128)(2,1)}, bf16[96,128]{1,0:T(8,128)(2,1)S(1)}, u32[]{:S(2)}, u32[]{:S(2)}) collective-permute-start(bf16[96,128]{1,0:T(8,128)(2,1)} %get-tuple-element.49), channel_id=1, source_target_pairs={{4,0},{8,4},{12,8},{5,1},{9,5},{13,9},{6,2},{10,6},{14,10},{7,3},{... | collective-permute-start | bytes 73736 | tf_op jit(solution)/shard_map/ppermute | solution.py:53
  9.5 4.9 %collective-permute-done.1.bottom_ref = bf16[96,128]{1,0:T(8,128)(2,1)S(1)} collective-permute-done((bf16[96,128]{1,0:T(8,128)(2,1)}, bf16[96,128]{1,0:T(8,128)(2,1)S(1)}, u32[]{:S(2)}, u32[]{:S(2)}) %collective-permute-start.1) | collective-permute-done | bytes 24608 | tf_op jit(solution)/shard_map/ppermute | solution.py:53
  14.4 0.0 collective-permute-done.refs_1_
  14.4 0.0 collective-permute-done.2.refs_2_
  14.4 0.0 collective-permute-done.3.refs_3_
  14.4 0.0 copy-start.3
  14.4 0.7 %copy-done.3 = bf16[2,56,128]{2,1,0:T(8,128)(2,1)S(1)} copy-done((bf16[2,56,128]{2,1,0:T(8,128)(2,1)S(1)}, bf16[2,56,128]{2,1,0:T(8,128)(2,1)}, u32[]{:S(2)}) %copy-start.3) | copy-done | bytes 28696
  15.2 0.0 copy-start.5
  15.2 0.0 copy-start.6
  15.2 0.1 collective-permute-start.4
  15.3 1.2 %collective-permute-done.4.refs_4_ = bf16[4,56,128]{2,1,0:T(8,128)(2,1)S(1)} collective-permute-done((bf16[4,56,128]{2,1,0:T(8,128)(2,1)S(1)}, bf16[4,56,128]{2,1,0:T(8,128)(2,1)S(1)}, u32[]{:S(2)}, u32[]{:S(2)}) %collective-permute-start.4) | collective-permute-done | bytes 57376 | tf_op jit(solution)/shard_map/ppermute | solution.py:58
  16.5 0.0 copy-start.9
  16.5 0.0 copy-start.10
  16.5 1.3 %patch.1 = (f32[144,128]{1,0:T(8,128)S(1)}, bf16[72,128]{1,0:T(8,128)(2,1)S(1)}, bf16[72,128]{1,0:T(8,128)(2,1)S(1)}) custom-call(s32[1]{0:T(128)} %bitcast.1.chan_ref.refs_5_, f32[1,16,96,128]{3,2,1,0:T(8,128)S(1)} %copy-done, bf16[96,128]{1,0:T(8,128)(2,1)S(1)} %collective-permute-done.1.bottom_ref, bf16[2,56,128]{2,1,0:T(8,128)(2,1)S(1)} %copy-done.4, ...), custom_call_target="tpu_custom_call" | custom-call | bytes 4428000 | tf_op jit(solution)/shard_map/patch/pallas_call | solution.py:521
  17.8 0.0 copy-start.1
  17.8 0.2 collective-permute-start.5
  18.1 2.3 %stem.1 = (bf16[1,192,128]{2,1,0:T(8,128)(2,1)S(1)}, f32[1,512,96]{2,1,0:T(8,128)S(1)}, f32[1,512,1]{2,1,0:T(8,128)S(1)}, f32[1,512,96]{2,1,0:T(8,128)S(1)}, f32...) custom-call(bf16[2,56,128]{2,1,0:T(8,128)(2,1)S(1)} %copy-done.4, ...), custom_call_target="tpu_custom_call" | custom-call | bytes 9963000 | tf_op jit(solution)/shard_map/stem/pallas_call | solution.py:561
  20.4 0.4 collective-permute-start.9
  20.8 1.8 %collective-permute-start.8 = (bf16[1,336,128]{2,1,0:T(8,128)(2,1)S(1)}, bf16[1,336,128]{2,1,0:T(8,128)(2,1)S(1)}, u32[]{:S(2)}, u32[]{:S(2)}) collective-permute-start(bf16[1,336,128]{2,1,0:T(8,128)(2,1)S(1)} %pad_maximum_fusion.2), channel_id=1, source_target_pairs={{0,8},{4,12},{8,0},{12,4},{1,9},{5,13},{9,1},{13,5},{2,10},{6,14},... | collective-permute-start | bytes 258056 | tf_op jit(solution)/shard_map/ppermute | solution.py:58
  22.6 2.9 %stem_back.1 = (f32[608,128]{1,0:T(8,128)S(1)}, bf16[608,128]{1,0:T(8,128)(2,1)S(1)}) custom-call(bf16[2,56,128]{2,1,0:T(8,128)(2,1)S(1)} %copy-done.4, bf16[2,56,128]{2,1,0:T(8,128)(2,1)S(1)} %collective-permute-done.refs_1_, bf16[2,56,128]{2,1,0:T(8,128)(2,1)S(1)} %collective-permute-done.2.refs_2_, ...), custom_call_target="tpu_custom_call" | custom-call | bytes 13653000 | tf_op jit(solution)/shard_map/stem_back/pallas_call | solution.py:629
  25.5 0.1 collective-permute-start.7
  25.5 0.0 collective-permute-done.9
  25.6 1.0 %spread.1 = (f32[144,96]{1,0:T(8,128)S(1)}, f32[96,128]{1,0:T(8,128)S(1)}) custom-call(bf16[2,192,128]{2,1,0:T(8,128)(2,1)S(1)} %pad_maximum_fusion.1.refs_0_, bf16[9,192,96]{2,1,0:T(8,128)(2,1)S(1)} %copy-done.1, f32[144,128]{1,0:T(8,128)S(1)} %get-tuple-element.67.refs_2_.key_ref), custom_call_target="tpu_custom_call" | custom-call | bytes 3690000 | tf_op jit(solution)/shard_map/spread/pallas_call | solution.py:597
  26.6 1.6 %collective-permute-done.8 = bf16[1,336,128]{2,1,0:T(8,128)(2,1)S(1)} collective-permute-done((bf16[1,336,128]{2,1,0:T(8,128)(2,1)S(1)}, bf16[1,336,128]{2,1,0:T(8,128)(2,1)S(1)}, u32[]{:S(2)}, u32[]{:S(2)}) %collective-permute-start.8) | collective-permute-done | bytes 86048 | tf_op jit(solution)/shard_map/ppermute | solution.py:58
  28.2 0.0 collective-permute-done.7
  28.3 1.6 %collective-permute-start.12 = (bf16[608,128]{1,0:T(8,128)(2,1)S(1)}, bf16[608,128]{1,0:T(8,128)(2,1)S(1)}, u32[]{:S(2)}, u32[]{:S(2)}) collective-permute-start(bf16[608,128]{1,0:T(8,128)(2,1)S(1)} %convert_add_fusion.1), channel_id=1, source_target_pairs={{0,2},{2,0},{1,3},{3,1},{4,6},{6,4},{5,7},{7,5},{8,10},{10,8},{9,1... | collective-permute-start | bytes 466952 | tf_op jit(solution)/shard_map/ppermute | solution.py:58
  29.9 1.3 %collective-permute-start.13 = (f32[96,128]{1,0:T(8,128)S(1)}, f32[96,128]{1,0:T(8,128)S(1)}, u32[]{:S(2)}, u32[]{:S(2)}) collective-permute-start(f32[96,128]{1,0:T(8,128)S(1)} %get-tuple-element.73), channel_id=1, source_target_pairs={{0,4},{4,8},{8,12},{1,5},{5,9},{9,13},{2,6},{6,10},{10,14},{3,7},{... | collective-permute-start | bytes 147464 | tf_op jit(solution)/shard_map/ppermute | solution.py:53
  31.2 1.2 %collective-permute-start.10 = (bf16[2,336,128]{2,1,0:T(8,128)(2,1)S(1)}, bf16[2,336,128]{2,1,0:T(8,128)(2,1)S(1)}, u32[]{:S(2)}, u32[]{:S(2)}) collective-permute-start(bf16[2,336,128]{2,1,0:T(8,128)(2,1)S(1)} %pad_maximum_fusion), channel_id=1, source_target_pairs={{0,4},{4,0},{8,12},{12,8},{1,5},{5,1},{9,13},{13,9},{2,6},{6,2},{1... | collective-permute-start | bytes 516104 | tf_op jit(solution)/shard_map/ppermute | solution.py:58
  32.3 1.8 %collective-permute-done.12 = bf16[608,128]{1,0:T(8,128)(2,1)S(1)} collective-permute-done((bf16[608,128]{1,0:T(8,128)(2,1)S(1)}, bf16[608,128]{1,0:T(8,128)(2,1)S(1)}, u32[]{:S(2)}, u32[]{:S(2)}) %collective-permute-start.12) | collective-permute-done | bytes 155680 | tf_op jit(solution)/shard_map/ppermute | solution.py:58
  34.2 1.5 %collective-permute-start.14 = (bf16[608,128]{1,0:T(8,128)(2,1)S(1)}, bf16[608,128]{1,0:T(8,128)(2,1)S(1)}, u32[]{:S(2)}, u32[]{:S(2)}) collective-permute-start(bf16[608,128]{1,0:T(8,128)(2,1)S(1)} %add_convert_fusion.2), channel_id=1, source_target_pairs={{0,4},{4,0},{8,12},{12,8},{1,5},{5,1},{9,13},{13,9},{2,6},{6,2},{1... | collective-permute-start | bytes 466952 | tf_op jit(solution)/shard_map/ppermute | solution.py:58
  35.8 2.7 %collective-permute-done.10 = bf16[2,336,128]{2,1,0:T(8,128)(2,1)S(1)} collective-permute-done((bf16[2,336,128]{2,1,0:T(8,128)(2,1)S(1)}, bf16[2,336,128]{2,1,0:T(8,128)(2,1)S(1)}, u32[]{:S(2)}, u32[]{:S(2)}) %collective-permute-start.10) | collective-permute-done | bytes 172064 | tf_op jit(solution)/shard_map/ppermute | solution.py:58
  38.4 0.1 collective-permute-start.11
  38.5 2.0 %collective-permute-done.14 = bf16[608,128]{1,0:T(8,128)(2,1)S(1)} collective-permute-done((bf16[608,128]{1,0:T(8,128)(2,1)S(1)}, bf16[608,128]{1,0:T(8,128)(2,1)S(1)}, u32[]{:S(2)}, u32[]{:S(2)}) %collective-permute-start.14) | collective-permute-done | bytes 155680 | tf_op jit(solution)/shard_map/ppermute | solution.py:58
  40.6 1.2 %collective-permute-start.15 = (bf16[608,128]{1,0:T(8,128)(2,1)S(1)}, bf16[608,128]{1,0:T(8,128)(2,1)S(1)}, u32[]{:S(2)}, u32[]{:S(2)}) collective-permute-start(bf16[608,128]{1,0:T(8,128)(2,1)S(1)} %add_convert_fusion.1), channel_id=1, source_target_pairs={{0,8},{4,12},{8,0},{12,4},{1,9},{5,13},{9,1},{13,5},{2,10},{6,14},... | collective-permute-start | bytes 466952 | tf_op jit(solution)/shard_map/ppermute | solution.py:58
  41.8 3.5 %agg_map.1 = bf16[16,96,128]{2,1,0:T(8,128)(2,1)} custom-call(f32[144,96]{1,0:T(8,128)S(1)} %get-tuple-element.71.y_ref, f32[144,128]{1,0:T(8,128)S(1)} %get-tuple-element.67.refs_2_.key_ref, f32[96,128]{1,0:T(8,128)S(1)} %collective-permute-done.13.above_ref), custom_call_target="tpu_custom_call" | custom-call | bytes 12915000 | tf_op jit(solution)/shard_map/agg_map/pallas_call | solution.py:691
  45.3 0.7 %collective-permute-done.11.refs_2_ = bf16[4,336,128]{2,1,0:T(8,128)(2,1)S(1)} collective-permute-done((bf16[4,336,128]{2,1,0:T(8,128)(2,1)S(1)}, bf16[4,336,128]{2,1,0:T(8,128)(2,1)S(1)}, u32[]{:S(2)}, u32[]{:S(2)}) %collective-permute-start.11) | collective-permute-done | bytes 344096 | tf_op jit(solution)/shard_map/ppermute | solution.py:58
  46.0 1.4 %agg_weight_grad.1 = (f32[9,192,96]{2,1,0:T(8,128)S(1)}, bf16[9,192,96]{2,1,0:T(8,128)(2,1)S(1)}) custom-call(s32[1]{0:T(128)} %bitcast.10.refs_0_, bf16[4,336,128]{2,1,0:T(8,128)(2,1)S(1)} %constant_dynamic-update-slice_fusion.refs_1_, bf16[4,336,128]{2,1,0:T(8,128)(2,1)S(1)} %collective-permute-done.11.refs_2_), custom_call_target="tpu_custom_call" | custom-call | bytes 5166000 | tf_op jit(solution)/shard_map/agg_weight_grad/pallas_call | solution.py:703
  47.4 0.1 collective-permute-start.16
  47.5 2.1 %collective-permute-done.15 = bf16[608,128]{1,0:T(8,128)(2,1)S(1)} collective-permute-done((bf16[608,128]{1,0:T(8,128)(2,1)S(1)}, bf16[608,128]{1,0:T(8,128)(2,1)S(1)}, u32[]{:S(2)}, u32[]{:S(2)}) %collective-permute-start.15) | collective-permute-done | bytes 155680 | tf_op jit(solution)/shard_map/ppermute | solution.py:58
  49.7 0.1 collective-permute-start.17
  49.8 1.0 %convert_add_fusion = f32[9,192,96]{2,1,0:T(8,128)} fusion(f32[9,192,96]{2,1,0:T(8,128)S(1)} %get-tuple-element.78, bf16[9,192,96]{2,1,0:T(8,128)(2,1)S(1)} %collective-permute-done.16), kind=kLoop, calls=%fused_computation | loop fusion | flops 331776 | bytes 1658880 | tf_op jit(solution)/shard_map/add | solution.py:725
  50.8 0.3 collective-permute-done.17.peer_ref
  51.2 0.9 %unpack.1 = (f32[49,96]{1,0:T(8,128)}, f32[96,384]{1,0:T(8,128)}, f32[96,384]{1,0:T(8,128)}, f32[192,384]{1,0:T(8,128)}) custom-call(s32[1]{0:T(128)} %bitcast.1.chan_ref.refs_5_, bf16[608,128]{1,0:T(8,128)(2,1)S(1)} %add_convert_fusion.own_ref, bf16[608,128]{1,0:T(8,128)(2,1)S(1)} %collective-permute-done.17.peer_ref), custom_call_target="tpu_custom_call" | custom-call | bytes 5535000 | tf_op jit(solution)/shard_map/unpack/pallas_call | solution.py:732
  (29 shorter events, 0.3 us)
Async XLA Ops:
  0.6 15.9 %copy-start = (f32[1,16,96,128]{3,2,1,0:T(8,128)S(1)}, f32[1,16,96,128]{3,2,1,0:T(8,128)}, u32[]{:S(2)}) copy-start(f32[1,16,96,128]{3,2,1,0:T(8,128)} %cot_ref.1) | copy-start | bytes 2359300
  2.6 20.0 %collective-permute-start.6 = (bf16[9,192,96]{2,1,0:T(8,128)(2,1)}, bf16[9,192,96]{2,1,0:T(8,128)(2,1)S(1)}, u32[]{:S(2)}, u32[]{:S(2)}) collective-permute-start(bf16[9,192,96]{2,1,0:T(8,128)(2,1)} %refs_1_.1), channel_id=1, source_target_pairs={{0,1},{1,0},{2,3},{3,2},{4,5},{5,4},{6,7},{7,6},{8,9},{9,8},{10,11... | collective-permute-start | bytes 995336 | tf_op jit(solution)/shard_map/ppermute | solution.py:58
  3.0 11.3 %collective-permute-start = (bf16[2,56,128]{2,1,0:T(8,128)(2,1)}, bf16[2,56,128]{2,1,0:T(8,128)(2,1)S(1)}, u32[]{:S(2)}, u32[]{:S(2)}) collective-permute-start(bf16[2,56,128]{2,1,0:T(8,128)(2,1)} %get-tuple-element.48), channel_id=1, source_target_pairs={{0,4},{4,0},{8,12},{12,8},{1,5},{5,1},{9,13},{13,9},{2,6},{6,2},{1... | collective-permute-start | bytes 86024 | tf_op jit(solution)/shard_map/ppermute | solution.py:58
  5.6 8.7 %collective-permute-start.2 = (bf16[2,56,128]{2,1,0:T(8,128)(2,1)}, bf16[2,56,128]{2,1,0:T(8,128)(2,1)S(1)}, u32[]{:S(2)}, u32[]{:S(2)}) collective-permute-start(bf16[2,56,128]{2,1,0:T(8,128)(2,1)} %get-tuple-element.51), channel_id=1, source_target_pairs={{0,8},{4,12},{8,0},{12,4},{1,9},{5,13},{9,1},{13,5},{2,10},{6,14},... | collective-permute-start | bytes 86024 | tf_op jit(solution)/shard_map/ppermute | solution.py:58
  8.2 6.2 %collective-permute-start.3 = (bf16[2,56,128]{2,1,0:T(8,128)(2,1)}, bf16[2,56,128]{2,1,0:T(8,128)(2,1)S(1)}, u32[]{:S(2)}, u32[]{:S(2)}) collective-permute-start(bf16[2,56,128]{2,1,0:T(8,128)(2,1)} %get-tuple-element.52), channel_id=1, source_target_pairs={{0,12},{4,8},{8,4},{12,0},{1,13},{5,9},{9,5},{13,1},{2,14},{6,10},... | collective-permute-start | bytes 86024 | tf_op jit(solution)/shard_map/ppermute | solution.py:58
  8.2 6.1 %collective-permute-start.1 = (bf16[96,128]{1,0:T(8,128)(2,1)}, bf16[96,128]{1,0:T(8,128)(2,1)S(1)}, u32[]{:S(2)}, u32[]{:S(2)}) collective-permute-start(bf16[96,128]{1,0:T(8,128)(2,1)} %get-tuple-element.49), channel_id=1, source_target_pairs={{4,0},{8,4},{12,8},{5,1},{9,5},{13,9},{6,2},{10,6},{14,10},{7,3},{... | collective-permute-start | bytes 73736 | tf_op jit(solution)/shard_map/ppermute | solution.py:53
  14.4 0.8 %copy-start.3 = (bf16[2,56,128]{2,1,0:T(8,128)(2,1)S(1)}, bf16[2,56,128]{2,1,0:T(8,128)(2,1)}, u32[]{:S(2)}) copy-start(bf16[2,56,128]{2,1,0:T(8,128)(2,1)} %get-tuple-element.47.refs_0_) | copy-start | bytes 86020
  15.1 1.4 %copy-start.4 = (bf16[2,56,128]{2,1,0:T(8,128)(2,1)S(1)}, bf16[2,56,128]{2,1,0:T(8,128)(2,1)}, u32[]{:S(2)}) copy-start(bf16[2,56,128]{2,1,0:T(8,128)(2,1)} %get-tuple-element.47.refs_0_) | copy-start | bytes 86020
  15.2 2.9 %copy-start.2 = (bf16[384,192]{0,1:T(8,128)(2,1)S(1)}, bf16[384,192]{0,1:T(8,128)(2,1)}, u32[]{:S(2)}) copy-start(bf16[384,192]{0,1:T(8,128)(2,1)} %param.20) | copy-start | bytes 442372
  15.2 2.9 %copy-start.5 = (bf16[96,384]{1,0:T(8,128)(2,1)S(1)}, bf16[96,384]{1,0:T(8,128)(2,1)}, u32[]{:S(2)}) copy-start(bf16[96,384]{1,0:T(8,128)(2,1)} %refs_18_.1) | copy-start | bytes 221188
  15.2 2.9 %copy-start.6 = (bf16[384,96]{0,1:T(8,128)(2,1)S(1)}, bf16[384,96]{0,1:T(8,128)(2,1)}, u32[]{:S(2)}) copy-start(bf16[384,96]{0,1:T(8,128)(2,1)} %param.17) | copy-start | bytes 221188
  15.2 1.3 %collective-permute-start.4 = (bf16[4,56,128]{2,1,0:T(8,128)(2,1)S(1)}, bf16[4,56,128]{2,1,0:T(8,128)(2,1)S(1)}, u32[]{:S(2)}, u32[]{:S(2)}) collective-permute-start(bf16[4,56,128]{2,1,0:T(8,128)(2,1)S(1)} %stack.1), channel_id=1, source_target_pairs={{0,1},{1,0},{2,3},{3,2},{4,5},{5,4},{6,7},{7,6},{8,9},{9,8},{10,11... | collective-permute-start | bytes 172040 | tf_op jit(solution)/shard_map/ppermute | solution.py:58
  16.5 1.5 %copy-start.7 = (f32[49,96]{1,0:T(8,128)S(1)}, f32[49,96]{1,0:T(8,128)}, u32[]{:S(2)}) copy-start(f32[49,96]{1,0:T(8,128)} %refs_5_.1) | copy-start | bytes 56452
  16.5 1.5 %copy-start.8 = (f32[96]{0:T(128)S(1)}, f32[96]{0:T(128)}, u32[]{:S(2)}) copy-start(f32[96]{0:T(128)} %param.15) | copy-start | bytes 1156
  16.5 1.5 %copy-start.9 = (f32[96]{0:T(128)S(1)}, f32[96]{0:T(128)}, u32[]{:S(2)}) copy-start(f32[96]{0:T(128)} %param.18) | copy-start | bytes 1156
  16.5 1.5 %copy-start.10 = (f32[96]{0:T(128)S(1)}, f32[96]{0:T(128)}, u32[]{:S(2)}) copy-start(f32[96]{0:T(128)} %param.19) | copy-start | bytes 1156
  17.8 4.8 %copy-start.1 = (bf16[9,192,96]{2,1,0:T(8,128)(2,1)S(1)}, bf16[9,192,96]{2,1,0:T(8,128)(2,1)}, u32[]{:S(2)}) copy-start(bf16[9,192,96]{2,1,0:T(8,128)(2,1)} %refs_1_.1) | copy-start | bytes 995332
  17.8 3.0 %collective-permute-start.5 = (bf16[72,128]{1,0:T(8,128)(2,1)S(1)}, bf16[72,128]{1,0:T(8,128)(2,1)S(1)}, u32[]{:S(2)}, u32[]{:S(2)}) collective-permute-start(bf16[72,128]{1,0:T(8,128)(2,1)S(1)} %get-tuple-element.55), channel_id=1, source_target_pairs={{0,1},{1,0},{2,3},{3,2},{4,5},{5,4},{6,7},{7,6},{8,9},{9,8},{10,11... | collective-permute-start | bytes 55304 | tf_op jit(solution)/shard_map/ppermute | solution.py:58
  20.4 5.2 %collective-permute-start.9 = (bf16[1,192,128]{2,1,0:T(8,128)(2,1)S(1)}, bf16[1,192,128]{2,1,0:T(8,128)(2,1)S(1)}, u32[]{:S(2)}, u32[]{:S(2)}) collective-permute-start(bf16[1,192,128]{2,1,0:T(8,128)(2,1)S(1)} %get-tuple-element.66), channel_id=1, source_target_pairs={{0,1},{1,0},{2,3},{3,2},{4,5},{5,4},{6,7},{7,6},{8,9},{9,8},{10,11... | collective-permute-start | bytes 147464 | tf_op jit(solution)/shard_map/ppermute | solution.py:58
  20.8 7.4 %collective-permute-start.8 = (bf16[1,336,128]{2,1,0:T(8,128)(2,1)S(1)}, bf16[1,336,128]{2,1,0:T(8,128)(2,1)S(1)}, u32[]{:S(2)}, u32[]{:S(2)}) collective-permute-start(bf16[1,336,128]{2,1,0:T(8,128)(2,1)S(1)} %pad_maximum_fusion.2), channel_id=1, source_target_pairs={{0,8},{4,12},{8,0},{12,4},{1,9},{5,13},{9,1},{13,5},{2,10},{6,14},... | collective-permute-start | bytes 258056 | tf_op jit(solution)/shard_map/ppermute | solution.py:58
  25.5 2.8 %collective-permute-start.7 = (bf16[608,128]{1,0:T(8,128)(2,1)S(1)}, bf16[608,128]{1,0:T(8,128)(2,1)S(1)}, u32[]{:S(2)}, u32[]{:S(2)}) collective-permute-start(bf16[608,128]{1,0:T(8,128)(2,1)S(1)} %get-tuple-element.65), channel_id=1, source_target_pairs={{0,1},{1,0},{2,3},{3,2},{4,5},{5,4},{6,7},{7,6},{8,9},{9,8},{10,11... | collective-permute-start | bytes 466952 | tf_op jit(solution)/shard_map/ppermute | solution.py:58
  28.3 5.9 %collective-permute-start.12 = (bf16[608,128]{1,0:T(8,128)(2,1)S(1)}, bf16[608,128]{1,0:T(8,128)(2,1)S(1)}, u32[]{:S(2)}, u32[]{:S(2)}) collective-permute-start(bf16[608,128]{1,0:T(8,128)(2,1)S(1)} %convert_add_fusion.1), channel_id=1, source_target_pairs={{0,2},{2,0},{1,3},{3,1},{4,6},{6,4},{5,7},{7,5},{8,10},{10,8},{9,1... | collective-permute-start | bytes 466952 | tf_op jit(solution)/shard_map/ppermute | solution.py:58
  29.9 4.3 %collective-permute-start.13 = (f32[96,128]{1,0:T(8,128)S(1)}, f32[96,128]{1,0:T(8,128)S(1)}, u32[]{:S(2)}, u32[]{:S(2)}) collective-permute-start(f32[96,128]{1,0:T(8,128)S(1)} %get-tuple-element.73), channel_id=1, source_target_pairs={{0,4},{4,8},{8,12},{1,5},{5,9},{9,13},{2,6},{6,10},{10,14},{3,7},{... | collective-permute-start | bytes 147464 | tf_op jit(solution)/shard_map/ppermute | solution.py:53
  31.2 7.2 %collective-permute-start.10 = (bf16[2,336,128]{2,1,0:T(8,128)(2,1)S(1)}, bf16[2,336,128]{2,1,0:T(8,128)(2,1)S(1)}, u32[]{:S(2)}, u32[]{:S(2)}) collective-permute-start(bf16[2,336,128]{2,1,0:T(8,128)(2,1)S(1)} %pad_maximum_fusion), channel_id=1, source_target_pairs={{0,4},{4,0},{8,12},{12,8},{1,5},{5,1},{9,13},{13,9},{2,6},{6,2},{1... | collective-permute-start | bytes 516104 | tf_op jit(solution)/shard_map/ppermute | solution.py:58
  34.2 6.3 %collective-permute-start.14 = (bf16[608,128]{1,0:T(8,128)(2,1)S(1)}, bf16[608,128]{1,0:T(8,128)(2,1)S(1)}, u32[]{:S(2)}, u32[]{:S(2)}) collective-permute-start(bf16[608,128]{1,0:T(8,128)(2,1)S(1)} %add_convert_fusion.2), channel_id=1, source_target_pairs={{0,4},{4,0},{8,12},{12,8},{1,5},{5,1},{9,13},{13,9},{2,6},{6,2},{1... | collective-permute-start | bytes 466952 | tf_op jit(solution)/shard_map/ppermute | solution.py:58
  38.4 7.6 %collective-permute-start.11 = (bf16[4,336,128]{2,1,0:T(8,128)(2,1)S(1)}, bf16[4,336,128]{2,1,0:T(8,128)(2,1)S(1)}, u32[]{:S(2)}, u32[]{:S(2)}) collective-permute-start(bf16[4,336,128]{2,1,0:T(8,128)(2,1)S(1)} %constant_dynamic-update-slice_fusion.refs_1_), channel_id=1, source_target_pairs={{0,2},{2,0},{1,3},{3,1},{4,6},{6,4},{5,7},{7,5},{8,10},{10,8},{9,1... | collective-permute-start | bytes 1032200 | tf_op jit(solution)/shard_map/ppermute | solution.py:58
  40.6 9.1 %collective-permute-start.15 = (bf16[608,128]{1,0:T(8,128)(2,1)S(1)}, bf16[608,128]{1,0:T(8,128)(2,1)S(1)}, u32[]{:S(2)}, u32[]{:S(2)}) collective-permute-start(bf16[608,128]{1,0:T(8,128)(2,1)S(1)} %add_convert_fusion.1), channel_id=1, source_target_pairs={{0,8},{4,12},{8,0},{12,4},{1,9},{5,13},{9,1},{13,5},{2,10},{6,14},... | collective-permute-start | bytes 466952 | tf_op jit(solution)/shard_map/ppermute | solution.py:58
  47.4 2.4 %collective-permute-start.16 = (bf16[9,192,96]{2,1,0:T(8,128)(2,1)S(1)}, bf16[9,192,96]{2,1,0:T(8,128)(2,1)S(1)}, u32[]{:S(2)}, u32[]{:S(2)}) collective-permute-start(bf16[9,192,96]{2,1,0:T(8,128)(2,1)S(1)} %get-tuple-element.79), channel_id=1, source_target_pairs={{0,1},{1,0},{2,3},{3,2},{4,5},{5,4},{6,7},{7,6},{8,9},{9,8},{10,11... | collective-permute-start | bytes 995336 | tf_op jit(solution)/shard_map/ppermute | solution.py:58
  49.7 1.4 %collective-permute-start.17 = (bf16[608,128]{1,0:T(8,128)(2,1)S(1)}, bf16[608,128]{1,0:T(8,128)(2,1)S(1)}, u32[]{:S(2)}, u32[]{:S(2)}) collective-permute-start(bf16[608,128]{1,0:T(8,128)(2,1)S(1)} %add_convert_fusion.own_ref), channel_id=1, source_target_pairs={{0,1},{1,0},{2,3},{3,2},{4,5},{5,4},{6,7},{7,6},{8,9},{9,8},{10,11... | collective-permute-start | bytes 466952 | tf_op jit(solution)/shard_map/ppermute | solution.py:58

commit v10 on v8

--- a/solution.py
+++ b/solution.py
@@ -9,8 +9,6 @@
 
 SIDE = 8
 CAP = 2
-GW = 64
-BAND_CELLS = 512
 PIX = SIDE * SIDE
 HALF_ROWS = 608
 FEAT_ROWS = 192
@@ -68,7 +66,7 @@
     pixch = pixels_ref.shape[1]
     cells = [cells_ref[0, t] for t in range(slots)]
     live = [cell >= 0 for cell in cells]
-    bands = [cell // BAND_CELLS for cell in cells]
+    bands = [cell >> 9 for cell in cells]
     places = []
     for t in range(slots):
         rank = jnp.int32(0)
@@ -91,9 +89,8 @@
     base = (lax.broadcasted_iota(jnp.int32, (rows, 128), 0) // CAP) * CAP
     notes = jnp.zeros((rows, 128), F32)
     for t in range(slots):
-        within = cells[t] % BAND_CELLS
-        own_row = (within // GW).astype(F32)
-        own_col = (within % GW).astype(F32)
+        own_row = ((cells[t] >> 6) & 7).astype(F32)
+        own_col = (cells[t] & 63).astype(F32)
         for rank in range(CAP):
             hit = base + rank == places[t]
             for at, value in enumerate((own_row, own_col, jnp.float32(1.0))):
@@ -127,13 +124,12 @@
     key = jnp.concatenate(blocks, axis=0)
     key_ref[...] = key
 
-    def step(o, total):
-        pick = (key == o.astype(F32)).astype(F32).astype(BF16)
-        return total + nt(pick, cot_ref[o].astype(BF16))
-
-    total = lax.fori_loop(
-        0, out_rows, step, jnp.zeros((key.shape[0], e_half), F32), unroll=4
-    )
+    total = jnp.zeros((key.shape[0], e_half), F32)
+    for first_row in range(0, out_rows, 4):
+        rows = range(first_row, first_row + 4)
+        picks = [(key == float(o)).astype(F32).astype(BF16) for o in rows]
+        cots = [cot_ref[o].astype(BF16) for o in rows]
+        total = total + nt(jnp.concatenate(picks, axis=1), jnp.concatenate(cots, axis=1))
     pick = (key == float(out_rows)).astype(F32).astype(BF16)
     total = total + nt(pick, below_ref[...])
     half = total.shape[0] // 2

time: 51 us -> 50.1 us (0.982)
  Pallas kernels: 15.2 us -> 14.4 us
  starting transfers between devices: 20.3 us -> 19.7 us
    pallas_call x1, Pallas kernels: 1.24 us -> 0.45 us  [on_device(): pl.pallas_call(patch_kernel, out_shape=(jax.ShapeDtypeStruct((blocks * CO...]
    ppermute x12, starting transfers between devices: 11.1 us -> 10.5 us  [swapped(): lax.ppermute(value, axis, [(place, place ^ step) for place in range(count)])]
  transfers between devices with their start and end apart: 15 -> 15, of which waited for: 7 -> 8; matrix products, arithmetic and copies ran while one was open for 2% -> 2% of each run, Pallas kernels for 24% -> 23%
where the time goes in v10:
time: 50.1 us; the launch traced here: 49.8 us
  starting transfers between devices  19.7 us (39%)
  Pallas kernels  14.4 us (29%)
  waiting for transfers between devices  13.2 us (26%)
  other arithmetic  1.2 us (2%)
  between operations  0.85 us (2%)
    ppermute x12, starting transfers between devices, swapped(): lax.ppermute(value, axis, [(place, place ^ step) for place in range(count)])  10.5 us
    ppermute x12, waiting for transfers between devices, swapped(): lax.ppermute(value, axis, [(place, place ^ step) for place in range(count)])  8.4 us
    all_to_all x1, starting transfers between devices, on_device(): lax.all_to_all(packed, ('slide', 'chan'), split_axis=0, concat_axis=0, ti...  6.46 us
    ppermute x2, waiting for transfers between devices, shifted(): lax.ppermute(value, axis, [(source, source + steps) for source in range(f...  4.84 us
    pallas_call x1, Pallas kernels, on_device(): agg_map = map_call(spread, key, above)  3.5 us
    pallas_call x1, Pallas kernels, on_device(): pl.pallas_call(lambda *refs: back_kernel(*refs, scale=loss_scale), grid=(...  2.95 us
    ppermute x2, starting transfers between devices, shifted(): lax.ppermute(value, axis, [(source, source + steps) for source in range(f...  2.75 us
    pallas_call x1, Pallas kernels, on_device(): pl.pallas_call(stem_kernel, grid=(chunks,), out_shape=(jax.ShapeDtypeStru...  2.25 us
  transfers between devices with their start and end apart: 15, of which 8 were waited for; matrix products, arithmetic and copies ran while one was open for 2% of the time, Pallas kernels for 23%

profile of v10, /device:TPU:0, one launch (start us, length us, event | category | flops | bytes accessed | tf_op | source)
XLA Modules:
  0.0 49.8 jit_solution(8596506360777046360)
XLA Ops:
  0.6 1.9 %pack.1 = (bf16[8,56,128]{2,1,0:T(8,128)(2,1)}, bf16[96,128]{1,0:T(8,128)(2,1)}) custom-call(s32[1,8]{1,0:T(1,128)} %cells_ref.1, bf16[1,8,6144]{2,1,0:T(8,128)(2,1)} %pixels_ref.1, f32[1,16,96,128]{3,2,1,0:T(8,128)} %cot_ref.1), custom_call_target="tpu_custom_call" | custom-call | bytes 5535000 | tf_op jit(solution)/shard_map/pack/pallas_call | solution.py:439
  2.5 6.5 %all-to-all-start = ((bf16[8,56,128]{2,1,0:T(8,128)(2,1)}), bf16[8,56,128]{2,1,0:T(8,128)(2,1)S(1)}, u32[]{:S(2)}, u32[]{:S(2)}) async-start(bf16[8,56,128]{2,1,0:T(8,128)(2,1)} %get-tuple-element.42), calls=%async_computation | async-start | bytes 229376 | tf_op jit(solution)/shard_map/all_to_all | solution.py:462
  9.0 0.5 %collective-permute-start.2 = (bf16[9,192,96]{2,1,0:T(8,128)(2,1)}, bf16[9,192,96]{2,1,0:T(8,128)(2,1)S(1)}, u32[]{:S(2)}, u32[]{:S(2)}) collective-permute-start(bf16[9,192,96]{2,1,0:T(8,128)(2,1)} %refs_1_.1), channel_id=1, source_target_pairs={{0,1},{1,0},{2,3},{3,2},{4,5},{5,4},{6,7},{7,6},{8,9},{9,8},{10,11... | collective-permute-start | bytes 995336 | tf_op jit(solution)/shard_map/ppermute | solution.py:56
  9.5 1.3 %collective-permute-start = (bf16[96,128]{1,0:T(8,128)(2,1)S(1)}, bf16[96,128]{1,0:T(8,128)(2,1)S(1)}, u32[]{:S(2)}, u32[]{:S(2)}) collective-permute-start(bf16[96,128]{1,0:T(8,128)(2,1)S(1)} %copy-done.9), channel_id=1, source_target_pairs={{4,0},{8,4},{12,8},{5,1},{9,5},{13,9},{6,2},{10,6},{14,10},{7,3},{... | collective-permute-start | bytes 73736 | tf_op jit(solution)/shard_map/ppermute | solution.py:51
  10.8 4.8 %collective-permute-done.below_ref = bf16[96,128]{1,0:T(8,128)(2,1)S(1)} collective-permute-done((bf16[96,128]{1,0:T(8,128)(2,1)S(1)}, bf16[96,128]{1,0:T(8,128)(2,1)S(1)}, u32[]{:S(2)}, u32[]{:S(2)}) %collective-permute-start) | collective-permute-done | bytes 24608 | tf_op jit(solution)/shard_map/ppermute | solution.py:51
  15.6 0.0 all-to-all-done.meta_ref.got_ref.refs_5_
  15.6 0.0 copy-start.3
  15.6 0.0 copy-start.4
  15.7 0.0 copy-start.5
  15.7 0.0 copy-start.6
  15.7 0.0 copy-start.7
  15.7 0.0 copy-start.8
  15.7 0.5 patch.1
  16.2 0.0 copy-start.1
  16.2 0.1 collective-permute-start.1
  16.3 0.3 copy-done.2
  16.5 0.0 copy-done.3
  16.6 0.0 copy-done.4
  16.6 2.2 %stem.1 = (bf16[1,192,128]{2,1,0:T(8,128)(2,1)S(1)}, f32[1,512,96]{2,1,0:T(8,128)S(1)}, f32[1,512,1]{2,1,0:T(8,128)S(1)}, f32[1,512,96]{2,1,0:T(8,128)S(1)}, f32...) custom-call(bf16[8,56,128]{2,1,0:T(8,128)(2,1)S(1)} %all-to-all-done, ...), custom_call_target="tpu_custom_call" | custom-call | bytes 9963000 | tf_op jit(solution)/shard_map/stem/pallas_call | solution.py:499
  18.9 0.2 collective-permute-start.5
  19.1 0.0 collective-permute-done.1
  19.1 2.2 %collective-permute-start.4 = (bf16[1,336,128]{2,1,0:T(8,128)(2,1)S(1)}, bf16[1,336,128]{2,1,0:T(8,128)(2,1)S(1)}, u32[]{:S(2)}, u32[]{:S(2)}) collective-permute-start(bf16[1,336,128]{2,1,0:T(8,128)(2,1)S(1)} %pad_maximum_fusion.2), channel_id=1, source_target_pairs={{0,8},{4,12},{8,0},{12,4},{1,9},{5,13},{9,1},{13,5},{2,10},{6,14},... | collective-permute-start | bytes 258056 | tf_op jit(solution)/shard_map/ppermute | solution.py:56
  21.3 0.0 collective-permute-done.2.refs_4_
  21.3 2.9 %stem_back.1 = (f32[608,128]{1,0:T(8,128)S(1)}, bf16[608,128]{1,0:T(8,128)(2,1)S(1)}) custom-call(s32[1]{0:T(128)} %bitcast.chan_ref.refs_0_, bf16[1,72,128]{2,1,0:T(8,128)(2,1)S(1)} %bitcast.17, bf16[1,72,128]{2,1,0:T(8,128)(2,1)S(1)} %bitcast.20, bf16[9,192,96]{2,1,0:T(8,128)(2,1)S(1)} %copy-done.1, ...), custom_call_target="tpu_custom_call" | custom-call | bytes 13653000 | tf_op jit(solution)/shard_map/stem_back/pallas_call | solution.py:567
  24.3 0.1 collective-permute-start.3
  24.4 0.0 collective-permute-done.5
  24.5 1.0 %spread.1 = (f32[144,96]{1,0:T(8,128)S(1)}, f32[96,128]{1,0:T(8,128)S(1)}) custom-call(bf16[2,192,128]{2,1,0:T(8,128)(2,1)S(1)} %pad_maximum_fusion.1.refs_0_, bf16[9,192,96]{2,1,0:T(8,128)(2,1)S(1)} %copy-done.1, f32[144,128]{1,0:T(8,128)S(1)} %get-tuple-element.57.refs_2_.key_ref), custom_call_target="tpu_custom_call" | custom-call | bytes 3690000 | tf_op jit(solution)/shard_map/spread/pallas_call | solution.py:535
  25.5 1.2 %collective-permute-done.4 = bf16[1,336,128]{2,1,0:T(8,128)(2,1)S(1)} collective-permute-done((bf16[1,336,128]{2,1,0:T(8,128)(2,1)S(1)}, bf16[1,336,128]{2,1,0:T(8,128)(2,1)S(1)}, u32[]{:S(2)}, u32[]{:S(2)}) %collective-permute-start.4) | collective-permute-done | bytes 86048 | tf_op jit(solution)/shard_map/ppermute | solution.py:56
  26.7 0.0 collective-permute-done.3
  26.8 1.6 %collective-permute-start.8 = (bf16[608,128]{1,0:T(8,128)(2,1)S(1)}, bf16[608,128]{1,0:T(8,128)(2,1)S(1)}, u32[]{:S(2)}, u32[]{:S(2)}) collective-permute-start(bf16[608,128]{1,0:T(8,128)(2,1)S(1)} %convert_add_fusion.1), channel_id=1, source_target_pairs={{0,2},{2,0},{1,3},{3,1},{4,6},{6,4},{5,7},{7,5},{8,10},{10,8},{9,1... | collective-permute-start | bytes 466952 | tf_op jit(solution)/shard_map/ppermute | solution.py:56
  28.4 1.5 %collective-permute-start.9 = (f32[96,128]{1,0:T(8,128)S(1)}, f32[96,128]{1,0:T(8,128)S(1)}, u32[]{:S(2)}, u32[]{:S(2)}) collective-permute-start(f32[96,128]{1,0:T(8,128)S(1)} %get-tuple-element.63), channel_id=1, source_target_pairs={{0,4},{4,8},{8,12},{1,5},{5,9},{9,13},{2,6},{6,10},{10,14},{3,7},{... | collective-permute-start | bytes 147464 | tf_op jit(solution)/shard_map/ppermute | solution.py:51
  29.8 1.5 %collective-permute-start.6 = (bf16[2,336,128]{2,1,0:T(8,128)(2,1)S(1)}, bf16[2,336,128]{2,1,0:T(8,128)(2,1)S(1)}, u32[]{:S(2)}, u32[]{:S(2)}) collective-permute-start(bf16[2,336,128]{2,1,0:T(8,128)(2,1)S(1)} %pad_maximum_fusion), channel_id=1, source_target_pairs={{0,4},{4,0},{8,12},{12,8},{1,5},{5,1},{9,13},{13,9},{2,6},{6,2},{1... | collective-permute-start | bytes 516104 | tf_op jit(solution)/shard_map/ppermute | solution.py:56
  31.3 1.0 %collective-permute-done.8 = bf16[608,128]{1,0:T(8,128)(2,1)S(1)} collective-permute-done((bf16[608,128]{1,0:T(8,128)(2,1)S(1)}, bf16[608,128]{1,0:T(8,128)(2,1)S(1)}, u32[]{:S(2)}, u32[]{:S(2)}) %collective-permute-start.8) | collective-permute-done | bytes 155680 | tf_op jit(solution)/shard_map/ppermute | solution.py:56
  32.4 0.0 collective-permute-done.9.above_ref
  32.4 1.9 %collective-permute-start.10 = (bf16[608,128]{1,0:T(8,128)(2,1)S(1)}, bf16[608,128]{1,0:T(8,128)(2,1)S(1)}, u32[]{:S(2)}, u32[]{:S(2)}) collective-permute-start(bf16[608,128]{1,0:T(8,128)(2,1)S(1)} %add_convert_fusion.2), channel_id=1, source_target_pairs={{0,4},{4,0},{8,12},{12,8},{1,5},{5,1},{9,13},{13,9},{2,6},{6,2},{1... | collective-permute-start | bytes 466952 | tf_op jit(solution)/shard_map/ppermute | solution.py:56
  34.3 2.6 %collective-permute-done.6 = bf16[2,336,128]{2,1,0:T(8,128)(2,1)S(1)} collective-permute-done((bf16[2,336,128]{2,1,0:T(8,128)(2,1)S(1)}, bf16[2,336,128]{2,1,0:T(8,128)(2,1)S(1)}, u32[]{:S(2)}, u32[]{:S(2)}) %collective-permute-start.6) | collective-permute-done | bytes 172064 | tf_op jit(solution)/shard_map/ppermute | solution.py:56
  36.9 0.1 collective-permute-start.7
  37.0 1.6 %collective-permute-done.10 = bf16[608,128]{1,0:T(8,128)(2,1)S(1)} collective-permute-done((bf16[608,128]{1,0:T(8,128)(2,1)S(1)}, bf16[608,128]{1,0:T(8,128)(2,1)S(1)}, u32[]{:S(2)}, u32[]{:S(2)}) %collective-permute-start.10) | collective-permute-done | bytes 155680 | tf_op jit(solution)/shard_map/ppermute | solution.py:56
  38.7 2.1 %collective-permute-start.11 = (bf16[608,128]{1,0:T(8,128)(2,1)S(1)}, bf16[608,128]{1,0:T(8,128)(2,1)S(1)}, u32[]{:S(2)}, u32[]{:S(2)}) collective-permute-start(bf16[608,128]{1,0:T(8,128)(2,1)S(1)} %add_convert_fusion.1), channel_id=1, source_target_pairs={{0,8},{4,12},{8,0},{12,4},{1,9},{5,13},{9,1},{13,5},{2,10},{6,14},... | collective-permute-start | bytes 466952 | tf_op jit(solution)/shard_map/ppermute | solution.py:56
  40.8 3.5 %agg_map.1 = bf16[16,96,128]{2,1,0:T(8,128)(2,1)} custom-call(f32[144,96]{1,0:T(8,128)S(1)} %get-tuple-element.61.y_ref, f32[144,128]{1,0:T(8,128)S(1)} %get-tuple-element.57.refs_2_.key_ref, f32[96,128]{1,0:T(8,128)S(1)} %collective-permute-done.9.above_ref), custom_call_target="tpu_custom_call" | custom-call | bytes 12915000 | tf_op jit(solution)/shard_map/agg_map/pallas_call | solution.py:628
  44.3 1.4 %agg_weight_grad.1 = (f32[9,192,96]{2,1,0:T(8,128)S(1)}, bf16[9,192,96]{2,1,0:T(8,128)(2,1)S(1)}) custom-call(s32[1]{0:T(128)} %bitcast.9.refs_0_, bf16[4,336,128]{2,1,0:T(8,128)(2,1)S(1)} %constant_dynamic-update-slice_fusion.refs_1_, bf16[4,336,128]{2,1,0:T(8,128)(2,1)S(1)} %collective-permute-done.7.refs_2_), custom_call_target="tpu_custom_call" | custom-call | bytes 5166000 | tf_op jit(solution)/shard_map/agg_weight_grad/pallas_call | solution.py:640
  45.8 0.1 collective-permute-start.12
  45.8 1.6 %collective-permute-done.11 = bf16[608,128]{1,0:T(8,128)(2,1)S(1)} collective-permute-done((bf16[608,128]{1,0:T(8,128)(2,1)S(1)}, bf16[608,128]{1,0:T(8,128)(2,1)S(1)}, u32[]{:S(2)}, u32[]{:S(2)}) %collective-permute-start.11) | collective-permute-done | bytes 155680 | tf_op jit(solution)/shard_map/ppermute | solution.py:56
  47.5 0.1 collective-permute-start.13
  47.5 0.1 collective-permute-done.12
  47.6 1.0 %convert_add_fusion = f32[9,192,96]{2,1,0:T(8,128)} fusion(f32[9,192,96]{2,1,0:T(8,128)S(1)} %get-tuple-element.68, bf16[9,192,96]{2,1,0:T(8,128)(2,1)S(1)} %collective-permute-done.12), kind=kLoop, calls=%fused_computation | loop fusion | flops 331776 | bytes 1658880 | tf_op jit(solution)/shard_map/add | solution.py:662
  48.6 0.3 collective-permute-done.13.peer_ref
  48.9 0.9 %unpack.1 = (f32[49,96]{1,0:T(8,128)}, f32[96,384]{1,0:T(8,128)}, f32[96,384]{1,0:T(8,128)}, f32[192,384]{1,0:T(8,128)}) custom-call(s32[1]{0:T(128)} %bitcast.chan_ref.refs_0_, bf16[608,128]{1,0:T(8,128)(2,1)S(1)} %add_convert_fusion.own_ref, bf16[608,128]{1,0:T(8,128)(2,1)S(1)} %collective-permute-done.13.peer_ref), custom_call_target="tpu_custom_call" | custom-call | bytes 5535000 | tf_op jit(solution)/shard_map/unpack/pallas_call | solution.py:669
  (20 shorter events, 0.3 us)
Async XLA Ops:
  0.6 15.0 %copy-start = (f32[1,16,96,128]{3,2,1,0:T(8,128)S(1)}, f32[1,16,96,128]{3,2,1,0:T(8,128)}, u32[]{:S(2)}) copy-start(f32[1,16,96,128]{3,2,1,0:T(8,128)} %cot_ref.1) | copy-start | bytes 2359300
  2.5 7.0 %copy-start.9 = (bf16[96,128]{1,0:T(8,128)(2,1)S(1)}, bf16[96,128]{1,0:T(8,128)(2,1)}, u32[]{:S(2)}) copy-start(bf16[96,128]{1,0:T(8,128)(2,1)} %get-tuple-element.43) | copy-start | bytes 73732
  2.5 13.1 %all-to-all-start = ((bf16[8,56,128]{2,1,0:T(8,128)(2,1)}), bf16[8,56,128]{2,1,0:T(8,128)(2,1)S(1)}, u32[]{:S(2)}, u32[]{:S(2)}) async-start(bf16[8,56,128]{2,1,0:T(8,128)(2,1)} %get-tuple-element.42), calls=%async_computation | async-start | bytes 229376 | tf_op jit(solution)/shard_map/all_to_all | solution.py:462
  9.0 12.4 %collective-permute-start.2 = (bf16[9,192,96]{2,1,0:T(8,128)(2,1)}, bf16[9,192,96]{2,1,0:T(8,128)(2,1)S(1)}, u32[]{:S(2)}, u32[]{:S(2)}) collective-permute-start(bf16[9,192,96]{2,1,0:T(8,128)(2,1)} %refs_1_.1), channel_id=1, source_target_pairs={{0,1},{1,0},{2,3},{3,2},{4,5},{5,4},{6,7},{7,6},{8,9},{9,8},{10,11... | collective-permute-start | bytes 995336 | tf_op jit(solution)/shard_map/ppermute | solution.py:56
  9.5 6.1 %collective-permute-start = (bf16[96,128]{1,0:T(8,128)(2,1)S(1)}, bf16[96,128]{1,0:T(8,128)(2,1)S(1)}, u32[]{:S(2)}, u32[]{:S(2)}) collective-permute-start(bf16[96,128]{1,0:T(8,128)(2,1)S(1)} %copy-done.9), channel_id=1, source_target_pairs={{4,0},{8,4},{12,8},{5,1},{9,5},{13,9},{6,2},{10,6},{14,10},{7,3},{... | collective-permute-start | bytes 73736 | tf_op jit(solution)/shard_map/ppermute | solution.py:51
  15.6 0.9 %copy-start.2 = (bf16[384,192]{0,1:T(8,128)(2,1)S(1)}, bf16[384,192]{0,1:T(8,128)(2,1)}, u32[]{:S(2)}) copy-start(bf16[384,192]{0,1:T(8,128)(2,1)} %param.20) | copy-start | bytes 442372
  15.6 1.0 %copy-start.3 = (bf16[96,384]{1,0:T(8,128)(2,1)S(1)}, bf16[96,384]{1,0:T(8,128)(2,1)}, u32[]{:S(2)}) copy-start(bf16[96,384]{1,0:T(8,128)(2,1)} %refs_14_.1) | copy-start | bytes 221188
  15.6 1.0 %copy-start.4 = (bf16[384,96]{0,1:T(8,128)(2,1)S(1)}, bf16[384,96]{0,1:T(8,128)(2,1)}, u32[]{:S(2)}) copy-start(bf16[384,96]{0,1:T(8,128)(2,1)} %param.17) | copy-start | bytes 221188
  15.7 1.0 %copy-start.5 = (f32[49,96]{1,0:T(8,128)S(1)}, f32[49,96]{1,0:T(8,128)}, u32[]{:S(2)}) copy-start(f32[49,96]{1,0:T(8,128)} %dw_ref.1) | copy-start | bytes 56452
  15.7 1.0 %copy-start.6 = (f32[96]{0:T(128)S(1)}, f32[96]{0:T(128)}, u32[]{:S(2)}) copy-start(f32[96]{0:T(128)} %param.15) | copy-start | bytes 1156
  15.7 1.0 %copy-start.7 = (f32[96]{0:T(128)S(1)}, f32[96]{0:T(128)}, u32[]{:S(2)}) copy-start(f32[96]{0:T(128)} %param.18) | copy-start | bytes 1156
  15.7 0.9 %copy-start.8 = (f32[96]{0:T(128)S(1)}, f32[96]{0:T(128)}, u32[]{:S(2)}) copy-start(f32[96]{0:T(128)} %param.19) | copy-start | bytes 1156
  16.2 5.2 %copy-start.1 = (bf16[9,192,96]{2,1,0:T(8,128)(2,1)S(1)}, bf16[9,192,96]{2,1,0:T(8,128)(2,1)}, u32[]{:S(2)}) copy-start(bf16[9,192,96]{2,1,0:T(8,128)(2,1)} %refs_1_.1) | copy-start | bytes 995332
  16.2 2.9 %collective-permute-start.1 = (bf16[72,128]{1,0:T(8,128)(2,1)S(1)}, bf16[72,128]{1,0:T(8,128)(2,1)S(1)}, u32[]{:S(2)}, u32[]{:S(2)}) collective-permute-start(bf16[72,128]{1,0:T(8,128)(2,1)S(1)} %get-tuple-element.45), channel_id=1, source_target_pairs={{0,1},{1,0},{2,3},{3,2},{4,5},{5,4},{6,7},{7,6},{8,9},{9,8},{10,11... | collective-permute-start | bytes 55304 | tf_op jit(solution)/shard_map/ppermute | solution.py:56
  18.9 5.6 %collective-permute-start.5 = (bf16[1,192,128]{2,1,0:T(8,128)(2,1)S(1)}, bf16[1,192,128]{2,1,0:T(8,128)(2,1)S(1)}, u32[]{:S(2)}, u32[]{:S(2)}) collective-permute-start(bf16[1,192,128]{2,1,0:T(8,128)(2,1)S(1)} %get-tuple-element.56), channel_id=1, source_target_pairs={{0,1},{1,0},{2,3},{3,2},{4,5},{5,4},{6,7},{7,6},{8,9},{9,8},{10,11... | collective-permute-start | bytes 147464 | tf_op jit(solution)/shard_map/ppermute | solution.py:56
  19.1 7.6 %collective-permute-start.4 = (bf16[1,336,128]{2,1,0:T(8,128)(2,1)S(1)}, bf16[1,336,128]{2,1,0:T(8,128)(2,1)S(1)}, u32[]{:S(2)}, u32[]{:S(2)}) collective-permute-start(bf16[1,336,128]{2,1,0:T(8,128)(2,1)S(1)} %pad_maximum_fusion.2), channel_id=1, source_target_pairs={{0,8},{4,12},{8,0},{12,4},{1,9},{5,13},{9,1},{13,5},{2,10},{6,14},... | collective-permute-start | bytes 258056 | tf_op jit(solution)/shard_map/ppermute | solution.py:56
  24.3 2.4 %collective-permute-start.3 = (bf16[608,128]{1,0:T(8,128)(2,1)S(1)}, bf16[608,128]{1,0:T(8,128)(2,1)S(1)}, u32[]{:S(2)}, u32[]{:S(2)}) collective-permute-start(bf16[608,128]{1,0:T(8,128)(2,1)S(1)} %get-tuple-element.55), channel_id=1, source_target_pairs={{0,1},{1,0},{2,3},{3,2},{4,5},{5,4},{6,7},{7,6},{8,9},{9,8},{10,11... | collective-permute-start | bytes 466952 | tf_op jit(solution)/shard_map/ppermute | solution.py:56
  26.8 5.5 %collective-permute-start.8 = (bf16[608,128]{1,0:T(8,128)(2,1)S(1)}, bf16[608,128]{1,0:T(8,128)(2,1)S(1)}, u32[]{:S(2)}, u32[]{:S(2)}) collective-permute-start(bf16[608,128]{1,0:T(8,128)(2,1)S(1)} %convert_add_fusion.1), channel_id=1, source_target_pairs={{0,2},{2,0},{1,3},{3,1},{4,6},{6,4},{5,7},{7,5},{8,10},{10,8},{9,1... | collective-permute-start | bytes 466952 | tf_op jit(solution)/shard_map/ppermute | solution.py:56
  28.4 4.0 %collective-permute-start.9 = (f32[96,128]{1,0:T(8,128)S(1)}, f32[96,128]{1,0:T(8,128)S(1)}, u32[]{:S(2)}, u32[]{:S(2)}) collective-permute-start(f32[96,128]{1,0:T(8,128)S(1)} %get-tuple-element.63), channel_id=1, source_target_pairs={{0,4},{4,8},{8,12},{1,5},{5,9},{9,13},{2,6},{6,10},{10,14},{3,7},{... | collective-permute-start | bytes 147464 | tf_op jit(solution)/shard_map/ppermute | solution.py:51
  29.8 7.1 %collective-permute-start.6 = (bf16[2,336,128]{2,1,0:T(8,128)(2,1)S(1)}, bf16[2,336,128]{2,1,0:T(8,128)(2,1)S(1)}, u32[]{:S(2)}, u32[]{:S(2)}) collective-permute-start(bf16[2,336,128]{2,1,0:T(8,128)(2,1)S(1)} %pad_maximum_fusion), channel_id=1, source_target_pairs={{0,4},{4,0},{8,12},{12,8},{1,5},{5,1},{9,13},{13,9},{2,6},{6,2},{1... | collective-permute-start | bytes 516104 | tf_op jit(solution)/shard_map/ppermute | solution.py:56
  32.4 6.2 %collective-permute-start.10 = (bf16[608,128]{1,0:T(8,128)(2,1)S(1)}, bf16[608,128]{1,0:T(8,128)(2,1)S(1)}, u32[]{:S(2)}, u32[]{:S(2)}) collective-permute-start(bf16[608,128]{1,0:T(8,128)(2,1)S(1)} %add_convert_fusion.2), channel_id=1, source_target_pairs={{0,4},{4,0},{8,12},{12,8},{1,5},{5,1},{9,13},{13,9},{2,6},{6,2},{1... | collective-permute-start | bytes 466952 | tf_op jit(solution)/shard_map/ppermute | solution.py:56
  36.9 7.4 %collective-permute-start.7 = (bf16[4,336,128]{2,1,0:T(8,128)(2,1)S(1)}, bf16[4,336,128]{2,1,0:T(8,128)(2,1)S(1)}, u32[]{:S(2)}, u32[]{:S(2)}) collective-permute-start(bf16[4,336,128]{2,1,0:T(8,128)(2,1)S(1)} %constant_dynamic-update-slice_fusion.refs_1_), channel_id=1, source_target_pairs={{0,2},{2,0},{1,3},{3,1},{4,6},{6,4},{5,7},{7,5},{8,10},{10,8},{9,1... | collective-permute-start | bytes 1032200 | tf_op jit(solution)/shard_map/ppermute | solution.py:56
  38.7 8.7 %collective-permute-start.11 = (bf16[608,128]{1,0:T(8,128)(2,1)S(1)}, bf16[608,128]{1,0:T(8,128)(2,1)S(1)}, u32[]{:S(2)}, u32[]{:S(2)}) collective-permute-start(bf16[608,128]{1,0:T(8,128)(2,1)S(1)} %add_convert_fusion.1), channel_id=1, source_target_pairs={{0,8},{4,12},{8,0},{12,4},{1,9},{5,13},{9,1},{13,5},{2,10},{6,14},... | collective-permute-start | bytes 466952 | tf_op jit(solution)/shard_map/ppermute | solution.py:56
  45.8 1.9 %collective-permute-start.12 = (bf16[9,192,96]{2,1,0:T(8,128)(2,1)S(1)}, bf16[9,192,96]{2,1,0:T(8,128)(2,1)S(1)}, u32[]{:S(2)}, u32[]{:S(2)}) collective-permute-start(bf16[9,192,96]{2,1,0:T(8,128)(2,1)S(1)} %get-tuple-element.69), channel_id=1, source_target_pairs={{0,1},{1,0},{2,3},{3,2},{4,5},{5,4},{6,7},{7,6},{8,9},{9,8},{10,11... | collective-permute-start | bytes 995336 | tf_op jit(solution)/shard_map/ppermute | solution.py:56
  47.5 1.4 %collective-permute-start.13 = (bf16[608,128]{1,0:T(8,128)(2,1)S(1)}, bf16[608,128]{1,0:T(8,128)(2,1)S(1)}, u32[]{:S(2)}, u32[]{:S(2)}) collective-permute-start(bf16[608,128]{1,0:T(8,128)(2,1)S(1)} %add_convert_fusion.own_ref), channel_id=1, source_target_pairs={{0,1},{1,0},{2,3},{3,2},{4,5},{5,4},{6,7},{7,6},{8,9},{9,8},{10,11... | collective-permute-start | bytes 466952 | tf_op jit(solution)/shard_map/ppermute | solution.py:56

commit v11 on v10

--- a/solution.py
+++ b/solution.py
@@ -613,8 +613,6 @@
             step *= 2
     for n, (axis, step) in enumerate(steps):
         wire = part.astype(BF16)
-        if n == 1:
-            wire, above = lax.optimization_barrier((wire, above))
         part = wire.astype(F32) + swapped(wire, axis, step).astype(F32)
     map_call = pl.pallas_call(
         map_kernel,
@@ -625,13 +623,15 @@
         cost_estimate=takes(3.5),
         name="agg_map",
     )
-    agg_map = map_call(spread, key, above)
 
     for n in range(1, len(spans) if gather else 0):
+        if n == len(spans) - 1:
+            near, above = lax.optimization_barrier((near, above))
         far, place = widen(n, near, place)
         if n < len(spans) - 1:
             near = jnp.concatenate([near, far], axis=0)
 
+    agg_map = map_call(spread, key, above)
     if gather:
         far, agg_map = lax.optimization_barrier((far, agg_map))
     count = 2 * near.shape[0] if gather else chunks

time: 50.1 us -> 50.1 us (level)
  waiting for transfers between devices: 13.2 us -> 15.1 us
  starting transfers between devices: 19.7 us -> 17.8 us
    ppermute x12, starting transfers between devices: 10.5 us -> 8.59 us  [swapped(): lax.ppermute(value, axis, [(place, place ^ step) for place in range(count)])]
    ppermute x12, waiting for transfers between devices: 8.4 us -> 10.3 us  [swapped(): lax.ppermute(value, axis, [(place, place ^ step) for place in range(count)])]
where the time goes in v11:
time: 50.1 us; the launch traced here: 49.8 us
  starting transfers between devices  17.8 us (36%)
  waiting for transfers between devices  15.1 us (30%)
  Pallas kernels  14.3 us (29%)
  other arithmetic  1.22 us (2%)
  between operations  0.85 us (2%)
    ppermute x12, waiting for transfers between devices, swapped(): lax.ppermute(value, axis, [(place, place ^ step) for place in range(count)])  10.3 us
    ppermute x12, starting transfers between devices, swapped(): lax.ppermute(value, axis, [(place, place ^ step) for place in range(count)])  8.59 us
    all_to_all x1, starting transfers between devices, on_device(): lax.all_to_all(packed, ('slide', 'chan'), split_axis=0, concat_axis=0, ti...  6.46 us
    ppermute x2, waiting for transfers between devices, shifted(): lax.ppermute(value, axis, [(source, source + steps) for source in range(f...  4.84 us
    pallas_call x1, Pallas kernels, on_device(): agg_map = map_call(spread, key, above)  3.5 us
    pallas_call x1, Pallas kernels, on_device(): pl.pallas_call(lambda *refs: back_kernel(*refs, scale=loss_scale), grid=(...  2.95 us
    ppermute x2, starting transfers between devices, shifted(): lax.ppermute(value, axis, [(source, source + steps) for source in range(f...  2.75 us
    pallas_call x1, Pallas kernels, on_device(): pl.pallas_call(stem_kernel, grid=(chunks,), out_shape=(jax.ShapeDtypeStru...  2.25 us
  transfers between devices with their start and end apart: 15, of which 8 were waited for; matrix products, arithmetic and copies ran while one was open for 2% of the time, Pallas kernels for 23%

profile of v11, /device:TPU:0, one launch (start us, length us, event | category | flops | bytes accessed | tf_op | source)
XLA Modules:
  0.0 49.8 jit_solution(8233450276426599516)
XLA Ops:
  0.6 1.9 %pack.1 = (bf16[8,56,128]{2,1,0:T(8,128)(2,1)}, bf16[96,128]{1,0:T(8,128)(2,1)}) custom-call(s32[1,8]{1,0:T(1,128)} %cells_ref.1, bf16[1,8,6144]{2,1,0:T(8,128)(2,1)} %pixels_ref.1, f32[1,16,96,128]{3,2,1,0:T(8,128)} %cot_ref.1), custom_call_target="tpu_custom_call" | custom-call | bytes 5535000 | tf_op jit(solution)/shard_map/pack/pallas_call | solution.py:439
  2.5 6.5 %all-to-all-start = ((bf16[8,56,128]{2,1,0:T(8,128)(2,1)}), bf16[8,56,128]{2,1,0:T(8,128)(2,1)S(1)}, u32[]{:S(2)}, u32[]{:S(2)}) async-start(bf16[8,56,128]{2,1,0:T(8,128)(2,1)} %get-tuple-element.42), calls=%async_computation | async-start | bytes 229376 | tf_op jit(solution)/shard_map/all_to_all | solution.py:462
  9.0 0.5 %collective-permute-start.2 = (bf16[9,192,96]{2,1,0:T(8,128)(2,1)}, bf16[9,192,96]{2,1,0:T(8,128)(2,1)S(1)}, u32[]{:S(2)}, u32[]{:S(2)}) collective-permute-start(bf16[9,192,96]{2,1,0:T(8,128)(2,1)} %refs_1_.1), channel_id=1, source_target_pairs={{0,1},{1,0},{2,3},{3,2},{4,5},{5,4},{6,7},{7,6},{8,9},{9,8},{10,11... | collective-permute-start | bytes 995336 | tf_op jit(solution)/shard_map/ppermute | solution.py:56
  9.5 1.3 %collective-permute-start = (bf16[96,128]{1,0:T(8,128)(2,1)S(1)}, bf16[96,128]{1,0:T(8,128)(2,1)S(1)}, u32[]{:S(2)}, u32[]{:S(2)}) collective-permute-start(bf16[96,128]{1,0:T(8,128)(2,1)S(1)} %copy-done.9), channel_id=1, source_target_pairs={{4,0},{8,4},{12,8},{5,1},{9,5},{13,9},{6,2},{10,6},{14,10},{7,3},{... | collective-permute-start | bytes 73736 | tf_op jit(solution)/shard_map/ppermute | solution.py:51
  10.8 4.8 %collective-permute-done.below_ref = bf16[96,128]{1,0:T(8,128)(2,1)S(1)} collective-permute-done((bf16[96,128]{1,0:T(8,128)(2,1)S(1)}, bf16[96,128]{1,0:T(8,128)(2,1)S(1)}, u32[]{:S(2)}, u32[]{:S(2)}) %collective-permute-start) | collective-permute-done | bytes 24608 | tf_op jit(solution)/shard_map/ppermute | solution.py:51
  15.6 0.0 all-to-all-done.meta_ref.got_ref.refs_5_
  15.6 0.0 copy-start.3
  15.6 0.0 copy-start.4
  15.7 0.0 copy-start.5
  15.7 0.0 copy-start.6
  15.7 0.0 copy-start.7
  15.7 0.0 copy-start.8
  15.7 0.5 patch.1
  16.2 0.0 copy-start.1
  16.2 0.1 collective-permute-start.1
  16.3 0.3 copy-done.2
  16.5 0.0 copy-done.3
  16.6 0.0 copy-done.4
  16.6 2.2 %stem.1 = (bf16[1,192,128]{2,1,0:T(8,128)(2,1)S(1)}, f32[1,512,96]{2,1,0:T(8,128)S(1)}, f32[1,512,1]{2,1,0:T(8,128)S(1)}, f32[1,512,96]{2,1,0:T(8,128)S(1)}, f32...) custom-call(bf16[8,56,128]{2,1,0:T(8,128)(2,1)S(1)} %all-to-all-done, ...), custom_call_target="tpu_custom_call" | custom-call | bytes 9963000 | tf_op jit(solution)/shard_map/stem/pallas_call | solution.py:499
  18.9 0.2 collective-permute-start.5
  19.1 0.0 collective-permute-done.1
  19.1 2.2 %collective-permute-start.4 = (bf16[1,336,128]{2,1,0:T(8,128)(2,1)S(1)}, bf16[1,336,128]{2,1,0:T(8,128)(2,1)S(1)}, u32[]{:S(2)}, u32[]{:S(2)}) collective-permute-start(bf16[1,336,128]{2,1,0:T(8,128)(2,1)S(1)} %pad_maximum_fusion.3), channel_id=1, source_target_pairs={{0,8},{4,12},{8,0},{12,4},{1,9},{5,13},{9,1},{13,5},{2,10},{6,14},... | collective-permute-start | bytes 258056 | tf_op jit(solution)/shard_map/ppermute | solution.py:56
  21.3 0.0 collective-permute-done.2.refs_4_
  21.3 2.9 %stem_back.1 = (f32[608,128]{1,0:T(8,128)S(1)}, bf16[608,128]{1,0:T(8,128)(2,1)S(1)}) custom-call(s32[1]{0:T(128)} %bitcast.chan_ref.refs_0_, bf16[1,72,128]{2,1,0:T(8,128)(2,1)S(1)} %bitcast.17, bf16[1,72,128]{2,1,0:T(8,128)(2,1)S(1)} %bitcast.20, bf16[9,192,96]{2,1,0:T(8,128)(2,1)S(1)} %copy-done.1, ...), custom_call_target="tpu_custom_call" | custom-call | bytes 13653000 | tf_op jit(solution)/shard_map/stem_back/pallas_call | solution.py:567
  24.3 0.1 collective-permute-start.3
  24.4 0.0 collective-permute-done.5
  24.5 1.0 %spread.1 = (f32[144,96]{1,0:T(8,128)S(1)}, f32[96,128]{1,0:T(8,128)S(1)}) custom-call(bf16[2,192,128]{2,1,0:T(8,128)(2,1)S(1)} %pad_maximum_fusion.2.refs_0_, bf16[9,192,96]{2,1,0:T(8,128)(2,1)S(1)} %copy-done.1, f32[144,128]{1,0:T(8,128)S(1)} %get-tuple-element.57.refs_2_.key_ref), custom_call_target="tpu_custom_call" | custom-call | bytes 3690000 | tf_op jit(solution)/shard_map/spread/pallas_call | solution.py:535
  25.5 1.2 %collective-permute-done.4 = bf16[1,336,128]{2,1,0:T(8,128)(2,1)S(1)} collective-permute-done((bf16[1,336,128]{2,1,0:T(8,128)(2,1)S(1)}, bf16[1,336,128]{2,1,0:T(8,128)(2,1)S(1)}, u32[]{:S(2)}, u32[]{:S(2)}) %collective-permute-start.4) | collective-permute-done | bytes 86048 | tf_op jit(solution)/shard_map/ppermute | solution.py:56
  26.7 0.0 collective-permute-done.3
  26.8 1.6 %collective-permute-start.9 = (bf16[608,128]{1,0:T(8,128)(2,1)S(1)}, bf16[608,128]{1,0:T(8,128)(2,1)S(1)}, u32[]{:S(2)}, u32[]{:S(2)}) collective-permute-start(bf16[608,128]{1,0:T(8,128)(2,1)S(1)} %convert_add_fusion.1), channel_id=1, source_target_pairs={{0,2},{2,0},{1,3},{3,1},{4,6},{6,4},{5,7},{7,5},{8,10},{10,8},{9,1... | collective-permute-start | bytes 466952 | tf_op jit(solution)/shard_map/ppermute | solution.py:56
  28.3 1.5 %collective-permute-start.7 = (f32[96,128]{1,0:T(8,128)S(1)}, f32[96,128]{1,0:T(8,128)S(1)}, u32[]{:S(2)}, u32[]{:S(2)}) collective-permute-start(f32[96,128]{1,0:T(8,128)S(1)} %get-tuple-element.61), channel_id=1, source_target_pairs={{0,4},{4,8},{8,12},{1,5},{5,9},{9,13},{2,6},{6,10},{10,14},{3,7},{... | collective-permute-start | bytes 147464 | tf_op jit(solution)/shard_map/ppermute | solution.py:51
  29.8 1.5 %collective-permute-start.6 = (bf16[2,336,128]{2,1,0:T(8,128)(2,1)S(1)}, bf16[2,336,128]{2,1,0:T(8,128)(2,1)S(1)}, u32[]{:S(2)}, u32[]{:S(2)}) collective-permute-start(bf16[2,336,128]{2,1,0:T(8,128)(2,1)S(1)} %pad_maximum_fusion.1), channel_id=1, source_target_pairs={{0,4},{4,0},{8,12},{12,8},{1,5},{5,1},{9,13},{13,9},{2,6},{6,2},{1... | collective-permute-start | bytes 516104 | tf_op jit(solution)/shard_map/ppermute | solution.py:56
  31.3 1.0 %collective-permute-done.9 = bf16[608,128]{1,0:T(8,128)(2,1)S(1)} collective-permute-done((bf16[608,128]{1,0:T(8,128)(2,1)S(1)}, bf16[608,128]{1,0:T(8,128)(2,1)S(1)}, u32[]{:S(2)}, u32[]{:S(2)}) %collective-permute-start.9) | collective-permute-done | bytes 155680 | tf_op jit(solution)/shard_map/ppermute | solution.py:56
  32.4 0.1 collective-permute-start.10
  32.5 4.4 %collective-permute-done.6 = bf16[2,336,128]{2,1,0:T(8,128)(2,1)S(1)} collective-permute-done((bf16[2,336,128]{2,1,0:T(8,128)(2,1)S(1)}, bf16[2,336,128]{2,1,0:T(8,128)(2,1)S(1)}, u32[]{:S(2)}, u32[]{:S(2)}) %collective-permute-start.6) | collective-permute-done | bytes 172064 | tf_op jit(solution)/shard_map/ppermute | solution.py:56
  37.0 0.1 collective-permute-start.8
  37.0 1.6 %collective-permute-done.10 = bf16[608,128]{1,0:T(8,128)(2,1)S(1)} collective-permute-done((bf16[608,128]{1,0:T(8,128)(2,1)S(1)}, bf16[608,128]{1,0:T(8,128)(2,1)S(1)}, u32[]{:S(2)}, u32[]{:S(2)}) %collective-permute-start.10) | collective-permute-done | bytes 155680 | tf_op jit(solution)/shard_map/ppermute | solution.py:56
  38.7 2.1 %collective-permute-start.11 = (bf16[608,128]{1,0:T(8,128)(2,1)S(1)}, bf16[608,128]{1,0:T(8,128)(2,1)S(1)}, u32[]{:S(2)}, u32[]{:S(2)}) collective-permute-start(bf16[608,128]{1,0:T(8,128)(2,1)S(1)} %add_convert_fusion.1), channel_id=1, source_target_pairs={{0,8},{4,12},{8,0},{12,4},{1,9},{5,13},{9,1},{13,5},{2,10},{6,14},... | collective-permute-start | bytes 466952 | tf_op jit(solution)/shard_map/ppermute | solution.py:56
  40.8 3.5 %agg_map.1 = bf16[16,96,128]{2,1,0:T(8,128)(2,1)} custom-call(f32[144,96]{1,0:T(8,128)S(1)} %get-tuple-element.63.y_ref, f32[144,128]{1,0:T(8,128)S(1)} %get-tuple-element.57.refs_2_.key_ref, f32[96,128]{1,0:T(8,128)S(1)} %collective-permute-done.7.above_ref), custom_call_target="tpu_custom_call" | custom-call | bytes 12915000 | tf_op jit(solution)/shard_map/agg_map/pallas_call | solution.py:634
  44.3 0.0 collective-permute-done.8.refs_2_
  44.3 1.4 %agg_weight_grad.1 = (f32[9,192,96]{2,1,0:T(8,128)S(1)}, bf16[9,192,96]{2,1,0:T(8,128)(2,1)S(1)}) custom-call(s32[1]{0:T(128)} %bitcast.9.refs_0_, bf16[4,336,128]{2,1,0:T(8,128)(2,1)S(1)} %pad_maximum_fusion.refs_1_, bf16[4,336,128]{2,1,0:T(8,128)(2,1)S(1)} %collective-permute-done.8.refs_2_), custom_call_target="tpu_custom_call" | custom-call | bytes 5166000 | tf_op jit(solution)/shard_map/agg_weight_grad/pallas_call | solution.py:640
  45.7 0.1 collective-permute-start.12
  45.8 1.6 %collective-permute-done.11 = bf16[608,128]{1,0:T(8,128)(2,1)S(1)} collective-permute-done((bf16[608,128]{1,0:T(8,128)(2,1)S(1)}, bf16[608,128]{1,0:T(8,128)(2,1)S(1)}, u32[]{:S(2)}, u32[]{:S(2)}) %collective-permute-start.11) | collective-permute-done | bytes 155680 | tf_op jit(solution)/shard_map/ppermute | solution.py:56
  47.5 0.1 collective-permute-start.13
  47.5 0.1 collective-permute-done.12
  47.6 1.0 %convert_add_fusion = f32[9,192,96]{2,1,0:T(8,128)} fusion(f32[9,192,96]{2,1,0:T(8,128)S(1)} %get-tuple-element.68, bf16[9,192,96]{2,1,0:T(8,128)(2,1)S(1)} %collective-permute-done.12), kind=kLoop, calls=%fused_computation | loop fusion | flops 331776 | bytes 1658880 | tf_op jit(solution)/shard_map/add | solution.py:662
  48.6 0.3 collective-permute-done.13.peer_ref
  48.9 0.9 %unpack.1 = (f32[49,96]{1,0:T(8,128)}, f32[96,384]{1,0:T(8,128)}, f32[96,384]{1,0:T(8,128)}, f32[192,384]{1,0:T(8,128)}) custom-call(s32[1]{0:T(128)} %bitcast.chan_ref.refs_0_, bf16[608,128]{1,0:T(8,128)(2,1)S(1)} %add_convert_fusion.own_ref, bf16[608,128]{1,0:T(8,128)(2,1)S(1)} %collective-permute-done.13.peer_ref), custom_call_target="tpu_custom_call" | custom-call | bytes 5535000 | tf_op jit(solution)/shard_map/unpack/pallas_call | solution.py:669
  (19 shorter events, 0.3 us)
Async XLA Ops:
  0.6 15.0 %copy-start = (f32[1,16,96,128]{3,2,1,0:T(8,128)S(1)}, f32[1,16,96,128]{3,2,1,0:T(8,128)}, u32[]{:S(2)}) copy-start(f32[1,16,96,128]{3,2,1,0:T(8,128)} %cot_ref.1) | copy-start | bytes 2359300
  2.5 7.0 %copy-start.9 = (bf16[96,128]{1,0:T(8,128)(2,1)S(1)}, bf16[96,128]{1,0:T(8,128)(2,1)}, u32[]{:S(2)}) copy-start(bf16[96,128]{1,0:T(8,128)(2,1)} %get-tuple-element.43) | copy-start | bytes 73732
  2.5 13.1 %all-to-all-start = ((bf16[8,56,128]{2,1,0:T(8,128)(2,1)}), bf16[8,56,128]{2,1,0:T(8,128)(2,1)S(1)}, u32[]{:S(2)}, u32[]{:S(2)}) async-start(bf16[8,56,128]{2,1,0:T(8,128)(2,1)} %get-tuple-element.42), calls=%async_computation | async-start | bytes 229376 | tf_op jit(solution)/shard_map/all_to_all | solution.py:462
  9.0 12.4 %collective-permute-start.2 = (bf16[9,192,96]{2,1,0:T(8,128)(2,1)}, bf16[9,192,96]{2,1,0:T(8,128)(2,1)S(1)}, u32[]{:S(2)}, u32[]{:S(2)}) collective-permute-start(bf16[9,192,96]{2,1,0:T(8,128)(2,1)} %refs_1_.1), channel_id=1, source_target_pairs={{0,1},{1,0},{2,3},{3,2},{4,5},{5,4},{6,7},{7,6},{8,9},{9,8},{10,11... | collective-permute-start | bytes 995336 | tf_op jit(solution)/shard_map/ppermute | solution.py:56
  9.5 6.1 %collective-permute-start = (bf16[96,128]{1,0:T(8,128)(2,1)S(1)}, bf16[96,128]{1,0:T(8,128)(2,1)S(1)}, u32[]{:S(2)}, u32[]{:S(2)}) collective-permute-start(bf16[96,128]{1,0:T(8,128)(2,1)S(1)} %copy-done.9), channel_id=1, source_target_pairs={{4,0},{8,4},{12,8},{5,1},{9,5},{13,9},{6,2},{10,6},{14,10},{7,3},{... | collective-permute-start | bytes 73736 | tf_op jit(solution)/shard_map/ppermute | solution.py:51
  15.6 0.9 %copy-start.2 = (bf16[384,192]{0,1:T(8,128)(2,1)S(1)}, bf16[384,192]{0,1:T(8,128)(2,1)}, u32[]{:S(2)}) copy-start(bf16[384,192]{0,1:T(8,128)(2,1)} %param.20) | copy-start | bytes 442372
  15.6 1.0 %copy-start.3 = (bf16[96,384]{1,0:T(8,128)(2,1)S(1)}, bf16[96,384]{1,0:T(8,128)(2,1)}, u32[]{:S(2)}) copy-start(bf16[96,384]{1,0:T(8,128)(2,1)} %refs_14_.1) | copy-start | bytes 221188
  15.6 1.0 %copy-start.4 = (bf16[384,96]{0,1:T(8,128)(2,1)S(1)}, bf16[384,96]{0,1:T(8,128)(2,1)}, u32[]{:S(2)}) copy-start(bf16[384,96]{0,1:T(8,128)(2,1)} %param.17) | copy-start | bytes 221188
  15.7 1.0 %copy-start.5 = (f32[49,96]{1,0:T(8,128)S(1)}, f32[49,96]{1,0:T(8,128)}, u32[]{:S(2)}) copy-start(f32[49,96]{1,0:T(8,128)} %dw_ref.1) | copy-start | bytes 56452
  15.7 1.0 %copy-start.6 = (f32[96]{0:T(128)S(1)}, f32[96]{0:T(128)}, u32[]{:S(2)}) copy-start(f32[96]{0:T(128)} %param.15) | copy-start | bytes 1156
  15.7 1.0 %copy-start.7 = (f32[96]{0:T(128)S(1)}, f32[96]{0:T(128)}, u32[]{:S(2)}) copy-start(f32[96]{0:T(128)} %param.18) | copy-start | bytes 1156
  15.7 0.9 %copy-start.8 = (f32[96]{0:T(128)S(1)}, f32[96]{0:T(128)}, u32[]{:S(2)}) copy-start(f32[96]{0:T(128)} %param.19) | copy-start | bytes 1156
  16.2 5.2 %copy-start.1 = (bf16[9,192,96]{2,1,0:T(8,128)(2,1)S(1)}, bf16[9,192,96]{2,1,0:T(8,128)(2,1)}, u32[]{:S(2)}) copy-start(bf16[9,192,96]{2,1,0:T(8,128)(2,1)} %refs_1_.1) | copy-start | bytes 995332
  16.2 2.9 %collective-permute-start.1 = (bf16[72,128]{1,0:T(8,128)(2,1)S(1)}, bf16[72,128]{1,0:T(8,128)(2,1)S(1)}, u32[]{:S(2)}, u32[]{:S(2)}) collective-permute-start(bf16[72,128]{1,0:T(8,128)(2,1)S(1)} %get-tuple-element.45), channel_id=1, source_target_pairs={{0,1},{1,0},{2,3},{3,2},{4,5},{5,4},{6,7},{7,6},{8,9},{9,8},{10,11... | collective-permute-start | bytes 55304 | tf_op jit(solution)/shard_map/ppermute | solution.py:56
  18.9 5.6 %collective-permute-start.5 = (bf16[1,192,128]{2,1,0:T(8,128)(2,1)S(1)}, bf16[1,192,128]{2,1,0:T(8,128)(2,1)S(1)}, u32[]{:S(2)}, u32[]{:S(2)}) collective-permute-start(bf16[1,192,128]{2,1,0:T(8,128)(2,1)S(1)} %get-tuple-element.56), channel_id=1, source_target_pairs={{0,1},{1,0},{2,3},{3,2},{4,5},{5,4},{6,7},{7,6},{8,9},{9,8},{10,11... | collective-permute-start | bytes 147464 | tf_op jit(solution)/shard_map/ppermute | solution.py:56
  19.1 7.6 %collective-permute-start.4 = (bf16[1,336,128]{2,1,0:T(8,128)(2,1)S(1)}, bf16[1,336,128]{2,1,0:T(8,128)(2,1)S(1)}, u32[]{:S(2)}, u32[]{:S(2)}) collective-permute-start(bf16[1,336,128]{2,1,0:T(8,128)(2,1)S(1)} %pad_maximum_fusion.3), channel_id=1, source_target_pairs={{0,8},{4,12},{8,0},{12,4},{1,9},{5,13},{9,1},{13,5},{2,10},{6,14},... | collective-permute-start | bytes 258056 | tf_op jit(solution)/shard_map/ppermute | solution.py:56
  24.3 2.4 %collective-permute-start.3 = (bf16[608,128]{1,0:T(8,128)(2,1)S(1)}, bf16[608,128]{1,0:T(8,128)(2,1)S(1)}, u32[]{:S(2)}, u32[]{:S(2)}) collective-permute-start(bf16[608,128]{1,0:T(8,128)(2,1)S(1)} %get-tuple-element.55), channel_id=1, source_target_pairs={{0,1},{1,0},{2,3},{3,2},{4,5},{5,4},{6,7},{7,6},{8,9},{9,8},{10,11... | collective-permute-start | bytes 466952 | tf_op jit(solution)/shard_map/ppermute | solution.py:56
  26.8 5.5 %collective-permute-start.9 = (bf16[608,128]{1,0:T(8,128)(2,1)S(1)}, bf16[608,128]{1,0:T(8,128)(2,1)S(1)}, u32[]{:S(2)}, u32[]{:S(2)}) collective-permute-start(bf16[608,128]{1,0:T(8,128)(2,1)S(1)} %convert_add_fusion.1), channel_id=1, source_target_pairs={{0,2},{2,0},{1,3},{3,1},{4,6},{6,4},{5,7},{7,5},{8,10},{10,8},{9,1... | collective-permute-start | bytes 466952 | tf_op jit(solution)/shard_map/ppermute | solution.py:56
  28.3 8.6 %collective-permute-start.7 = (f32[96,128]{1,0:T(8,128)S(1)}, f32[96,128]{1,0:T(8,128)S(1)}, u32[]{:S(2)}, u32[]{:S(2)}) collective-permute-start(f32[96,128]{1,0:T(8,128)S(1)} %get-tuple-element.61), channel_id=1, source_target_pairs={{0,4},{4,8},{8,12},{1,5},{5,9},{9,13},{2,6},{6,10},{10,14},{3,7},{... | collective-permute-start | bytes 147464 | tf_op jit(solution)/shard_map/ppermute | solution.py:51
  29.8 7.1 %collective-permute-start.6 = (bf16[2,336,128]{2,1,0:T(8,128)(2,1)S(1)}, bf16[2,336,128]{2,1,0:T(8,128)(2,1)S(1)}, u32[]{:S(2)}, u32[]{:S(2)}) collective-permute-start(bf16[2,336,128]{2,1,0:T(8,128)(2,1)S(1)} %pad_maximum_fusion.1), channel_id=1, source_target_pairs={{0,4},{4,0},{8,12},{12,8},{1,5},{5,1},{9,13},{13,9},{2,6},{6,2},{1... | collective-permute-start | bytes 516104 | tf_op jit(solution)/shard_map/ppermute | solution.py:56
  32.4 6.2 %collective-permute-start.10 = (bf16[608,128]{1,0:T(8,128)(2,1)S(1)}, bf16[608,128]{1,0:T(8,128)(2,1)S(1)}, u32[]{:S(2)}, u32[]{:S(2)}) collective-permute-start(bf16[608,128]{1,0:T(8,128)(2,1)S(1)} %add_convert_fusion.2), channel_id=1, source_target_pairs={{0,4},{4,0},{8,12},{12,8},{1,5},{5,1},{9,13},{13,9},{2,6},{6,2},{1... | collective-permute-start | bytes 466952 | tf_op jit(solution)/shard_map/ppermute | solution.py:56
  37.0 7.4 %collective-permute-start.8 = (bf16[4,336,128]{2,1,0:T(8,128)(2,1)S(1)}, bf16[4,336,128]{2,1,0:T(8,128)(2,1)S(1)}, u32[]{:S(2)}, u32[]{:S(2)}) collective-permute-start(bf16[4,336,128]{2,1,0:T(8,128)(2,1)S(1)} %pad_maximum_fusion.refs_1_), channel_id=1, source_target_pairs={{0,2},{2,0},{1,3},{3,1},{4,6},{6,4},{5,7},{7,5},{8,10},{10,8},{9,1... | collective-permute-start | bytes 1032200 | tf_op jit(solution)/shard_map/ppermute | solution.py:56
  38.7 8.7 %collective-permute-start.11 = (bf16[608,128]{1,0:T(8,128)(2,1)S(1)}, bf16[608,128]{1,0:T(8,128)(2,1)S(1)}, u32[]{:S(2)}, u32[]{:S(2)}) collective-permute-start(bf16[608,128]{1,0:T(8,128)(2,1)S(1)} %add_convert_fusion.1), channel_id=1, source_target_pairs={{0,8},{4,12},{8,0},{12,4},{1,9},{5,13},{9,1},{13,5},{2,10},{6,14},... | collective-permute-start | bytes 466952 | tf_op jit(solution)/shard_map/ppermute | solution.py:56
  45.7 1.9 %collective-permute-start.12 = (bf16[9,192,96]{2,1,0:T(8,128)(2,1)S(1)}, bf16[9,192,96]{2,1,0:T(8,128)(2,1)S(1)}, u32[]{:S(2)}, u32[]{:S(2)}) collective-permute-start(bf16[9,192,96]{2,1,0:T(8,128)(2,1)S(1)} %get-tuple-element.69), channel_id=1, source_target_pairs={{0,1},{1,0},{2,3},{3,2},{4,5},{5,4},{6,7},{7,6},{8,9},{9,8},{10,11... | collective-permute-start | bytes 995336 | tf_op jit(solution)/shard_map/ppermute | solution.py:56
  47.5 1.4 %collective-permute-start.13 = (bf16[608,128]{1,0:T(8,128)(2,1)S(1)}, bf16[608,128]{1,0:T(8,128)(2,1)S(1)}, u32[]{:S(2)}, u32[]{:S(2)}) collective-permute-start(bf16[608,128]{1,0:T(8,128)(2,1)S(1)} %add_convert_fusion.own_ref), channel_id=1, source_target_pairs={{0,1},{1,0},{2,3},{3,2},{4,5},{5,4},{6,7},{7,6},{8,9},{9,8},{10,11... | collective-permute-start | bytes 466952 | tf_op jit(solution)/shard_map/ppermute | solution.py:56

commit v12 on v11

--- a/solution.py
+++ b/solution.py
@@ -607,10 +607,8 @@
     above = shifted(below, "slide", 1)
     steps = []
     for axis in ("rep", "slide"):
-        step = 1
-        while step < lax.axis_size(axis):
-            steps.append((axis, step))
-            step *= 2
+        for n in reversed(range(lax.axis_size(axis).bit_length() - 1)):
+            steps.append((axis, 1 << n))
     for n, (axis, step) in enumerate(steps):
         wire = part.astype(BF16)
         part = wire.astype(F32) + swapped(wire, axis, step).astype(F32)

time: 50.1 us -> 50.5 us (level)
  waiting for transfers between devices: 15.1 us -> 16.7 us
  starting transfers between devices: 17.8 us -> 16.5 us
    ppermute x12, waiting for transfers between devices: 10.3 us -> 11.9 us  [swapped(): lax.ppermute(value, axis, [(place, place ^ step) for place in range(count)])]
    ppermute x12, starting transfers between devices: 8.59 us -> 7.31 us  [swapped(): lax.ppermute(value, axis, [(place, place ^ step) for place in range(count)])]
  transfers between devices with their start and end apart: 15 -> 15, of which waited for: 8 -> 7; matrix products, arithmetic and copies ran while one was open for 2% -> 2% of each run, Pallas kernels for 23% -> 23%
where the time goes in v12:
time: 50.5 us; the launch traced here: 50.1 us
  waiting for transfers between devices  16.7 us (33%)
  starting transfers between devices  16.5 us (33%)
  Pallas kernels  14.4 us (29%)
  other arithmetic  1.22 us (2%)
  between operations  0.89 us (2%)
    ppermute x12, waiting for transfers between devices, swapped(): lax.ppermute(value, axis, [(place, place ^ step) for place in range(count)])  11.9 us
    ppermute x12, starting transfers between devices, swapped(): lax.ppermute(value, axis, [(place, place ^ step) for place in range(count)])  7.31 us
    all_to_all x1, starting transfers between devices, on_device(): lax.all_to_all(packed, ('slide', 'chan'), split_axis=0, concat_axis=0, ti...  6.46 us
    ppermute x2, waiting for transfers between devices, shifted(): lax.ppermute(value, axis, [(source, source + steps) for source in range(f...  4.84 us
    pallas_call x1, Pallas kernels, on_device(): agg_map = map_call(spread, key, above)  3.5 us
    pallas_call x1, Pallas kernels, on_device(): pl.pallas_call(lambda *refs: back_kernel(*refs, scale=loss_scale), grid=(...  2.95 us
    ppermute x2, starting transfers between devices, shifted(): lax.ppermute(value, axis, [(source, source + steps) for source in range(f...  2.75 us
    pallas_call x1, Pallas kernels, on_device(): pl.pallas_call(stem_kernel, grid=(chunks,), out_shape=(jax.ShapeDtypeStru...  2.25 us
  transfers between devices with their start and end apart: 15, of which 7 were waited for; matrix products, arithmetic and copies ran while one was open for 2% of the time, Pallas kernels for 23%

profile of v12, /device:TPU:0, one launch (start us, length us, event | category | flops | bytes accessed | tf_op | source)
XLA Modules:
  0.0 50.1 jit_solution(17117224074190134668)
XLA Ops:
  0.6 1.9 %pack.1 = (bf16[8,56,128]{2,1,0:T(8,128)(2,1)}, bf16[96,128]{1,0:T(8,128)(2,1)}) custom-call(s32[1,8]{1,0:T(1,128)} %cells_ref.1, bf16[1,8,6144]{2,1,0:T(8,128)(2,1)} %pixels_ref.1, f32[1,16,96,128]{3,2,1,0:T(8,128)} %cot_ref.1), custom_call_target="tpu_custom_call" | custom-call | bytes 5535000 | tf_op jit(solution)/shard_map/pack/pallas_call | solution.py:439
  2.5 6.5 %all-to-all-start = ((bf16[8,56,128]{2,1,0:T(8,128)(2,1)}), bf16[8,56,128]{2,1,0:T(8,128)(2,1)S(1)}, u32[]{:S(2)}, u32[]{:S(2)}) async-start(bf16[8,56,128]{2,1,0:T(8,128)(2,1)} %get-tuple-element.42), calls=%async_computation | async-start | bytes 229376 | tf_op jit(solution)/shard_map/all_to_all | solution.py:462
  9.0 0.5 %collective-permute-start.2 = (bf16[9,192,96]{2,1,0:T(8,128)(2,1)}, bf16[9,192,96]{2,1,0:T(8,128)(2,1)S(1)}, u32[]{:S(2)}, u32[]{:S(2)}) collective-permute-start(bf16[9,192,96]{2,1,0:T(8,128)(2,1)} %refs_1_.1), channel_id=1, source_target_pairs={{0,1},{1,0},{2,3},{3,2},{4,5},{5,4},{6,7},{7,6},{8,9},{9,8},{10,11... | collective-permute-start | bytes 995336 | tf_op jit(solution)/shard_map/ppermute | solution.py:56
  9.5 1.3 %collective-permute-start = (bf16[96,128]{1,0:T(8,128)(2,1)S(1)}, bf16[96,128]{1,0:T(8,128)(2,1)S(1)}, u32[]{:S(2)}, u32[]{:S(2)}) collective-permute-start(bf16[96,128]{1,0:T(8,128)(2,1)S(1)} %copy-done.9), channel_id=1, source_target_pairs={{4,0},{8,4},{12,8},{5,1},{9,5},{13,9},{6,2},{10,6},{14,10},{7,3},{... | collective-permute-start | bytes 73736 | tf_op jit(solution)/shard_map/ppermute | solution.py:51
  10.8 4.8 %collective-permute-done.below_ref = bf16[96,128]{1,0:T(8,128)(2,1)S(1)} collective-permute-done((bf16[96,128]{1,0:T(8,128)(2,1)S(1)}, bf16[96,128]{1,0:T(8,128)(2,1)S(1)}, u32[]{:S(2)}, u32[]{:S(2)}) %collective-permute-start) | collective-permute-done | bytes 24608 | tf_op jit(solution)/shard_map/ppermute | solution.py:51
  15.6 0.0 all-to-all-done.meta_ref.got_ref.refs_5_
  15.6 0.0 copy-start.3
  15.6 0.0 copy-start.4
  15.7 0.0 copy-start.5
  15.7 0.0 copy-start.6
  15.7 0.0 copy-start.7
  15.7 0.0 copy-start.8
  15.7 0.5 patch.1
  16.2 0.0 copy-start.1
  16.2 0.1 collective-permute-start.1
  16.3 0.3 copy-done.2
  16.5 0.0 copy-done.3
  16.6 0.0 copy-done.4
  16.6 2.2 %stem.1 = (bf16[1,192,128]{2,1,0:T(8,128)(2,1)S(1)}, f32[1,512,96]{2,1,0:T(8,128)S(1)}, f32[1,512,1]{2,1,0:T(8,128)S(1)}, f32[1,512,96]{2,1,0:T(8,128)S(1)}, f32...) custom-call(bf16[8,56,128]{2,1,0:T(8,128)(2,1)S(1)} %all-to-all-done, ...), custom_call_target="tpu_custom_call" | custom-call | bytes 9963000 | tf_op jit(solution)/shard_map/stem/pallas_call | solution.py:499
  18.9 0.2 collective-permute-start.5
  19.1 0.0 collective-permute-done.1
  19.1 2.2 %collective-permute-start.4 = (bf16[1,336,128]{2,1,0:T(8,128)(2,1)S(1)}, bf16[1,336,128]{2,1,0:T(8,128)(2,1)S(1)}, u32[]{:S(2)}, u32[]{:S(2)}) collective-permute-start(bf16[1,336,128]{2,1,0:T(8,128)(2,1)S(1)} %pad_maximum_fusion.3), channel_id=1, source_target_pairs={{0,8},{4,12},{8,0},{12,4},{1,9},{5,13},{9,1},{13,5},{2,10},{6,14},... | collective-permute-start | bytes 258056 | tf_op jit(solution)/shard_map/ppermute | solution.py:56
  21.3 0.0 collective-permute-done.2.refs_4_
  21.4 2.9 %stem_back.1 = (f32[608,128]{1,0:T(8,128)S(1)}, bf16[608,128]{1,0:T(8,128)(2,1)S(1)}) custom-call(s32[1]{0:T(128)} %bitcast.chan_ref.refs_0_, bf16[1,72,128]{2,1,0:T(8,128)(2,1)S(1)} %bitcast.17, bf16[1,72,128]{2,1,0:T(8,128)(2,1)S(1)} %bitcast.20, bf16[9,192,96]{2,1,0:T(8,128)(2,1)S(1)} %copy-done.1, ...), custom_call_target="tpu_custom_call" | custom-call | bytes 13653000 | tf_op jit(solution)/shard_map/stem_back/pallas_call | solution.py:567
  24.3 0.1 collective-permute-start.3
  24.4 0.0 collective-permute-done.5
  24.5 1.0 %spread.1 = (f32[144,96]{1,0:T(8,128)S(1)}, f32[96,128]{1,0:T(8,128)S(1)}) custom-call(bf16[2,192,128]{2,1,0:T(8,128)(2,1)S(1)} %pad_maximum_fusion.2.refs_0_, bf16[9,192,96]{2,1,0:T(8,128)(2,1)S(1)} %copy-done.1, f32[144,128]{1,0:T(8,128)S(1)} %get-tuple-element.57.refs_2_.key_ref), custom_call_target="tpu_custom_call" | custom-call | bytes 3690000 | tf_op jit(solution)/shard_map/spread/pallas_call | solution.py:535
  25.5 1.2 %collective-permute-done.4 = bf16[1,336,128]{2,1,0:T(8,128)(2,1)S(1)} collective-permute-done((bf16[1,336,128]{2,1,0:T(8,128)(2,1)S(1)}, bf16[1,336,128]{2,1,0:T(8,128)(2,1)S(1)}, u32[]{:S(2)}, u32[]{:S(2)}) %collective-permute-start.4) | collective-permute-done | bytes 86048 | tf_op jit(solution)/shard_map/ppermute | solution.py:56
  26.7 0.0 collective-permute-done.3
  26.8 1.6 %collective-permute-start.9 = (bf16[608,128]{1,0:T(8,128)(2,1)S(1)}, bf16[608,128]{1,0:T(8,128)(2,1)S(1)}, u32[]{:S(2)}, u32[]{:S(2)}) collective-permute-start(bf16[608,128]{1,0:T(8,128)(2,1)S(1)} %convert_add_fusion.1), channel_id=1, source_target_pairs={{0,2},{2,0},{1,3},{3,1},{4,6},{6,4},{5,7},{7,5},{8,10},{10,8},{9,1... | collective-permute-start | bytes 466952 | tf_op jit(solution)/shard_map/ppermute | solution.py:56
  28.3 1.5 %collective-permute-start.7 = (f32[96,128]{1,0:T(8,128)S(1)}, f32[96,128]{1,0:T(8,128)S(1)}, u32[]{:S(2)}, u32[]{:S(2)}) collective-permute-start(f32[96,128]{1,0:T(8,128)S(1)} %get-tuple-element.61), channel_id=1, source_target_pairs={{0,4},{4,8},{8,12},{1,5},{5,9},{9,13},{2,6},{6,10},{10,14},{3,7},{... | collective-permute-start | bytes 147464 | tf_op jit(solution)/shard_map/ppermute | solution.py:51
  29.8 1.5 %collective-permute-start.6 = (bf16[2,336,128]{2,1,0:T(8,128)(2,1)S(1)}, bf16[2,336,128]{2,1,0:T(8,128)(2,1)S(1)}, u32[]{:S(2)}, u32[]{:S(2)}) collective-permute-start(bf16[2,336,128]{2,1,0:T(8,128)(2,1)S(1)} %pad_maximum_fusion.1), channel_id=1, source_target_pairs={{0,4},{4,0},{8,12},{12,8},{1,5},{5,1},{9,13},{13,9},{2,6},{6,2},{1... | collective-permute-start | bytes 516104 | tf_op jit(solution)/shard_map/ppermute | solution.py:56
  31.3 1.0 %collective-permute-done.9 = bf16[608,128]{1,0:T(8,128)(2,1)S(1)} collective-permute-done((bf16[608,128]{1,0:T(8,128)(2,1)S(1)}, bf16[608,128]{1,0:T(8,128)(2,1)S(1)}, u32[]{:S(2)}, u32[]{:S(2)}) %collective-permute-start.9) | collective-permute-done | bytes 155680 | tf_op jit(solution)/shard_map/ppermute | solution.py:56
  32.4 0.5 %collective-permute-start.10 = (bf16[608,128]{1,0:T(8,128)(2,1)S(1)}, bf16[608,128]{1,0:T(8,128)(2,1)S(1)}, u32[]{:S(2)}, u32[]{:S(2)}) collective-permute-start(bf16[608,128]{1,0:T(8,128)(2,1)S(1)} %add_convert_fusion.2), channel_id=1, source_target_pairs={{0,8},{4,12},{8,0},{12,4},{1,9},{5,13},{9,1},{13,5},{2,10},{6,14},... | collective-permute-start | bytes 466952 | tf_op jit(solution)/shard_map/ppermute | solution.py:56
  32.9 4.0 %collective-permute-done.6 = bf16[2,336,128]{2,1,0:T(8,128)(2,1)S(1)} collective-permute-done((bf16[2,336,128]{2,1,0:T(8,128)(2,1)S(1)}, bf16[2,336,128]{2,1,0:T(8,128)(2,1)S(1)}, u32[]{:S(2)}, u32[]{:S(2)}) %collective-permute-start.6) | collective-permute-done | bytes 172064 | tf_op jit(solution)/shard_map/ppermute | solution.py:56
  37.0 0.1 collective-permute-start.8
  37.0 4.3 %collective-permute-done.10 = bf16[608,128]{1,0:T(8,128)(2,1)S(1)} collective-permute-done((bf16[608,128]{1,0:T(8,128)(2,1)S(1)}, bf16[608,128]{1,0:T(8,128)(2,1)S(1)}, u32[]{:S(2)}, u32[]{:S(2)}) %collective-permute-start.10) | collective-permute-done | bytes 155680 | tf_op jit(solution)/shard_map/ppermute | solution.py:56
  41.4 0.1 collective-permute-start.11
  41.5 3.5 %agg_map.1 = bf16[16,96,128]{2,1,0:T(8,128)(2,1)} custom-call(f32[144,96]{1,0:T(8,128)S(1)} %get-tuple-element.63.y_ref, f32[144,128]{1,0:T(8,128)S(1)} %get-tuple-element.57.refs_2_.key_ref, f32[96,128]{1,0:T(8,128)S(1)} %collective-permute-done.7.above_ref), custom_call_target="tpu_custom_call" | custom-call | bytes 12915000 | tf_op jit(solution)/shard_map/agg_map/pallas_call | solution.py:632
  45.0 0.0 collective-permute-done.8.refs_2_
  45.0 1.4 %agg_weight_grad.1 = (f32[9,192,96]{2,1,0:T(8,128)S(1)}, bf16[9,192,96]{2,1,0:T(8,128)(2,1)S(1)}) custom-call(s32[1]{0:T(128)} %bitcast.9.refs_0_, bf16[4,336,128]{2,1,0:T(8,128)(2,1)S(1)} %pad_maximum_fusion.refs_1_, bf16[4,336,128]{2,1,0:T(8,128)(2,1)S(1)} %collective-permute-done.8.refs_2_), custom_call_target="tpu_custom_call" | custom-call | bytes 5166000 | tf_op jit(solution)/shard_map/agg_weight_grad/pallas_call | solution.py:638
  46.4 0.1 collective-permute-start.12
  46.5 0.2 collective-permute-done.11
  46.7 0.4 collective-permute-start.13
  47.1 1.2 %collective-permute-done.12 = bf16[9,192,96]{2,1,0:T(8,128)(2,1)S(1)} collective-permute-done((bf16[9,192,96]{2,1,0:T(8,128)(2,1)S(1)}, bf16[9,192,96]{2,1,0:T(8,128)(2,1)S(1)}, u32[]{:S(2)}, u32[]{:S(2)}) %collective-permute-start.12) | collective-permute-done | bytes 331808 | tf_op jit(solution)/shard_map/ppermute | solution.py:56
  48.3 1.0 %convert_add_fusion = f32[9,192,96]{2,1,0:T(8,128)} fusion(f32[9,192,96]{2,1,0:T(8,128)S(1)} %get-tuple-element.68, bf16[9,192,96]{2,1,0:T(8,128)(2,1)S(1)} %collective-permute-done.12), kind=kLoop, calls=%fused_computation | loop fusion | flops 331776 | bytes 1658880 | tf_op jit(solution)/shard_map/add | solution.py:660
  49.3 0.0 collective-permute-done.13.peer_ref
  49.3 0.9 %unpack.1 = (f32[49,96]{1,0:T(8,128)}, f32[96,384]{1,0:T(8,128)}, f32[96,384]{1,0:T(8,128)}, f32[192,384]{1,0:T(8,128)}) custom-call(s32[1]{0:T(128)} %bitcast.chan_ref.refs_0_, bf16[608,128]{1,0:T(8,128)(2,1)S(1)} %add_convert_fusion.own_ref, bf16[608,128]{1,0:T(8,128)(2,1)S(1)} %collective-permute-done.13.peer_ref), custom_call_target="tpu_custom_call" | custom-call | bytes 5535000 | tf_op jit(solution)/shard_map/unpack/pallas_call | solution.py:667
  (19 shorter events, 0.3 us)
Async XLA Ops:
  0.6 15.0 %copy-start = (f32[1,16,96,128]{3,2,1,0:T(8,128)S(1)}, f32[1,16,96,128]{3,2,1,0:T(8,128)}, u32[]{:S(2)}) copy-start(f32[1,16,96,128]{3,2,1,0:T(8,128)} %cot_ref.1) | copy-start | bytes 2359300
  2.5 7.0 %copy-start.9 = (bf16[96,128]{1,0:T(8,128)(2,1)S(1)}, bf16[96,128]{1,0:T(8,128)(2,1)}, u32[]{:S(2)}) copy-start(bf16[96,128]{1,0:T(8,128)(2,1)} %get-tuple-element.43) | copy-start | bytes 73732
  2.5 13.1 %all-to-all-start = ((bf16[8,56,128]{2,1,0:T(8,128)(2,1)}), bf16[8,56,128]{2,1,0:T(8,128)(2,1)S(1)}, u32[]{:S(2)}, u32[]{:S(2)}) async-start(bf16[8,56,128]{2,1,0:T(8,128)(2,1)} %get-tuple-element.42), calls=%async_computation | async-start | bytes 229376 | tf_op jit(solution)/shard_map/all_to_all | solution.py:462
  9.0 12.4 %collective-permute-start.2 = (bf16[9,192,96]{2,1,0:T(8,128)(2,1)}, bf16[9,192,96]{2,1,0:T(8,128)(2,1)S(1)}, u32[]{:S(2)}, u32[]{:S(2)}) collective-permute-start(bf16[9,192,96]{2,1,0:T(8,128)(2,1)} %refs_1_.1), channel_id=1, source_target_pairs={{0,1},{1,0},{2,3},{3,2},{4,5},{5,4},{6,7},{7,6},{8,9},{9,8},{10,11... | collective-permute-start | bytes 995336 | tf_op jit(solution)/shard_map/ppermute | solution.py:56
  9.5 6.1 %collective-permute-start = (bf16[96,128]{1,0:T(8,128)(2,1)S(1)}, bf16[96,128]{1,0:T(8,128)(2,1)S(1)}, u32[]{:S(2)}, u32[]{:S(2)}) collective-permute-start(bf16[96,128]{1,0:T(8,128)(2,1)S(1)} %copy-done.9), channel_id=1, source_target_pairs={{4,0},{8,4},{12,8},{5,1},{9,5},{13,9},{6,2},{10,6},{14,10},{7,3},{... | collective-permute-start | bytes 73736 | tf_op jit(solution)/shard_map/ppermute | solution.py:51
  15.6 0.9 %copy-start.2 = (bf16[384,192]{0,1:T(8,128)(2,1)S(1)}, bf16[384,192]{0,1:T(8,128)(2,1)}, u32[]{:S(2)}) copy-start(bf16[384,192]{0,1:T(8,128)(2,1)} %param.20) | copy-start | bytes 442372
  15.6 1.0 %copy-start.3 = (bf16[96,384]{1,0:T(8,128)(2,1)S(1)}, bf16[96,384]{1,0:T(8,128)(2,1)}, u32[]{:S(2)}) copy-start(bf16[96,384]{1,0:T(8,128)(2,1)} %refs_14_.1) | copy-start | bytes 221188
  15.6 1.0 %copy-start.4 = (bf16[384,96]{0,1:T(8,128)(2,1)S(1)}, bf16[384,96]{0,1:T(8,128)(2,1)}, u32[]{:S(2)}) copy-start(bf16[384,96]{0,1:T(8,128)(2,1)} %param.17) | copy-start | bytes 221188
  15.7 1.0 %copy-start.5 = (f32[49,96]{1,0:T(8,128)S(1)}, f32[49,96]{1,0:T(8,128)}, u32[]{:S(2)}) copy-start(f32[49,96]{1,0:T(8,128)} %dw_ref.1) | copy-start | bytes 56452
  15.7 1.0 %copy-start.6 = (f32[96]{0:T(128)S(1)}, f32[96]{0:T(128)}, u32[]{:S(2)}) copy-start(f32[96]{0:T(128)} %param.15) | copy-start | bytes 1156
  15.7 1.0 %copy-start.7 = (f32[96]{0:T(128)S(1)}, f32[96]{0:T(128)}, u32[]{:S(2)}) copy-start(f32[96]{0:T(128)} %param.18) | copy-start | bytes 1156
  15.7 0.9 %copy-start.8 = (f32[96]{0:T(128)S(1)}, f32[96]{0:T(128)}, u32[]{:S(2)}) copy-start(f32[96]{0:T(128)} %param.19) | copy-start | bytes 1156
  16.2 5.2 %copy-start.1 = (bf16[9,192,96]{2,1,0:T(8,128)(2,1)S(1)}, bf16[9,192,96]{2,1,0:T(8,128)(2,1)}, u32[]{:S(2)}) copy-start(bf16[9,192,96]{2,1,0:T(8,128)(2,1)} %refs_1_.1) | copy-start | bytes 995332
  16.2 2.9 %collective-permute-start.1 = (bf16[72,128]{1,0:T(8,128)(2,1)S(1)}, bf16[72,128]{1,0:T(8,128)(2,1)S(1)}, u32[]{:S(2)}, u32[]{:S(2)}) collective-permute-start(bf16[72,128]{1,0:T(8,128)(2,1)S(1)} %get-tuple-element.45), channel_id=1, source_target_pairs={{0,1},{1,0},{2,3},{3,2},{4,5},{5,4},{6,7},{7,6},{8,9},{9,8},{10,11... | collective-permute-start | bytes 55304 | tf_op jit(solution)/shard_map/ppermute | solution.py:56
  18.9 5.6 %collective-permute-start.5 = (bf16[1,192,128]{2,1,0:T(8,128)(2,1)S(1)}, bf16[1,192,128]{2,1,0:T(8,128)(2,1)S(1)}, u32[]{:S(2)}, u32[]{:S(2)}) collective-permute-start(bf16[1,192,128]{2,1,0:T(8,128)(2,1)S(1)} %get-tuple-element.56), channel_id=1, source_target_pairs={{0,1},{1,0},{2,3},{3,2},{4,5},{5,4},{6,7},{7,6},{8,9},{9,8},{10,11... | collective-permute-start | bytes 147464 | tf_op jit(solution)/shard_map/ppermute | solution.py:56
  19.1 7.6 %collective-permute-start.4 = (bf16[1,336,128]{2,1,0:T(8,128)(2,1)S(1)}, bf16[1,336,128]{2,1,0:T(8,128)(2,1)S(1)}, u32[]{:S(2)}, u32[]{:S(2)}) collective-permute-start(bf16[1,336,128]{2,1,0:T(8,128)(2,1)S(1)} %pad_maximum_fusion.3), channel_id=1, source_target_pairs={{0,8},{4,12},{8,0},{12,4},{1,9},{5,13},{9,1},{13,5},{2,10},{6,14},... | collective-permute-start | bytes 258056 | tf_op jit(solution)/shard_map/ppermute | solution.py:56
  24.3 2.4 %collective-permute-start.3 = (bf16[608,128]{1,0:T(8,128)(2,1)S(1)}, bf16[608,128]{1,0:T(8,128)(2,1)S(1)}, u32[]{:S(2)}, u32[]{:S(2)}) collective-permute-start(bf16[608,128]{1,0:T(8,128)(2,1)S(1)} %get-tuple-element.55), channel_id=1, source_target_pairs={{0,1},{1,0},{2,3},{3,2},{4,5},{5,4},{6,7},{7,6},{8,9},{9,8},{10,11... | collective-permute-start | bytes 466952 | tf_op jit(solution)/shard_map/ppermute | solution.py:56
  26.8 5.5 %collective-permute-start.9 = (bf16[608,128]{1,0:T(8,128)(2,1)S(1)}, bf16[608,128]{1,0:T(8,128)(2,1)S(1)}, u32[]{:S(2)}, u32[]{:S(2)}) collective-permute-start(bf16[608,128]{1,0:T(8,128)(2,1)S(1)} %convert_add_fusion.1), channel_id=1, source_target_pairs={{0,2},{2,0},{1,3},{3,1},{4,6},{6,4},{5,7},{7,5},{8,10},{10,8},{9,1... | collective-permute-start | bytes 466952 | tf_op jit(solution)/shard_map/ppermute | solution.py:56
  28.3 8.6 %collective-permute-start.7 = (f32[96,128]{1,0:T(8,128)S(1)}, f32[96,128]{1,0:T(8,128)S(1)}, u32[]{:S(2)}, u32[]{:S(2)}) collective-permute-start(f32[96,128]{1,0:T(8,128)S(1)} %get-tuple-element.61), channel_id=1, source_target_pairs={{0,4},{4,8},{8,12},{1,5},{5,9},{9,13},{2,6},{6,10},{10,14},{3,7},{... | collective-permute-start | bytes 147464 | tf_op jit(solution)/shard_map/ppermute | solution.py:51
  29.8 7.1 %collective-permute-start.6 = (bf16[2,336,128]{2,1,0:T(8,128)(2,1)S(1)}, bf16[2,336,128]{2,1,0:T(8,128)(2,1)S(1)}, u32[]{:S(2)}, u32[]{:S(2)}) collective-permute-start(bf16[2,336,128]{2,1,0:T(8,128)(2,1)S(1)} %pad_maximum_fusion.1), channel_id=1, source_target_pairs={{0,4},{4,0},{8,12},{12,8},{1,5},{5,1},{9,13},{13,9},{2,6},{6,2},{1... | collective-permute-start | bytes 516104 | tf_op jit(solution)/shard_map/ppermute | solution.py:56
  32.4 9.0 %collective-permute-start.10 = (bf16[608,128]{1,0:T(8,128)(2,1)S(1)}, bf16[608,128]{1,0:T(8,128)(2,1)S(1)}, u32[]{:S(2)}, u32[]{:S(2)}) collective-permute-start(bf16[608,128]{1,0:T(8,128)(2,1)S(1)} %add_convert_fusion.2), channel_id=1, source_target_pairs={{0,8},{4,12},{8,0},{12,4},{1,9},{5,13},{9,1},{13,5},{2,10},{6,14},... | collective-permute-start | bytes 466952 | tf_op jit(solution)/shard_map/ppermute | solution.py:56
  37.0 8.1 %collective-permute-start.8 = (bf16[4,336,128]{2,1,0:T(8,128)(2,1)S(1)}, bf16[4,336,128]{2,1,0:T(8,128)(2,1)S(1)}, u32[]{:S(2)}, u32[]{:S(2)}) collective-permute-start(bf16[4,336,128]{2,1,0:T(8,128)(2,1)S(1)} %pad_maximum_fusion.refs_1_), channel_id=1, source_target_pairs={{0,2},{2,0},{1,3},{3,1},{4,6},{6,4},{5,7},{7,5},{8,10},{10,8},{9,1... | collective-permute-start | bytes 1032200 | tf_op jit(solution)/shard_map/ppermute | solution.py:56
  41.4 5.3 %collective-permute-start.11 = (bf16[608,128]{1,0:T(8,128)(2,1)S(1)}, bf16[608,128]{1,0:T(8,128)(2,1)S(1)}, u32[]{:S(2)}, u32[]{:S(2)}) collective-permute-start(bf16[608,128]{1,0:T(8,128)(2,1)S(1)} %add_convert_fusion.1), channel_id=1, source_target_pairs={{0,4},{4,0},{8,12},{12,8},{1,5},{5,1},{9,13},{13,9},{2,6},{6,2},{1... | collective-permute-start | bytes 466952 | tf_op jit(solution)/shard_map/ppermute | solution.py:56
  46.4 1.9 %collective-permute-start.12 = (bf16[9,192,96]{2,1,0:T(8,128)(2,1)S(1)}, bf16[9,192,96]{2,1,0:T(8,128)(2,1)S(1)}, u32[]{:S(2)}, u32[]{:S(2)}) collective-permute-start(bf16[9,192,96]{2,1,0:T(8,128)(2,1)S(1)} %get-tuple-element.69), channel_id=1, source_target_pairs={{0,1},{1,0},{2,3},{3,2},{4,5},{5,4},{6,7},{7,6},{8,9},{9,8},{10,11... | collective-permute-start | bytes 995336 | tf_op jit(solution)/shard_map/ppermute | solution.py:56
  46.7 2.6 %collective-permute-start.13 = (bf16[608,128]{1,0:T(8,128)(2,1)S(1)}, bf16[608,128]{1,0:T(8,128)(2,1)S(1)}, u32[]{:S(2)}, u32[]{:S(2)}) collective-permute-start(bf16[608,128]{1,0:T(8,128)(2,1)S(1)} %add_convert_fusion.own_ref), channel_id=1, source_target_pairs={{0,1},{1,0},{2,3},{3,2},{4,5},{5,4},{6,7},{7,6},{8,9},{9,8},{10,11... | collective-permute-start | bytes 466952 | tf_op jit(solution)/shard_map/ppermute | solution.py:56

commit v13 on v12

--- a/solution.py
+++ b/solution.py
@@ -605,13 +605,12 @@
     if gather:
         part, near, spread, below = lax.optimization_barrier((part, near, spread, below))
     above = shifted(below, "slide", 1)
-    steps = []
-    for axis in ("rep", "slide"):
-        for n in reversed(range(lax.axis_size(axis).bit_length() - 1)):
-            steps.append((axis, 1 << n))
-    for n, (axis, step) in enumerate(steps):
-        wire = part.astype(BF16)
-        part = wire.astype(F32) + swapped(wire, axis, step).astype(F32)
+    for n in range(1, len(spans) if gather else 0):
+        if n == len(spans) - 1:
+            near, above = lax.optimization_barrier((near, above))
+        far, place = widen(n, near, place)
+        if n < len(spans) - 1:
+            near = jnp.concatenate([near, far], axis=0)
     map_call = pl.pallas_call(
         map_kernel,
         out_shape=jax.ShapeDtypeStruct((out_rows, e_half, cols), BF16),
@@ -621,17 +620,18 @@
         cost_estimate=takes(3.5),
         name="agg_map",
     )
-
-    for n in range(1, len(spans) if gather else 0):
-        if n == len(spans) - 1:
-            near, above = lax.optimization_barrier((near, above))
-        far, place = widen(n, near, place)
-        if n < len(spans) - 1:
-            near = jnp.concatenate([near, far], axis=0)
-
     agg_map = map_call(spread, key, above)
-    if gather:
-        far, agg_map = lax.optimization_barrier((far, agg_map))
+
+    steps = []
+    for axis in ("rep", "slide"):
+        for n in reversed(range(lax.axis_size(axis).bit_length() - 1)):
+            steps.append((axis, 1 << n))
+    for n, (axis, step) in enumerate(steps):
+        wire = part.astype(BF16)
+        if n == len(steps) - 1:
+            wire, agg_map = lax.optimization_barrier((wire, agg_map))
+        part = wire.astype(F32) + swapped(wire, axis, step).astype(F32)
+
     count = 2 * near.shape[0] if gather else chunks
     per = count if gather else 1
     near_count = near.shape[0] if gather else 1

time: 50.5 us -> 49.7 us (0.984)
  waiting for transfers between devices: 16.7 us -> 15 us
  starting transfers between devices: 16.5 us -> 17.5 us
    ppermute x12, waiting for transfers between devices: 11.9 us -> 10.2 us  [swapped(): lax.ppermute(value, axis, [(place, place ^ step) for place in range(count)])]
    ppermute x12, starting transfers between devices: 7.31 us -> 8.32 us  [swapped(): lax.ppermute(value, axis, [(place, place ^ step) for place in range(count)])]
  transfers between devices with their start and end apart: 15 -> 15, of which waited for: 7 -> 8; matrix products, arithmetic and copies ran while one was open for 2% -> 2% of each run, Pallas kernels for 23% -> 23%
where the time goes in v13:
time: 49.7 us; the launch traced here: 49.3 us
  starting transfers between devices  17.5 us (35%)
  waiting for transfers between devices  15 us (30%)
  Pallas kernels  14.3 us (29%)
  other arithmetic  1.22 us (2%)
  between operations  0.85 us (2%)
    ppermute x12, waiting for transfers between devices, swapped(): lax.ppermute(value, axis, [(place, place ^ step) for place in range(count)])  10.2 us
    ppermute x12, starting transfers between devices, swapped(): lax.ppermute(value, axis, [(place, place ^ step) for place in range(count)])  8.32 us
    all_to_all x1, starting transfers between devices, on_device(): lax.all_to_all(packed, ('slide', 'chan'), split_axis=0, concat_axis=0, ti...  6.46 us
    ppermute x2, waiting for transfers between devices, shifted(): lax.ppermute(value, axis, [(source, source + steps) for source in range(f...  4.84 us
    pallas_call x1, Pallas kernels, on_device(): agg_map = map_call(spread, key, above)  3.5 us
    pallas_call x1, Pallas kernels, on_device(): pl.pallas_call(lambda *refs: back_kernel(*refs, scale=loss_scale), grid=(...  2.88 us
    ppermute x2, starting transfers between devices, shifted(): lax.ppermute(value, axis, [(source, source + steps) for source in range(f...  2.75 us
    pallas_call x1, Pallas kernels, on_device(): pl.pallas_call(stem_kernel, grid=(chunks,), out_shape=(jax.ShapeDtypeStru...  2.25 us
  transfers between devices with their start and end apart: 15, of which 8 were waited for; matrix products, arithmetic and copies ran while one was open for 2% of the time, Pallas kernels for 23%

profile of v13, /device:TPU:0, one launch (start us, length us, event | category | flops | bytes accessed | tf_op | source)
XLA Modules:
  0.0 49.3 jit_solution(17419048703912536823)
XLA Ops:
  0.6 1.9 %pack.1 = (bf16[8,56,128]{2,1,0:T(8,128)(2,1)}, bf16[96,128]{1,0:T(8,128)(2,1)}) custom-call(s32[1,8]{1,0:T(1,128)} %cells_ref.1, bf16[1,8,6144]{2,1,0:T(8,128)(2,1)} %pixels_ref.1, f32[1,16,96,128]{3,2,1,0:T(8,128)} %cot_ref.1), custom_call_target="tpu_custom_call" | custom-call | bytes 5535000 | tf_op jit(solution)/shard_map/pack/pallas_call | solution.py:439
  2.5 6.5 %all-to-all-start = ((bf16[8,56,128]{2,1,0:T(8,128)(2,1)}), bf16[8,56,128]{2,1,0:T(8,128)(2,1)S(1)}, u32[]{:S(2)}, u32[]{:S(2)}) async-start(bf16[8,56,128]{2,1,0:T(8,128)(2,1)} %get-tuple-element.42), calls=%async_computation | async-start | bytes 229376 | tf_op jit(solution)/shard_map/all_to_all | solution.py:462
  9.0 0.5 %collective-permute-start.2 = (bf16[9,192,96]{2,1,0:T(8,128)(2,1)}, bf16[9,192,96]{2,1,0:T(8,128)(2,1)S(1)}, u32[]{:S(2)}, u32[]{:S(2)}) collective-permute-start(bf16[9,192,96]{2,1,0:T(8,128)(2,1)} %refs_1_.1), channel_id=1, source_target_pairs={{0,1},{1,0},{2,3},{3,2},{4,5},{5,4},{6,7},{7,6},{8,9},{9,8},{10,11... | collective-permute-start | bytes 995336 | tf_op jit(solution)/shard_map/ppermute | solution.py:56
  9.5 1.3 %collective-permute-start = (bf16[96,128]{1,0:T(8,128)(2,1)S(1)}, bf16[96,128]{1,0:T(8,128)(2,1)S(1)}, u32[]{:S(2)}, u32[]{:S(2)}) collective-permute-start(bf16[96,128]{1,0:T(8,128)(2,1)S(1)} %copy-done.9), channel_id=1, source_target_pairs={{4,0},{8,4},{12,8},{5,1},{9,5},{13,9},{6,2},{10,6},{14,10},{7,3},{... | collective-permute-start | bytes 73736 | tf_op jit(solution)/shard_map/ppermute | solution.py:51
  10.8 4.8 %collective-permute-done.below_ref = bf16[96,128]{1,0:T(8,128)(2,1)S(1)} collective-permute-done((bf16[96,128]{1,0:T(8,128)(2,1)S(1)}, bf16[96,128]{1,0:T(8,128)(2,1)S(1)}, u32[]{:S(2)}, u32[]{:S(2)}) %collective-permute-start) | collective-permute-done | bytes 24608 | tf_op jit(solution)/shard_map/ppermute | solution.py:51
  15.6 0.0 all-to-all-done.meta_ref.got_ref.refs_5_
  15.6 0.0 copy-start.3
  15.6 0.0 copy-start.4
  15.7 0.0 copy-start.5
  15.7 0.0 copy-start.6
  15.7 0.0 copy-start.7
  15.7 0.0 copy-start.8
  15.7 0.5 patch.1
  16.2 0.0 copy-start.1
  16.2 0.1 collective-permute-start.1
  16.3 0.3 copy-done.2
  16.5 0.0 copy-done.3
  16.6 0.0 copy-done.4
  16.6 2.2 %stem.1 = (bf16[1,192,128]{2,1,0:T(8,128)(2,1)S(1)}, f32[1,512,96]{2,1,0:T(8,128)S(1)}, f32[1,512,1]{2,1,0:T(8,128)S(1)}, f32[1,512,96]{2,1,0:T(8,128)S(1)}, f32...) custom-call(bf16[8,56,128]{2,1,0:T(8,128)(2,1)S(1)} %all-to-all-done, ...), custom_call_target="tpu_custom_call" | custom-call | bytes 9963000 | tf_op jit(solution)/shard_map/stem/pallas_call | solution.py:499
  18.9 0.2 collective-permute-start.5
  19.1 0.0 collective-permute-done.1
  19.1 2.2 %collective-permute-start.4 = (bf16[1,336,128]{2,1,0:T(8,128)(2,1)S(1)}, bf16[1,336,128]{2,1,0:T(8,128)(2,1)S(1)}, u32[]{:S(2)}, u32[]{:S(2)}) collective-permute-start(bf16[1,336,128]{2,1,0:T(8,128)(2,1)S(1)} %pad_maximum_fusion.3), channel_id=1, source_target_pairs={{0,8},{4,12},{8,0},{12,4},{1,9},{5,13},{9,1},{13,5},{2,10},{6,14},... | collective-permute-start | bytes 258056 | tf_op jit(solution)/shard_map/ppermute | solution.py:56
  21.3 0.0 collective-permute-done.2.refs_4_
  21.3 2.9 %stem_back.1 = (f32[608,128]{1,0:T(8,128)S(1)}, bf16[608,128]{1,0:T(8,128)(2,1)S(1)}) custom-call(s32[1]{0:T(128)} %bitcast.chan_ref.refs_0_, bf16[1,72,128]{2,1,0:T(8,128)(2,1)S(1)} %bitcast.17, bf16[1,72,128]{2,1,0:T(8,128)(2,1)S(1)} %bitcast.20, bf16[9,192,96]{2,1,0:T(8,128)(2,1)S(1)} %copy-done.1, ...), custom_call_target="tpu_custom_call" | custom-call | bytes 13653000 | tf_op jit(solution)/shard_map/stem_back/pallas_call | solution.py:567
  24.2 0.1 collective-permute-start.3
  24.4 0.0 collective-permute-done.5
  24.4 1.0 %spread.1 = (f32[144,96]{1,0:T(8,128)S(1)}, f32[96,128]{1,0:T(8,128)S(1)}) custom-call(bf16[2,192,128]{2,1,0:T(8,128)(2,1)S(1)} %pad_maximum_fusion.2.refs_0_, bf16[9,192,96]{2,1,0:T(8,128)(2,1)S(1)} %copy-done.1, f32[144,128]{1,0:T(8,128)S(1)} %get-tuple-element.57.refs_2_.key_ref), custom_call_target="tpu_custom_call" | custom-call | bytes 3690000 | tf_op jit(solution)/shard_map/spread/pallas_call | solution.py:535
  25.4 1.3 %collective-permute-done.4 = bf16[1,336,128]{2,1,0:T(8,128)(2,1)S(1)} collective-permute-done((bf16[1,336,128]{2,1,0:T(8,128)(2,1)S(1)}, bf16[1,336,128]{2,1,0:T(8,128)(2,1)S(1)}, u32[]{:S(2)}, u32[]{:S(2)}) %collective-permute-start.4) | collective-permute-done | bytes 86048 | tf_op jit(solution)/shard_map/ppermute | solution.py:56
  26.7 0.0 collective-permute-done.3
  26.8 1.6 %collective-permute-start.6 = (bf16[608,128]{1,0:T(8,128)(2,1)S(1)}, bf16[608,128]{1,0:T(8,128)(2,1)S(1)}, u32[]{:S(2)}, u32[]{:S(2)}) collective-permute-start(bf16[608,128]{1,0:T(8,128)(2,1)S(1)} %convert_add_fusion.1), channel_id=1, source_target_pairs={{0,2},{2,0},{1,3},{3,1},{4,6},{6,4},{5,7},{7,5},{8,10},{10,8},{9,1... | collective-permute-start | bytes 466952 | tf_op jit(solution)/shard_map/ppermute | solution.py:56
  28.3 1.5 %collective-permute-start.9 = (f32[96,128]{1,0:T(8,128)S(1)}, f32[96,128]{1,0:T(8,128)S(1)}, u32[]{:S(2)}, u32[]{:S(2)}) collective-permute-start(f32[96,128]{1,0:T(8,128)S(1)} %get-tuple-element.63), channel_id=1, source_target_pairs={{0,4},{4,8},{8,12},{1,5},{5,9},{9,13},{2,6},{6,10},{10,14},{3,7},{... | collective-permute-start | bytes 147464 | tf_op jit(solution)/shard_map/ppermute | solution.py:51
  29.8 1.5 %collective-permute-start.8 = (bf16[2,336,128]{2,1,0:T(8,128)(2,1)S(1)}, bf16[2,336,128]{2,1,0:T(8,128)(2,1)S(1)}, u32[]{:S(2)}, u32[]{:S(2)}) collective-permute-start(bf16[2,336,128]{2,1,0:T(8,128)(2,1)S(1)} %pad_maximum_fusion.1), channel_id=1, source_target_pairs={{0,4},{4,0},{8,12},{12,8},{1,5},{5,1},{9,13},{13,9},{2,6},{6,2},{1... | collective-permute-start | bytes 516104 | tf_op jit(solution)/shard_map/ppermute | solution.py:56
  31.3 1.0 %collective-permute-done.6 = bf16[608,128]{1,0:T(8,128)(2,1)S(1)} collective-permute-done((bf16[608,128]{1,0:T(8,128)(2,1)S(1)}, bf16[608,128]{1,0:T(8,128)(2,1)S(1)}, u32[]{:S(2)}, u32[]{:S(2)}) %collective-permute-start.6) | collective-permute-done | bytes 155680 | tf_op jit(solution)/shard_map/ppermute | solution.py:56
  32.4 0.5 collective-permute-start.7
  32.8 4.0 %collective-permute-done.8 = bf16[2,336,128]{2,1,0:T(8,128)(2,1)S(1)} collective-permute-done((bf16[2,336,128]{2,1,0:T(8,128)(2,1)S(1)}, bf16[2,336,128]{2,1,0:T(8,128)(2,1)S(1)}, u32[]{:S(2)}, u32[]{:S(2)}) %collective-permute-start.8) | collective-permute-done | bytes 172064 | tf_op jit(solution)/shard_map/ppermute | solution.py:56
  36.9 0.0 collective-permute-done.9.above_ref
  36.9 0.1 collective-permute-start.11
  37.0 3.5 %agg_map.1 = bf16[16,96,128]{2,1,0:T(8,128)(2,1)} custom-call(f32[144,96]{1,0:T(8,128)S(1)} %get-tuple-element.61.y_ref, f32[144,128]{1,0:T(8,128)S(1)} %get-tuple-element.57.refs_2_.key_ref, f32[96,128]{1,0:T(8,128)S(1)} %collective-permute-done.9.above_ref), custom_call_target="tpu_custom_call" | custom-call | bytes 12915000 | tf_op jit(solution)/shard_map/agg_map/pallas_call | solution.py:623
  40.5 0.9 %collective-permute-done.7 = bf16[608,128]{1,0:T(8,128)(2,1)S(1)} collective-permute-done((bf16[608,128]{1,0:T(8,128)(2,1)S(1)}, bf16[608,128]{1,0:T(8,128)(2,1)S(1)}, u32[]{:S(2)}, u32[]{:S(2)}) %collective-permute-start.7) | collective-permute-done | bytes 155680 | tf_op jit(solution)/shard_map/ppermute | solution.py:56
  41.4 1.5 %collective-permute-start.10 = (bf16[608,128]{1,0:T(8,128)(2,1)S(1)}, bf16[608,128]{1,0:T(8,128)(2,1)S(1)}, u32[]{:S(2)}, u32[]{:S(2)}) collective-permute-start(bf16[608,128]{1,0:T(8,128)(2,1)S(1)} %add_convert_fusion.1), channel_id=1, source_target_pairs={{0,4},{4,0},{8,12},{12,8},{1,5},{5,1},{9,13},{13,9},{2,6},{6,2},{1... | collective-permute-start | bytes 466952 | tf_op jit(solution)/shard_map/ppermute | solution.py:56
  42.9 1.3 %collective-permute-done.11.refs_2_ = bf16[4,336,128]{2,1,0:T(8,128)(2,1)S(1)} collective-permute-done((bf16[4,336,128]{2,1,0:T(8,128)(2,1)S(1)}, bf16[4,336,128]{2,1,0:T(8,128)(2,1)S(1)}, u32[]{:S(2)}, u32[]{:S(2)}) %collective-permute-start.11) | collective-permute-done | bytes 344096 | tf_op jit(solution)/shard_map/ppermute | solution.py:56
  44.2 1.4 %agg_weight_grad.1 = (f32[9,192,96]{2,1,0:T(8,128)S(1)}, bf16[9,192,96]{2,1,0:T(8,128)(2,1)S(1)}) custom-call(s32[1]{0:T(128)} %bitcast.9.refs_0_, bf16[4,336,128]{2,1,0:T(8,128)(2,1)S(1)} %pad_maximum_fusion.refs_1_, bf16[4,336,128]{2,1,0:T(8,128)(2,1)S(1)} %collective-permute-done.11.refs_2_), custom_call_target="tpu_custom_call" | custom-call | bytes 5166000 | tf_op jit(solution)/shard_map/agg_weight_grad/pallas_call | solution.py:638
  45.6 0.1 collective-permute-start.12
  45.7 1.0 %collective-permute-done.10 = bf16[608,128]{1,0:T(8,128)(2,1)S(1)} collective-permute-done((bf16[608,128]{1,0:T(8,128)(2,1)S(1)}, bf16[608,128]{1,0:T(8,128)(2,1)S(1)}, u32[]{:S(2)}, u32[]{:S(2)}) %collective-permute-start.10) | collective-permute-done | bytes 155680 | tf_op jit(solution)/shard_map/ppermute | solution.py:56
  46.7 0.1 collective-permute-start.13
  46.8 0.7 %collective-permute-done.12 = bf16[9,192,96]{2,1,0:T(8,128)(2,1)S(1)} collective-permute-done((bf16[9,192,96]{2,1,0:T(8,128)(2,1)S(1)}, bf16[9,192,96]{2,1,0:T(8,128)(2,1)S(1)}, u32[]{:S(2)}, u32[]{:S(2)}) %collective-permute-start.12) | collective-permute-done | bytes 331808 | tf_op jit(solution)/shard_map/ppermute | solution.py:56
  47.5 1.0 %convert_add_fusion = f32[9,192,96]{2,1,0:T(8,128)} fusion(f32[9,192,96]{2,1,0:T(8,128)S(1)} %get-tuple-element.68, bf16[9,192,96]{2,1,0:T(8,128)(2,1)S(1)} %collective-permute-done.12), kind=kLoop, calls=%fused_computation | loop fusion | flops 331776 | bytes 1658880 | tf_op jit(solution)/shard_map/add | solution.py:660
  48.5 0.9 %unpack.1 = (f32[49,96]{1,0:T(8,128)}, f32[96,384]{1,0:T(8,128)}, f32[96,384]{1,0:T(8,128)}, f32[192,384]{1,0:T(8,128)}) custom-call(s32[1]{0:T(128)} %bitcast.chan_ref.refs_0_, bf16[608,128]{1,0:T(8,128)(2,1)S(1)} %add_convert_fusion.own_ref, bf16[608,128]{1,0:T(8,128)(2,1)S(1)} %collective-permute-done.13.peer_ref), custom_call_target="tpu_custom_call" | custom-call | bytes 5535000 | tf_op jit(solution)/shard_map/unpack/pallas_call | solution.py:667
  (19 shorter events, 0.3 us)
Async XLA Ops:
  0.6 15.0 %copy-start = (f32[1,16,96,128]{3,2,1,0:T(8,128)S(1)}, f32[1,16,96,128]{3,2,1,0:T(8,128)}, u32[]{:S(2)}) copy-start(f32[1,16,96,128]{3,2,1,0:T(8,128)} %cot_ref.1) | copy-start | bytes 2359300
  2.5 7.0 %copy-start.9 = (bf16[96,128]{1,0:T(8,128)(2,1)S(1)}, bf16[96,128]{1,0:T(8,128)(2,1)}, u32[]{:S(2)}) copy-start(bf16[96,128]{1,0:T(8,128)(2,1)} %get-tuple-element.43) | copy-start | bytes 73732
  2.5 13.1 %all-to-all-start = ((bf16[8,56,128]{2,1,0:T(8,128)(2,1)}), bf16[8,56,128]{2,1,0:T(8,128)(2,1)S(1)}, u32[]{:S(2)}, u32[]{:S(2)}) async-start(bf16[8,56,128]{2,1,0:T(8,128)(2,1)} %get-tuple-element.42), calls=%async_computation | async-start | bytes 229376 | tf_op jit(solution)/shard_map/all_to_all | solution.py:462
  9.0 12.4 %collective-permute-start.2 = (bf16[9,192,96]{2,1,0:T(8,128)(2,1)}, bf16[9,192,96]{2,1,0:T(8,128)(2,1)S(1)}, u32[]{:S(2)}, u32[]{:S(2)}) collective-permute-start(bf16[9,192,96]{2,1,0:T(8,128)(2,1)} %refs_1_.1), channel_id=1, source_target_pairs={{0,1},{1,0},{2,3},{3,2},{4,5},{5,4},{6,7},{7,6},{8,9},{9,8},{10,11... | collective-permute-start | bytes 995336 | tf_op jit(solution)/shard_map/ppermute | solution.py:56
  9.5 6.1 %collective-permute-start = (bf16[96,128]{1,0:T(8,128)(2,1)S(1)}, bf16[96,128]{1,0:T(8,128)(2,1)S(1)}, u32[]{:S(2)}, u32[]{:S(2)}) collective-permute-start(bf16[96,128]{1,0:T(8,128)(2,1)S(1)} %copy-done.9), channel_id=1, source_target_pairs={{4,0},{8,4},{12,8},{5,1},{9,5},{13,9},{6,2},{10,6},{14,10},{7,3},{... | collective-permute-start | bytes 73736 | tf_op jit(solution)/shard_map/ppermute | solution.py:51
  15.6 0.9 %copy-start.2 = (bf16[384,192]{0,1:T(8,128)(2,1)S(1)}, bf16[384,192]{0,1:T(8,128)(2,1)}, u32[]{:S(2)}) copy-start(bf16[384,192]{0,1:T(8,128)(2,1)} %param.20) | copy-start | bytes 442372
  15.6 1.0 %copy-start.3 = (bf16[96,384]{1,0:T(8,128)(2,1)S(1)}, bf16[96,384]{1,0:T(8,128)(2,1)}, u32[]{:S(2)}) copy-start(bf16[96,384]{1,0:T(8,128)(2,1)} %refs_14_.1) | copy-start | bytes 221188
  15.6 1.0 %copy-start.4 = (bf16[384,96]{0,1:T(8,128)(2,1)S(1)}, bf16[384,96]{0,1:T(8,128)(2,1)}, u32[]{:S(2)}) copy-start(bf16[384,96]{0,1:T(8,128)(2,1)} %param.17) | copy-start | bytes 221188
  15.7 1.0 %copy-start.5 = (f32[49,96]{1,0:T(8,128)S(1)}, f32[49,96]{1,0:T(8,128)}, u32[]{:S(2)}) copy-start(f32[49,96]{1,0:T(8,128)} %dw_ref.1) | copy-start | bytes 56452
  15.7 1.0 %copy-start.6 = (f32[96]{0:T(128)S(1)}, f32[96]{0:T(128)}, u32[]{:S(2)}) copy-start(f32[96]{0:T(128)} %param.15) | copy-start | bytes 1156
  15.7 1.0 %copy-start.7 = (f32[96]{0:T(128)S(1)}, f32[96]{0:T(128)}, u32[]{:S(2)}) copy-start(f32[96]{0:T(128)} %param.18) | copy-start | bytes 1156
  15.7 0.9 %copy-start.8 = (f32[96]{0:T(128)S(1)}, f32[96]{0:T(128)}, u32[]{:S(2)}) copy-start(f32[96]{0:T(128)} %param.19) | copy-start | bytes 1156
  16.2 5.2 %copy-start.1 = (bf16[9,192,96]{2,1,0:T(8,128)(2,1)S(1)}, bf16[9,192,96]{2,1,0:T(8,128)(2,1)}, u32[]{:S(2)}) copy-start(bf16[9,192,96]{2,1,0:T(8,128)(2,1)} %refs_1_.1) | copy-start | bytes 995332
  16.2 2.9 %collective-permute-start.1 = (bf16[72,128]{1,0:T(8,128)(2,1)S(1)}, bf16[72,128]{1,0:T(8,128)(2,1)S(1)}, u32[]{:S(2)}, u32[]{:S(2)}) collective-permute-start(bf16[72,128]{1,0:T(8,128)(2,1)S(1)} %get-tuple-element.45), channel_id=1, source_target_pairs={{0,1},{1,0},{2,3},{3,2},{4,5},{5,4},{6,7},{7,6},{8,9},{9,8},{10,11... | collective-permute-start | bytes 55304 | tf_op jit(solution)/shard_map/ppermute | solution.py:56
  18.9 5.5 %collective-permute-start.5 = (bf16[1,192,128]{2,1,0:T(8,128)(2,1)S(1)}, bf16[1,192,128]{2,1,0:T(8,128)(2,1)S(1)}, u32[]{:S(2)}, u32[]{:S(2)}) collective-permute-start(bf16[1,192,128]{2,1,0:T(8,128)(2,1)S(1)} %get-tuple-element.56), channel_id=1, source_target_pairs={{0,1},{1,0},{2,3},{3,2},{4,5},{5,4},{6,7},{7,6},{8,9},{9,8},{10,11... | collective-permute-start | bytes 147464 | tf_op jit(solution)/shard_map/ppermute | solution.py:56
  19.1 7.6 %collective-permute-start.4 = (bf16[1,336,128]{2,1,0:T(8,128)(2,1)S(1)}, bf16[1,336,128]{2,1,0:T(8,128)(2,1)S(1)}, u32[]{:S(2)}, u32[]{:S(2)}) collective-permute-start(bf16[1,336,128]{2,1,0:T(8,128)(2,1)S(1)} %pad_maximum_fusion.3), channel_id=1, source_target_pairs={{0,8},{4,12},{8,0},{12,4},{1,9},{5,13},{9,1},{13,5},{2,10},{6,14},... | collective-permute-start | bytes 258056 | tf_op jit(solution)/shard_map/ppermute | solution.py:56
  24.2 2.5 %collective-permute-start.3 = (bf16[608,128]{1,0:T(8,128)(2,1)S(1)}, bf16[608,128]{1,0:T(8,128)(2,1)S(1)}, u32[]{:S(2)}, u32[]{:S(2)}) collective-permute-start(bf16[608,128]{1,0:T(8,128)(2,1)S(1)} %get-tuple-element.55), channel_id=1, source_target_pairs={{0,1},{1,0},{2,3},{3,2},{4,5},{5,4},{6,7},{7,6},{8,9},{9,8},{10,11... | collective-permute-start | bytes 466952 | tf_op jit(solution)/shard_map/ppermute | solution.py:56
  26.8 5.5 %collective-permute-start.6 = (bf16[608,128]{1,0:T(8,128)(2,1)S(1)}, bf16[608,128]{1,0:T(8,128)(2,1)S(1)}, u32[]{:S(2)}, u32[]{:S(2)}) collective-permute-start(bf16[608,128]{1,0:T(8,128)(2,1)S(1)} %convert_add_fusion.1), channel_id=1, source_target_pairs={{0,2},{2,0},{1,3},{3,1},{4,6},{6,4},{5,7},{7,5},{8,10},{10,8},{9,1... | collective-permute-start | bytes 466952 | tf_op jit(solution)/shard_map/ppermute | solution.py:56
  28.3 8.5 %collective-permute-start.9 = (f32[96,128]{1,0:T(8,128)S(1)}, f32[96,128]{1,0:T(8,128)S(1)}, u32[]{:S(2)}, u32[]{:S(2)}) collective-permute-start(f32[96,128]{1,0:T(8,128)S(1)} %get-tuple-element.63), channel_id=1, source_target_pairs={{0,4},{4,8},{8,12},{1,5},{5,9},{9,13},{2,6},{6,10},{10,14},{3,7},{... | collective-permute-start | bytes 147464 | tf_op jit(solution)/shard_map/ppermute | solution.py:51
  29.8 7.0 %collective-permute-start.8 = (bf16[2,336,128]{2,1,0:T(8,128)(2,1)S(1)}, bf16[2,336,128]{2,1,0:T(8,128)(2,1)S(1)}, u32[]{:S(2)}, u32[]{:S(2)}) collective-permute-start(bf16[2,336,128]{2,1,0:T(8,128)(2,1)S(1)} %pad_maximum_fusion.1), channel_id=1, source_target_pairs={{0,4},{4,0},{8,12},{12,8},{1,5},{5,1},{9,13},{13,9},{2,6},{6,2},{1... | collective-permute-start | bytes 516104 | tf_op jit(solution)/shard_map/ppermute | solution.py:56
  32.4 9.0 %collective-permute-start.7 = (bf16[608,128]{1,0:T(8,128)(2,1)S(1)}, bf16[608,128]{1,0:T(8,128)(2,1)S(1)}, u32[]{:S(2)}, u32[]{:S(2)}) collective-permute-start(bf16[608,128]{1,0:T(8,128)(2,1)S(1)} %add_convert_fusion.2), channel_id=1, source_target_pairs={{0,8},{4,12},{8,0},{12,4},{1,9},{5,13},{9,1},{13,5},{2,10},{6,14},... | collective-permute-start | bytes 466952 | tf_op jit(solution)/shard_map/ppermute | solution.py:56
  36.9 7.3 %collective-permute-start.11 = (bf16[4,336,128]{2,1,0:T(8,128)(2,1)S(1)}, bf16[4,336,128]{2,1,0:T(8,128)(2,1)S(1)}, u32[]{:S(2)}, u32[]{:S(2)}) collective-permute-start(bf16[4,336,128]{2,1,0:T(8,128)(2,1)S(1)} %pad_maximum_fusion.refs_1_), channel_id=1, source_target_pairs={{0,2},{2,0},{1,3},{3,1},{4,6},{6,4},{5,7},{7,5},{8,10},{10,8},{9,1... | collective-permute-start | bytes 1032200 | tf_op jit(solution)/shard_map/ppermute | solution.py:56
  41.4 5.3 %collective-permute-start.10 = (bf16[608,128]{1,0:T(8,128)(2,1)S(1)}, bf16[608,128]{1,0:T(8,128)(2,1)S(1)}, u32[]{:S(2)}, u32[]{:S(2)}) collective-permute-start(bf16[608,128]{1,0:T(8,128)(2,1)S(1)} %add_convert_fusion.1), channel_id=1, source_target_pairs={{0,4},{4,0},{8,12},{12,8},{1,5},{5,1},{9,13},{13,9},{2,6},{6,2},{1... | collective-permute-start | bytes 466952 | tf_op jit(solution)/shard_map/ppermute | solution.py:56
  45.6 1.9 %collective-permute-start.12 = (bf16[9,192,96]{2,1,0:T(8,128)(2,1)S(1)}, bf16[9,192,96]{2,1,0:T(8,128)(2,1)S(1)}, u32[]{:S(2)}, u32[]{:S(2)}) collective-permute-start(bf16[9,192,96]{2,1,0:T(8,128)(2,1)S(1)} %get-tuple-element.69), channel_id=1, source_target_pairs={{0,1},{1,0},{2,3},{3,2},{4,5},{5,4},{6,7},{7,6},{8,9},{9,8},{10,11... | collective-permute-start | bytes 995336 | tf_op jit(solution)/shard_map/ppermute | solution.py:56
  46.7 1.8 %collective-permute-start.13 = (bf16[608,128]{1,0:T(8,128)(2,1)S(1)}, bf16[608,128]{1,0:T(8,128)(2,1)S(1)}, u32[]{:S(2)}, u32[]{:S(2)}) collective-permute-start(bf16[608,128]{1,0:T(8,128)(2,1)S(1)} %add_convert_fusion.own_ref), channel_id=1, source_target_pairs={{0,1},{1,0},{2,3},{3,2},{4,5},{5,4},{6,7},{7,6},{8,9},{9,8},{10,11... | collective-permute-start | bytes 466952 | tf_op jit(solution)/shard_map/ppermute | solution.py:56

commit v14 on v13

--- a/solution.py
+++ b/solution.py
@@ -604,10 +604,7 @@
     part = keep + swapped(send, "chan", 1).astype(F32)
     if gather:
         part, near, spread, below = lax.optimization_barrier((part, near, spread, below))
-    above = shifted(below, "slide", 1)
     for n in range(1, len(spans) if gather else 0):
-        if n == len(spans) - 1:
-            near, above = lax.optimization_barrier((near, above))
         far, place = widen(n, near, place)
         if n < len(spans) - 1:
             near = jnp.concatenate([near, far], axis=0)
@@ -620,7 +617,6 @@
         cost_estimate=takes(3.5),
         name="agg_map",
     )
-    agg_map = map_call(spread, key, above)
 
     steps = []
     for axis in ("rep", "slide"):
@@ -628,6 +624,9 @@
             steps.append((axis, 1 << n))
     for n, (axis, step) in enumerate(steps):
         wire = part.astype(BF16)
+        if n == max(0, len(steps) - 2):
+            wire, below = lax.optimization_barrier((wire, below))
+            agg_map = map_call(spread, key, shifted(below, "slide", 1))
         if n == len(steps) - 1:
             wire, agg_map = lax.optimization_barrier((wire, agg_map))
         part = wire.astype(F32) + swapped(wire, axis, step).astype(F32)

time: 49.7 us -> 50.9 us (1.024)
  starting transfers between devices: 17.5 us -> 19.3 us
  waiting for transfers between devices: 15 us -> 14.4 us
    ppermute x12, starting transfers between devices: 8.32 us -> 10.1 us  [swapped(): lax.ppermute(value, axis, [(place, place ^ step) for place in range(count)])]
    ppermute x12, waiting for transfers between devices: 10.2 us -> 9.57 us  [swapped(): lax.ppermute(value, axis, [(place, place ^ step) for place in range(count)])]
  transfers between devices with their start and end apart: 15 -> 15, of which waited for: 8 -> 7; matrix products, arithmetic and copies ran while one was open for 2% -> 2% of each run, Pallas kernels for 23% -> 23%
where the time goes in v14:
time: 50.9 us; the launch traced here: 50.5 us
  starting transfers between devices  19.3 us (38%)
  waiting for transfers between devices  14.4 us (28%)
  Pallas kernels  14.3 us (28%)
  other arithmetic  1.19 us (2%)
  between operations  0.84 us (2%)
    ppermute x12, starting transfers between devices, swapped(): lax.ppermute(value, axis, [(place, place ^ step) for place in range(count)])  10.1 us
    ppermute x12, waiting for transfers between devices, swapped(): lax.ppermute(value, axis, [(place, place ^ step) for place in range(count)])  9.57 us
    all_to_all x1, starting transfers between devices, on_device(): lax.all_to_all(packed, ('slide', 'chan'), split_axis=0, concat_axis=0, ti...  6.46 us
    ppermute x2, waiting for transfers between devices, shifted(): lax.ppermute(value, axis, [(source, source + steps) for source in range(f...  4.84 us
    pallas_call x1, Pallas kernels, on_device(): agg_map = map_call(spread, key, shifted(below, 'slide', 1))  3.5 us
    pallas_call x1, Pallas kernels, on_device(): pl.pallas_call(lambda *refs: back_kernel(*refs, scale=loss_scale), grid=(...  2.94 us
    ppermute x2, starting transfers between devices, shifted(): lax.ppermute(value, axis, [(source, source + steps) for source in range(f...  2.71 us
    pallas_call x1, Pallas kernels, on_device(): pl.pallas_call(stem_kernel, grid=(chunks,), out_shape=(jax.ShapeDtypeStru...  2.24 us
  transfers between devices with their start and end apart: 15, of which 7 were waited for; matrix products, arithmetic and copies ran while one was open for 2% of the time, Pallas kernels for 23%

profile of v14, /device:TPU:0, one launch (start us, length us, event | category | flops | bytes accessed | tf_op | source)
XLA Modules:
  0.0 50.5 jit_solution(4336137152949580445)
XLA Ops:
  0.6 1.9 %pack.1 = (bf16[8,56,128]{2,1,0:T(8,128)(2,1)}, bf16[96,128]{1,0:T(8,128)(2,1)}) custom-call(s32[1,8]{1,0:T(1,128)} %cells_ref.1, bf16[1,8,6144]{2,1,0:T(8,128)(2,1)} %pixels_ref.1, f32[1,16,96,128]{3,2,1,0:T(8,128)} %cot_ref.1), custom_call_target="tpu_custom_call" | custom-call | bytes 5535000 | tf_op jit(solution)/shard_map/pack/pallas_call | solution.py:439
  2.5 6.5 %all-to-all-start = ((bf16[8,56,128]{2,1,0:T(8,128)(2,1)}), bf16[8,56,128]{2,1,0:T(8,128)(2,1)S(1)}, u32[]{:S(2)}, u32[]{:S(2)}) async-start(bf16[8,56,128]{2,1,0:T(8,128)(2,1)} %get-tuple-element.42), calls=%async_computation | async-start | bytes 229376 | tf_op jit(solution)/shard_map/all_to_all | solution.py:462
  9.0 0.5 collective-permute-start.2
  9.5 1.3 %collective-permute-start = (bf16[96,128]{1,0:T(8,128)(2,1)S(1)}, bf16[96,128]{1,0:T(8,128)(2,1)S(1)}, u32[]{:S(2)}, u32[]{:S(2)}) collective-permute-start(bf16[96,128]{1,0:T(8,128)(2,1)S(1)} %copy-done.9), channel_id=1, source_target_pairs={{4,0},{8,4},{12,8},{5,1},{9,5},{13,9},{6,2},{10,6},{14,10},{7,3},{... | collective-permute-start | bytes 73736 | tf_op jit(solution)/shard_map/ppermute | solution.py:51
  10.8 4.8 %collective-permute-done.below_ref = bf16[96,128]{1,0:T(8,128)(2,1)S(1)} collective-permute-done((bf16[96,128]{1,0:T(8,128)(2,1)S(1)}, bf16[96,128]{1,0:T(8,128)(2,1)S(1)}, u32[]{:S(2)}, u32[]{:S(2)}) %collective-permute-start) | collective-permute-done | bytes 24608 | tf_op jit(solution)/shard_map/ppermute | solution.py:51
  15.6 0.0 all-to-all-done.meta_ref.got_ref.refs_5_
  15.6 0.0 copy-start.3
  15.6 0.0 copy-start.4
  15.7 0.0 copy-start.5
  15.7 0.0 copy-start.6
  15.7 0.0 copy-start.7
  15.7 0.0 copy-start.8
  15.7 0.5 patch.1
  16.2 0.0 copy-start.1
  16.2 0.1 collective-permute-start.1
  16.3 0.3 copy-done.2
  16.5 0.0 copy-done.3
  16.6 0.0 copy-done.4
  16.6 2.2 %stem.1 = (bf16[1,192,128]{2,1,0:T(8,128)(2,1)S(1)}, f32[1,512,96]{2,1,0:T(8,128)S(1)}, f32[1,512,1]{2,1,0:T(8,128)S(1)}, f32[1,512,96]{2,1,0:T(8,128)S(1)}, f32...) custom-call(bf16[8,56,128]{2,1,0:T(8,128)(2,1)S(1)} %all-to-all-done, ...), custom_call_target="tpu_custom_call" | custom-call | bytes 9963000 | tf_op jit(solution)/shard_map/stem/pallas_call | solution.py:499
  18.9 0.2 collective-permute-start.5
  19.1 0.0 collective-permute-done.1
  19.1 2.2 %collective-permute-start.4 = (bf16[1,336,128]{2,1,0:T(8,128)(2,1)S(1)}, bf16[1,336,128]{2,1,0:T(8,128)(2,1)S(1)}, u32[]{:S(2)}, u32[]{:S(2)}) collective-permute-start(bf16[1,336,128]{2,1,0:T(8,128)(2,1)S(1)} %pad_maximum_fusion.2), channel_id=1, source_target_pairs={{0,8},{4,12},{8,0},{12,4},{1,9},{5,13},{9,1},{13,5},{2,10},{6,14},... | collective-permute-start | bytes 258056 | tf_op jit(solution)/shard_map/ppermute | solution.py:56
  21.3 0.0 collective-permute-done.2.refs_4_
  21.3 2.9 %stem_back.1 = (f32[608,128]{1,0:T(8,128)S(1)}, bf16[608,128]{1,0:T(8,128)(2,1)S(1)}) custom-call(s32[1]{0:T(128)} %bitcast.chan_ref.refs_0_, bf16[1,72,128]{2,1,0:T(8,128)(2,1)S(1)} %bitcast.17, bf16[1,72,128]{2,1,0:T(8,128)(2,1)S(1)} %bitcast.20, bf16[9,192,96]{2,1,0:T(8,128)(2,1)S(1)} %copy-done.1, ...), custom_call_target="tpu_custom_call" | custom-call | bytes 13653000 | tf_op jit(solution)/shard_map/stem_back/pallas_call | solution.py:567
  24.3 0.1 collective-permute-start.3
  24.4 0.0 collective-permute-done.5
  24.4 1.0 %spread.1 = (f32[144,96]{1,0:T(8,128)S(1)}, f32[96,128]{1,0:T(8,128)S(1)}) custom-call(bf16[2,192,128]{2,1,0:T(8,128)(2,1)S(1)} %pad_maximum_fusion.1.refs_0_, bf16[9,192,96]{2,1,0:T(8,128)(2,1)S(1)} %copy-done.1, f32[144,128]{1,0:T(8,128)S(1)} %get-tuple-element.57.refs_2_.key_ref), custom_call_target="tpu_custom_call" | custom-call | bytes 3690000 | tf_op jit(solution)/shard_map/spread/pallas_call | solution.py:535
  25.5 1.2 %collective-permute-done.4 = bf16[1,336,128]{2,1,0:T(8,128)(2,1)S(1)} collective-permute-done((bf16[1,336,128]{2,1,0:T(8,128)(2,1)S(1)}, bf16[1,336,128]{2,1,0:T(8,128)(2,1)S(1)}, u32[]{:S(2)}, u32[]{:S(2)}) %collective-permute-start.4) | collective-permute-done | bytes 86048 | tf_op jit(solution)/shard_map/ppermute | solution.py:56
  26.7 0.0 collective-permute-done.3
  26.8 1.6 %collective-permute-start.6 = (bf16[608,128]{1,0:T(8,128)(2,1)S(1)}, bf16[608,128]{1,0:T(8,128)(2,1)S(1)}, u32[]{:S(2)}, u32[]{:S(2)}) collective-permute-start(bf16[608,128]{1,0:T(8,128)(2,1)S(1)} %convert_add_fusion.1), channel_id=1, source_target_pairs={{0,2},{2,0},{1,3},{3,1},{4,6},{6,4},{5,7},{7,5},{8,10},{10,8},{9,1... | collective-permute-start | bytes 466952 | tf_op jit(solution)/shard_map/ppermute | solution.py:56
  28.4 4.0 %collective-permute-done.6 = bf16[608,128]{1,0:T(8,128)(2,1)S(1)} collective-permute-done((bf16[608,128]{1,0:T(8,128)(2,1)S(1)}, bf16[608,128]{1,0:T(8,128)(2,1)S(1)}, u32[]{:S(2)}, u32[]{:S(2)}) %collective-permute-start.6) | collective-permute-done | bytes 155680 | tf_op jit(solution)/shard_map/ppermute | solution.py:56
  32.4 1.4 %collective-permute-start.8 = (f32[96,128]{1,0:T(8,128)S(1)}, f32[96,128]{1,0:T(8,128)S(1)}, u32[]{:S(2)}, u32[]{:S(2)}) collective-permute-start(f32[96,128]{1,0:T(8,128)S(1)} %get-tuple-element.64), channel_id=1, source_target_pairs={{0,4},{4,8},{8,12},{1,5},{5,9},{9,13},{2,6},{6,10},{10,14},{3,7},{... | collective-permute-start | bytes 147464 | tf_op jit(solution)/shard_map/ppermute | solution.py:51
  33.8 2.3 %collective-permute-start.7 = (bf16[608,128]{1,0:T(8,128)(2,1)S(1)}, bf16[608,128]{1,0:T(8,128)(2,1)S(1)}, u32[]{:S(2)}, u32[]{:S(2)}) collective-permute-start(bf16[608,128]{1,0:T(8,128)(2,1)S(1)} %add_convert_fusion.2), channel_id=1, source_target_pairs={{0,8},{4,12},{8,0},{12,4},{1,9},{5,13},{9,1},{13,5},{2,10},{6,14},... | collective-permute-start | bytes 466952 | tf_op jit(solution)/shard_map/ppermute | solution.py:56
  36.1 0.0 collective-permute-done.10
  36.2 1.6 %collective-permute-start.11 = (bf16[4,336,128]{2,1,0:T(8,128)(2,1)S(1)}, bf16[4,336,128]{2,1,0:T(8,128)(2,1)S(1)}, u32[]{:S(2)}, u32[]{:S(2)}) collective-permute-start(bf16[4,336,128]{2,1,0:T(8,128)(2,1)S(1)} %constant_dynamic-update-slice_fusion.refs_1_), channel_id=1, source_target_pairs={{0,2},{2,0},{1,3},{3,1},{4,6},{6,4},{5,7},{7,5},{8,10},{10,8},{9,1... | collective-permute-start | bytes 1032200 | tf_op jit(solution)/shard_map/ppermute | solution.py:56
  37.7 0.0 collective-permute-done.8.above_ref
  37.7 3.5 %agg_map.1 = bf16[16,96,128]{2,1,0:T(8,128)(2,1)} custom-call(f32[144,96]{1,0:T(8,128)S(1)} %get-tuple-element.63.y_ref, f32[144,128]{1,0:T(8,128)S(1)} %get-tuple-element.57.refs_2_.key_ref, f32[96,128]{1,0:T(8,128)S(1)} %collective-permute-done.8.above_ref), custom_call_target="tpu_custom_call" | custom-call | bytes 12915000 | tf_op jit(solution)/shard_map/agg_map/pallas_call | solution.py:629
  41.2 1.6 %collective-permute-done.7 = bf16[608,128]{1,0:T(8,128)(2,1)S(1)} collective-permute-done((bf16[608,128]{1,0:T(8,128)(2,1)S(1)}, bf16[608,128]{1,0:T(8,128)(2,1)S(1)}, u32[]{:S(2)}, u32[]{:S(2)}) %collective-permute-start.7) | collective-permute-done | bytes 155680 | tf_op jit(solution)/shard_map/ppermute | solution.py:56
  42.8 1.4 %collective-permute-start.9 = (bf16[608,128]{1,0:T(8,128)(2,1)S(1)}, bf16[608,128]{1,0:T(8,128)(2,1)S(1)}, u32[]{:S(2)}, u32[]{:S(2)}) collective-permute-start(bf16[608,128]{1,0:T(8,128)(2,1)S(1)} %add_convert_fusion.1), channel_id=1, source_target_pairs={{0,4},{4,0},{8,12},{12,8},{1,5},{5,1},{9,13},{13,9},{2,6},{6,2},{1... | collective-permute-start | bytes 466952 | tf_op jit(solution)/shard_map/ppermute | solution.py:56
  44.3 0.8 %collective-permute-done.11.refs_2_ = bf16[4,336,128]{2,1,0:T(8,128)(2,1)S(1)} collective-permute-done((bf16[4,336,128]{2,1,0:T(8,128)(2,1)S(1)}, bf16[4,336,128]{2,1,0:T(8,128)(2,1)S(1)}, u32[]{:S(2)}, u32[]{:S(2)}) %collective-permute-start.11) | collective-permute-done | bytes 344096 | tf_op jit(solution)/shard_map/ppermute | solution.py:56
  45.1 1.4 %agg_weight_grad.1 = (f32[9,192,96]{2,1,0:T(8,128)S(1)}, bf16[9,192,96]{2,1,0:T(8,128)(2,1)S(1)}) custom-call(s32[1]{0:T(128)} %bitcast.9.refs_0_, bf16[4,336,128]{2,1,0:T(8,128)(2,1)S(1)} %constant_dynamic-update-slice_fusion.refs_1_, bf16[4,336,128]{2,1,0:T(8,128)(2,1)S(1)} %collective-permute-done.11.refs_2_), custom_call_target="tpu_custom_call" | custom-call | bytes 5166000 | tf_op jit(solution)/shard_map/agg_weight_grad/pallas_call | solution.py:637
  46.5 0.1 collective-permute-start.12
  46.6 1.6 %collective-permute-done.9 = bf16[608,128]{1,0:T(8,128)(2,1)S(1)} collective-permute-done((bf16[608,128]{1,0:T(8,128)(2,1)S(1)}, bf16[608,128]{1,0:T(8,128)(2,1)S(1)}, u32[]{:S(2)}, u32[]{:S(2)}) %collective-permute-start.9) | collective-permute-done | bytes 155680 | tf_op jit(solution)/shard_map/ppermute | solution.py:56
  48.2 0.1 collective-permute-start.13
  48.3 0.0 collective-permute-done.12
  48.3 1.0 %convert_add_fusion = f32[9,192,96]{2,1,0:T(8,128)} fusion(f32[9,192,96]{2,1,0:T(8,128)S(1)} %get-tuple-element.68, bf16[9,192,96]{2,1,0:T(8,128)(2,1)S(1)} %collective-permute-done.12), kind=kLoop, calls=%fused_computation | loop fusion | flops 331776 | bytes 1658880 | tf_op jit(solution)/shard_map/add | solution.py:659
  49.3 0.4 collective-permute-done.13.peer_ref
  49.7 0.9 %unpack.1 = (f32[49,96]{1,0:T(8,128)}, f32[96,384]{1,0:T(8,128)}, f32[96,384]{1,0:T(8,128)}, f32[192,384]{1,0:T(8,128)}) custom-call(s32[1]{0:T(128)} %bitcast.chan_ref.refs_0_, bf16[608,128]{1,0:T(8,128)(2,1)S(1)} %add_convert_fusion.own_ref, bf16[608,128]{1,0:T(8,128)(2,1)S(1)} %collective-permute-done.13.peer_ref), custom_call_target="tpu_custom_call" | custom-call | bytes 5535000 | tf_op jit(solution)/shard_map/unpack/pallas_call | solution.py:666
  (20 shorter events, 0.3 us)
Async XLA Ops:
  0.6 15.0 %copy-start = (f32[1,16,96,128]{3,2,1,0:T(8,128)S(1)}, f32[1,16,96,128]{3,2,1,0:T(8,128)}, u32[]{:S(2)}) copy-start(f32[1,16,96,128]{3,2,1,0:T(8,128)} %cot_ref.1) | copy-start | bytes 2359300
  2.5 7.0 %copy-start.9 = (bf16[96,128]{1,0:T(8,128)(2,1)S(1)}, bf16[96,128]{1,0:T(8,128)(2,1)}, u32[]{:S(2)}) copy-start(bf16[96,128]{1,0:T(8,128)(2,1)} %get-tuple-element.43) | copy-start | bytes 73732
  2.5 13.1 %all-to-all-start = ((bf16[8,56,128]{2,1,0:T(8,128)(2,1)}), bf16[8,56,128]{2,1,0:T(8,128)(2,1)S(1)}, u32[]{:S(2)}, u32[]{:S(2)}) async-start(bf16[8,56,128]{2,1,0:T(8,128)(2,1)} %get-tuple-element.42), calls=%async_computation | async-start | bytes 229376 | tf_op jit(solution)/shard_map/all_to_all | solution.py:462
  9.0 12.4 %collective-permute-start.2 = (bf16[9,192,96]{2,1,0:T(8,128)(2,1)}, bf16[9,192,96]{2,1,0:T(8,128)(2,1)S(1)}, u32[]{:S(2)}, u32[]{:S(2)}) collective-permute-start(bf16[9,192,96]{2,1,0:T(8,128)(2,1)} %refs_1_.1), channel_id=1, source_target_pairs={{0,1},{1,0},{2,3},{3,2},{4,5},{5,4},{6,7},{7,6},{8,9},{9,8},{10,11... | collective-permute-start | bytes 995336 | tf_op jit(solution)/shard_map/ppermute | solution.py:56
  9.5 6.1 %collective-permute-start = (bf16[96,128]{1,0:T(8,128)(2,1)S(1)}, bf16[96,128]{1,0:T(8,128)(2,1)S(1)}, u32[]{:S(2)}, u32[]{:S(2)}) collective-permute-start(bf16[96,128]{1,0:T(8,128)(2,1)S(1)} %copy-done.9), channel_id=1, source_target_pairs={{4,0},{8,4},{12,8},{5,1},{9,5},{13,9},{6,2},{10,6},{14,10},{7,3},{... | collective-permute-start | bytes 73736 | tf_op jit(solution)/shard_map/ppermute | solution.py:51
  15.6 0.9 %copy-start.2 = (bf16[384,192]{0,1:T(8,128)(2,1)S(1)}, bf16[384,192]{0,1:T(8,128)(2,1)}, u32[]{:S(2)}) copy-start(bf16[384,192]{0,1:T(8,128)(2,1)} %param.20) | copy-start | bytes 442372
  15.6 1.0 %copy-start.3 = (bf16[96,384]{1,0:T(8,128)(2,1)S(1)}, bf16[96,384]{1,0:T(8,128)(2,1)}, u32[]{:S(2)}) copy-start(bf16[96,384]{1,0:T(8,128)(2,1)} %refs_14_.1) | copy-start | bytes 221188
  15.6 1.0 %copy-start.4 = (bf16[384,96]{0,1:T(8,128)(2,1)S(1)}, bf16[384,96]{0,1:T(8,128)(2,1)}, u32[]{:S(2)}) copy-start(bf16[384,96]{0,1:T(8,128)(2,1)} %param.17) | copy-start | bytes 221188
  15.7 1.0 %copy-start.5 = (f32[49,96]{1,0:T(8,128)S(1)}, f32[49,96]{1,0:T(8,128)}, u32[]{:S(2)}) copy-start(f32[49,96]{1,0:T(8,128)} %dw_ref.1) | copy-start | bytes 56452
  15.7 1.0 %copy-start.6 = (f32[96]{0:T(128)S(1)}, f32[96]{0:T(128)}, u32[]{:S(2)}) copy-start(f32[96]{0:T(128)} %param.15) | copy-start | bytes 1156
  15.7 1.0 %copy-start.7 = (f32[96]{0:T(128)S(1)}, f32[96]{0:T(128)}, u32[]{:S(2)}) copy-start(f32[96]{0:T(128)} %param.18) | copy-start | bytes 1156
  15.7 0.9 %copy-start.8 = (f32[96]{0:T(128)S(1)}, f32[96]{0:T(128)}, u32[]{:S(2)}) copy-start(f32[96]{0:T(128)} %param.19) | copy-start | bytes 1156
  16.2 5.2 %copy-start.1 = (bf16[9,192,96]{2,1,0:T(8,128)(2,1)S(1)}, bf16[9,192,96]{2,1,0:T(8,128)(2,1)}, u32[]{:S(2)}) copy-start(bf16[9,192,96]{2,1,0:T(8,128)(2,1)} %refs_1_.1) | copy-start | bytes 995332
  16.2 2.9 %collective-permute-start.1 = (bf16[72,128]{1,0:T(8,128)(2,1)S(1)}, bf16[72,128]{1,0:T(8,128)(2,1)S(1)}, u32[]{:S(2)}, u32[]{:S(2)}) collective-permute-start(bf16[72,128]{1,0:T(8,128)(2,1)S(1)} %get-tuple-element.45), channel_id=1, source_target_pairs={{0,1},{1,0},{2,3},{3,2},{4,5},{5,4},{6,7},{7,6},{8,9},{9,8},{10,11... | collective-permute-start | bytes 55304 | tf_op jit(solution)/shard_map/ppermute | solution.py:56
  18.9 5.5 %collective-permute-start.5 = (bf16[1,192,128]{2,1,0:T(8,128)(2,1)S(1)}, bf16[1,192,128]{2,1,0:T(8,128)(2,1)S(1)}, u32[]{:S(2)}, u32[]{:S(2)}) collective-permute-start(bf16[1,192,128]{2,1,0:T(8,128)(2,1)S(1)} %get-tuple-element.56), channel_id=1, source_target_pairs={{0,1},{1,0},{2,3},{3,2},{4,5},{5,4},{6,7},{7,6},{8,9},{9,8},{10,11... | collective-permute-start | bytes 147464 | tf_op jit(solution)/shard_map/ppermute | solution.py:56
  19.1 7.6 %collective-permute-start.4 = (bf16[1,336,128]{2,1,0:T(8,128)(2,1)S(1)}, bf16[1,336,128]{2,1,0:T(8,128)(2,1)S(1)}, u32[]{:S(2)}, u32[]{:S(2)}) collective-permute-start(bf16[1,336,128]{2,1,0:T(8,128)(2,1)S(1)} %pad_maximum_fusion.2), channel_id=1, source_target_pairs={{0,8},{4,12},{8,0},{12,4},{1,9},{5,13},{9,1},{13,5},{2,10},{6,14},... | collective-permute-start | bytes 258056 | tf_op jit(solution)/shard_map/ppermute | solution.py:56
  24.3 2.4 %collective-permute-start.3 = (bf16[608,128]{1,0:T(8,128)(2,1)S(1)}, bf16[608,128]{1,0:T(8,128)(2,1)S(1)}, u32[]{:S(2)}, u32[]{:S(2)}) collective-permute-start(bf16[608,128]{1,0:T(8,128)(2,1)S(1)} %get-tuple-element.55), channel_id=1, source_target_pairs={{0,1},{1,0},{2,3},{3,2},{4,5},{5,4},{6,7},{7,6},{8,9},{9,8},{10,11... | collective-permute-start | bytes 466952 | tf_op jit(solution)/shard_map/ppermute | solution.py:56
  26.8 5.5 %collective-permute-start.6 = (bf16[608,128]{1,0:T(8,128)(2,1)S(1)}, bf16[608,128]{1,0:T(8,128)(2,1)S(1)}, u32[]{:S(2)}, u32[]{:S(2)}) collective-permute-start(bf16[608,128]{1,0:T(8,128)(2,1)S(1)} %convert_add_fusion.1), channel_id=1, source_target_pairs={{0,2},{2,0},{1,3},{3,1},{4,6},{6,4},{5,7},{7,5},{8,10},{10,8},{9,1... | collective-permute-start | bytes 466952 | tf_op jit(solution)/shard_map/ppermute | solution.py:56
  28.3 7.8 %collective-permute-start.10 = (bf16[2,336,128]{2,1,0:T(8,128)(2,1)S(1)}, bf16[2,336,128]{2,1,0:T(8,128)(2,1)S(1)}, u32[]{:S(2)}, u32[]{:S(2)}) collective-permute-start(bf16[2,336,128]{2,1,0:T(8,128)(2,1)S(1)} %pad_maximum_fusion), channel_id=1, source_target_pairs={{0,4},{4,0},{8,12},{12,8},{1,5},{5,1},{9,13},{13,9},{2,6},{6,2},{1... | collective-permute-start | bytes 516104 | tf_op jit(solution)/shard_map/ppermute | solution.py:56
  32.4 5.3 %collective-permute-start.8 = (f32[96,128]{1,0:T(8,128)S(1)}, f32[96,128]{1,0:T(8,128)S(1)}, u32[]{:S(2)}, u32[]{:S(2)}) collective-permute-start(f32[96,128]{1,0:T(8,128)S(1)} %get-tuple-element.64), channel_id=1, source_target_pairs={{0,4},{4,8},{8,12},{1,5},{5,9},{9,13},{2,6},{6,10},{10,14},{3,7},{... | collective-permute-start | bytes 147464 | tf_op jit(solution)/shard_map/ppermute | solution.py:51
  33.8 9.0 %collective-permute-start.7 = (bf16[608,128]{1,0:T(8,128)(2,1)S(1)}, bf16[608,128]{1,0:T(8,128)(2,1)S(1)}, u32[]{:S(2)}, u32[]{:S(2)}) collective-permute-start(bf16[608,128]{1,0:T(8,128)(2,1)S(1)} %add_convert_fusion.2), channel_id=1, source_target_pairs={{0,8},{4,12},{8,0},{12,4},{1,9},{5,13},{9,1},{13,5},{2,10},{6,14},... | collective-permute-start | bytes 466952 | tf_op jit(solution)/shard_map/ppermute | solution.py:56
  36.2 8.9 %collective-permute-start.11 = (bf16[4,336,128]{2,1,0:T(8,128)(2,1)S(1)}, bf16[4,336,128]{2,1,0:T(8,128)(2,1)S(1)}, u32[]{:S(2)}, u32[]{:S(2)}) collective-permute-start(bf16[4,336,128]{2,1,0:T(8,128)(2,1)S(1)} %constant_dynamic-update-slice_fusion.refs_1_), channel_id=1, source_target_pairs={{0,2},{2,0},{1,3},{3,1},{4,6},{6,4},{5,7},{7,5},{8,10},{10,8},{9,1... | collective-permute-start | bytes 1032200 | tf_op jit(solution)/shard_map/ppermute | solution.py:56
  42.8 5.3 %collective-permute-start.9 = (bf16[608,128]{1,0:T(8,128)(2,1)S(1)}, bf16[608,128]{1,0:T(8,128)(2,1)S(1)}, u32[]{:S(2)}, u32[]{:S(2)}) collective-permute-start(bf16[608,128]{1,0:T(8,128)(2,1)S(1)} %add_convert_fusion.1), channel_id=1, source_target_pairs={{0,4},{4,0},{8,12},{12,8},{1,5},{5,1},{9,13},{13,9},{2,6},{6,2},{1... | collective-permute-start | bytes 466952 | tf_op jit(solution)/shard_map/ppermute | solution.py:56
  46.5 1.9 %collective-permute-start.12 = (bf16[9,192,96]{2,1,0:T(8,128)(2,1)S(1)}, bf16[9,192,96]{2,1,0:T(8,128)(2,1)S(1)}, u32[]{:S(2)}, u32[]{:S(2)}) collective-permute-start(bf16[9,192,96]{2,1,0:T(8,128)(2,1)S(1)} %get-tuple-element.69), channel_id=1, source_target_pairs={{0,1},{1,0},{2,3},{3,2},{4,5},{5,4},{6,7},{7,6},{8,9},{9,8},{10,11... | collective-permute-start | bytes 995336 | tf_op jit(solution)/shard_map/ppermute | solution.py:56
  48.2 1.4 %collective-permute-start.13 = (bf16[608,128]{1,0:T(8,128)(2,1)S(1)}, bf16[608,128]{1,0:T(8,128)(2,1)S(1)}, u32[]{:S(2)}, u32[]{:S(2)}) collective-permute-start(bf16[608,128]{1,0:T(8,128)(2,1)S(1)} %add_convert_fusion.own_ref), channel_id=1, source_target_pairs={{0,1},{1,0},{2,3},{3,2},{4,5},{5,4},{6,7},{7,6},{8,9},{9,8},{10,11... | collective-permute-start | bytes 466952 | tf_op jit(solution)/shard_map/ppermute | solution.py:56

commit v15 on v11

--- a/solution.py
+++ b/solution.py
@@ -552,7 +552,7 @@
     gather = chunks == 1
     near = far = tile_blocks
     place = jnp.zeros((1,), jnp.int32)
-    spans = [("slide", 1 << n) for n in reversed(range(bands.bit_length() - 1))]
+    spans = [("slide", 1 << n) for n in range(bands.bit_length() - 1)]
     spans += [("rep", 1 << n) for n in range(lax.axis_size("rep").bit_length() - 1)]
 
     def widen(n, near, place):

time: 50.1 us -> 55 us (1.098)
  waiting for transfers between devices: 15.1 us -> 19.5 us
    ppermute x12, waiting for transfers between devices: 10.3 us -> 14.6 us  [swapped(): lax.ppermute(value, axis, [(place, place ^ step) for place in range(count)])]
    ppermute x2, starting transfers between devices: 2.75 us -> 3.88 us  [shifted(): lax.ppermute(value, axis, [(source, source + steps) for source in range(f...]
    ppermute x12, starting transfers between devices: 8.59 us -> 7.99 us  [swapped(): lax.ppermute(value, axis, [(place, place ^ step) for place in range(count)])]
  transfers between devices with their start and end apart: 15 -> 15, of which waited for: 8 -> 5; matrix products, arithmetic and copies ran while one was open for 2% -> 2% of each run, Pallas kernels for 23% -> 21%
where the time goes in v15:
time: 55 us; the launch traced here: 54.7 us
  waiting for transfers between devices  19.5 us (35%)
  starting transfers between devices  18.3 us (33%)
  Pallas kernels  14.4 us (26%)
  other arithmetic  1.23 us (2%)
  between operations  0.9 us (2%)
    ppermute x12, waiting for transfers between devices, swapped(): lax.ppermute(value, axis, [(place, place ^ step) for place in range(count)])  14.6 us
    ppermute x12, starting transfers between devices, swapped(): lax.ppermute(value, axis, [(place, place ^ step) for place in range(count)])  7.99 us
    all_to_all x1, starting transfers between devices, on_device(): lax.all_to_all(packed, ('slide', 'chan'), split_axis=0, concat_axis=0, ti...  6.46 us
    ppermute x2, waiting for transfers between devices, shifted(): lax.ppermute(value, axis, [(source, source + steps) for source in range(f...  4.84 us
    ppermute x2, starting transfers between devices, shifted(): lax.ppermute(value, axis, [(source, source + steps) for source in range(f...  3.88 us
    pallas_call x1, Pallas kernels, on_device(): agg_map = map_call(spread, key, above)  3.5 us
    pallas_call x1, Pallas kernels, on_device(): pl.pallas_call(lambda *refs: back_kernel(*refs, scale=loss_scale), grid=(...  2.95 us
    pallas_call x1, Pallas kernels, on_device(): pl.pallas_call(stem_kernel, grid=(chunks,), out_shape=(jax.ShapeDtypeStru...  2.25 us
  transfers between devices with their start and end apart: 15, of which 5 were waited for; matrix products, arithmetic and copies ran while one was open for 2% of the time, Pallas kernels for 21%

profile of v15, /device:TPU:0, one launch (start us, length us, event | category | flops | bytes accessed | tf_op | source)
XLA Modules:
  0.0 54.7 jit_solution(4080073683189814607)
XLA Ops:
  0.6 1.9 %pack.1 = (bf16[8,56,128]{2,1,0:T(8,128)(2,1)}, bf16[96,128]{1,0:T(8,128)(2,1)}) custom-call(s32[1,8]{1,0:T(1,128)} %cells_ref.1, bf16[1,8,6144]{2,1,0:T(8,128)(2,1)} %pixels_ref.1, f32[1,16,96,128]{3,2,1,0:T(8,128)} %cot_ref.1), custom_call_target="tpu_custom_call" | custom-call | bytes 5535000 | tf_op jit(solution)/shard_map/pack/pallas_call | solution.py:439
  2.5 6.5 %all-to-all-start = ((bf16[8,56,128]{2,1,0:T(8,128)(2,1)}), bf16[8,56,128]{2,1,0:T(8,128)(2,1)S(1)}, u32[]{:S(2)}, u32[]{:S(2)}) async-start(bf16[8,56,128]{2,1,0:T(8,128)(2,1)} %get-tuple-element.42), calls=%async_computation | async-start | bytes 229376 | tf_op jit(solution)/shard_map/all_to_all | solution.py:462
  9.0 0.5 collective-permute-start.2
  9.5 1.3 %collective-permute-start = (bf16[96,128]{1,0:T(8,128)(2,1)S(1)}, bf16[96,128]{1,0:T(8,128)(2,1)S(1)}, u32[]{:S(2)}, u32[]{:S(2)}) collective-permute-start(bf16[96,128]{1,0:T(8,128)(2,1)S(1)} %copy-done.9), channel_id=1, source_target_pairs={{4,0},{8,4},{12,8},{5,1},{9,5},{13,9},{6,2},{10,6},{14,10},{7,3},{... | collective-permute-start | bytes 73736 | tf_op jit(solution)/shard_map/ppermute | solution.py:51
  10.8 4.8 %collective-permute-done.below_ref = bf16[96,128]{1,0:T(8,128)(2,1)S(1)} collective-permute-done((bf16[96,128]{1,0:T(8,128)(2,1)S(1)}, bf16[96,128]{1,0:T(8,128)(2,1)S(1)}, u32[]{:S(2)}, u32[]{:S(2)}) %collective-permute-start) | collective-permute-done | bytes 24608 | tf_op jit(solution)/shard_map/ppermute | solution.py:51
  15.6 0.0 all-to-all-done.meta_ref.got_ref.refs_5_
  15.6 0.0 copy-start.3
  15.6 0.0 copy-start.4
  15.7 0.0 copy-start.5
  15.7 0.0 copy-start.6
  15.7 0.0 copy-start.7
  15.7 0.0 copy-start.8
  15.7 0.5 patch.1
  16.2 0.0 copy-start.1
  16.2 0.1 collective-permute-start.1
  16.3 0.3 copy-done.2
  16.5 0.0 copy-done.3
  16.6 0.0 copy-done.4
  16.6 2.2 %stem.1 = (bf16[1,192,128]{2,1,0:T(8,128)(2,1)S(1)}, f32[1,512,96]{2,1,0:T(8,128)S(1)}, f32[1,512,1]{2,1,0:T(8,128)S(1)}, f32[1,512,96]{2,1,0:T(8,128)S(1)}, f32...) custom-call(bf16[8,56,128]{2,1,0:T(8,128)(2,1)S(1)} %all-to-all-done, ...), custom_call_target="tpu_custom_call" | custom-call | bytes 9963000 | tf_op jit(solution)/shard_map/stem/pallas_call | solution.py:499
  18.9 0.2 collective-permute-start.5
  19.1 0.0 collective-permute-done.1
  19.1 1.4 %collective-permute-start.4 = (bf16[1,336,128]{2,1,0:T(8,128)(2,1)S(1)}, bf16[1,336,128]{2,1,0:T(8,128)(2,1)S(1)}, u32[]{:S(2)}, u32[]{:S(2)}) collective-permute-start(bf16[1,336,128]{2,1,0:T(8,128)(2,1)S(1)} %pad_maximum_fusion.3), channel_id=1, source_target_pairs={{0,4},{4,0},{8,12},{12,8},{1,5},{5,1},{9,13},{13,9},{2,6},{6,2},{1... | collective-permute-start | bytes 258056 | tf_op jit(solution)/shard_map/ppermute | solution.py:56
  20.5 0.0 collective-permute-done.2.refs_4_
  20.5 2.9 %stem_back.1 = (f32[608,128]{1,0:T(8,128)S(1)}, bf16[608,128]{1,0:T(8,128)(2,1)S(1)}) custom-call(s32[1]{0:T(128)} %bitcast.chan_ref.refs_0_, bf16[1,72,128]{2,1,0:T(8,128)(2,1)S(1)} %bitcast.17, bf16[1,72,128]{2,1,0:T(8,128)(2,1)S(1)} %bitcast.20, bf16[9,192,96]{2,1,0:T(8,128)(2,1)S(1)} %copy-done.1, ...), custom_call_target="tpu_custom_call" | custom-call | bytes 13653000 | tf_op jit(solution)/shard_map/stem_back/pallas_call | solution.py:567
  23.5 0.1 collective-permute-start.3
  23.6 0.0 collective-permute-done.5
  23.6 1.0 %spread.1 = (f32[144,96]{1,0:T(8,128)S(1)}, f32[96,128]{1,0:T(8,128)S(1)}) custom-call(bf16[2,192,128]{2,1,0:T(8,128)(2,1)S(1)} %pad_maximum_fusion.2.refs_0_, bf16[9,192,96]{2,1,0:T(8,128)(2,1)S(1)} %copy-done.1, f32[144,128]{1,0:T(8,128)S(1)} %get-tuple-element.57.refs_2_.key_ref), custom_call_target="tpu_custom_call" | custom-call | bytes 3690000 | tf_op jit(solution)/shard_map/spread/pallas_call | solution.py:535
  24.7 0.0 collective-permute-done.4
  24.7 0.2 collective-permute-done.3
  25.0 1.6 %collective-permute-start.9 = (bf16[608,128]{1,0:T(8,128)(2,1)S(1)}, bf16[608,128]{1,0:T(8,128)(2,1)S(1)}, u32[]{:S(2)}, u32[]{:S(2)}) collective-permute-start(bf16[608,128]{1,0:T(8,128)(2,1)S(1)} %convert_add_fusion.1), channel_id=1, source_target_pairs={{0,2},{2,0},{1,3},{3,1},{4,6},{6,4},{5,7},{7,5},{8,10},{10,8},{9,1... | collective-permute-start | bytes 466952 | tf_op jit(solution)/shard_map/ppermute | solution.py:56
  26.5 2.6 %collective-permute-start.7 = (f32[96,128]{1,0:T(8,128)S(1)}, f32[96,128]{1,0:T(8,128)S(1)}, u32[]{:S(2)}, u32[]{:S(2)}) collective-permute-start(f32[96,128]{1,0:T(8,128)S(1)} %get-tuple-element.61), channel_id=1, source_target_pairs={{0,4},{4,8},{8,12},{1,5},{5,9},{9,13},{2,6},{6,10},{10,14},{3,7},{... | collective-permute-start | bytes 147464 | tf_op jit(solution)/shard_map/ppermute | solution.py:51
  29.1 2.2 %collective-permute-start.6 = (bf16[2,336,128]{2,1,0:T(8,128)(2,1)S(1)}, bf16[2,336,128]{2,1,0:T(8,128)(2,1)S(1)}, u32[]{:S(2)}, u32[]{:S(2)}) collective-permute-start(bf16[2,336,128]{2,1,0:T(8,128)(2,1)S(1)} %pad_maximum_fusion.1), channel_id=1, source_target_pairs={{0,8},{4,12},{8,0},{12,4},{1,9},{5,13},{9,1},{13,5},{2,10},{6,14},... | collective-permute-start | bytes 516104 | tf_op jit(solution)/shard_map/ppermute | solution.py:56
  31.3 0.0 collective-permute-done.9
  31.4 0.6 %collective-permute-start.10 = (bf16[608,128]{1,0:T(8,128)(2,1)S(1)}, bf16[608,128]{1,0:T(8,128)(2,1)S(1)}, u32[]{:S(2)}, u32[]{:S(2)}) collective-permute-start(bf16[608,128]{1,0:T(8,128)(2,1)S(1)} %add_convert_fusion.2), channel_id=1, source_target_pairs={{0,4},{4,0},{8,12},{12,8},{1,5},{5,1},{9,13},{13,9},{2,6},{6,2},{1... | collective-permute-start | bytes 466952 | tf_op jit(solution)/shard_map/ppermute | solution.py:56
  32.0 7.8 %collective-permute-done.6 = bf16[2,336,128]{2,1,0:T(8,128)(2,1)S(1)} collective-permute-done((bf16[2,336,128]{2,1,0:T(8,128)(2,1)S(1)}, bf16[2,336,128]{2,1,0:T(8,128)(2,1)S(1)}, u32[]{:S(2)}, u32[]{:S(2)}) %collective-permute-start.6) | collective-permute-done | bytes 172064 | tf_op jit(solution)/shard_map/ppermute | solution.py:56
  39.9 0.0 collective-permute-done.7.above_ref
  39.9 0.6 %collective-permute-start.8 = (bf16[4,336,128]{2,1,0:T(8,128)(2,1)S(1)}, bf16[4,336,128]{2,1,0:T(8,128)(2,1)S(1)}, u32[]{:S(2)}, u32[]{:S(2)}) collective-permute-start(bf16[4,336,128]{2,1,0:T(8,128)(2,1)S(1)} %pad_maximum_fusion.refs_1_), channel_id=1, source_target_pairs={{0,2},{2,0},{1,3},{3,1},{4,6},{6,4},{5,7},{7,5},{8,10},{10,8},{9,1... | collective-permute-start | bytes 1032200 | tf_op jit(solution)/shard_map/ppermute | solution.py:56
  40.5 0.0 collective-permute-done.10
  40.5 0.1 collective-permute-start.11
  40.7 3.5 %agg_map.1 = bf16[16,96,128]{2,1,0:T(8,128)(2,1)} custom-call(f32[144,96]{1,0:T(8,128)S(1)} %get-tuple-element.63.y_ref, f32[144,128]{1,0:T(8,128)S(1)} %get-tuple-element.57.refs_2_.key_ref, f32[96,128]{1,0:T(8,128)S(1)} %collective-permute-done.7.above_ref), custom_call_target="tpu_custom_call" | custom-call | bytes 12915000 | tf_op jit(solution)/shard_map/agg_map/pallas_call | solution.py:634
  44.2 5.4 %collective-permute-done.8.refs_2_ = bf16[4,336,128]{2,1,0:T(8,128)(2,1)S(1)} collective-permute-done((bf16[4,336,128]{2,1,0:T(8,128)(2,1)S(1)}, bf16[4,336,128]{2,1,0:T(8,128)(2,1)S(1)}, u32[]{:S(2)}, u32[]{:S(2)}) %collective-permute-start.8) | collective-permute-done | bytes 344096 | tf_op jit(solution)/shard_map/ppermute | solution.py:56
  49.6 1.4 %agg_weight_grad.1 = (f32[9,192,96]{2,1,0:T(8,128)S(1)}, bf16[9,192,96]{2,1,0:T(8,128)(2,1)S(1)}) custom-call(s32[1]{0:T(128)} %bitcast.9.refs_0_, bf16[4,336,128]{2,1,0:T(8,128)(2,1)S(1)} %pad_maximum_fusion.refs_1_, bf16[4,336,128]{2,1,0:T(8,128)(2,1)S(1)} %collective-permute-done.8.refs_2_), custom_call_target="tpu_custom_call" | custom-call | bytes 5166000 | tf_op jit(solution)/shard_map/agg_weight_grad/pallas_call | solution.py:640
  51.0 0.1 collective-permute-start.12
  51.1 0.0 collective-permute-done.11
  51.1 0.6 %collective-permute-start.13 = (bf16[608,128]{1,0:T(8,128)(2,1)S(1)}, bf16[608,128]{1,0:T(8,128)(2,1)S(1)}, u32[]{:S(2)}, u32[]{:S(2)}) collective-permute-start(bf16[608,128]{1,0:T(8,128)(2,1)S(1)} %add_convert_fusion.own_ref), channel_id=1, source_target_pairs={{0,1},{1,0},{2,3},{3,2},{4,5},{5,4},{6,7},{7,6},{8,9},{9,8},{10,11... | collective-permute-start | bytes 466952 | tf_op jit(solution)/shard_map/ppermute | solution.py:56
  51.7 1.2 %collective-permute-done.12 = bf16[9,192,96]{2,1,0:T(8,128)(2,1)S(1)} collective-permute-done((bf16[9,192,96]{2,1,0:T(8,128)(2,1)S(1)}, bf16[9,192,96]{2,1,0:T(8,128)(2,1)S(1)}, u32[]{:S(2)}, u32[]{:S(2)}) %collective-permute-start.12) | collective-permute-done | bytes 331808 | tf_op jit(solution)/shard_map/ppermute | solution.py:56
  52.9 1.0 %convert_add_fusion = f32[9,192,96]{2,1,0:T(8,128)} fusion(f32[9,192,96]{2,1,0:T(8,128)S(1)} %get-tuple-element.68, bf16[9,192,96]{2,1,0:T(8,128)(2,1)S(1)} %collective-permute-done.12), kind=kLoop, calls=%fused_computation | loop fusion | flops 331776 | bytes 1658880 | tf_op jit(solution)/shard_map/add | solution.py:662
  53.8 0.9 %unpack.1 = (f32[49,96]{1,0:T(8,128)}, f32[96,384]{1,0:T(8,128)}, f32[96,384]{1,0:T(8,128)}, f32[192,384]{1,0:T(8,128)}) custom-call(s32[1]{0:T(128)} %bitcast.chan_ref.refs_0_, bf16[608,128]{1,0:T(8,128)(2,1)S(1)} %add_convert_fusion.own_ref, bf16[608,128]{1,0:T(8,128)(2,1)S(1)} %collective-permute-done.13.peer_ref), custom_call_target="tpu_custom_call" | custom-call | bytes 5535000 | tf_op jit(solution)/shard_map/unpack/pallas_call | solution.py:669
  (19 shorter events, 0.3 us)
Async XLA Ops:
  0.6 15.0 %copy-start = (f32[1,16,96,128]{3,2,1,0:T(8,128)S(1)}, f32[1,16,96,128]{3,2,1,0:T(8,128)}, u32[]{:S(2)}) copy-start(f32[1,16,96,128]{3,2,1,0:T(8,128)} %cot_ref.1) | copy-start | bytes 2359300
  2.5 7.0 %copy-start.9 = (bf16[96,128]{1,0:T(8,128)(2,1)S(1)}, bf16[96,128]{1,0:T(8,128)(2,1)}, u32[]{:S(2)}) copy-start(bf16[96,128]{1,0:T(8,128)(2,1)} %get-tuple-element.43) | copy-start | bytes 73732
  2.5 13.1 %all-to-all-start = ((bf16[8,56,128]{2,1,0:T(8,128)(2,1)}), bf16[8,56,128]{2,1,0:T(8,128)(2,1)S(1)}, u32[]{:S(2)}, u32[]{:S(2)}) async-start(bf16[8,56,128]{2,1,0:T(8,128)(2,1)} %get-tuple-element.42), calls=%async_computation | async-start | bytes 229376 | tf_op jit(solution)/shard_map/all_to_all | solution.py:462
  9.0 11.5 %collective-permute-start.2 = (bf16[9,192,96]{2,1,0:T(8,128)(2,1)}, bf16[9,192,96]{2,1,0:T(8,128)(2,1)S(1)}, u32[]{:S(2)}, u32[]{:S(2)}) collective-permute-start(bf16[9,192,96]{2,1,0:T(8,128)(2,1)} %refs_1_.1), channel_id=1, source_target_pairs={{0,1},{1,0},{2,3},{3,2},{4,5},{5,4},{6,7},{7,6},{8,9},{9,8},{10,11... | collective-permute-start | bytes 995336 | tf_op jit(solution)/shard_map/ppermute | solution.py:56
  9.5 6.1 %collective-permute-start = (bf16[96,128]{1,0:T(8,128)(2,1)S(1)}, bf16[96,128]{1,0:T(8,128)(2,1)S(1)}, u32[]{:S(2)}, u32[]{:S(2)}) collective-permute-start(bf16[96,128]{1,0:T(8,128)(2,1)S(1)} %copy-done.9), channel_id=1, source_target_pairs={{4,0},{8,4},{12,8},{5,1},{9,5},{13,9},{6,2},{10,6},{14,10},{7,3},{... | collective-permute-start | bytes 73736 | tf_op jit(solution)/shard_map/ppermute | solution.py:51
  15.6 0.9 %copy-start.2 = (bf16[384,192]{0,1:T(8,128)(2,1)S(1)}, bf16[384,192]{0,1:T(8,128)(2,1)}, u32[]{:S(2)}) copy-start(bf16[384,192]{0,1:T(8,128)(2,1)} %param.20) | copy-start | bytes 442372
  15.6 1.0 %copy-start.3 = (bf16[96,384]{1,0:T(8,128)(2,1)S(1)}, bf16[96,384]{1,0:T(8,128)(2,1)}, u32[]{:S(2)}) copy-start(bf16[96,384]{1,0:T(8,128)(2,1)} %refs_14_.1) | copy-start | bytes 221188
  15.6 1.0 %copy-start.4 = (bf16[384,96]{0,1:T(8,128)(2,1)S(1)}, bf16[384,96]{0,1:T(8,128)(2,1)}, u32[]{:S(2)}) copy-start(bf16[384,96]{0,1:T(8,128)(2,1)} %param.17) | copy-start | bytes 221188
  15.7 1.0 %copy-start.5 = (f32[49,96]{1,0:T(8,128)S(1)}, f32[49,96]{1,0:T(8,128)}, u32[]{:S(2)}) copy-start(f32[49,96]{1,0:T(8,128)} %dw_ref.1) | copy-start | bytes 56452
  15.7 1.0 %copy-start.6 = (f32[96]{0:T(128)S(1)}, f32[96]{0:T(128)}, u32[]{:S(2)}) copy-start(f32[96]{0:T(128)} %param.15) | copy-start | bytes 1156
  15.7 1.0 %copy-start.7 = (f32[96]{0:T(128)S(1)}, f32[96]{0:T(128)}, u32[]{:S(2)}) copy-start(f32[96]{0:T(128)} %param.18) | copy-start | bytes 1156
  15.7 0.9 %copy-start.8 = (f32[96]{0:T(128)S(1)}, f32[96]{0:T(128)}, u32[]{:S(2)}) copy-start(f32[96]{0:T(128)} %param.19) | copy-start | bytes 1156
  16.2 4.3 %copy-start.1 = (bf16[9,192,96]{2,1,0:T(8,128)(2,1)S(1)}, bf16[9,192,96]{2,1,0:T(8,128)(2,1)}, u32[]{:S(2)}) copy-start(bf16[9,192,96]{2,1,0:T(8,128)(2,1)} %refs_1_.1) | copy-start | bytes 995332
  16.2 2.9 %collective-permute-start.1 = (bf16[72,128]{1,0:T(8,128)(2,1)S(1)}, bf16[72,128]{1,0:T(8,128)(2,1)S(1)}, u32[]{:S(2)}, u32[]{:S(2)}) collective-permute-start(bf16[72,128]{1,0:T(8,128)(2,1)S(1)} %get-tuple-element.45), channel_id=1, source_target_pairs={{0,1},{1,0},{2,3},{3,2},{4,5},{5,4},{6,7},{7,6},{8,9},{9,8},{10,11... | collective-permute-start | bytes 55304 | tf_op jit(solution)/shard_map/ppermute | solution.py:56
  18.9 4.7 %collective-permute-start.5 = (bf16[1,192,128]{2,1,0:T(8,128)(2,1)S(1)}, bf16[1,192,128]{2,1,0:T(8,128)(2,1)S(1)}, u32[]{:S(2)}, u32[]{:S(2)}) collective-permute-start(bf16[1,192,128]{2,1,0:T(8,128)(2,1)S(1)} %get-tuple-element.56), channel_id=1, source_target_pairs={{0,1},{1,0},{2,3},{3,2},{4,5},{5,4},{6,7},{7,6},{8,9},{9,8},{10,11... | collective-permute-start | bytes 147464 | tf_op jit(solution)/shard_map/ppermute | solution.py:56
  19.1 5.6 %collective-permute-start.4 = (bf16[1,336,128]{2,1,0:T(8,128)(2,1)S(1)}, bf16[1,336,128]{2,1,0:T(8,128)(2,1)S(1)}, u32[]{:S(2)}, u32[]{:S(2)}) collective-permute-start(bf16[1,336,128]{2,1,0:T(8,128)(2,1)S(1)} %pad_maximum_fusion.3), channel_id=1, source_target_pairs={{0,4},{4,0},{8,12},{12,8},{1,5},{5,1},{9,13},{13,9},{2,6},{6,2},{1... | collective-permute-start | bytes 258056 | tf_op jit(solution)/shard_map/ppermute | solution.py:56
  23.5 1.4 %collective-permute-start.3 = (bf16[608,128]{1,0:T(8,128)(2,1)S(1)}, bf16[608,128]{1,0:T(8,128)(2,1)S(1)}, u32[]{:S(2)}, u32[]{:S(2)}) collective-permute-start(bf16[608,128]{1,0:T(8,128)(2,1)S(1)} %get-tuple-element.55), channel_id=1, source_target_pairs={{0,1},{1,0},{2,3},{3,2},{4,5},{5,4},{6,7},{7,6},{8,9},{9,8},{10,11... | collective-permute-start | bytes 466952 | tf_op jit(solution)/shard_map/ppermute | solution.py:56
  25.0 6.4 %collective-permute-start.9 = (bf16[608,128]{1,0:T(8,128)(2,1)S(1)}, bf16[608,128]{1,0:T(8,128)(2,1)S(1)}, u32[]{:S(2)}, u32[]{:S(2)}) collective-permute-start(bf16[608,128]{1,0:T(8,128)(2,1)S(1)} %convert_add_fusion.1), channel_id=1, source_target_pairs={{0,2},{2,0},{1,3},{3,1},{4,6},{6,4},{5,7},{7,5},{8,10},{10,8},{9,1... | collective-permute-start | bytes 466952 | tf_op jit(solution)/shard_map/ppermute | solution.py:56
  26.5 13.4 %collective-permute-start.7 = (f32[96,128]{1,0:T(8,128)S(1)}, f32[96,128]{1,0:T(8,128)S(1)}, u32[]{:S(2)}, u32[]{:S(2)}) collective-permute-start(f32[96,128]{1,0:T(8,128)S(1)} %get-tuple-element.61), channel_id=1, source_target_pairs={{0,4},{4,8},{8,12},{1,5},{5,9},{9,13},{2,6},{6,10},{10,14},{3,7},{... | collective-permute-start | bytes 147464 | tf_op jit(solution)/shard_map/ppermute | solution.py:51
  29.1 10.7 %collective-permute-start.6 = (bf16[2,336,128]{2,1,0:T(8,128)(2,1)S(1)}, bf16[2,336,128]{2,1,0:T(8,128)(2,1)S(1)}, u32[]{:S(2)}, u32[]{:S(2)}) collective-permute-start(bf16[2,336,128]{2,1,0:T(8,128)(2,1)S(1)} %pad_maximum_fusion.1), channel_id=1, source_target_pairs={{0,8},{4,12},{8,0},{12,4},{1,9},{5,13},{9,1},{13,5},{2,10},{6,14},... | collective-permute-start | bytes 516104 | tf_op jit(solution)/shard_map/ppermute | solution.py:56
  31.4 9.1 %collective-permute-start.10 = (bf16[608,128]{1,0:T(8,128)(2,1)S(1)}, bf16[608,128]{1,0:T(8,128)(2,1)S(1)}, u32[]{:S(2)}, u32[]{:S(2)}) collective-permute-start(bf16[608,128]{1,0:T(8,128)(2,1)S(1)} %add_convert_fusion.2), channel_id=1, source_target_pairs={{0,4},{4,0},{8,12},{12,8},{1,5},{5,1},{9,13},{13,9},{2,6},{6,2},{1... | collective-permute-start | bytes 466952 | tf_op jit(solution)/shard_map/ppermute | solution.py:56
  39.9 9.7 %collective-permute-start.8 = (bf16[4,336,128]{2,1,0:T(8,128)(2,1)S(1)}, bf16[4,336,128]{2,1,0:T(8,128)(2,1)S(1)}, u32[]{:S(2)}, u32[]{:S(2)}) collective-permute-start(bf16[4,336,128]{2,1,0:T(8,128)(2,1)S(1)} %pad_maximum_fusion.refs_1_), channel_id=1, source_target_pairs={{0,2},{2,0},{1,3},{3,1},{4,6},{6,4},{5,7},{7,5},{8,10},{10,8},{9,1... | collective-permute-start | bytes 1032200 | tf_op jit(solution)/shard_map/ppermute | solution.py:56
  40.5 10.5 %collective-permute-start.11 = (bf16[608,128]{1,0:T(8,128)(2,1)S(1)}, bf16[608,128]{1,0:T(8,128)(2,1)S(1)}, u32[]{:S(2)}, u32[]{:S(2)}) collective-permute-start(bf16[608,128]{1,0:T(8,128)(2,1)S(1)} %add_convert_fusion.1), channel_id=1, source_target_pairs={{0,8},{4,12},{8,0},{12,4},{1,9},{5,13},{9,1},{13,5},{2,10},{6,14},... | collective-permute-start | bytes 466952 | tf_op jit(solution)/shard_map/ppermute | solution.py:56
  51.0 1.9 %collective-permute-start.12 = (bf16[9,192,96]{2,1,0:T(8,128)(2,1)S(1)}, bf16[9,192,96]{2,1,0:T(8,128)(2,1)S(1)}, u32[]{:S(2)}, u32[]{:S(2)}) collective-permute-start(bf16[9,192,96]{2,1,0:T(8,128)(2,1)S(1)} %get-tuple-element.69), channel_id=1, source_target_pairs={{0,1},{1,0},{2,3},{3,2},{4,5},{5,4},{6,7},{7,6},{8,9},{9,8},{10,11... | collective-permute-start | bytes 995336 | tf_op jit(solution)/shard_map/ppermute | solution.py:56
  51.1 2.7 %collective-permute-start.13 = (bf16[608,128]{1,0:T(8,128)(2,1)S(1)}, bf16[608,128]{1,0:T(8,128)(2,1)S(1)}, u32[]{:S(2)}, u32[]{:S(2)}) collective-permute-start(bf16[608,128]{1,0:T(8,128)(2,1)S(1)} %add_convert_fusion.own_ref), channel_id=1, source_target_pairs={{0,1},{1,0},{2,3},{3,2},{4,5},{5,4},{6,7},{7,6},{8,9},{9,8},{10,11... | collective-permute-start | bytes 466952 | tf_op jit(solution)/shard_map/ppermute | solution.py:56

commit v16 on v13

--- a/solution.py
+++ b/solution.py
@@ -606,8 +606,6 @@
         part, near, spread, below = lax.optimization_barrier((part, near, spread, below))
     above = shifted(below, "slide", 1)
     for n in range(1, len(spans) if gather else 0):
-        if n == len(spans) - 1:
-            near, above = lax.optimization_barrier((near, above))
         far, place = widen(n, near, place)
         if n < len(spans) - 1:
             near = jnp.concatenate([near, far], axis=0)

time: 49.7 us -> 49.7 us (level)
  no operation moved by 1% of the time
where the time goes in v16:
time: 49.7 us; the launch traced here: 49.4 us
  starting transfers between devices  17.6 us (35%)
  waiting for transfers between devices  15 us (30%)
  Pallas kernels  14.3 us (29%)
  other arithmetic  1.19 us (2%)
  between operations  0.85 us (2%)
    ppermute x12, waiting for transfers between devices, swapped(): lax.ppermute(value, axis, [(place, place ^ step) for place in range(count)])  10.1 us
    ppermute x12, starting transfers between devices, swapped(): lax.ppermute(value, axis, [(place, place ^ step) for place in range(count)])  8.38 us
    all_to_all x1, starting transfers between devices, on_device(): lax.all_to_all(packed, ('slide', 'chan'), split_axis=0, concat_axis=0, ti...  6.46 us
    ppermute x2, waiting for transfers between devices, shifted(): lax.ppermute(value, axis, [(source, source + steps) for source in range(f...  4.84 us
    pallas_call x1, Pallas kernels, on_device(): agg_map = map_call(spread, key, above)  3.5 us
    pallas_call x1, Pallas kernels, on_device(): pl.pallas_call(lambda *refs: back_kernel(*refs, scale=loss_scale), grid=(...  2.94 us
    ppermute x2, starting transfers between devices, shifted(): lax.ppermute(value, axis, [(source, source + steps) for source in range(f...  2.75 us
    pallas_call x1, Pallas kernels, on_device(): pl.pallas_call(stem_kernel, grid=(chunks,), out_shape=(jax.ShapeDtypeStru...  2.24 us
  transfers between devices with their start and end apart: 15, of which 8 were waited for; matrix products, arithmetic and copies ran while one was open for 2% of the time, Pallas kernels for 23%

profile of v16, /device:TPU:0, one launch (start us, length us, event | category | flops | bytes accessed | tf_op | source)
XLA Modules:
  0.0 49.4 jit_solution(10244680421280587288)
XLA Ops:
  0.6 1.9 %pack.1 = (bf16[8,56,128]{2,1,0:T(8,128)(2,1)}, bf16[96,128]{1,0:T(8,128)(2,1)}) custom-call(s32[1,8]{1,0:T(1,128)} %cells_ref.1, bf16[1,8,6144]{2,1,0:T(8,128)(2,1)} %pixels_ref.1, f32[1,16,96,128]{3,2,1,0:T(8,128)} %cot_ref.1), custom_call_target="tpu_custom_call" | custom-call | bytes 5535000 | tf_op jit(solution)/shard_map/pack/pallas_call | solution.py:439
  2.5 6.5 %all-to-all-start = ((bf16[8,56,128]{2,1,0:T(8,128)(2,1)}), bf16[8,56,128]{2,1,0:T(8,128)(2,1)S(1)}, u32[]{:S(2)}, u32[]{:S(2)}) async-start(bf16[8,56,128]{2,1,0:T(8,128)(2,1)} %get-tuple-element.40), calls=%async_computation | async-start | bytes 229376 | tf_op jit(solution)/shard_map/all_to_all | solution.py:462
  9.0 0.5 %collective-permute-start.2 = (bf16[9,192,96]{2,1,0:T(8,128)(2,1)}, bf16[9,192,96]{2,1,0:T(8,128)(2,1)S(1)}, u32[]{:S(2)}, u32[]{:S(2)}) collective-permute-start(bf16[9,192,96]{2,1,0:T(8,128)(2,1)} %refs_1_.1), channel_id=1, source_target_pairs={{0,1},{1,0},{2,3},{3,2},{4,5},{5,4},{6,7},{7,6},{8,9},{9,8},{10,11... | collective-permute-start | bytes 995336 | tf_op jit(solution)/shard_map/ppermute | solution.py:56
  9.5 1.3 %collective-permute-start = (bf16[96,128]{1,0:T(8,128)(2,1)S(1)}, bf16[96,128]{1,0:T(8,128)(2,1)S(1)}, u32[]{:S(2)}, u32[]{:S(2)}) collective-permute-start(bf16[96,128]{1,0:T(8,128)(2,1)S(1)} %copy-done.9), channel_id=1, source_target_pairs={{4,0},{8,4},{12,8},{5,1},{9,5},{13,9},{6,2},{10,6},{14,10},{7,3},{... | collective-permute-start | bytes 73736 | tf_op jit(solution)/shard_map/ppermute | solution.py:51
  10.8 4.8 %collective-permute-done.below_ref = bf16[96,128]{1,0:T(8,128)(2,1)S(1)} collective-permute-done((bf16[96,128]{1,0:T(8,128)(2,1)S(1)}, bf16[96,128]{1,0:T(8,128)(2,1)S(1)}, u32[]{:S(2)}, u32[]{:S(2)}) %collective-permute-start) | collective-permute-done | bytes 24608 | tf_op jit(solution)/shard_map/ppermute | solution.py:51
  15.6 0.0 all-to-all-done.meta_ref.got_ref.refs_5_
  15.6 0.0 copy-start.3
  15.6 0.0 copy-start.4
  15.7 0.0 copy-start.5
  15.7 0.0 copy-start.6
  15.7 0.0 copy-start.7
  15.7 0.0 copy-start.8
  15.7 0.5 patch.1
  16.2 0.0 copy-start.1
  16.2 0.1 collective-permute-start.1
  16.3 0.3 copy-done.2
  16.5 0.0 copy-done.3
  16.6 0.0 copy-done.4
  16.6 2.2 %stem.1 = (bf16[1,192,128]{2,1,0:T(8,128)(2,1)S(1)}, f32[1,512,96]{2,1,0:T(8,128)S(1)}, f32[1,512,1]{2,1,0:T(8,128)S(1)}, f32[1,512,96]{2,1,0:T(8,128)S(1)}, f32...) custom-call(bf16[8,56,128]{2,1,0:T(8,128)(2,1)S(1)} %all-to-all-done, ...), custom_call_target="tpu_custom_call" | custom-call | bytes 9963000 | tf_op jit(solution)/shard_map/stem/pallas_call | solution.py:499
  18.9 0.2 collective-permute-start.5
  19.1 0.0 collective-permute-done.1
  19.1 2.2 %collective-permute-start.4 = (bf16[1,336,128]{2,1,0:T(8,128)(2,1)S(1)}, bf16[1,336,128]{2,1,0:T(8,128)(2,1)S(1)}, u32[]{:S(2)}, u32[]{:S(2)}) collective-permute-start(bf16[1,336,128]{2,1,0:T(8,128)(2,1)S(1)} %pad_maximum_fusion.2), channel_id=1, source_target_pairs={{0,8},{4,12},{8,0},{12,4},{1,9},{5,13},{9,1},{13,5},{2,10},{6,14},... | collective-permute-start | bytes 258056 | tf_op jit(solution)/shard_map/ppermute | solution.py:56
  21.3 0.0 collective-permute-done.2.refs_4_
  21.3 2.9 %stem_back.1 = (f32[608,128]{1,0:T(8,128)S(1)}, bf16[608,128]{1,0:T(8,128)(2,1)S(1)}) custom-call(s32[1]{0:T(128)} %bitcast.chan_ref.refs_0_, bf16[1,72,128]{2,1,0:T(8,128)(2,1)S(1)} %bitcast.17, bf16[1,72,128]{2,1,0:T(8,128)(2,1)S(1)} %bitcast.20, bf16[9,192,96]{2,1,0:T(8,128)(2,1)S(1)} %copy-done.1, ...), custom_call_target="tpu_custom_call" | custom-call | bytes 13653000 | tf_op jit(solution)/shard_map/stem_back/pallas_call | solution.py:567
  24.3 0.1 collective-permute-start.3
  24.4 0.0 collective-permute-done.5
  24.4 1.0 %spread.1 = (f32[144,96]{1,0:T(8,128)S(1)}, f32[96,128]{1,0:T(8,128)S(1)}) custom-call(bf16[2,192,128]{2,1,0:T(8,128)(2,1)S(1)} %pad_maximum_fusion.1.refs_0_, bf16[9,192,96]{2,1,0:T(8,128)(2,1)S(1)} %copy-done.1, f32[144,128]{1,0:T(8,128)S(1)} %get-tuple-element.55.refs_2_.key_ref), custom_call_target="tpu_custom_call" | custom-call | bytes 3690000 | tf_op jit(solution)/shard_map/spread/pallas_call | solution.py:535
  25.5 1.2 %collective-permute-done.4 = bf16[1,336,128]{2,1,0:T(8,128)(2,1)S(1)} collective-permute-done((bf16[1,336,128]{2,1,0:T(8,128)(2,1)S(1)}, bf16[1,336,128]{2,1,0:T(8,128)(2,1)S(1)}, u32[]{:S(2)}, u32[]{:S(2)}) %collective-permute-start.4) | collective-permute-done | bytes 86048 | tf_op jit(solution)/shard_map/ppermute | solution.py:56
  26.7 0.0 collective-permute-done.3
  26.8 1.6 %collective-permute-start.6 = (bf16[608,128]{1,0:T(8,128)(2,1)S(1)}, bf16[608,128]{1,0:T(8,128)(2,1)S(1)}, u32[]{:S(2)}, u32[]{:S(2)}) collective-permute-start(bf16[608,128]{1,0:T(8,128)(2,1)S(1)} %convert_add_fusion.1), channel_id=1, source_target_pairs={{0,2},{2,0},{1,3},{3,1},{4,6},{6,4},{5,7},{7,5},{8,10},{10,8},{9,1... | collective-permute-start | bytes 466952 | tf_op jit(solution)/shard_map/ppermute | solution.py:56
  28.3 1.5 %collective-permute-start.8 = (f32[96,128]{1,0:T(8,128)S(1)}, f32[96,128]{1,0:T(8,128)S(1)}, u32[]{:S(2)}, u32[]{:S(2)}) collective-permute-start(f32[96,128]{1,0:T(8,128)S(1)} %get-tuple-element.60), channel_id=1, source_target_pairs={{0,4},{4,8},{8,12},{1,5},{5,9},{9,13},{2,6},{6,10},{10,14},{3,7},{... | collective-permute-start | bytes 147464 | tf_op jit(solution)/shard_map/ppermute | solution.py:51
  29.8 1.5 %collective-permute-start.10 = (bf16[2,336,128]{2,1,0:T(8,128)(2,1)S(1)}, bf16[2,336,128]{2,1,0:T(8,128)(2,1)S(1)}, u32[]{:S(2)}, u32[]{:S(2)}) collective-permute-start(bf16[2,336,128]{2,1,0:T(8,128)(2,1)S(1)} %pad_maximum_fusion), channel_id=1, source_target_pairs={{0,4},{4,0},{8,12},{12,8},{1,5},{5,1},{9,13},{13,9},{2,6},{6,2},{1... | collective-permute-start | bytes 516104 | tf_op jit(solution)/shard_map/ppermute | solution.py:56
  31.3 1.0 %collective-permute-done.6 = bf16[608,128]{1,0:T(8,128)(2,1)S(1)} collective-permute-done((bf16[608,128]{1,0:T(8,128)(2,1)S(1)}, bf16[608,128]{1,0:T(8,128)(2,1)S(1)}, u32[]{:S(2)}, u32[]{:S(2)}) %collective-permute-start.6) | collective-permute-done | bytes 155680 | tf_op jit(solution)/shard_map/ppermute | solution.py:56
  32.4 0.5 %collective-permute-start.7 = (bf16[608,128]{1,0:T(8,128)(2,1)S(1)}, bf16[608,128]{1,0:T(8,128)(2,1)S(1)}, u32[]{:S(2)}, u32[]{:S(2)}) collective-permute-start(bf16[608,128]{1,0:T(8,128)(2,1)S(1)} %add_convert_fusion.2), channel_id=1, source_target_pairs={{0,8},{4,12},{8,0},{12,4},{1,9},{5,13},{9,1},{13,5},{2,10},{6,14},... | collective-permute-start | bytes 466952 | tf_op jit(solution)/shard_map/ppermute | solution.py:56
  32.9 4.0 %collective-permute-done.10 = bf16[2,336,128]{2,1,0:T(8,128)(2,1)S(1)} collective-permute-done((bf16[2,336,128]{2,1,0:T(8,128)(2,1)S(1)}, bf16[2,336,128]{2,1,0:T(8,128)(2,1)S(1)}, u32[]{:S(2)}, u32[]{:S(2)}) %collective-permute-start.10) | collective-permute-done | bytes 172064 | tf_op jit(solution)/shard_map/ppermute | solution.py:56
  36.9 0.1 collective-permute-start.11
  37.0 0.0 collective-permute-done.8.above_ref
  37.0 3.5 %agg_map.1 = bf16[16,96,128]{2,1,0:T(8,128)(2,1)} custom-call(f32[144,96]{1,0:T(8,128)S(1)} %get-tuple-element.59.y_ref, f32[144,128]{1,0:T(8,128)S(1)} %get-tuple-element.55.refs_2_.key_ref, f32[96,128]{1,0:T(8,128)S(1)} %collective-permute-done.8.above_ref), custom_call_target="tpu_custom_call" | custom-call | bytes 12915000 | tf_op jit(solution)/shard_map/agg_map/pallas_call | solution.py:621
  40.5 0.8 %collective-permute-done.7 = bf16[608,128]{1,0:T(8,128)(2,1)S(1)} collective-permute-done((bf16[608,128]{1,0:T(8,128)(2,1)S(1)}, bf16[608,128]{1,0:T(8,128)(2,1)S(1)}, u32[]{:S(2)}, u32[]{:S(2)}) %collective-permute-start.7) | collective-permute-done | bytes 155680 | tf_op jit(solution)/shard_map/ppermute | solution.py:56
  41.4 1.5 %collective-permute-start.9 = (bf16[608,128]{1,0:T(8,128)(2,1)S(1)}, bf16[608,128]{1,0:T(8,128)(2,1)S(1)}, u32[]{:S(2)}, u32[]{:S(2)}) collective-permute-start(bf16[608,128]{1,0:T(8,128)(2,1)S(1)} %add_convert_fusion.1), channel_id=1, source_target_pairs={{0,4},{4,0},{8,12},{12,8},{1,5},{5,1},{9,13},{13,9},{2,6},{6,2},{1... | collective-permute-start | bytes 466952 | tf_op jit(solution)/shard_map/ppermute | solution.py:56
  42.8 1.4 %collective-permute-done.11.refs_2_ = bf16[4,336,128]{2,1,0:T(8,128)(2,1)S(1)} collective-permute-done((bf16[4,336,128]{2,1,0:T(8,128)(2,1)S(1)}, bf16[4,336,128]{2,1,0:T(8,128)(2,1)S(1)}, u32[]{:S(2)}, u32[]{:S(2)}) %collective-permute-start.11) | collective-permute-done | bytes 344096 | tf_op jit(solution)/shard_map/ppermute | solution.py:56
  44.2 1.4 %agg_weight_grad.1 = (f32[9,192,96]{2,1,0:T(8,128)S(1)}, bf16[9,192,96]{2,1,0:T(8,128)(2,1)S(1)}) custom-call(s32[1]{0:T(128)} %bitcast.9.refs_0_, bf16[4,336,128]{2,1,0:T(8,128)(2,1)S(1)} %constant_dynamic-update-slice_fusion.refs_1_, bf16[4,336,128]{2,1,0:T(8,128)(2,1)S(1)} %collective-permute-done.11.refs_2_), custom_call_target="tpu_custom_call" | custom-call | bytes 5166000 | tf_op jit(solution)/shard_map/agg_weight_grad/pallas_call | solution.py:636
  45.7 0.1 collective-permute-start.12
  45.7 0.9 %collective-permute-done.9 = bf16[608,128]{1,0:T(8,128)(2,1)S(1)} collective-permute-done((bf16[608,128]{1,0:T(8,128)(2,1)S(1)}, bf16[608,128]{1,0:T(8,128)(2,1)S(1)}, u32[]{:S(2)}, u32[]{:S(2)}) %collective-permute-start.9) | collective-permute-done | bytes 155680 | tf_op jit(solution)/shard_map/ppermute | solution.py:56
  46.7 0.1 collective-permute-start.13
  46.8 0.7 %collective-permute-done.12 = bf16[9,192,96]{2,1,0:T(8,128)(2,1)S(1)} collective-permute-done((bf16[9,192,96]{2,1,0:T(8,128)(2,1)S(1)}, bf16[9,192,96]{2,1,0:T(8,128)(2,1)S(1)}, u32[]{:S(2)}, u32[]{:S(2)}) %collective-permute-start.12) | collective-permute-done | bytes 331808 | tf_op jit(solution)/shard_map/ppermute | solution.py:56
  47.5 1.0 %convert_add_fusion = f32[9,192,96]{2,1,0:T(8,128)} fusion(f32[9,192,96]{2,1,0:T(8,128)S(1)} %get-tuple-element.64, bf16[9,192,96]{2,1,0:T(8,128)(2,1)S(1)} %collective-permute-done.12), kind=kLoop, calls=%fused_computation | loop fusion | flops 331776 | bytes 1658880 | tf_op jit(solution)/shard_map/add | solution.py:658
  48.5 0.9 %unpack.1 = (f32[49,96]{1,0:T(8,128)}, f32[96,384]{1,0:T(8,128)}, f32[96,384]{1,0:T(8,128)}, f32[192,384]{1,0:T(8,128)}) custom-call(s32[1]{0:T(128)} %bitcast.chan_ref.refs_0_, bf16[608,128]{1,0:T(8,128)(2,1)S(1)} %add_convert_fusion.own_ref, bf16[608,128]{1,0:T(8,128)(2,1)S(1)} %collective-permute-done.13.peer_ref), custom_call_target="tpu_custom_call" | custom-call | bytes 5535000 | tf_op jit(solution)/shard_map/unpack/pallas_call | solution.py:665
  (20 shorter events, 0.3 us)
Async XLA Ops:
  0.6 15.0 %copy-start = (f32[1,16,96,128]{3,2,1,0:T(8,128)S(1)}, f32[1,16,96,128]{3,2,1,0:T(8,128)}, u32[]{:S(2)}) copy-start(f32[1,16,96,128]{3,2,1,0:T(8,128)} %cot_ref.1) | copy-start | bytes 2359300
  2.5 7.0 %copy-start.9 = (bf16[96,128]{1,0:T(8,128)(2,1)S(1)}, bf16[96,128]{1,0:T(8,128)(2,1)}, u32[]{:S(2)}) copy-start(bf16[96,128]{1,0:T(8,128)(2,1)} %get-tuple-element.41) | copy-start | bytes 73732
  2.5 13.1 %all-to-all-start = ((bf16[8,56,128]{2,1,0:T(8,128)(2,1)}), bf16[8,56,128]{2,1,0:T(8,128)(2,1)S(1)}, u32[]{:S(2)}, u32[]{:S(2)}) async-start(bf16[8,56,128]{2,1,0:T(8,128)(2,1)} %get-tuple-element.40), calls=%async_computation | async-start | bytes 229376 | tf_op jit(solution)/shard_map/all_to_all | solution.py:462
  9.0 12.4 %collective-permute-start.2 = (bf16[9,192,96]{2,1,0:T(8,128)(2,1)}, bf16[9,192,96]{2,1,0:T(8,128)(2,1)S(1)}, u32[]{:S(2)}, u32[]{:S(2)}) collective-permute-start(bf16[9,192,96]{2,1,0:T(8,128)(2,1)} %refs_1_.1), channel_id=1, source_target_pairs={{0,1},{1,0},{2,3},{3,2},{4,5},{5,4},{6,7},{7,6},{8,9},{9,8},{10,11... | collective-permute-start | bytes 995336 | tf_op jit(solution)/shard_map/ppermute | solution.py:56
  9.5 6.1 %collective-permute-start = (bf16[96,128]{1,0:T(8,128)(2,1)S(1)}, bf16[96,128]{1,0:T(8,128)(2,1)S(1)}, u32[]{:S(2)}, u32[]{:S(2)}) collective-permute-start(bf16[96,128]{1,0:T(8,128)(2,1)S(1)} %copy-done.9), channel_id=1, source_target_pairs={{4,0},{8,4},{12,8},{5,1},{9,5},{13,9},{6,2},{10,6},{14,10},{7,3},{... | collective-permute-start | bytes 73736 | tf_op jit(solution)/shard_map/ppermute | solution.py:51
  15.6 0.9 %copy-start.2 = (bf16[384,192]{0,1:T(8,128)(2,1)S(1)}, bf16[384,192]{0,1:T(8,128)(2,1)}, u32[]{:S(2)}) copy-start(bf16[384,192]{0,1:T(8,128)(2,1)} %param.20) | copy-start | bytes 442372
  15.6 1.0 %copy-start.3 = (bf16[96,384]{1,0:T(8,128)(2,1)S(1)}, bf16[96,384]{1,0:T(8,128)(2,1)}, u32[]{:S(2)}) copy-start(bf16[96,384]{1,0:T(8,128)(2,1)} %refs_14_.1) | copy-start | bytes 221188
  15.6 1.0 %copy-start.4 = (bf16[384,96]{0,1:T(8,128)(2,1)S(1)}, bf16[384,96]{0,1:T(8,128)(2,1)}, u32[]{:S(2)}) copy-start(bf16[384,96]{0,1:T(8,128)(2,1)} %param.17) | copy-start | bytes 221188
  15.7 1.0 %copy-start.5 = (f32[49,96]{1,0:T(8,128)S(1)}, f32[49,96]{1,0:T(8,128)}, u32[]{:S(2)}) copy-start(f32[49,96]{1,0:T(8,128)} %dw_ref.1) | copy-start | bytes 56452
  15.7 1.0 %copy-start.6 = (f32[96]{0:T(128)S(1)}, f32[96]{0:T(128)}, u32[]{:S(2)}) copy-start(f32[96]{0:T(128)} %param.15) | copy-start | bytes 1156
  15.7 1.0 %copy-start.7 = (f32[96]{0:T(128)S(1)}, f32[96]{0:T(128)}, u32[]{:S(2)}) copy-start(f32[96]{0:T(128)} %param.18) | copy-start | bytes 1156
  15.7 0.9 %copy-start.8 = (f32[96]{0:T(128)S(1)}, f32[96]{0:T(128)}, u32[]{:S(2)}) copy-start(f32[96]{0:T(128)} %param.19) | copy-start | bytes 1156
  16.2 5.2 %copy-start.1 = (bf16[9,192,96]{2,1,0:T(8,128)(2,1)S(1)}, bf16[9,192,96]{2,1,0:T(8,128)(2,1)}, u32[]{:S(2)}) copy-start(bf16[9,192,96]{2,1,0:T(8,128)(2,1)} %refs_1_.1) | copy-start | bytes 995332
  16.2 2.9 %collective-permute-start.1 = (bf16[72,128]{1,0:T(8,128)(2,1)S(1)}, bf16[72,128]{1,0:T(8,128)(2,1)S(1)}, u32[]{:S(2)}, u32[]{:S(2)}) collective-permute-start(bf16[72,128]{1,0:T(8,128)(2,1)S(1)} %get-tuple-element.43), channel_id=1, source_target_pairs={{0,1},{1,0},{2,3},{3,2},{4,5},{5,4},{6,7},{7,6},{8,9},{9,8},{10,11... | collective-permute-start | bytes 55304 | tf_op jit(solution)/shard_map/ppermute | solution.py:56
  18.9 5.5 %collective-permute-start.5 = (bf16[1,192,128]{2,1,0:T(8,128)(2,1)S(1)}, bf16[1,192,128]{2,1,0:T(8,128)(2,1)S(1)}, u32[]{:S(2)}, u32[]{:S(2)}) collective-permute-start(bf16[1,192,128]{2,1,0:T(8,128)(2,1)S(1)} %get-tuple-element.54), channel_id=1, source_target_pairs={{0,1},{1,0},{2,3},{3,2},{4,5},{5,4},{6,7},{7,6},{8,9},{9,8},{10,11... | collective-permute-start | bytes 147464 | tf_op jit(solution)/shard_map/ppermute | solution.py:56
  19.1 7.6 %collective-permute-start.4 = (bf16[1,336,128]{2,1,0:T(8,128)(2,1)S(1)}, bf16[1,336,128]{2,1,0:T(8,128)(2,1)S(1)}, u32[]{:S(2)}, u32[]{:S(2)}) collective-permute-start(bf16[1,336,128]{2,1,0:T(8,128)(2,1)S(1)} %pad_maximum_fusion.2), channel_id=1, source_target_pairs={{0,8},{4,12},{8,0},{12,4},{1,9},{5,13},{9,1},{13,5},{2,10},{6,14},... | collective-permute-start | bytes 258056 | tf_op jit(solution)/shard_map/ppermute | solution.py:56
  24.3 2.4 %collective-permute-start.3 = (bf16[608,128]{1,0:T(8,128)(2,1)S(1)}, bf16[608,128]{1,0:T(8,128)(2,1)S(1)}, u32[]{:S(2)}, u32[]{:S(2)}) collective-permute-start(bf16[608,128]{1,0:T(8,128)(2,1)S(1)} %get-tuple-element.53), channel_id=1, source_target_pairs={{0,1},{1,0},{2,3},{3,2},{4,5},{5,4},{6,7},{7,6},{8,9},{9,8},{10,11... | collective-permute-start | bytes 466952 | tf_op jit(solution)/shard_map/ppermute | solution.py:56
  26.8 5.5 %collective-permute-start.6 = (bf16[608,128]{1,0:T(8,128)(2,1)S(1)}, bf16[608,128]{1,0:T(8,128)(2,1)S(1)}, u32[]{:S(2)}, u32[]{:S(2)}) collective-permute-start(bf16[608,128]{1,0:T(8,128)(2,1)S(1)} %convert_add_fusion.1), channel_id=1, source_target_pairs={{0,2},{2,0},{1,3},{3,1},{4,6},{6,4},{5,7},{7,5},{8,10},{10,8},{9,1... | collective-permute-start | bytes 466952 | tf_op jit(solution)/shard_map/ppermute | solution.py:56
  28.3 8.7 %collective-permute-start.8 = (f32[96,128]{1,0:T(8,128)S(1)}, f32[96,128]{1,0:T(8,128)S(1)}, u32[]{:S(2)}, u32[]{:S(2)}) collective-permute-start(f32[96,128]{1,0:T(8,128)S(1)} %get-tuple-element.60), channel_id=1, source_target_pairs={{0,4},{4,8},{8,12},{1,5},{5,9},{9,13},{2,6},{6,10},{10,14},{3,7},{... | collective-permute-start | bytes 147464 | tf_op jit(solution)/shard_map/ppermute | solution.py:51
  29.8 7.1 %collective-permute-start.10 = (bf16[2,336,128]{2,1,0:T(8,128)(2,1)S(1)}, bf16[2,336,128]{2,1,0:T(8,128)(2,1)S(1)}, u32[]{:S(2)}, u32[]{:S(2)}) collective-permute-start(bf16[2,336,128]{2,1,0:T(8,128)(2,1)S(1)} %pad_maximum_fusion), channel_id=1, source_target_pairs={{0,4},{4,0},{8,12},{12,8},{1,5},{5,1},{9,13},{13,9},{2,6},{6,2},{1... | collective-permute-start | bytes 516104 | tf_op jit(solution)/shard_map/ppermute | solution.py:56
  32.4 8.9 %collective-permute-start.7 = (bf16[608,128]{1,0:T(8,128)(2,1)S(1)}, bf16[608,128]{1,0:T(8,128)(2,1)S(1)}, u32[]{:S(2)}, u32[]{:S(2)}) collective-permute-start(bf16[608,128]{1,0:T(8,128)(2,1)S(1)} %add_convert_fusion.2), channel_id=1, source_target_pairs={{0,8},{4,12},{8,0},{12,4},{1,9},{5,13},{9,1},{13,5},{2,10},{6,14},... | collective-permute-start | bytes 466952 | tf_op jit(solution)/shard_map/ppermute | solution.py:56
  36.9 7.3 %collective-permute-start.11 = (bf16[4,336,128]{2,1,0:T(8,128)(2,1)S(1)}, bf16[4,336,128]{2,1,0:T(8,128)(2,1)S(1)}, u32[]{:S(2)}, u32[]{:S(2)}) collective-permute-start(bf16[4,336,128]{2,1,0:T(8,128)(2,1)S(1)} %constant_dynamic-update-slice_fusion.refs_1_), channel_id=1, source_target_pairs={{0,2},{2,0},{1,3},{3,1},{4,6},{6,4},{5,7},{7,5},{8,10},{10,8},{9,1... | collective-permute-start | bytes 1032200 | tf_op jit(solution)/shard_map/ppermute | solution.py:56
  41.4 5.3 %collective-permute-start.9 = (bf16[608,128]{1,0:T(8,128)(2,1)S(1)}, bf16[608,128]{1,0:T(8,128)(2,1)S(1)}, u32[]{:S(2)}, u32[]{:S(2)}) collective-permute-start(bf16[608,128]{1,0:T(8,128)(2,1)S(1)} %add_convert_fusion.1), channel_id=1, source_target_pairs={{0,4},{4,0},{8,12},{12,8},{1,5},{5,1},{9,13},{13,9},{2,6},{6,2},{1... | collective-permute-start | bytes 466952 | tf_op jit(solution)/shard_map/ppermute | solution.py:56
  45.7 1.9 %collective-permute-start.12 = (bf16[9,192,96]{2,1,0:T(8,128)(2,1)S(1)}, bf16[9,192,96]{2,1,0:T(8,128)(2,1)S(1)}, u32[]{:S(2)}, u32[]{:S(2)}) collective-permute-start(bf16[9,192,96]{2,1,0:T(8,128)(2,1)S(1)} %get-tuple-element.65), channel_id=1, source_target_pairs={{0,1},{1,0},{2,3},{3,2},{4,5},{5,4},{6,7},{7,6},{8,9},{9,8},{10,11... | collective-permute-start | bytes 995336 | tf_op jit(solution)/shard_map/ppermute | solution.py:56
  46.7 1.8 %collective-permute-start.13 = (bf16[608,128]{1,0:T(8,128)(2,1)S(1)}, bf16[608,128]{1,0:T(8,128)(2,1)S(1)}, u32[]{:S(2)}, u32[]{:S(2)}) collective-permute-start(bf16[608,128]{1,0:T(8,128)(2,1)S(1)} %add_convert_fusion.own_ref), channel_id=1, source_target_pairs={{0,1},{1,0},{2,3},{3,2},{4,5},{5,4},{6,7},{7,6},{8,9},{9,8},{10,11... | collective-permute-start | bytes 466952 | tf_op jit(solution)/shard_map/ppermute | solution.py:56
